TPU v7x, 32 devices: a whole 2x2x4 slice. The times are simulated.
32 devices in a mesh: group: 8 (over y, x, core), replica: 4 (over z).
Axes of the slice: x: 2, y: 2, z: 4, core: 2. Of those that a mesh axis runs over, the one named last changes fastest.
Arguments:
- inputs: bfloat16 [64, 512, 768], P(('group', 'replica')), may hold values from -6 to 6
- cotangent: bfloat16 [64, 512, 768], P(('group', 'replica')), may hold values from -6 to 6
- lengths: int32 [64], P(('group', 'replica')), may hold values from 128 to 512, as said below
- query_weight: bfloat16 [768, 768], P('group'), may hold values from -0.21875 to 0.21875
- key_weight: bfloat16 [768, 768], P('group'), may hold values from -0.21875 to 0.21875
- value_weight: bfloat16 [768, 768], P('group'), may hold values from -0.21875 to 0.21875
- out_weight: bfloat16 [768, 768], P('group'), may hold values from -3.5 to 3.5
- in_weight: bfloat16 [768, 3072], P('group'), may hold values from -0.21875 to 0.21875
- back_weight: bfloat16 [3072, 768], P('group'), may hold values from -0.109375 to 0.109375
- query_bias: bfloat16 [768], P('group'), may hold values from -1.796875 to 1.796875
- value_bias: bfloat16 [768], P('group'), may hold values from -1.796875 to 1.796875
- out_bias: bfloat16 [768], P('group'), may hold values from -1.796875 to 1.796875
- in_bias: bfloat16 [3072], P('group'), may hold values from -1.796875 to 1.796875
- back_bias: bfloat16 [768], P('group'), may hold values from -1.796875 to 1.796875
- first_gain: bfloat16 [768], P('group'), may hold values from 0.5 to 1.5
- first_shift: bfloat16 [768], P('group'), may hold values from -1.796875 to 1.796875
- second_gain: bfloat16 [768], P('group'), may hold values from 0.5 to 1.5
- second_shift: bfloat16 [768], P('group'), may hold values from -1.796875 to 1.796875
Outputs:
- layer_out: bfloat16 [64, 512, 768], P(('group', 'replica'))
- input_grad: bfloat16 [64, 512, 768], P(('group', 'replica'))
- query_weight_grad: float32 [768, 768], P('group')
- key_weight_grad: float32 [768, 768], P('group')
- value_weight_grad: float32 [768, 768], P('group')
- out_weight_grad: float32 [768, 768], P('group')
- in_weight_grad: float32 [768, 3072], P('group')
- back_weight_grad: float32 [3072, 768], P('group')
- query_bias_grad: float32 [768], P('group')
- value_bias_grad: float32 [768], P('group')
- out_bias_grad: float32 [768], P('group')
- in_bias_grad: float32 [3072], P('group')
- back_bias_grad: float32 [768], P('group')
- first_gain_grad: float32 [768], P('group')
- first_shift_grad: float32 [768], P('group')
- second_gain_grad: float32 [768], P('group')
- second_shift_grad: float32 [768], P('group')
Inputs may be any that keep to these rules, and one draw needn't show every extreme that they name: `lengths`: each sequence's valid tokens fill its first slots; some sequence has all 512 slots valid.
All inputs are finite; a program needn't handle non-finite values.
Results may differ from a plain program's by a relative error of at most 0.02.
Values may be sent and summed in bfloat16 or wider, within the bound.
No kernel may reach another device: no remote copies, remote signals or barrier semaphores. Data moves between devices by JAX's collectives and lax.ppermute only.
A program may use at most 192 MiB of HBM per device.

v0:
```python
import math

import jax
import jax.numpy as jnp
from jax import lax
from jax.sharding import PartitionSpec as P

HEADS = 12
HEAD_DIM = 64


NORM_EPS = 1e-12
inverse_root_two = 0.7071067811865476
inverse_root_tau = 0.3989422804014327


def for_sending(array):
    return jax.tree.map(lambda a: a.astype(jnp.bfloat16) if a.dtype == jnp.float32 else a, array)


def project(left, right):
    return jnp.dot(left, right, preferred_element_type=jnp.float32)


def outer_sum(left, right):
    return jnp.einsum("rd,re->de", left, right, preferred_element_type=jnp.float32)


def back_project(grad_rows, weight_full):
    return jnp.einsum("re,de->rd", grad_rows, weight_full, preferred_element_type=jnp.float32)


def norm_forward(hidden, norm_gain, norm_shift):
    centre = hidden - jnp.mean(hidden, -1, keepdims=True)
    inverse = lax.rsqrt(jnp.mean(centre * centre, -1, keepdims=True) + NORM_EPS)
    normed = centre * inverse
    return (normed * norm_gain + norm_shift, normed, inverse)


def norm_backward(grad_out, norm_gain, normed, inverse):
    scaled = grad_out * norm_gain
    centred = (
        scaled
        - jnp.mean(scaled, -1, keepdims=True)
        - normed * jnp.mean(scaled * normed, -1, keepdims=True)
    )
    return (inverse * centred, jnp.sum(grad_out * normed, 0), jnp.sum(grad_out, 0))


def gelu_slope(hidden):
    normal_cdf = 0.5 * (1.0 + lax.erf(hidden * inverse_root_two))
    density = jnp.exp(-0.5 * hidden * hidden) * inverse_root_tau
    return normal_cdf + hidden * density


def per_device(
    inputs,
    cotangent,
    lengths,
    query_weight,
    key_weight,
    value_weight,
    out_weight,
    in_weight,
    back_weight,
    query_bias,
    value_bias,
    out_bias,
    in_bias,
    back_bias,
    first_gain,
    first_shift,
    second_gain,
    second_shift,
):
    whole = (
        lax.all_gather(query_weight, "group", axis=0, tiled=True),
        lax.all_gather(key_weight, "group", axis=0, tiled=True),
        lax.all_gather(value_weight, "group", axis=0, tiled=True),
        lax.all_gather(out_weight, "group", axis=0, tiled=True),
        lax.all_gather(in_weight, "group", axis=0, tiled=True),
        lax.all_gather(back_weight, "group", axis=0, tiled=True),
        lax.all_gather(query_bias, "group", axis=0, tiled=True),
        lax.all_gather(value_bias, "group", axis=0, tiled=True),
        lax.all_gather(out_bias, "group", axis=0, tiled=True),
        lax.all_gather(in_bias, "group", axis=0, tiled=True),
        lax.all_gather(back_bias, "group", axis=0, tiled=True),
        lax.all_gather(first_gain, "group", axis=0, tiled=True),
        lax.all_gather(first_shift, "group", axis=0, tiled=True),
        lax.all_gather(second_gain, "group", axis=0, tiled=True),
        lax.all_gather(second_shift, "group", axis=0, tiled=True),
    )
    (
        full_query,
        full_key,
        full_value,
        full_out,
        full_in,
        full_back,
        bias_query,
        bias_value,
        bias_out,
        bias_in,
        bias_back,
        gain_first,
        shift_first,
        gain_second,
        shift_second,
    ) = whole
    seq_count, slot_count, model_width = inputs.shape
    total_rows = seq_count * slot_count
    block_rows = min(512, slot_count)
    seq_blocks = slot_count // block_rows
    item_count = seq_count * seq_blocks
    score_scale = 1.0 / math.sqrt(HEAD_DIM)
    flat_rows = inputs.reshape(total_rows, model_width)
    positions = lax.broadcasted_iota(jnp.int32, (seq_count, slot_count), 1)
    key_valid = positions < lengths[:, None]
    row_valid = key_valid.reshape(total_rows, 1).astype(jnp.float32)
    queries = (project(flat_rows, full_query) + bias_query.astype(jnp.float32)).astype(jnp.bfloat16)
    key_rows = project(flat_rows, full_key).astype(jnp.bfloat16)
    value_rows = (project(flat_rows, full_value) + bias_value.astype(jnp.float32)).astype(
        jnp.bfloat16
    )
    query_blocks = queries.reshape(item_count, block_rows, HEADS, HEAD_DIM)
    key_seqs = key_rows.reshape(seq_count, slot_count, HEADS, HEAD_DIM)
    value_seqs = value_rows.reshape(seq_count, slot_count, HEADS, HEAD_DIM)
    item_ids = jnp.arange(item_count, dtype=jnp.int32)

    def select_seq(item_id):
        seq_id = item_id // seq_blocks
        return (
            lax.dynamic_index_in_dim(key_seqs, seq_id, 0, False),
            lax.dynamic_index_in_dim(value_seqs, seq_id, 0, False),
            lax.dynamic_index_in_dim(key_valid, seq_id, 0, False),
        )

    def block_scores(query_part, key_part, valid_part):
        scores = (
            jnp.einsum("qhd,khd->hqk", query_part, key_part, preferred_element_type=jnp.float32)
            * score_scale
        )
        return jnp.where(valid_part[None, None, :], scores, -1e30)

    def attend(packed):
        query_part, item_id = packed
        key_part, value_part, valid_part = select_seq(item_id)
        scores = block_scores(query_part, key_part, valid_part)
        row_peak = jnp.max(scores, -1, keepdims=True)
        lifted = jnp.exp(scores - row_peak)
        normalizer = jnp.sum(lifted, -1, keepdims=True)
        soft_weights = (lifted / normalizer).astype(jnp.bfloat16)
        mixed_heads = jnp.einsum(
            "hqk,khd->qhd", soft_weights, value_part, preferred_element_type=jnp.float32
        )
        return (mixed_heads.astype(jnp.bfloat16), (row_peak + jnp.log(normalizer))[:, :, 0])

    mixed_blocks, log_sums = lax.map(attend, (query_blocks, item_ids))
    mixed_rows = mixed_blocks.reshape(total_rows, model_width)
    branch = project(mixed_rows, full_out) + bias_out.astype(jnp.float32)
    after_attn, normed_first, inverse_first = norm_forward(
        flat_rows.astype(jnp.float32) + branch,
        gain_first.astype(jnp.float32),
        shift_first.astype(jnp.float32),
    )
    after_low = after_attn.astype(jnp.bfloat16)
    hidden = project(after_low, full_in) + bias_in.astype(jnp.float32)
    active = jax.nn.gelu(hidden, approximate=False).astype(jnp.bfloat16)
    ffn_out = project(active, full_back) + bias_back.astype(jnp.float32)
    result_rows, normed_second, inverse_second = norm_forward(
        after_attn + ffn_out, gain_second.astype(jnp.float32), shift_second.astype(jnp.float32)
    )
    layer_out = result_rows.astype(jnp.bfloat16).reshape(seq_count, slot_count, model_width)
    again = (
        lax.all_gather(query_weight, "group", axis=0, tiled=True),
        lax.all_gather(key_weight, "group", axis=0, tiled=True),
        lax.all_gather(value_weight, "group", axis=0, tiled=True),
        lax.all_gather(out_weight, "group", axis=0, tiled=True),
        lax.all_gather(in_weight, "group", axis=0, tiled=True),
        lax.all_gather(back_weight, "group", axis=0, tiled=True),
        lax.all_gather(query_bias, "group", axis=0, tiled=True),
        lax.all_gather(value_bias, "group", axis=0, tiled=True),
        lax.all_gather(out_bias, "group", axis=0, tiled=True),
        lax.all_gather(in_bias, "group", axis=0, tiled=True),
        lax.all_gather(back_bias, "group", axis=0, tiled=True),
        lax.all_gather(first_gain, "group", axis=0, tiled=True),
        lax.all_gather(first_shift, "group", axis=0, tiled=True),
        lax.all_gather(second_gain, "group", axis=0, tiled=True),
        lax.all_gather(second_shift, "group", axis=0, tiled=True),
    )
    (
        back_query,
        back_key,
        back_value,
        back_out,
        back_in,
        back_ffn,
        unused_one,
        unused_two,
        unused_three,
        unused_four,
        unused_five,
        gain_first_b,
        unused_six,
        gain_second_b,
        unused_seven,
    ) = again
    grad_result = cotangent.reshape(total_rows, model_width).astype(jnp.float32) * row_valid
    grad_h2, second_gain_grad, second_shift_grad = norm_backward(
        grad_result, gain_second_b.astype(jnp.float32), normed_second, inverse_second
    )
    grad_ffn = grad_h2.astype(jnp.bfloat16)
    back_bias_grad = jnp.sum(grad_ffn.astype(jnp.float32), 0)
    back_weight_grad = outer_sum(active, grad_ffn)
    grad_hidden = (back_project(grad_ffn, back_ffn) * gelu_slope(hidden)).astype(jnp.bfloat16)
    in_bias_grad = jnp.sum(grad_hidden.astype(jnp.float32), 0)
    in_weight_grad = outer_sum(after_low, grad_hidden)
    grad_after = back_project(grad_hidden, back_in) + grad_h2
    grad_h1, first_gain_grad, first_shift_grad = norm_backward(
        grad_after, gain_first_b.astype(jnp.float32), normed_first, inverse_first
    )
    grad_branch = grad_h1.astype(jnp.bfloat16)
    out_bias_grad = jnp.sum(grad_branch.astype(jnp.float32), 0)
    out_weight_grad = outer_sum(mixed_rows, grad_branch)
    grad_mixed = back_project(grad_branch, back_out).astype(jnp.bfloat16)

    def attend_back(packed):
        query_part, grad_part, lse_part, item_id = packed
        key_part, value_part, valid_part = select_seq(item_id)
        scores = block_scores(query_part, key_part, valid_part)
        soft_weights = jnp.exp(scores - lse_part[:, :, None])
        grad_weights = jnp.einsum(
            "qhd,khd->hqk", grad_part, value_part, preferred_element_type=jnp.float32
        )
        grad_values = jnp.einsum(
            "hqk,qhd->khd",
            soft_weights.astype(jnp.bfloat16),
            grad_part,
            preferred_element_type=jnp.float32,
        )
        row_inner = jnp.sum(soft_weights * grad_weights, -1, keepdims=True)
        grad_scores = (soft_weights * (grad_weights - row_inner)).astype(jnp.bfloat16)
        grad_queries = (
            jnp.einsum("hqk,khd->qhd", grad_scores, key_part, preferred_element_type=jnp.float32)
            * score_scale
        )
        grad_keys = (
            jnp.einsum("hqk,qhd->khd", grad_scores, query_part, preferred_element_type=jnp.float32)
            * score_scale
        )
        return (grad_queries, grad_keys, grad_values)

    query_grad_blocks, key_grad_items, value_grad_items = lax.map(
        attend_back,
        (
            query_blocks,
            grad_mixed.reshape(item_count, block_rows, HEADS, HEAD_DIM),
            log_sums,
            item_ids,
        ),
    )
    grad_queries = query_grad_blocks.reshape(total_rows, model_width).astype(jnp.bfloat16)
    grad_keys = key_grad_items.reshape(seq_count, seq_blocks, slot_count, model_width).sum(1)
    grad_keys = grad_keys.reshape(total_rows, model_width).astype(jnp.bfloat16)
    grad_values = value_grad_items.reshape(seq_count, seq_blocks, slot_count, model_width).sum(1)
    grad_values = grad_values.reshape(total_rows, model_width).astype(jnp.bfloat16)
    query_bias_grad = jnp.sum(grad_queries.astype(jnp.float32), 0)
    value_bias_grad = jnp.sum(grad_values.astype(jnp.float32), 0)
    query_weight_grad = outer_sum(flat_rows, grad_queries)
    key_weight_grad = outer_sum(flat_rows, grad_keys)
    value_weight_grad = outer_sum(flat_rows, grad_values)
    input_rows = (
        grad_h1
        + back_project(grad_queries, back_query)
        + back_project(grad_keys, back_key)
        + back_project(grad_values, back_value)
    )
    input_grad = input_rows.astype(jnp.bfloat16).reshape(seq_count, slot_count, model_width)
    owned = (
        lax.psum_scatter(
            query_weight_grad.astype(jnp.bfloat16), "group", scatter_dimension=0, tiled=True
        ).astype(jnp.float32),
        lax.psum_scatter(
            key_weight_grad.astype(jnp.bfloat16), "group", scatter_dimension=0, tiled=True
        ).astype(jnp.float32),
        lax.psum_scatter(
            value_weight_grad.astype(jnp.bfloat16), "group", scatter_dimension=0, tiled=True
        ).astype(jnp.float32),
        lax.psum_scatter(
            out_weight_grad.astype(jnp.bfloat16), "group", scatter_dimension=0, tiled=True
        ).astype(jnp.float32),
        lax.psum_scatter(
            in_weight_grad.astype(jnp.bfloat16), "group", scatter_dimension=0, tiled=True
        ).astype(jnp.float32),
        lax.psum_scatter(
            back_weight_grad.astype(jnp.bfloat16), "group", scatter_dimension=0, tiled=True
        ).astype(jnp.float32),
        lax.psum_scatter(
            query_bias_grad.astype(jnp.bfloat16), "group", scatter_dimension=0, tiled=True
        ).astype(jnp.float32),
        lax.psum_scatter(
            value_bias_grad.astype(jnp.bfloat16), "group", scatter_dimension=0, tiled=True
        ).astype(jnp.float32),
        lax.psum_scatter(
            out_bias_grad.astype(jnp.bfloat16), "group", scatter_dimension=0, tiled=True
        ).astype(jnp.float32),
        lax.psum_scatter(
            in_bias_grad.astype(jnp.bfloat16), "group", scatter_dimension=0, tiled=True
        ).astype(jnp.float32),
        lax.psum_scatter(
            back_bias_grad.astype(jnp.bfloat16), "group", scatter_dimension=0, tiled=True
        ).astype(jnp.float32),
        lax.psum_scatter(
            first_gain_grad.astype(jnp.bfloat16), "group", scatter_dimension=0, tiled=True
        ).astype(jnp.float32),
        lax.psum_scatter(
            first_shift_grad.astype(jnp.bfloat16), "group", scatter_dimension=0, tiled=True
        ).astype(jnp.float32),
        lax.psum_scatter(
            second_gain_grad.astype(jnp.bfloat16), "group", scatter_dimension=0, tiled=True
        ).astype(jnp.float32),
        lax.psum_scatter(
            second_shift_grad.astype(jnp.bfloat16), "group", scatter_dimension=0, tiled=True
        ).astype(jnp.float32),
    )
    summed = tuple(
        jax.tree.map(
            lambda part: part.astype(jnp.float32), lax.psum(for_sending(tuple(owned)), "replica")
        )
    )
    return (layer_out, input_grad) + summed


def solution(mesh):
    return jax.shard_map(
        per_device,
        mesh=mesh,
        in_specs=(
            P(("group", "replica"), None, None),
            P(("group", "replica"), None, None),
            P(("group", "replica")),
            P("group", None),
            P("group", None),
            P("group", None),
            P("group", None),
            P("group", None),
            P("group", None),
            P("group"),
            P("group"),
            P("group"),
            P("group"),
            P("group"),
            P("group"),
            P("group"),
            P("group"),
            P("group"),
        ),
        out_specs=(
            P(("group", "replica"), None, None),
            P(("group", "replica"), None, None),
            P("group", None),
            P("group", None),
            P("group", None),
            P("group", None),
            P("group", None),
            P("group", None),
            P("group"),
            P("group"),
            P("group"),
            P("group"),
            P("group"),
            P("group"),
            P("group"),
            P("group"),
            P("group"),
        ),
        check_vma=False,
    )
```

profile of v0, /device:TPU:0, one launch (start us, length us, event | category | flops | bytes accessed | tf_op | source)
XLA Modules:
  0.0 682.1 jit_solution(8906284838521225156)
XLA Ops:
  19.8 25.9 %all-reduce.18 = (bf16[768]{0:T(1024)(128)(2,1)S(1)}, bf16[768]{0:T(1024)(128)(2,1)S(1)}, bf16[768]{0:T(1024)(128)(2,1)S(1)}, bf16[768]{0:T(1024)(128)(2,1)S(1)}...) all-reduce(bf16[768]{0:T(1024)(128)(2,1)S(1)} %dynamic-update-slice, ...), channel_id=1, replica_groups=mesh['group'=8,'replica'=4] {'group'}, use_global_device_ids=true, to_apply=%add.1 | all-reduce | flops 5376 | bytes 21504
  51.0 7.9 %all-gather = bf16[8,1,384]{2,1,0:T(2,128)(2,1)S(1)} all-gather(bf16[1,1,384]{2,1,0:T(2,128)(2,1)S(1)} %reshape.248), channel_id=1, replica_groups=mesh['group'=8,'replica'=4] {'group'}, dimensions={0}, use_global_device_ids=true | all-gather | bytes 6912 | tf_op jit(solution)/shard_map/all_gather | solution.py:86
  58.9 3.2 add_convert_fusion.3
  70.7 17.6 %all-gather.12.cloned.1.call-done = bf16[768,768]{1,0:T(8,128)(2,1)} async-done(((bf16[96,768]{1,0:T(8,128)(2,1)}), bf16[768,768]{1,0:T(8,128)(2,1)}) %all-gather.12.cloned.1.call-update) | async-done | bytes 1179664 | tf_op jit(solution)/shard_map/all_gather | solution.py:78
  88.4 4.3 convolution_convert_fusion.3
  98.6 25.1 %while.30 = (s32[]{:T(128)}, bf16[2,512,12,64]{1,3,2,0:T(8,128)(2,1)}, f32[2,12,512]{2,1,0:T(8,128)S(1)}, s32[2]{0:T(128)S(1)}, bf16[2,512,12,64]{1,3,2,0:T(8,12...) while((s32[]{:T(128)}, ...), condition=%wide.region_3.4_spmd, body=%wide.region_0.3_spmd.sunk | while | flops 843442176 | bytes 47426260 | solution.py:158
  107.0 4.2 fusion.130
  119.5 4.2 fusion.130
  123.7 3.2 copy.81
  128.4 3.9 fusion.77
  134.5 20.1 %all-gather.16.cloned.1.call-done = bf16[768,3072]{1,0:T(8,128)(2,1)} async-done(((bf16[96,3072]{1,0:T(8,128)(2,1)}), bf16[768,3072]{1,0:T(8,128)(2,1)}) %all-gather.16.cloned.1.call-update) | async-done | bytes 4718608 | tf_op jit(solution)/shard_map/all_gather | solution.py:81
  154.6 37.4 %fusion.48 = (bf16[1024,3072]{1,0:T(8,128)(2,1)}, f32[1024,3072]{1,0:T(8,128)}) fusion(f32[3072]{0:T(1024)S(1)} %bitcast.208, bf16[768,3072]{1,0:T(8,128)(2,1)} %all-gather.16.cloned.1.call-done, f32[1024,768]{1,0:T(8,128)} %copy-done.6, f32[768]{0:T(1024)S(1)} %convert_element_type.280, f32[768]{0:T(1024)S(1)} %convert_element_type.279, ...), kind=kOutput, calls=%fused_computation.60 | convolution fusion | flops 5043388416 | bytes 26765312 | tf_op jit(solution)/shard_map/dot_general | solution.py:22
  195.2 9.3 %fusion.78 = (f32[1024]{0:T(1024)S(1)}, f32[1024,768]{1,0:T(8,128)S(1)}) fusion(f32[768]{0:T(1024)S(1)} %copy-done.51, bf16[1024,3072]{1,0:T(8,128)(2,1)} %get-tuple-element.468, bf16[3072,768]{1,0:T(8,128)(2,1)} %all-gather.18.cloned.1.call-done, f32[768]{0:T(1024)S(1)} %convert_element_type.280, f32[768]{0:T(1024)S(1)} %convert_element_type.279, ...), kind=kOutput, calls=%fused_computation.138 | convolution fusion | flops 4837342208 | bytes 17323008 | tf_op jit(solution)/shard_map/dot_general | solution.py:22
  211.5 13.4 %fusion.79 = (bf16[3072]{0:T(1024)(128)(2,1)}, bf16[1024,3072]{1,0:T(8,128)(2,1)S(1)}) fusion(f32[1024,3072]{1,0:T(8,128)} %get-tuple-element.469, f32[3072]{0:T(1024)S(1)} %bitcast.209, bf16[3072,768]{1,0:T(8,128)(2,1)S(1)} %copy-done.54, f32[1024,768]{1,0:T(8,128)S(1)} %get-tuple-element.454), kind=kOutput, calls=%fused_computation.139 | convolution fusion | flops 4870370304 | bytes 26757120 | tf_op jit(solution)/shard_map/re,de->rd/dot_general | solution.py:30
  225.0 6.6 multiply_reduce_fusion.2
  240.3 3.9 reshape.220
  247.1 53.6 %while.31 = (s32[]{:T(128)}, bf16[2,512,12,64]{1,3,2,0:T(8,128)(2,1)}, bf16[2,512,12,64]{1,3,2,0:T(8,128)(2,1)}, bf16[2,512,12,64]{1,3,2,0:T(8,128)(2,1)}, s32[2...) while((s32[]{:T(128)}, ...), condition=%wide.region_14.15_spmd, body=%wide.region_12.14_spmd.sunk | while | flops 2061232128 | bytes 155120608 | solution.py:253
  254.9 7.3 %multiply_reduce_fusion.10 = (f32[12,512]{1,0:T(8,128)S(1)}, f32[12,512,512]{1,2,0:T(8,128)}) fusion(f32[12,512,512]{1,2,0:T(8,128)S(1)} %fusion.139, f32[12,512]{1,0:T(8,128)S(1)} %dynamic-slice_bitcast_fusion.2, pred[512]{0:T(512)(128)(4,1)S(1)} %dynamic-slice_reduce_fusion.5, bf16[2,512,12,64]{1,3,2,0:T(8,128)(2,1)S(1)} %copy-done.3, ...), kind=kOutput, calls=%fused_computation.23.clone.1 | convolution fusion | flops 418375680 | bytes 26796552 | tf_op jit(solution)/shard_map/while/body/eval_jaxpr/qhd,khd->hqk/dot_general | solution.py:232
  262.2 7.2 %multiply_convert_fusion.2 = bf16[12,512,512]{1,2,0:T(8,128)(2,1)S(1)} fusion(f32[12,512,512]{1,2,0:T(8,128)} %get-tuple-element.599, f32[12,512,512]{1,2,0:T(8,128)S(1)} %fusion.139, f32[12,512]{1,0:T(8,128)S(1)} %get-tuple-element.600, f32[12,512]{1,0:T(8,128)S(1)} %dynamic-slice_bitcast_fusion.2, pred[512]{0:T(512)(128)(4,1)S(1)} %dynamic-slice_reduce_fusion.5), kind=kLoop, calls=%fused_computation.22.clone.1 | loop fusion | flops 18874368 | bytes 31506944 | tf_op jit(solution)/shard_map/while/body/eval_jaxpr/convert_element_type | solution.py:242
  281.6 7.3 %multiply_reduce_fusion.10 = (f32[12,512]{1,0:T(8,128)S(1)}, f32[12,512,512]{1,2,0:T(8,128)}) fusion(f32[12,512,512]{1,2,0:T(8,128)S(1)} %fusion.139, f32[12,512]{1,0:T(8,128)S(1)} %dynamic-slice_bitcast_fusion.2, pred[512]{0:T(512)(128)(4,1)S(1)} %dynamic-slice_reduce_fusion.5, bf16[2,512,12,64]{1,3,2,0:T(8,128)(2,1)S(1)} %copy-done.3, ...), kind=kOutput, calls=%fused_computation.23.clone.1 | convolution fusion | flops 418375680 | bytes 26796552 | tf_op jit(solution)/shard_map/while/body/eval_jaxpr/qhd,khd->hqk/dot_general | solution.py:232
  288.9 7.2 %multiply_convert_fusion.2 = bf16[12,512,512]{1,2,0:T(8,128)(2,1)S(1)} fusion(f32[12,512,512]{1,2,0:T(8,128)} %get-tuple-element.599, f32[12,512,512]{1,2,0:T(8,128)S(1)} %fusion.139, f32[12,512]{1,0:T(8,128)S(1)} %get-tuple-element.600, f32[12,512]{1,0:T(8,128)S(1)} %dynamic-slice_bitcast_fusion.2, pred[512]{0:T(512)(128)(4,1)S(1)} %dynamic-slice_reduce_fusion.5), kind=kLoop, calls=%fused_computation.22.clone.1 | loop fusion | flops 18874368 | bytes 31506944 | tf_op jit(solution)/shard_map/while/body/eval_jaxpr/convert_element_type | solution.py:242
  300.7 3.1 copy.87
  323.2 3.8 convolution_convert_fusion.4
  327.1 9.9 %convolution_convert_fusion = bf16[3072,768]{1,0:T(8,128)(2,1)} fusion(bf16[1024,3072]{1,0:T(8,128)(2,1)} %get-tuple-element.468, f32[1024,768]{1,0:T(8,128)} %copy-done.19), kind=kOutput, calls=%fused_computation.82 | convolution fusion | flops 4834983936 | bytes 14155776 | tf_op jit(solution)/shard_map/rd,re->de/dot_general | solution.py:26
  338.9 10.0 %convolution_convert_fusion.1 = bf16[768,3072]{1,0:T(8,128)(2,1)} fusion(bf16[1024,3072]{1,0:T(8,128)(2,1)} %copy-done.63, f32[1024,768]{1,0:T(8,128)S(1)} %copy-done.8, f32[768]{0:T(1024)S(1)} %copy-done.50, f32[768]{0:T(1024)S(1)} %copy-done.40, f32[1024]{0:T(1024)S(1)} %copy-done.42, f32[1024]{0:T(1024)S(1)} %copy-done.37), kind=kOutput, calls=%fused_computation.83 | convolution fusion | flops 4838129664 | bytes 14170112 | tf_op jit(solution)/shard_map/rd,re->de/dot_general | solution.py:26
  354.6 23.1 %all-reduce.17 = (bf16[768]{0:T(1024)(128)(2,1)S(1)}, bf16[768]{0:T(1024)(128)(2,1)S(1)}, bf16[768]{0:T(1024)(128)(2,1)S(1)}, bf16[768]{0:T(1024)(128)(2,1)S(1)}...) all-reduce(bf16[768]{0:T(1024)(128)(2,1)S(1)} %dynamic-update-slice, ...), channel_id=1, replica_groups=mesh['group'=8,'replica'=4] {'group'}, use_global_device_ids=true, to_apply=%add.7 | all-reduce | flops 9984 | bytes 39936
  378.4 11.8 %all-reduce.19 = (bf16[96]{0:T(256)(128)(2,1)S(1)}, bf16[96]{0:T(256)(128)(2,1)S(1)}, bf16[96]{0:T(256)(128)(2,1)S(1)}, bf16[384]{0:T(512)(128)(2,1)S(1)}, bf16[...) all-reduce(bf16[96]{0:T(256)(128)(2,1)S(1)} %dynamic-slice.9, ...), channel_id=1, replica_groups=mesh['group'=8,'replica'=4] {'replica'}, use_global_device_ids=true, to_apply=%region_29.30 | all-reduce | flops 1152 | bytes 4608 | tf_op jit(solution)/shard_map/psum | solution.py:328
  398.4 27.4 %reduce-scatter.21.cloned.1.call-done = bf16[96,768]{1,0:T(8,128)(2,1)} async-done(((bf16[768,768]{1,0:T(8,128)(2,1)}), bf16[96,768]{1,0:T(8,128)(2,1)}) %reduce-scatter.21.cloned.1.call-update) | async-done | bytes 147472
  427.5 38.6 %reduce-scatter.13.cloned.1.call-done = bf16[96,768]{1,0:T(8,128)(2,1)} async-done(((bf16[768,768]{1,0:T(8,128)(2,1)}), bf16[96,768]{1,0:T(8,128)(2,1)}) %reduce-scatter.13.cloned.1.call-update) | async-done | bytes 147472 | tf_op jit(solution)/shard_map/reduce_scatter | solution.py:289
  466.2 57.3 %reduce-scatter.17.cloned.1.call-done = bf16[384,768]{1,0:T(8,128)(2,1)} async-done(((bf16[3072,768]{1,0:T(8,128)(2,1)}), bf16[384,768]{1,0:T(8,128)(2,1)}) %reduce-scatter.17.cloned.1.call-update) | async-done | bytes 589840 | tf_op jit(solution)/shard_map/reduce_scatter | solution.py:295
  523.4 57.1 %reduce-scatter.15.cloned.1.call-done = bf16[96,3072]{1,0:T(8,128)(2,1)} async-done(((bf16[768,3072]{1,0:T(8,128)(2,1)}), bf16[96,3072]{1,0:T(8,128)(2,1)}) %reduce-scatter.15.cloned.1.call-update) | async-done | bytes 589840 | tf_op jit(solution)/shard_map/reduce_scatter | solution.py:292
  590.1 74.8 %all-reduce.23.cloned.1.call-done = (bf16[96,768]{0,1:T(8,128)(2,1)}, bf16[96,768]{0,1:T(8,128)(2,1)}, bf16[96,768]{0,1:T(8,128)(2,1)}, bf16[96,768]{1,0:T(8,128...) async-done(((bf16[96,768]{0,1:T(8,128)(2,1)}, bf16[96,768]{0,1:T(8,128)(2,1)}, bf16[96,768]{0,1:T(8,128)(2,1)}, bf16[96,768]{1,0:T(8,128)(2,1)}, ...) | async-done | bytes 1769488 | tf_op jit(solution)/shard_map/psum | solution.py:328
  (317 shorter events, 145.1 us)
Async XLA Ops:
  7.2 51.7 %all-gather.8.cloned.1.call-start = ((), (), s32[]{:S(2)}) async-start(), calls=%async_computation.6 | async-start | bytes 1327104 | tf_op jit(solution)/shard_map/all_gather | solution.py:79
  7.9 57.6 %all-gather.10.cloned.1.call-start = ((), (), s32[]{:S(2)}) async-start(), calls=%async_computation.7 | async-start | bytes 1327104 | tf_op jit(solution)/shard_map/all_gather | solution.py:77
  8.7 79.7 %all-gather.12.cloned.1.call-start = ((), (), s32[]{:S(2)}) async-start(), calls=%async_computation.8 | async-start | bytes 1327104 | tf_op jit(solution)/shard_map/all_gather | solution.py:78
  9.4 119.0 %all-gather.14.cloned.1.call-start = ((), (), s32[]{:S(2)}) async-start(), calls=%async_computation.9 | async-start | bytes 1327104 | tf_op jit(solution)/shard_map/all_gather | solution.py:80
  10.0 144.6 %all-gather.16.cloned.1.call-start = ((), (), s32[]{:S(2)}) async-start(), calls=%async_computation.10 | async-start | bytes 5308416 | tf_op jit(solution)/shard_map/all_gather | solution.py:81
  10.6 184.6 %all-gather.18.cloned.1.call-start = ((), (), s32[]{:S(2)}) async-start(), calls=%async_computation.11 | async-start | bytes 5308416 | tf_op jit(solution)/shard_map/all_gather | solution.py:82
  11.1 383.8 %reduce-scatter.19.cloned.1.call-start = ((), (), s32[]{:S(2)}) async-start(), calls=%async_computation.15 | async-start | bytes 1327104
  45.7 186.0 %copy-start.39 = (f32[768]{0:T(1024)}, f32[768]{0:T(1024)S(1)}, u32[]{:S(2)}) copy-start(f32[768]{0:T(1024)S(1)} %convert_element_type.279) | copy-start | bytes 9220
  45.7 149.5 %copy-start.49 = (f32[768]{0:T(1024)}, f32[768]{0:T(1024)S(1)}, u32[]{:S(2)}) copy-start(f32[768]{0:T(1024)S(1)} %convert_element_type.280) | copy-start | bytes 9220
  132.4 99.2 %copy-start.36 = (f32[1024]{0:T(1024)}, f32[1024]{0:T(1024)S(1)}, u32[]{:S(2)}) copy-start(f32[1024]{0:T(1024)S(1)} %broadcast_multiply_fusion.4) | copy-start | bytes 12292
  134.5 97.1 %copy-start.41 = (f32[1024]{0:T(1024)}, f32[1024]{0:T(1024)S(1)}, u32[]{:S(2)}) copy-start(f32[1024]{0:T(1024)S(1)} %add_rsqrt_fusion.1) | copy-start | bytes 12292
  154.6 40.6 %copy-start.51 = (f32[768]{0:T(1024)S(1)}, f32[768]{0:T(1024)}, u32[]{:S(2)}) copy-start(f32[768]{0:T(1024)} %convert_element_type.284) | copy-start | bytes 9220
  209.2 15.8 %slice-start = ((s8[4718592]{0:T(1024)(128)(4,1)}), s8[4194304]{0:T(1024)(128)(4,1)S(1)}, s32[]{:S(2)}) async-start(s8[4718592]{0:T(1024)(128)(4,1)} %bitcast.210), calls=%async_computation.19 | async-start | bytes 8388608
  211.5 13.5 %copy-start.19 = (f32[1024,768]{1,0:T(8,128)}, f32[1024,768]{1,0:T(8,128)S(1)}, u32[]{:S(2)}) copy-start(f32[1024,768]{1,0:T(8,128)S(1)} %get-tuple-element.454) | copy-start | bytes 9437188
  211.5 13.5 %copy-start.7 = (f32[1024,768]{1,0:T(8,128)S(1)}, f32[1024,768]{1,0:T(8,128)}, u32[]{:S(2)}) copy-start(f32[1024,768]{1,0:T(8,128)} %copy-done.6) | copy-start | bytes 9437188
  211.5 13.5 %slice-start.1 = ((s8[4718592]{0:T(1024)(128)(4,1)}), s8[524288]{0:T(1024)(128)(4,1)S(1)}, s32[]{:S(2)}) async-start(s8[4718592]{0:T(1024)(128)(4,1)} %bitcast.210), calls=%async_computation.20 | async-start | bytes 1048576
  225.0 6.6 copy-start.63
  254.8 7.3 %copy-start.13 = (bf16[2,512,12,64]{1,3,2,0:T(8,128)(2,1)}, bf16[2,512,12,64]{1,3,2,0:T(8,128)(2,1)S(1)}, u32[]{:S(2)}) copy-start(bf16[2,512,12,64]{1,3,2,0:T(8,128)(2,1)S(1)} %bitcast_dynamic-update-slice_fusion.11) | copy-start | bytes 4718596 | tf_op jit(solution)/shard_map/while
  262.2 7.3 %copy-start.15 = (bf16[2,512,12,64]{1,3,2,0:T(8,128)(2,1)S(1)}, bf16[2,512,12,64]{1,3,2,0:T(8,128)(2,1)}, u32[]{:S(2)}) copy-start(bf16[2,512,12,64]{1,3,2,0:T(8,128)(2,1)} %get-tuple-element.649) | copy-start | bytes 4718596 | tf_op jit(solution)/shard_map/while
  281.6 7.3 %copy-start.13 = (bf16[2,512,12,64]{1,3,2,0:T(8,128)(2,1)}, bf16[2,512,12,64]{1,3,2,0:T(8,128)(2,1)S(1)}, u32[]{:S(2)}) copy-start(bf16[2,512,12,64]{1,3,2,0:T(8,128)(2,1)S(1)} %bitcast_dynamic-update-slice_fusion.11) | copy-start | bytes 4718596 | tf_op jit(solution)/shard_map/while
  288.9 7.3 %copy-start.15 = (bf16[2,512,12,64]{1,3,2,0:T(8,128)(2,1)S(1)}, bf16[2,512,12,64]{1,3,2,0:T(8,128)(2,1)}, u32[]{:S(2)}) copy-start(bf16[2,512,12,64]{1,3,2,0:T(8,128)(2,1)} %get-tuple-element.649) | copy-start | bytes 4718596 | tf_op jit(solution)/shard_map/while
  308.4 88.3 %reduce-scatter.23.cloned.1.call-start = ((), (), s32[]{:S(2)}) async-start(), calls=%async_computation.17 | async-start | bytes 1327104
  314.8 111.0 %reduce-scatter.21.cloned.1.call-start = ((), (), s32[]{:S(2)}) async-start(), calls=%async_computation.16 | async-start | bytes 1327104
  323.1 143.0 %reduce-scatter.13.cloned.1.call-start = ((), (), s32[]{:S(2)}) async-start(), calls=%async_computation.12 | async-start | bytes 1327104 | tf_op jit(solution)/shard_map/reduce_scatter | solution.py:289
  327.0 196.4 %reduce-scatter.17.cloned.1.call-start = ((), (), s32[]{:S(2)}) async-start(), calls=%async_computation.14 | async-start | bytes 5308416 | tf_op jit(solution)/shard_map/reduce_scatter | solution.py:295
  337.0 243.5 %reduce-scatter.15.cloned.1.call-start = ((), (), s32[]{:S(2)}) async-start(), calls=%async_computation.13 | async-start | bytes 5308416 | tf_op jit(solution)/shard_map/reduce_scatter | solution.py:292
  349.0 231.6 %copy-start.1 = (f32[1024,768]{1,0:T(8,128)S(1)}, f32[1024,768]{1,0:T(8,128)}, u32[]{:S(2)}) copy-start(f32[1024,768]{1,0:T(8,128)} %copy-done) | copy-start | bytes 9437188
  349.0 231.6 %copy-start.31 = (f32[768]{0:T(1024)S(1)}, f32[768]{0:T(1024)}, u32[]{:S(2)}) copy-start(f32[768]{0:T(1024)} %copy-done.29) | copy-start | bytes 9220
  349.0 231.6 %copy-start.33 = (f32[1024]{0:T(1024)S(1)}, f32[1024]{0:T(1024)}, u32[]{:S(2)}) copy-start(f32[1024]{0:T(1024)} %copy-done.32) | copy-start | bytes 12292
  349.0 231.6 %copy-start.35 = (f32[1024]{0:T(1024)S(1)}, f32[1024]{0:T(1024)}, u32[]{:S(2)}) copy-start(f32[1024]{0:T(1024)} %copy-done.34) | copy-start | bytes 12292
  349.0 315.8 %all-reduce.23.cloned.1.call-start = ((), (), s32[]{:S(2)}) async-start(), calls=%async_computation.18 | async-start | bytes 3833856 | tf_op jit(solution)/shard_map/psum | solution.py:328
  664.8 9.2 %copy-start.28 = (bf16[384,768]{1,0:T(8,128)(2,1)S(1)}, bf16[384,768]{1,0:T(8,128)(2,1)}, u32[]{:S(2)}) copy-start(bf16[384,768]{1,0:T(8,128)(2,1)} %get-tuple-element.452) | copy-start | bytes 1769476
  (56 other events, 155.3 us)
Sparse Core Ops, SparseCore 0:
  9.9 26.7 all-gather.7
  38.5 23.9 all-gather.9
  64.4 23.9 all-gather.11
  90.1 23.9 all-gather.13
  115.8 38.7 all-gather.15
  156.3 38.7 all-gather.17
  308.5 36.6 reduce-scatter.18
  348.4 36.8 reduce-scatter.22
  389.1 36.6 reduce-scatter.20
  429.5 36.6 reduce-scatter.12
  469.6 53.7 reduce-scatter.16
  526.7 53.7 reduce-scatter.14
  584.0 80.8 all-reduce.22
where the time goes:
time: 690 us; the launch traced here: 682 us
  waiting for transfers between devices  300 us (43%)
  matrix products  163 us (24%)
  local copies, waits for them, and re-layouts  77.8 us (11%)
  blocking collectives  68.7 us (10%)
  other arithmetic  45.7 us (7%)
  between operations  17.4 us (3%)
  loops' own time  8.45 us (1%)
    psum x1, waiting for transfers between devices, per_device(): lax.psum(for_sending(tuple(owned)), 'replica')  74.8 us
    dot_general x6, matrix products, project(): return jnp.dot(left, right, preferred_element_type=jnp.float32)  60.8 us
    reduce_scatter x1, waiting for transfers between devices, per_device(): lax.psum_scatter(back_weight_grad.astype(jnp.bfloat16), 'group', scatter_...  57.3 us
    reduce_scatter x1, waiting for transfers between devices, per_device(): lax.psum_scatter(in_weight_grad.astype(jnp.bfloat16), 'group', scatter_di...  57.1 us
    unnamed x2, blocking collectives  49 us
    unnamed x156, local copies, waits for them, and re-layouts  41.7 us
    reduce_scatter x1, waiting for transfers between devices, per_device(): lax.psum_scatter(out_weight_grad.astype(jnp.bfloat16), 'group', scatter_d...  38.6 us
    unnamed x16, waiting for transfers between devices  31.2 us
  transfers between devices with their start and end apart: 13, of which 8 were waited for; matrix products, arithmetic and copies ran while one was open for 23% of the time, Pallas kernels for 0%

commit v1 on v0

--- a/solution.py
+++ b/solution.py
@@ -14,8 +14,103 @@
 inverse_root_tau = 0.3989422804014327
 
 
-def for_sending(array):
-    return jax.tree.map(lambda a: a.astype(jnp.bfloat16) if a.dtype == jnp.float32 else a, array)
+AXES = ("group", "replica")
+
+
+def swap_with(array, group_mask, replica_mask=0):
+    groups, replicas = lax.axis_size("group"), lax.axis_size("replica")
+    pairs = [
+        (g * replicas + r, (g ^ group_mask) * replicas + (r ^ replica_mask))
+        for g in range(groups)
+        for r in range(replicas)
+    ]
+    return lax.ppermute(array, AXES, pairs)
+
+
+def after(array, *others):
+    return lax.optimization_barrier((array,) + others)[0] if others else array
+
+
+def gather_group(shard, bits, wait_for):
+    plane = [1 << b for b in range(1, bits)]
+    half = shard.shape[0] // 32 * 16
+    orders = (plane, plane[::-1])
+    cut = (slice(0, half), slice(half, None))
+    shard = after(shard, *wait_for)
+    pieces = {0: [shard]}
+    first = []
+    for mask in plane:
+        pieces[mask] = [swap_with(shard, mask)]
+        first.append(pieces[mask][0])
+    halves = {d: [p[0][c] for c in cut] for d, p in pieces.items()}
+    for count in range(2, len(plane) + 1):
+        for d in range(2, 1 << bits, 2):
+            if bin(d).count("1") != count:
+                continue
+            got = []
+            for which, order in enumerate(orders):
+                last = [m for m in order if m & d][-1]
+                got.append(swap_with(halves[d ^ last][which], last))
+            pieces[d] = got
+            halves[d] = got
+    for d in list(pieces):
+        pieces[d | 1] = [swap_with(p, 1) for p in pieces[d]]
+    return pieces, first
+
+
+def place(pieces, me, group_size):
+    rows = sum(p.shape[0] for p in pieces[0])
+    full = jnp.zeros((group_size, rows, pieces[0][0].shape[1]), jnp.bfloat16)
+    for d, parts in pieces.items():
+        at = 0
+        for part in parts:
+            full = lax.dynamic_update_slice(full, part[None], (me ^ d, at, 0))
+            at += part.shape[0]
+    return full
+
+
+def pick(array, axis, index):
+    return lax.dynamic_index_in_dim(array, index, axis, keepdims=False)
+
+
+def add_low(left, right):
+    return (left.astype(jnp.float32) + right.astype(jnp.float32)).astype(jnp.bfloat16)
+
+
+def reduce_all(chunks, me, bits):
+    rows, model = chunks.shape[1:]
+    chunks = chunks.reshape((2,) * bits + (rows, model))
+    mine = [(me >> b) & 1 for b in range(bits)]
+    axis = bits - 1
+    received = swap_with(pick(chunks, axis, 1 - mine[0]), 1)
+    chunks = add_low(pick(chunks, axis, mine[0]), received)
+    half = rows // 32 * 16
+    done = []
+    for part, order in ((chunks[..., :half, :], 0), (chunks[..., half:, :], 1)):
+        left = list(range(1, bits))
+        for b in (left[:] if order == 0 else left[::-1]):
+            axis = len(left) - 1 - left.index(b)
+            received = swap_with(pick(part, axis, 1 - mine[b]), 1 << b)
+            part = add_low(pick(part, axis, mine[b]), received)
+            left.remove(b)
+        done.append(part)
+    total = jnp.concatenate(done)
+    replicas = lax.axis_size("replica")
+    if replicas == 1:
+        return total
+    at = lax.axis_index("replica")
+    half = rows // 32 * 16
+    pair = total.reshape(2, rows // 2, model)
+    received = swap_with(pick(pair, 0, 1 - (at & 1)), 0, 1)
+    kept = add_low(pick(pair, 0, at & 1), received)
+    mask = 2
+    while mask < replicas:
+        kept = add_low(kept, swap_with(kept, 0, mask))
+        mask *= 2
+    other = swap_with(kept, 0, 1)
+    low_first = jnp.concatenate([kept, other])
+    high_first = jnp.concatenate([other, kept])
+    return jnp.where((at & 1) == 0, low_first, high_first)
 
 
 def project(left, right):
@@ -73,40 +168,49 @@
     second_gain,
     second_shift,
 ):
-    whole = (
-        lax.all_gather(query_weight, "group", axis=0, tiled=True),
-        lax.all_gather(key_weight, "group", axis=0, tiled=True),
-        lax.all_gather(value_weight, "group", axis=0, tiled=True),
-        lax.all_gather(out_weight, "group", axis=0, tiled=True),
-        lax.all_gather(in_weight, "group", axis=0, tiled=True),
-        lax.all_gather(back_weight, "group", axis=0, tiled=True),
-        lax.all_gather(query_bias, "group", axis=0, tiled=True),
-        lax.all_gather(value_bias, "group", axis=0, tiled=True),
-        lax.all_gather(out_bias, "group", axis=0, tiled=True),
-        lax.all_gather(in_bias, "group", axis=0, tiled=True),
-        lax.all_gather(back_bias, "group", axis=0, tiled=True),
-        lax.all_gather(first_gain, "group", axis=0, tiled=True),
-        lax.all_gather(first_shift, "group", axis=0, tiled=True),
-        lax.all_gather(second_gain, "group", axis=0, tiled=True),
-        lax.all_gather(second_shift, "group", axis=0, tiled=True),
-    )
+    me = lax.axis_index("group")
+    group_size = lax.axis_size("group")
+    bits = group_size.bit_length() - 1
+    plane_bits = tuple(range(1, bits))
+    small_shards = (
+        query_bias, value_bias, out_bias, in_bias, back_bias,
+        first_gain, first_shift, second_gain, second_shift,
+    )
+    small_sizes = tuple(a.shape[0] for a in small_shards)
+    model = inputs.shape[2]
+    small_rows = -(-sum(small_sizes) // (model * 16)) * 16
+    small = jnp.concatenate(small_shards)
+    small = jnp.pad(small, (0, small_rows * model - small.shape[0])).reshape(small_rows, model)
+    shard_a = jnp.concatenate([query_weight, key_weight, value_weight, small])
+    in_rows = in_weight.shape[0]
+    in_cols = in_weight.shape[1] // model
+    in_blocks = [in_weight[:, n * model : (n + 1) * model] for n in range(in_cols)]
+    shard_b = jnp.concatenate([out_weight] + in_blocks)
+    shard_c = back_weight
+    gathered_a = gather_group(shard_a, bits, ())
+    gathered_b = gather_group(shard_b, bits, gathered_a[1])
+    gathered_c = gather_group(shard_c, bits, gathered_b[1])
+    full_a = place(gathered_a[0], me, group_size)
+    full_b = place(gathered_b[0], me, group_size)
+    full_c = place(gathered_c[0], me, group_size)
+    rows = query_weight.shape[0]
+    full_query = full_a[:, :rows].reshape(model, model)
+    full_key = full_a[:, rows : 2 * rows].reshape(model, model)
+    full_value = full_a[:, 2 * rows : 3 * rows].reshape(model, model)
+    flat_small = full_a[:, 3 * rows :].reshape(group_size, small_rows * model)
+    small_full, at = [], 0
+    for size in small_sizes:
+        small_full.append(flat_small[:, at : at + size].reshape(-1))
+        at += size
+    full_out = full_b[:, :rows].reshape(model, model)
+    full_in = jnp.concatenate(
+        [full_b[:, rows + n * in_rows : rows + (n + 1) * in_rows] for n in range(in_cols)], axis=2
+    ).reshape(model, in_cols * model)
+    full_back = full_c.reshape(-1, model)
     (
-        full_query,
-        full_key,
-        full_value,
-        full_out,
-        full_in,
-        full_back,
-        bias_query,
-        bias_value,
-        bias_out,
-        bias_in,
-        bias_back,
-        gain_first,
-        shift_first,
-        gain_second,
-        shift_second,
-    ) = whole
+        bias_query, bias_value, bias_out, bias_in, bias_back,
+        gain_first, shift_first, gain_second, shift_second,
+    ) = small_full
     seq_count, slot_count, model_width = inputs.shape
     total_rows = seq_count * slot_count
     block_rows = min(512, slot_count)
@@ -171,40 +275,9 @@
         after_attn + ffn_out, gain_second.astype(jnp.float32), shift_second.astype(jnp.float32)
     )
     layer_out = result_rows.astype(jnp.bfloat16).reshape(seq_count, slot_count, model_width)
-    again = (
-        lax.all_gather(query_weight, "group", axis=0, tiled=True),
-        lax.all_gather(key_weight, "group", axis=0, tiled=True),
-        lax.all_gather(value_weight, "group", axis=0, tiled=True),
-        lax.all_gather(out_weight, "group", axis=0, tiled=True),
-        lax.all_gather(in_weight, "group", axis=0, tiled=True),
-        lax.all_gather(back_weight, "group", axis=0, tiled=True),
-        lax.all_gather(query_bias, "group", axis=0, tiled=True),
-        lax.all_gather(value_bias, "group", axis=0, tiled=True),
-        lax.all_gather(out_bias, "group", axis=0, tiled=True),
-        lax.all_gather(in_bias, "group", axis=0, tiled=True),
-        lax.all_gather(back_bias, "group", axis=0, tiled=True),
-        lax.all_gather(first_gain, "group", axis=0, tiled=True),
-        lax.all_gather(first_shift, "group", axis=0, tiled=True),
-        lax.all_gather(second_gain, "group", axis=0, tiled=True),
-        lax.all_gather(second_shift, "group", axis=0, tiled=True),
-    )
-    (
-        back_query,
-        back_key,
-        back_value,
-        back_out,
-        back_in,
-        back_ffn,
-        unused_one,
-        unused_two,
-        unused_three,
-        unused_four,
-        unused_five,
-        gain_first_b,
-        unused_six,
-        gain_second_b,
-        unused_seven,
-    ) = again
+    back_query, back_key, back_value = full_query, full_key, full_value
+    back_out, back_in, back_ffn = full_out, full_in, full_back
+    gain_first_b, gain_second_b = gain_first, gain_second
     grad_result = cotangent.reshape(total_rows, model_width).astype(jnp.float32) * row_valid
     grad_h2, second_gain_grad, second_shift_grad = norm_backward(
         grad_result, gain_second_b.astype(jnp.float32), normed_second, inverse_second
@@ -276,58 +349,46 @@
         + back_project(grad_values, back_value)
     )
     input_grad = input_rows.astype(jnp.bfloat16).reshape(seq_count, slot_count, model_width)
-    owned = (
-        lax.psum_scatter(
-            query_weight_grad.astype(jnp.bfloat16), "group", scatter_dimension=0, tiled=True
-        ).astype(jnp.float32),
-        lax.psum_scatter(
-            key_weight_grad.astype(jnp.bfloat16), "group", scatter_dimension=0, tiled=True
-        ).astype(jnp.float32),
-        lax.psum_scatter(
-            value_weight_grad.astype(jnp.bfloat16), "group", scatter_dimension=0, tiled=True
-        ).astype(jnp.float32),
-        lax.psum_scatter(
-            out_weight_grad.astype(jnp.bfloat16), "group", scatter_dimension=0, tiled=True
-        ).astype(jnp.float32),
-        lax.psum_scatter(
-            in_weight_grad.astype(jnp.bfloat16), "group", scatter_dimension=0, tiled=True
-        ).astype(jnp.float32),
-        lax.psum_scatter(
-            back_weight_grad.astype(jnp.bfloat16), "group", scatter_dimension=0, tiled=True
-        ).astype(jnp.float32),
-        lax.psum_scatter(
-            query_bias_grad.astype(jnp.bfloat16), "group", scatter_dimension=0, tiled=True
-        ).astype(jnp.float32),
-        lax.psum_scatter(
-            value_bias_grad.astype(jnp.bfloat16), "group", scatter_dimension=0, tiled=True
-        ).astype(jnp.float32),
-        lax.psum_scatter(
-            out_bias_grad.astype(jnp.bfloat16), "group", scatter_dimension=0, tiled=True
-        ).astype(jnp.float32),
-        lax.psum_scatter(
-            in_bias_grad.astype(jnp.bfloat16), "group", scatter_dimension=0, tiled=True
-        ).astype(jnp.float32),
-        lax.psum_scatter(
-            back_bias_grad.astype(jnp.bfloat16), "group", scatter_dimension=0, tiled=True
-        ).astype(jnp.float32),
-        lax.psum_scatter(
-            first_gain_grad.astype(jnp.bfloat16), "group", scatter_dimension=0, tiled=True
-        ).astype(jnp.float32),
-        lax.psum_scatter(
-            first_shift_grad.astype(jnp.bfloat16), "group", scatter_dimension=0, tiled=True
-        ).astype(jnp.float32),
-        lax.psum_scatter(
-            second_gain_grad.astype(jnp.bfloat16), "group", scatter_dimension=0, tiled=True
-        ).astype(jnp.float32),
-        lax.psum_scatter(
-            second_shift_grad.astype(jnp.bfloat16), "group", scatter_dimension=0, tiled=True
-        ).astype(jnp.float32),
-    )
-    summed = tuple(
-        jax.tree.map(
-            lambda part: part.astype(jnp.float32), lax.psum(for_sending(tuple(owned)), "replica")
-        )
-    )
+    by_group = lambda a: a.astype(jnp.bfloat16).reshape((group_size, -1, model))
+    in_grad_blocks = [
+        in_weight_grad[:, n * model : (n + 1) * model].astype(jnp.bfloat16).reshape(group_size, -1, model)
+        for n in range(in_cols)
+    ]
+    small_grads = (
+        query_bias_grad, value_bias_grad, out_bias_grad, in_bias_grad, back_bias_grad,
+        first_gain_grad, first_shift_grad, second_gain_grad, second_shift_grad,
+    )
+    small_grad = jnp.concatenate([a.reshape(group_size, -1) for a in small_grads], axis=1)
+    small_grad = jnp.pad(small_grad, ((0, 0), (0, small_rows * model - small_grad.shape[1])))
+    small_grad = small_grad.astype(jnp.bfloat16).reshape(group_size, small_rows, model)
+    sum_c = reduce_all(by_group(back_weight_grad), me, bits)
+    sum_b = reduce_all(jnp.concatenate([by_group(out_weight_grad)] + in_grad_blocks, axis=1), me, bits)
+    sum_a = reduce_all(
+        jnp.concatenate(
+            [by_group(query_weight_grad), by_group(key_weight_grad), by_group(value_weight_grad), small_grad],
+            axis=1,
+        ),
+        me,
+        bits,
+    )
+    wide = lambda a: a.astype(jnp.float32)
+    flat_sum = sum_a[3 * rows :].reshape(-1)
+    small_sums, at = [], 0
+    for size in small_sizes:
+        small_sums.append(wide(flat_sum[at : at + size]))
+        at += size
+    summed = (
+        wide(sum_a[:rows]),
+        wide(sum_a[rows : 2 * rows]),
+        wide(sum_a[2 * rows : 3 * rows]),
+        wide(sum_b[:rows]),
+        wide(
+            jnp.concatenate(
+                [sum_b[rows + n * in_rows : rows + (n + 1) * in_rows] for n in range(in_cols)], axis=1
+            )
+        ),
+        wide(sum_c),
+    ) + tuple(small_sums)
     return (layer_out, input_grad) + summed
 
 

time: 690 us -> 454 us (0.66)
  waiting for transfers between devices: 300 us -> 117 us
  blocking collectives: 68.7 us -> 0 us
  starting transfers between devices: 0.98 us -> 41 us
  between operations: 17.4 us -> 2.57 us
  matrix products: 163 us -> 149 us
    reduce_scatter x3 -> x0, waiting for transfers between devices: 153 us -> none  [the longest x1 57.3 us: per_device(): lax.psum_scatter(back_weight_grad.astype(jnp.bfloat16), 'group', scatter_...]
    ppermute x0 -> x51, waiting for transfers between devices: none -> 117 us  [swap_with(): return lax.ppermute(array, AXES, pairs)]
    psum x1 -> x0, waiting for transfers between devices: 74.8 us -> none  [per_device(): lax.psum(for_sending(tuple(owned)), 'replica')]
    unnamed x2 -> x0, blocking collectives: 49 us -> none
    ppermute x0 -> x51, starting transfers between devices: none -> 41 us  [swap_with(): return lax.ppermute(array, AXES, pairs)]
    all_gather x6 -> x0, waiting for transfers between devices: 40.9 us -> none  [the longest x1 20.1 us: per_device(): lax.all_gather(in_weight, 'group', axis=0, tiled=True)]
    unnamed x16 -> x0, waiting for transfers between devices: 31.2 us -> none
    unnamed x156 -> x112, local copies, waits for them, and re-layouts: 41.7 us -> 24.1 us
  transfers between devices with their start and end apart: 13 -> 51, of which waited for: 8 -> 29; matrix products, arithmetic and copies ran while one was open for 23% -> 28% of each run, Pallas kernels for 0% -> 0%
where the time goes in v1:
time: 454 us; the launch traced here: 446 us
  matrix products  149 us (33%)
  waiting for transfers between devices  117 us (26%)
  local copies, waits for them, and re-layouts  82.9 us (18%)
  other arithmetic  44.9 us (10%)
  starting transfers between devices  41 us (9%)
  loops' own time  9.11 us (2%)
    ppermute x51, waiting for transfers between devices, swap_with(): return lax.ppermute(array, AXES, pairs)  117 us
    dot_general x6, matrix products, project(): return jnp.dot(left, right, preferred_element_type=jnp.float32)  49.2 us
    ppermute x51, starting transfers between devices, swap_with(): return lax.ppermute(array, AXES, pairs)  41 us
    dot_general x6, matrix products, back_project(): jnp.einsum('re,de->rd', grad_rows, weight_full, preferred_element_type=jn...  27.6 us
    dot_general x6, matrix products, outer_sum(): jnp.einsum('rd,re->de', left, right, preferred_element_type=jnp.float32)  25.5 us
    unnamed x112, local copies, waits for them, and re-layouts  24.1 us
    dot_general x2, matrix products, attend_back(): jnp.einsum('qhd,khd->hqk', grad_part, value_part, preferred_element_type=...  14.6 us
    convert_element_type x2, other arithmetic, attend_back(): (soft_weights * (grad_weights - row_inner)).astype(jnp.bfloat16)  14.5 us
  transfers between devices with their start and end apart: 51, of which 29 were waited for; matrix products, arithmetic and copies ran while one was open for 28% of the time, Pallas kernels for 0%

profile of v1, /device:TPU:0, one launch (start us, length us, event | category | flops | bytes accessed | tf_op | source)
XLA Modules:
  0.0 446.2 jit_solution(2758573805505493176)
XLA Ops:
  1.6 6.1 %concatenate.72 = bf16[1152]{0:T(1024)(128)(2,1)S(1)} concatenate(bf16[96]{0:T(256)(128)(2,1)} %param.31, bf16[96]{0:T(256)(128)(2,1)} %param.32, bf16[96]{0:T(256)(128)(2,1)} %param.33, bf16[384]{0:T(512)(128)(2,1)} %param.34, bf16[96]{0:T(256)(128)(2,1)} %param.35, bf16[96]{0:T(256)(128)(2,1)} %param.36, bf16[96]{0:T(256)(128)(2,1)} %param.37, bf16[96]{0:T(256)(128)(2,1)} %param.38, ...), dimensions={0} | concatenate | bytes 4608 | tf_op jit(solution)/shard_map/concatenate | solution.py:182
  30.7 16.9 %collective-permute-done.2 = bf16[144,768]{1,0:T(8,128)(2,1)S(1)} collective-permute-done((bf16[144,768]{1,0:T(8,128)(2,1)S(1)}, bf16[144,768]{1,0:T(8,128)(2,1)S(1)}, u32[]{:S(2)}, u32[]{:S(2)}) %collective-permute-start.2) | collective-permute-done | bytes 221216 | tf_op jit(solution)/shard_map/ppermute | solution.py:27
  72.9 25.6 %while.30 = (s32[]{:T(128)}, bf16[2,512,12,64]{1,3,2,0:T(8,128)(2,1)}, f32[2,12,512]{2,1,0:T(8,128)S(1)}, s32[2]{0:T(128)S(1)}, bf16[2,512,12,64]{1,3,2,0:T(8,12...) while((s32[]{:T(128)}, ...), condition=%wide.region_3.4_spmd, body=%wide.region_0.3_spmd.sunk | while | flops 843442176 | bytes 47426764 | solution.py:262
  81.8 4.2 fusion.154
  94.2 4.2 fusion.154
  98.6 4.2 copy.56
  118.3 13.0 %collective-permute-done.11 = bf16[240,768]{1,0:T(8,128)(2,1)S(1)} collective-permute-done((bf16[240,768]{1,0:T(8,128)(2,1)S(1)}, bf16[240,768]{1,0:T(8,128)(2,1)S(1)}, u32[]{:S(2)}, u32[]{:S(2)}) %collective-permute-start.11) | collective-permute-done | bytes 368672 | tf_op jit(solution)/shard_map/ppermute | solution.py:27
  143.0 34.8 %fusion.48 = (bf16[1024,3072]{1,0:T(8,128)(2,1)S(1)}, f32[1024,3072]{1,0:T(8,128)}) fusion(f32[3072]{0:T(1024)S(1)} %reshape.453, bf16[768,3072]{1,0:T(8,128)(2,1)S(1)} %bitcast.393, f32[1024,768]{1,0:T(8,128)S(1)} %get-tuple-element.408, f32[768]{0:T(1024)S(1)} %reshape.452, f32[768]{0:T(1024)S(1)} %reshape.451, f32[1024]{0:T(1024)S(1)} %add_rsqrt_fusion.1, ...), kind=kOutput, calls=%fused_computation.60 | convolution fusion | flops 5043388416 | bytes 26765312 | tf_op jit(solution)/shard_map/dot_general | solution.py:117
  179.9 5.4 %fusion.102 = (f32[1024]{0:T(1024)S(1)}, f32[1024,768]{1,0:T(8,128)S(1)}) fusion(f32[768]{0:T(1024)S(1)} %reshape.454, bf16[1024,3072]{1,0:T(8,128)(2,1)S(1)} %get-tuple-element.409, bf16[3072,768]{1,0:T(8,128)(2,1)S(1)} %bitcast.395, f32[768]{0:T(1024)S(1)} %reshape.452, f32[768]{0:T(1024)S(1)} %reshape.451, f32[1024]{0:T(1024)S(1)} %add_rsqrt_fusion.1, ...), kind=kOutput, calls=%fused_computation.277 | convolution fusion | flops 4837342208 | bytes 17323008 | tf_op jit(solution)/shard_map/dot_general | solution.py:117
  192.0 7.1 %convolution_convert_fusion = bf16[3072,768]{1,0:T(8,128)(2,1)} fusion(bf16[1024,3072]{1,0:T(8,128)(2,1)S(1)} %get-tuple-element.409, f32[1024,768]{1,0:T(8,128)S(1)} %get-tuple-element.356), kind=kOutput, calls=%fused_computation.84 | convolution fusion | flops 4834983936 | bytes 14155776 | tf_op jit(solution)/shard_map/rd,re->de/dot_general | solution.py:121
  199.0 13.6 %fusion.103 = (bf16[3072]{0:T(1024)(128)(2,1)}, bf16[1024,3072]{1,0:T(8,128)(2,1)}) fusion(f32[1024,3072]{1,0:T(8,128)} %get-tuple-element.410, f32[3072]{0:T(1024)S(1)} %reshape.453, bf16[3072,768]{1,0:T(8,128)(2,1)S(1)} %bitcast.396, f32[1024,768]{1,0:T(8,128)S(1)} %get-tuple-element.356), kind=kOutput, calls=%fused_computation.278 | convolution fusion | flops 4870370304 | bytes 26757120 | tf_op jit(solution)/shard_map/re,de->rd/dot_general | solution.py:125
  212.7 10.5 %convolution_convert_fusion.1 = bf16[768,3072]{1,0:T(8,128)(2,1)} fusion(bf16[1024,3072]{1,0:T(8,128)(2,1)} %get-tuple-element.415, f32[1024,768]{1,0:T(8,128)S(1)} %get-tuple-element.408, f32[768]{0:T(1024)S(1)} %reshape.452, f32[768]{0:T(1024)S(1)} %reshape.451, f32[1024]{0:T(1024)S(1)} %add_rsqrt_fusion.1, f32[1024]{0:T(1024)S(1)} %broadcast_multiply_fusion.4), kind=kOutput, calls=%fused_computation.85 | convolution fusion | flops 4838129664 | bytes 14170112 | tf_op jit(solution)/shard_map/rd,re->de/dot_general | solution.py:121
  223.2 6.6 %multiply_reduce_fusion.2 = (bf16[768]{0:T(1024)(128)(2,1)}, f32[1024]{0:T(1024)S(1)}, f32[1024]{0:T(1024)S(1)}, bf16[768]{0:T(1024)(128)(2,1)}, f32[1024,768]{1,0:T(8,128)S(1)}) fusion(f32[1024,768]{1,0:T(8,128)S(1)} %get-tuple-element.408, f32[1024]{0:T(1024)S(1)} %add_rsqrt_fusion.1, f32[1024]{0:T(1024)S(1)} %broadcast_multiply_fusion.4, ...), kind=kOutput, calls=%fused_computation.94 | convolution fusion | flops 4839698432 | bytes 20469760 | tf_op jit(solution)/shard_map/re,de->rd/dot_general | solution.py:125
  236.2 4.0 reshape.433
  243.1 54.7 %while.31 = (s32[]{:T(128)}, bf16[2,512,12,64]{1,3,2,0:T(8,128)(2,1)}, bf16[2,512,12,64]{1,3,2,0:T(8,128)(2,1)}, bf16[2,512,12,64]{1,3,2,0:T(8,128)(2,1)}, s32[2...) while((s32[]{:T(128)}, ...), condition=%wide.region_14.15_spmd, body=%wide.region_12.14_spmd.sunk | while | flops 2061232128 | bytes 142537600 | solution.py:326
  247.7 7.3 %multiply_reduce_fusion.10 = (f32[12,512]{1,0:T(8,128)S(1)}, f32[12,512,512]{1,2,0:T(8,128)}) fusion(f32[12,512,512]{1,2,0:T(8,128)S(1)} %fusion.163, f32[12,512]{1,0:T(8,128)S(1)} %dynamic-slice_bitcast_fusion.20, pred[512]{0:T(512)(128)(4,1)S(1)} %dynamic-slice_reduce_fusion.5, bf16[2,512,12,64]{1,3,2,0:T(8,128)(2,1)S(1)} %copy-done.7, ...), kind=kOutput, calls=%fused_computation.23.clone.1 | convolution fusion | flops 418375680 | bytes 26796552 | tf_op jit(solution)/shard_map/while/body/eval_jaxpr/qhd,khd->hqk/dot_general | solution.py:305
  255.0 7.2 %multiply_convert_fusion.2 = bf16[12,512,512]{1,2,0:T(8,128)(2,1)S(1)} fusion(f32[12,512,512]{1,2,0:T(8,128)} %get-tuple-element.540, f32[12,512,512]{1,2,0:T(8,128)S(1)} %fusion.163, f32[12,512]{1,0:T(8,128)S(1)} %get-tuple-element.541, f32[12,512]{1,0:T(8,128)S(1)} %dynamic-slice_bitcast_fusion.20, pred[512]{0:T(512)(128)(4,1)S(1)} %dynamic-slice_reduce_fusion.5), kind=kLoop, calls=%fused_computation.22.clone.1 | loop fusion | flops 18874368 | bytes 31506944 | tf_op jit(solution)/shard_map/while/body/eval_jaxpr/convert_element_type | solution.py:315
  266.6 3.9 bitcast_dynamic-update-slice_fusion.41
  274.9 7.3 %multiply_reduce_fusion.10 = (f32[12,512]{1,0:T(8,128)S(1)}, f32[12,512,512]{1,2,0:T(8,128)}) fusion(f32[12,512,512]{1,2,0:T(8,128)S(1)} %fusion.163, f32[12,512]{1,0:T(8,128)S(1)} %dynamic-slice_bitcast_fusion.20, pred[512]{0:T(512)(128)(4,1)S(1)} %dynamic-slice_reduce_fusion.5, bf16[2,512,12,64]{1,3,2,0:T(8,128)(2,1)S(1)} %copy-done.7, ...), kind=kOutput, calls=%fused_computation.23.clone.1 | convolution fusion | flops 418375680 | bytes 26796552 | tf_op jit(solution)/shard_map/while/body/eval_jaxpr/qhd,khd->hqk/dot_general | solution.py:305
  282.2 7.2 %multiply_convert_fusion.2 = bf16[12,512,512]{1,2,0:T(8,128)(2,1)S(1)} fusion(f32[12,512,512]{1,2,0:T(8,128)} %get-tuple-element.540, f32[12,512,512]{1,2,0:T(8,128)S(1)} %fusion.163, f32[12,512]{1,0:T(8,128)S(1)} %get-tuple-element.541, f32[12,512]{1,0:T(8,128)S(1)} %dynamic-slice_bitcast_fusion.20, pred[512]{0:T(512)(128)(4,1)S(1)} %dynamic-slice_reduce_fusion.5), kind=kLoop, calls=%fused_computation.22.clone.1 | loop fusion | flops 18874368 | bytes 31506944 | tf_op jit(solution)/shard_map/while/body/eval_jaxpr/convert_element_type | solution.py:315
  293.8 3.8 bitcast_dynamic-update-slice_fusion.41
  299.6 4.2 copy.62
  331.2 10.2 %collective-permute-done.28 = bf16[2,144,768]{2,1,0:T(8,128)(2,1)S(1)} collective-permute-done((bf16[2,144,768]{2,1,0:T(8,128)(2,1)S(1)}, bf16[2,144,768]{2,1,0:T(8,128)(2,1)S(1)}, u32[]{:S(2)}, u32[]{:S(2)}) %collective-permute-start.28) | collective-permute-done | bytes 442400 | tf_op jit(solution)/shard_map/ppermute | solution.py:27
  348.3 3.7 collective-permute-done.31
  356.4 3.7 collective-permute-done.32
  364.2 5.2 %collective-permute-done.46 = bf16[2,192,768]{2,1,0:T(8,128)(2,1)S(1)} collective-permute-done((bf16[2,192,768]{2,1,0:T(8,128)(2,1)S(1)}, bf16[2,192,768]{2,1,0:T(8,128)(2,1)S(1)}, u32[]{:S(2)}, u32[]{:S(2)}) %collective-permute-start.46) | collective-permute-done | bytes 589856 | tf_op jit(solution)/shard_map/ppermute | solution.py:27
  379.1 7.8 %collective-permute-done.36 = bf16[2,240,768]{2,1,0:T(8,128)(2,1)S(1)} collective-permute-done((bf16[2,240,768]{2,1,0:T(8,128)(2,1)S(1)}, bf16[2,240,768]{2,1,0:T(8,128)(2,1)S(1)}, u32[]{:S(2)}, u32[]{:S(2)}) %collective-permute-start.36) | collective-permute-done | bytes 737312 | tf_op jit(solution)/shard_map/ppermute | solution.py:27
  388.3 4.1 collective-permute-done.38
  407.1 4.0 collective-permute-done.40
  415.6 12.7 %collective-permute-done.49 = bf16[192,768]{1,0:T(8,128)(2,1)S(1)} collective-permute-done((bf16[192,768]{1,0:T(8,128)(2,1)S(1)}, bf16[192,768]{1,0:T(8,128)(2,1)S(1)}, u32[]{:S(2)}, u32[]{:S(2)}) %collective-permute-start.49) | collective-permute-done | bytes 294944 | tf_op jit(solution)/shard_map/ppermute | solution.py:27
  428.5 4.0 collective-permute-done.41
  434.0 4.8 %collective-permute-done.50 = bf16[192,768]{1,0:T(8,128)(2,1)S(1)} collective-permute-done((bf16[192,768]{1,0:T(8,128)(2,1)S(1)}, bf16[192,768]{1,0:T(8,128)(2,1)S(1)}, u32[]{:S(2)}, u32[]{:S(2)}) %collective-permute-start.50) | collective-permute-done | bytes 294944 | tf_op jit(solution)/shard_map/ppermute | solution.py:27
  (426 shorter events, 202.7 us)
Async XLA Ops:
  9.6 14.1 %collective-permute-start = (bf16[304,768]{1,0:T(8,128)(2,1)S(1)}, bf16[304,768]{1,0:T(8,128)(2,1)S(1)}, u32[]{:S(2)}, u32[]{:S(2)}) collective-permute-start(bf16[304,768]{1,0:T(8,128)(2,1)S(1)} %constant_dynamic-update-slice_fusion), channel_id=1, source_target_pairs={{0,8},{1,9},{2,10},{3,11},{4,12},{5,13},{6,14},{7,15},{8,0},{9,1},... | collective-permute-start | bytes 1400840 | tf_op jit(solution)/shard_map/ppermute | solution.py:27
  12.7 12.2 %collective-permute-start.1 = (bf16[304,768]{1,0:T(8,128)(2,1)S(1)}, bf16[304,768]{1,0:T(8,128)(2,1)S(1)}, u32[]{:S(2)}, u32[]{:S(2)}) collective-permute-start(bf16[304,768]{1,0:T(8,128)(2,1)S(1)} %constant_dynamic-update-slice_fusion), channel_id=1, source_target_pairs={{0,16},{1,17},{2,18},{3,19},{4,20},{5,21},{6,22},{7,23},{8,24},{9,... | collective-permute-start | bytes 1400840 | tf_op jit(solution)/shard_map/ppermute | solution.py:27
  14.2 34.5 %collective-permute-start.4 = (bf16[304,768]{1,0:T(8,128)(2,1)S(1)}, bf16[304,768]{1,0:T(8,128)(2,1)S(1)}, u32[]{:S(2)}, u32[]{:S(2)}) collective-permute-start(bf16[304,768]{1,0:T(8,128)(2,1)S(1)} %constant_dynamic-update-slice_fusion), channel_id=1, source_target_pairs={{0,4},{1,5},{2,6},{3,7},{4,0},{5,1},{6,2},{7,3},{8,12},{9,13},{10,... | collective-permute-start | bytes 1400840 | tf_op jit(solution)/shard_map/ppermute | solution.py:27
  24.8 82.8 %collective-permute-start.10 = (bf16[480,768]{1,0:T(8,128)(2,1)}, bf16[480,768]{1,0:T(8,128)(2,1)}, u32[]{:S(2)}, u32[]{:S(2)}) collective-permute-start(bf16[480,768]{1,0:T(8,128)(2,1)} %slice_dynamic-update-slice_fusion), channel_id=1, source_target_pairs={{0,16},{1,17},{2,18},{3,19},{4,20},{5,21},{6,22},{7,23},{8,24},{9,... | collective-permute-start | bytes 2211848 | tf_op jit(solution)/shard_map/ppermute | solution.py:27
  26.3 81.3 %collective-permute-start.9 = (bf16[480,768]{1,0:T(8,128)(2,1)}, bf16[480,768]{1,0:T(8,128)(2,1)}, u32[]{:S(2)}, u32[]{:S(2)}) collective-permute-start(bf16[480,768]{1,0:T(8,128)(2,1)} %slice_dynamic-update-slice_fusion), channel_id=1, source_target_pairs={{0,8},{1,9},{2,10},{3,11},{4,12},{5,13},{6,14},{7,15},{8,0},{9,1},... | collective-permute-start | bytes 2211848 | tf_op jit(solution)/shard_map/ppermute | solution.py:27
  26.9 20.8 %collective-permute-start.2 = (bf16[144,768]{1,0:T(8,128)(2,1)S(1)}, bf16[144,768]{1,0:T(8,128)(2,1)S(1)}, u32[]{:S(2)}, u32[]{:S(2)}) collective-permute-start(bf16[144,768]{1,0:T(8,128)(2,1)S(1)} %slice.228), channel_id=1, source_target_pairs={{0,16},{1,17},{2,18},{3,19},{4,20},{5,21},{6,22},{7,23},{8,24},{9,... | collective-permute-start | bytes 663560 | tf_op jit(solution)/shard_map/ppermute | solution.py:27
  27.3 21.3 %collective-permute-start.3 = (bf16[160,768]{1,0:T(8,128)(2,1)S(1)}, bf16[160,768]{1,0:T(8,128)(2,1)S(1)}, u32[]{:S(2)}, u32[]{:S(2)}) collective-permute-start(bf16[160,768]{1,0:T(8,128)(2,1)S(1)} %slice.229), channel_id=1, source_target_pairs={{0,8},{1,9},{2,10},{3,11},{4,12},{5,13},{6,14},{7,15},{8,0},{9,1},... | collective-permute-start | bytes 737288 | tf_op jit(solution)/shard_map/ppermute | solution.py:27
  47.6 84.4 %collective-permute-start.13 = (bf16[480,768]{1,0:T(8,128)(2,1)}, bf16[480,768]{1,0:T(8,128)(2,1)}, u32[]{:S(2)}, u32[]{:S(2)}) collective-permute-start(bf16[480,768]{1,0:T(8,128)(2,1)} %slice_dynamic-update-slice_fusion), channel_id=1, source_target_pairs={{0,4},{1,5},{2,6},{3,7},{4,0},{5,1},{6,2},{7,3},{8,12},{9,13},{10,... | collective-permute-start | bytes 2211848 | tf_op jit(solution)/shard_map/ppermute | solution.py:27
  107.6 25.7 %collective-permute-start.18 = (bf16[384,768]{1,0:T(8,128)(2,1)}, bf16[384,768]{1,0:T(8,128)(2,1)S(1)}, u32[]{:S(2)}, u32[]{:S(2)}) collective-permute-start(bf16[384,768]{1,0:T(8,128)(2,1)} %param.30), channel_id=1, source_target_pairs={{0,8},{1,9},{2,10},{3,11},{4,12},{5,13},{6,14},{7,15},{8,0},{9,1},... | collective-permute-start | bytes 1769480 | tf_op jit(solution)/shard_map/ppermute | solution.py:27
  108.2 25.7 %collective-permute-start.19 = (bf16[384,768]{1,0:T(8,128)(2,1)}, bf16[384,768]{1,0:T(8,128)(2,1)S(1)}, u32[]{:S(2)}, u32[]{:S(2)}) collective-permute-start(bf16[384,768]{1,0:T(8,128)(2,1)} %param.30), channel_id=1, source_target_pairs={{0,16},{1,17},{2,18},{3,19},{4,20},{5,21},{6,22},{7,23},{8,24},{9,... | collective-permute-start | bytes 1769480 | tf_op jit(solution)/shard_map/ppermute | solution.py:27
  110.2 21.2 %collective-permute-start.11 = (bf16[240,768]{1,0:T(8,128)(2,1)S(1)}, bf16[240,768]{1,0:T(8,128)(2,1)S(1)}, u32[]{:S(2)}, u32[]{:S(2)}) collective-permute-start(bf16[240,768]{1,0:T(8,128)(2,1)S(1)} %slice.236), channel_id=1, source_target_pairs={{0,16},{1,17},{2,18},{3,19},{4,20},{5,21},{6,22},{7,23},{8,24},{9,... | collective-permute-start | bytes 1105928 | tf_op jit(solution)/shard_map/ppermute | solution.py:27
  112.3 19.1 %collective-permute-start.12 = (bf16[240,768]{1,0:T(8,128)(2,1)S(1)}, bf16[240,768]{1,0:T(8,128)(2,1)S(1)}, u32[]{:S(2)}, u32[]{:S(2)}) collective-permute-start(bf16[240,768]{1,0:T(8,128)(2,1)S(1)} %slice.237), channel_id=1, source_target_pairs={{0,8},{1,9},{2,10},{3,11},{4,12},{5,13},{6,14},{7,15},{8,0},{9,1},... | collective-permute-start | bytes 1105928 | tf_op jit(solution)/shard_map/ppermute | solution.py:27
  131.4 47.2 %collective-permute-start.22 = (bf16[384,768]{1,0:T(8,128)(2,1)S(1)}, bf16[384,768]{1,0:T(8,128)(2,1)S(1)}, u32[]{:S(2)}, u32[]{:S(2)}) collective-permute-start(bf16[384,768]{1,0:T(8,128)(2,1)S(1)} %copy-done.32), channel_id=1, source_target_pairs={{0,4},{1,5},{2,6},{3,7},{4,0},{5,1},{6,2},{7,3},{8,12},{9,13},{10,... | collective-permute-start | bytes 1769480 | tf_op jit(solution)/shard_map/ppermute | solution.py:27
  134.4 43.4 %collective-permute-start.20 = (bf16[192,768]{1,0:T(8,128)(2,1)S(1)}, bf16[192,768]{1,0:T(8,128)(2,1)S(1)}, u32[]{:S(2)}, u32[]{:S(2)}) collective-permute-start(bf16[192,768]{1,0:T(8,128)(2,1)S(1)} %slice.247), channel_id=1, source_target_pairs={{0,16},{1,17},{2,18},{3,19},{4,20},{5,21},{6,22},{7,23},{8,24},{9,... | collective-permute-start | bytes 884744 | tf_op jit(solution)/shard_map/ppermute | solution.py:27
  135.5 42.5 %collective-permute-start.21 = (bf16[192,768]{1,0:T(8,128)(2,1)S(1)}, bf16[192,768]{1,0:T(8,128)(2,1)S(1)}, u32[]{:S(2)}, u32[]{:S(2)}) collective-permute-start(bf16[192,768]{1,0:T(8,128)(2,1)S(1)} %slice.248), channel_id=1, source_target_pairs={{0,8},{1,9},{2,10},{3,11},{4,12},{5,13},{6,14},{7,15},{8,0},{9,1},... | collective-permute-start | bytes 884744 | tf_op jit(solution)/shard_map/ppermute | solution.py:27
  137.1 41.5 %collective-permute-start.23 = (bf16[384,768]{1,0:T(8,128)(2,1)S(1)}, bf16[384,768]{1,0:T(8,128)(2,1)S(1)}, u32[]{:S(2)}, u32[]{:S(2)}) collective-permute-start(bf16[384,768]{1,0:T(8,128)(2,1)S(1)} %collective-permute-done.18), channel_id=1, source_target_pairs={{0,4},{1,5},{2,6},{3,7},{4,0},{5,1},{6,2},{7,3},{8,12},{9,13},{10,... | collective-permute-start | bytes 1769480 | tf_op jit(solution)/shard_map/ppermute | solution.py:27
  137.2 41.4 %collective-permute-start.24 = (bf16[384,768]{1,0:T(8,128)(2,1)S(1)}, bf16[384,768]{1,0:T(8,128)(2,1)S(1)}, u32[]{:S(2)}, u32[]{:S(2)}) collective-permute-start(bf16[384,768]{1,0:T(8,128)(2,1)S(1)} %collective-permute-done.19), channel_id=1, source_target_pairs={{0,4},{1,5},{2,6},{3,7},{4,0},{5,1},{6,2},{7,3},{8,12},{9,13},{10,... | collective-permute-start | bytes 1769480 | tf_op jit(solution)/shard_map/ppermute | solution.py:27
  319.9 25.1 %collective-permute-start.43 = (bf16[2,2,384,768]{3,2,1,0:T(8,128)(2,1)S(1)}, bf16[2,2,384,768]{3,2,1,0:T(8,128)(2,1)S(1)}, u32[]{:S(2)}, u32[]{:S(2)}) collective-permute-start(bf16[2,2,384,768]{3,2,1,0:T(8,128)(2,1)S(1)} %dynamic-slice_bitcast_fusion.2), channel_id=1, source_target_pairs={{0,4},{1,5},{2,6},{3,7},{4,0},{5,1},{6,2},{7,3},{8,12},{9,13},{10,... | collective-permute-start | bytes 7077896 | tf_op jit(solution)/shard_map/ppermute | solution.py:27
  329.0 12.3 %collective-permute-start.28 = (bf16[2,144,768]{2,1,0:T(8,128)(2,1)S(1)}, bf16[2,144,768]{2,1,0:T(8,128)(2,1)S(1)}, u32[]{:S(2)}, u32[]{:S(2)}) collective-permute-start(bf16[2,144,768]{2,1,0:T(8,128)(2,1)S(1)} %dynamic-slice_bitcast_fusion.9), channel_id=1, source_target_pairs={{0,8},{1,9},{2,10},{3,11},{4,12},{5,13},{6,14},{7,15},{8,0},{9,1},... | collective-permute-start | bytes 1327112 | tf_op jit(solution)/shard_map/ppermute | solution.py:27
  329.8 13.1 %collective-permute-start.30 = (bf16[2,160,768]{2,1,0:T(8,128)(2,1)S(1)}, bf16[2,160,768]{2,1,0:T(8,128)(2,1)S(1)}, u32[]{:S(2)}, u32[]{:S(2)}) collective-permute-start(bf16[2,160,768]{2,1,0:T(8,128)(2,1)S(1)} %dynamic-slice_bitcast_fusion.8), channel_id=1, source_target_pairs={{0,16},{1,17},{2,18},{3,19},{4,20},{5,21},{6,22},{7,23},{8,24},{9,... | collective-permute-start | bytes 1474568 | tf_op jit(solution)/shard_map/ppermute | solution.py:27
  331.1 39.7 %collective-permute-start.35 = (bf16[2,2,480,768]{3,2,1,0:T(8,128)(2,1)S(1)}, bf16[2,2,480,768]{3,2,1,0:T(8,128)(2,1)S(1)}, u32[]{:S(2)}, u32[]{:S(2)}) collective-permute-start(bf16[2,2,480,768]{3,2,1,0:T(8,128)(2,1)S(1)} %dynamic-slice_bitcast_fusion.1), channel_id=1, source_target_pairs={{0,4},{1,5},{2,6},{3,7},{4,0},{5,1},{6,2},{7,3},{8,12},{9,13},{10,... | collective-permute-start | bytes 8847368 | tf_op jit(solution)/shard_map/ppermute | solution.py:27
  345.9 17.0 %collective-permute-start.44 = (bf16[2,192,768]{2,1,0:T(8,128)(2,1)S(1)}, bf16[2,192,768]{2,1,0:T(8,128)(2,1)S(1)}, u32[]{:S(2)}, u32[]{:S(2)}) collective-permute-start(bf16[2,192,768]{2,1,0:T(8,128)(2,1)S(1)} %dynamic-slice_bitcast_fusion.7), channel_id=1, source_target_pairs={{0,8},{1,9},{2,10},{3,11},{4,12},{5,13},{6,14},{7,15},{8,0},{9,1},... | collective-permute-start | bytes 1769480 | tf_op jit(solution)/shard_map/ppermute | solution.py:27
  355.3 14.2 %collective-permute-start.46 = (bf16[2,192,768]{2,1,0:T(8,128)(2,1)S(1)}, bf16[2,192,768]{2,1,0:T(8,128)(2,1)S(1)}, u32[]{:S(2)}, u32[]{:S(2)}) collective-permute-start(bf16[2,192,768]{2,1,0:T(8,128)(2,1)S(1)} %dynamic-slice_bitcast_fusion.6), channel_id=1, source_target_pairs={{0,16},{1,17},{2,18},{3,19},{4,20},{5,21},{6,22},{7,23},{8,24},{9,... | collective-permute-start | bytes 1769480 | tf_op jit(solution)/shard_map/ppermute | solution.py:27
  360.2 13.9 %collective-permute-start.33 = (bf16[152,768]{1,0:T(8,128)(2,1)S(1)}, bf16[152,768]{1,0:T(8,128)(2,1)S(1)}, u32[]{:S(2)}, u32[]{:S(2)}) collective-permute-start(bf16[152,768]{1,0:T(8,128)(2,1)S(1)} %fusion.85), channel_id=1, source_target_pairs={{0,2},{1,3},{2,0},{3,1},{4,6},{5,7},{6,4},{7,5},{8,10},{9,11},{10,... | collective-permute-start | bytes 700424 | tf_op jit(solution)/shard_map/ppermute | solution.py:27
  363.1 12.7 %collective-permute-start.45 = (bf16[192,768]{1,0:T(8,128)(2,1)S(1)}, bf16[192,768]{1,0:T(8,128)(2,1)S(1)}, u32[]{:S(2)}, u32[]{:S(2)}) collective-permute-start(bf16[192,768]{1,0:T(8,128)(2,1)S(1)} %dynamic-slice_bitcast_fusion.15), channel_id=1, source_target_pairs={{0,16},{1,17},{2,18},{3,19},{4,20},{5,21},{6,22},{7,23},{8,24},{9,... | collective-permute-start | bytes 884744 | tf_op jit(solution)/shard_map/ppermute | solution.py:27
  371.9 15.0 %collective-permute-start.36 = (bf16[2,240,768]{2,1,0:T(8,128)(2,1)S(1)}, bf16[2,240,768]{2,1,0:T(8,128)(2,1)S(1)}, u32[]{:S(2)}, u32[]{:S(2)}) collective-permute-start(bf16[2,240,768]{2,1,0:T(8,128)(2,1)S(1)} %dynamic-slice_bitcast_fusion.5), channel_id=1, source_target_pairs={{0,8},{1,9},{2,10},{3,11},{4,12},{5,13},{6,14},{7,15},{8,0},{9,1},... | collective-permute-start | bytes 2211848 | tf_op jit(solution)/shard_map/ppermute | solution.py:27
  372.9 19.4 %collective-permute-start.38 = (bf16[2,240,768]{2,1,0:T(8,128)(2,1)S(1)}, bf16[2,240,768]{2,1,0:T(8,128)(2,1)S(1)}, u32[]{:S(2)}, u32[]{:S(2)}) collective-permute-start(bf16[2,240,768]{2,1,0:T(8,128)(2,1)S(1)} %dynamic-slice_bitcast_fusion.4), channel_id=1, source_target_pairs={{0,16},{1,17},{2,18},{3,19},{4,20},{5,21},{6,22},{7,23},{8,24},{9,... | collective-permute-start | bytes 2211848 | tf_op jit(solution)/shard_map/ppermute | solution.py:27
  374.1 29.4 %collective-permute-start.34 = (bf16[152,768]{1,0:T(8,128)(2,1)S(1)}, bf16[152,768]{1,0:T(8,128)(2,1)S(1)}, u32[]{:S(2)}, u32[]{:S(2)}) collective-permute-start(bf16[152,768]{1,0:T(8,128)(2,1)S(1)} %add_convert_fusion.6), channel_id=1, source_target_pairs={{0,1},{1,0},{2,3},{3,2},{4,5},{5,4},{6,7},{7,6},{8,9},{9,8},{10,11... | collective-permute-start | bytes 700424 | tf_op jit(solution)/shard_map/ppermute | solution.py:27
  393.9 12.6 %collective-permute-start.48 = (bf16[192,768]{1,0:T(8,128)(2,1)S(1)}, bf16[192,768]{1,0:T(8,128)(2,1)S(1)}, u32[]{:S(2)}, u32[]{:S(2)}) collective-permute-start(bf16[192,768]{1,0:T(8,128)(2,1)S(1)} %dynamic-slice_bitcast_fusion.13), channel_id=1, source_target_pairs={{0,1},{1,0},{2,3},{3,2},{4,5},{5,4},{6,7},{7,6},{8,9},{9,8},{10,11... | collective-permute-start | bytes 884744 | tf_op jit(solution)/shard_map/ppermute | solution.py:27
  406.6 21.8 %collective-permute-start.49 = (bf16[192,768]{1,0:T(8,128)(2,1)S(1)}, bf16[192,768]{1,0:T(8,128)(2,1)S(1)}, u32[]{:S(2)}, u32[]{:S(2)}) collective-permute-start(bf16[192,768]{1,0:T(8,128)(2,1)S(1)} %fusion.81), channel_id=1, source_target_pairs={{0,2},{1,3},{2,0},{3,1},{4,6},{5,7},{6,4},{7,5},{8,10},{9,11},{10,... | collective-permute-start | bytes 884744 | tf_op jit(solution)/shard_map/ppermute | solution.py:27
  411.2 21.3 %collective-permute-start.41 = (bf16[240,768]{1,0:T(8,128)(2,1)S(1)}, bf16[240,768]{1,0:T(8,128)(2,1)S(1)}, u32[]{:S(2)}, u32[]{:S(2)}) collective-permute-start(bf16[240,768]{1,0:T(8,128)(2,1)S(1)} %fusion.77), channel_id=1, source_target_pairs={{0,2},{1,3},{2,0},{3,1},{4,6},{5,7},{6,4},{7,5},{8,10},{9,11},{10,... | collective-permute-start | bytes 1105928 | tf_op jit(solution)/shard_map/ppermute | solution.py:27
  432.6 10.9 %collective-permute-start.42 = (bf16[240,768]{1,0:T(8,128)(2,1)S(1)}, bf16[240,768]{1,0:T(8,128)(2,1)S(1)}, u32[]{:S(2)}, u32[]{:S(2)}) collective-permute-start(bf16[240,768]{1,0:T(8,128)(2,1)S(1)} %add_convert_fusion.4), channel_id=1, source_target_pairs={{0,1},{1,0},{2,3},{3,2},{4,5},{5,4},{6,7},{7,6},{8,9},{9,8},{10,11... | collective-permute-start | bytes 1105928 | tf_op jit(solution)/shard_map/ppermute | solution.py:27
  (79 other events, 337.5 us)

commit v2 on v1

v2 whole, which is shorter than its diff:
```python
import jax
import jax.numpy as jnp
from jax import lax
from jax.experimental import pallas as pl
from jax.experimental.pallas import tpu as pltpu
from jax.sharding import PartitionSpec as P

HEADS = 12
HEAD_DIM = 64


NORM_EPS = 1e-12
inverse_root_two = 0.7071067811865476
inverse_root_tau = 0.3989422804014327


AXES = ("group", "replica")


def swap_with(array, group_mask, replica_mask=0):
    groups, replicas = lax.axis_size("group"), lax.axis_size("replica")
    pairs = [
        (g * replicas + r, (g ^ group_mask) * replicas + (r ^ replica_mask))
        for g in range(groups)
        for r in range(replicas)
    ]
    return lax.ppermute(array, AXES, pairs)


def after(array, *others):
    return lax.optimization_barrier((array,) + others)[0] if others else array


def gather_group(shard, bits, wait_for):
    plane = [1 << b for b in range(1, bits)]
    half = shard.shape[0] // 32 * 16
    orders = (plane, plane[::-1])
    cut = (slice(0, half), slice(half, None))
    shard = after(shard, *wait_for)
    pieces = {0: [shard]}
    first = []
    for mask in plane:
        pieces[mask] = [swap_with(shard, mask)]
        first.append(pieces[mask][0])
    halves = {d: [p[0][c] for c in cut] for d, p in pieces.items()}
    for count in range(2, len(plane) + 1):
        for d in range(2, 1 << bits, 2):
            if bin(d).count("1") != count:
                continue
            got = []
            for which, order in enumerate(orders):
                last = [m for m in order if m & d][-1]
                got.append(swap_with(halves[d ^ last][which], last))
            pieces[d] = got
            halves[d] = got
    for d in list(pieces):
        pieces[d | 1] = [swap_with(p, 1) for p in pieces[d]]
    return pieces, first


def place(pieces, me, group_size):
    rows = sum(p.shape[0] for p in pieces[0])
    full = jnp.zeros((group_size, rows, pieces[0][0].shape[1]), jnp.bfloat16)
    for d, parts in pieces.items():
        at = 0
        for part in parts:
            full = lax.dynamic_update_slice(full, part[None], (me ^ d, at, 0))
            at += part.shape[0]
    return full


def pick(array, axis, index):
    return lax.dynamic_index_in_dim(array, index, axis, keepdims=False)


def add_low(left, right):
    return (left.astype(jnp.float32) + right.astype(jnp.float32)).astype(jnp.bfloat16)


def reduce_all(own, send, bits):
    rows, width = own.shape[1:]
    chunks = add_low(own, swap_with(send, 1)).reshape((2,) * (bits - 1) + (rows, width))
    half = rows // 32 * 16
    done = []
    for part, order in ((chunks[..., :half, :], 0), (chunks[..., half:, :], 1)):
        left = list(range(1, bits))
        for b in left[:] if order == 0 else left[::-1]:
            axis = len(left) - 1 - left.index(b)
            kept, away = (lax.index_in_dim(part, i, axis, keepdims=False) for i in (0, 1))
            part = add_low(kept, swap_with(away, 1 << b))
            left.remove(b)
        done.append(part)
    return sum_replicas(jnp.concatenate(done))


def sum_replicas(total):
    replicas = lax.axis_size("replica")
    if replicas == 1:
        return total
    rows, width = total.shape
    at = lax.axis_index("replica")
    pair = total.reshape(2, rows // 2, width)
    kept = add_low(pick(pair, 0, at & 1), swap_with(pick(pair, 0, 1 - (at & 1)), 0, 1))
    mask = 2
    while mask < replicas:
        kept = add_low(kept, swap_with(kept, 0, mask))
        mask *= 2
    other = swap_with(kept, 0, 1)
    return jnp.where(
        (at & 1) == 0, jnp.concatenate([kept, other]), jnp.concatenate([other, kept])
    )


def sum_everywhere(array, bits):
    for b in range(bits):
        array = array + swap_with(array, 1 << b)
    mask = 1
    while mask < lax.axis_size("replica"):
        array = array + swap_with(array, 0, mask)
        mask *= 2
    return array


VMEM_LIMIT = 60 * 1024 * 1024
GROUP_HEADS = 4
GROUP_COLS = GROUP_HEADS * HEAD_DIM


def nt(left, right):
    return lax.dot_general(left, right, (((1,), (1,)), ((), ())), preferred_element_type=jnp.float32)


def nn(left, right):
    return lax.dot_general(left, right, (((1,), (0,)), ((), ())), preferred_element_type=jnp.float32)


def tn(left, right):
    return lax.dot_general(left, right, (((0,), (0,)), ((), ())), preferred_element_type=jnp.float32)


def kernel_params(**more):
    return pltpu.CompilerParams(vmem_limit_bytes=VMEM_LIMIT, **more)


def cost(flops, moved):
    return pl.CostEstimate(flops=int(flops), bytes_accessed=int(moved), transcendentals=0)


def one_head(pair, head):
    lanes = lax.broadcasted_iota(jnp.int32, pair.shape, 1)
    keep = lanes < HEAD_DIM if head % 2 == 0 else lanes >= HEAD_DIM
    return jnp.where(keep, pair, jnp.zeros_like(pair))


def attend_kernel(lens, x, wq, wk, wv, bq, bv, q_out, k_out, v_out, mixed_out, probs_out):
    slots = x.shape[0]
    rows = x[...]
    q = ((nn(rows, wq[...]) + bq[...]).astype(jnp.bfloat16) * 0.125).astype(jnp.bfloat16)
    k = nn(rows, wk[...]).astype(jnp.bfloat16)
    v = (nn(rows, wv[...]) + bv[...]).astype(jnp.bfloat16)
    q_out[...] = q
    k_out[...] = k
    v_out[...] = v
    turned = v.astype(jnp.float32).T.astype(jnp.bfloat16)
    valid = lax.broadcasted_iota(jnp.int32, (slots, 1), 0) < lens[pl.program_id(0)]
    block = min(256, slots)
    for head in range(GROUP_HEADS):
        pair = slice(head // 2 * 128, head // 2 * 128 + 128)
        keys = one_head(k[:, pair], head)
        for at in range(0, slots, block):
            scores = nt(keys, q[at : at + block, pair])
            scores = jnp.where(valid, scores, -1e30)
            lifted = jnp.exp(scores - jnp.max(scores, axis=0, keepdims=True))
            share = 1.0 / jnp.sum(lifted, axis=0, keepdims=True)
            probs_out[head, :, at : at + block] = (lifted * share).astype(jnp.bfloat16)
    joined = jnp.concatenate(
        [
            nn(turned[h * HEAD_DIM : (h + 1) * HEAD_DIM], probs_out[h])
            for h in range(GROUP_HEADS)
        ]
    )
    mixed_out[...] = joined.T.astype(jnp.bfloat16)


def attend(lengths, rows, wq, wk, wv, bq, bv):
    seqs = lengths.shape[0]
    total, width = rows.shape
    slots = total // seqs
    groups = width // GROUP_COLS
    weight = pl.BlockSpec((width, GROUP_COLS), lambda s, j, lens: (0, j))
    bias = pl.BlockSpec((1, GROUP_COLS), lambda s, j, lens: (0, j))
    part = pl.BlockSpec((slots, GROUP_COLS), lambda s, j, lens: (s, j))
    table = jax.ShapeDtypeStruct((total, width), jnp.bfloat16)
    return pl.pallas_call(
        attend_kernel,
        out_shape=[table] * 4
        + [jax.ShapeDtypeStruct((seqs * groups * GROUP_HEADS, slots, slots), jnp.bfloat16)],
        grid_spec=pltpu.PrefetchScalarGridSpec(
            num_scalar_prefetch=1,
            grid=(seqs, groups),
            in_specs=[pl.BlockSpec((slots, width), lambda s, j, lens: (s, 0))]
            + [weight] * 3
            + [bias] * 2,
            out_specs=[part] * 4
            + [
                pl.BlockSpec(
                    (GROUP_HEADS, slots, slots), lambda s, j, lens: (s * groups + j, 0, 0)
                )
            ],
        ),
        compiler_params=kernel_params(),
        cost_estimate=cost(6 * total * width * width + 8 * total * slots * width, 3e7),
        name="attend",
    )(lengths, rows, wq, wk, wv, bq, bv)


def attend_back_kernel(q, k, v, grad, probs, grads_out, sums_out, held):
    slots = q.shape[0]
    block = min(256, slots)
    key_turned = k[...].astype(jnp.float32).T.astype(jnp.bfloat16)
    dq_parts = []
    for which in range(GROUP_HEADS // 2):
        pair = slice(which * 128, which * 128 + 128)
        grads, queries, values = grad[:, pair], q[:, pair], v[:, pair]
        dv = dk = None
        for head in (2 * which, 2 * which + 1):
            own_values = one_head(values, head)
            for at in range(0, slots, block):
                cols = slice(at, at + block)
                grad_probs = nt(own_values, grads[cols])
                soft = probs[head, :, cols].astype(jnp.float32)
                inner = jnp.sum(soft * grad_probs, axis=0, keepdims=True)
                held[:, cols] = (soft * (grad_probs - inner)).astype(jnp.bfloat16)
            scores_grad = held[...]
            more_v = nn(probs[head], one_head(grads, head))
            more_k = nn(scores_grad, one_head(queries, head))
            dv = more_v if dv is None else dv + more_v
            dk = more_k if dk is None else dk + more_k
            dq_parts.append(nn(key_turned[head * HEAD_DIM : (head + 1) * HEAD_DIM], scores_grad))
        grads_out[1, :, pair] = dk.astype(jnp.bfloat16)
        grads_out[2, :, pair] = dv.astype(jnp.bfloat16)
    grads_out[0] = (jnp.concatenate(dq_parts).T * 0.125).astype(jnp.bfloat16)
    sums_out[0, 0:1, :] = jnp.sum(grads_out[0].astype(jnp.float32), axis=0, keepdims=True)
    sums_out[0, 1:2, :] = jnp.sum(grads_out[2].astype(jnp.float32), axis=0, keepdims=True)


def attend_back(seqs, q, k, v, grad, probs):
    total, width = q.shape
    slots = total // seqs
    groups = width // GROUP_COLS
    part = pl.BlockSpec((slots, GROUP_COLS), lambda s, j: (s, j))
    return pl.pallas_call(
        attend_back_kernel,
        out_shape=[
            jax.ShapeDtypeStruct((3, total, width), jnp.bfloat16),
            jax.ShapeDtypeStruct((seqs, 2, width), jnp.float32),
        ],
        grid=(seqs, groups),
        in_specs=[part] * 4
        + [pl.BlockSpec((GROUP_HEADS, slots, slots), lambda s, j: (s * groups + j, 0, 0))],
        out_specs=[
            pl.BlockSpec((3, slots, GROUP_COLS), lambda s, j: (0, s, j)),
            pl.BlockSpec((1, 2, GROUP_COLS), lambda s, j: (s, 0, j)),
        ],
        scratch_shapes=[pltpu.VMEM((slots, slots), jnp.bfloat16)],
        compiler_params=kernel_params(),
        cost_estimate=cost(14 * total * slots * width, 3e7),
        name="attend_back",
    )(q, k, v, grad, probs)


def row_mean(array):
    return jnp.mean(array, -1, keepdims=True)


def feed_kernel(mixed, x, wo, wi, bo, g1, s1, bi, after_out, normed_out, inverse_out, active_out, slope_out):
    hidden_in = x[...].astype(jnp.float32) + (nn(mixed[...], wo[...]) + bo[...])
    centre = hidden_in - row_mean(hidden_in)
    inverse = lax.rsqrt(row_mean(centre * centre) + NORM_EPS)
    normed = centre * inverse
    after = (normed * g1[...] + s1[...]).astype(jnp.bfloat16)
    normed_out[...] = normed
    inverse_out[...] = jnp.broadcast_to(inverse, inverse_out.shape)
    after_out[...] = after
    width = after.shape[1]
    for at in range(0, wi.shape[1], width):
        cols = slice(at, at + width)
        hidden = nn(after, wi[:, cols]) + bi[:, cols]
        cdf = 0.5 * (1.0 + lax.erf(hidden * inverse_root_two))
        density = jnp.exp(-0.5 * hidden * hidden) * inverse_root_tau
        active_out[:, cols] = (hidden * cdf).astype(jnp.bfloat16)
        slope_out[:, cols] = (cdf + hidden * density).astype(jnp.bfloat16)


def whole(array):
    return pl.BlockSpec(array.shape, lambda *_: (0,) * array.ndim, pipeline_mode=pl.Buffered(1))


def by_rows(rows, width):
    return pl.BlockSpec((rows, width), lambda i, *_: (i, 0))


def shape(rows, width, dtype):
    return jax.ShapeDtypeStruct((rows, width), dtype)


def feed(mixed, x, wo, wi, bo, g1, s1, bi):
    total, width = x.shape
    wide = wi.shape[1]
    rows = min(256, total)
    bf, f32 = jnp.bfloat16, jnp.float32
    return pl.pallas_call(
        feed_kernel,
        out_shape=[
            shape(total, width, bf), shape(total, width, f32), shape(total, 128, f32),
            shape(total, wide, bf), shape(total, wide, bf),
        ],
        grid=(total // rows,),
        in_specs=[by_rows(rows, width)] * 2 + [whole(a) for a in (wo, wi, bo, g1, s1, bi)],
        out_specs=[by_rows(rows, n) for n in (width, width, 128, wide, wide)],
        compiler_params=kernel_params(),
        cost_estimate=cost(2 * total * width * (width + wide), 3e7),
        name="feed",
    )(mixed, x, wo, wi, bo, g1, s1, bi)


def column_sum(array):
    return jnp.sum(array, axis=0, keepdims=True)


def turn_kernel(lens, slots, active, normed1, slope, cot, wb, bb, g1, s1, g2, s2,
                layer_out, ffn_grad_out, hidden_grad_out, h2_grad_out, sums_out, wide_sums_out):
    step = pl.program_id(0)

    @pl.when(step == 0)
    def _():
        sums_out[...] = jnp.zeros_like(sums_out)
        wide_sums_out[...] = jnp.zeros_like(wide_sums_out)

    rows, width = normed1.shape
    after = normed1[...] * g1[...] + s1[...]
    h2 = after + (nn(active[...], wb[...]) + bb[...])
    centre = h2 - row_mean(h2)
    inverse = lax.rsqrt(row_mean(centre * centre) + NORM_EPS)
    normed = centre * inverse
    layer_out[...] = (normed * g2[...] + s2[...]).astype(jnp.bfloat16)
    first = step * rows
    place_in = first % slots + lax.broadcasted_iota(jnp.int32, (rows, 1), 0)
    grad = jnp.where(place_in < lens[first // slots], cot[...].astype(jnp.float32), 0.0)
    scaled = grad * g2[...]
    h2_grad = inverse * (scaled - row_mean(scaled) - normed * row_mean(scaled * normed))
    h2_grad_out[...] = h2_grad
    low = h2_grad.astype(jnp.bfloat16)
    ffn_grad_out[...] = low
    sums_out[0:1, :] += column_sum(grad * normed)
    sums_out[1:2, :] += column_sum(grad)
    sums_out[2:3, :] += column_sum(low.astype(jnp.float32))
    for at in range(0, wb.shape[0], width):
        cols = slice(at, at + width)
        piece = (nt(low, wb[cols, :]) * slope[:, cols].astype(jnp.float32)).astype(jnp.bfloat16)
        hidden_grad_out[:, cols] = piece
        wide_sums_out[:, cols] += column_sum(piece.astype(jnp.float32))


def turn(lengths, slots, active, normed1, slope, cot, wb, bb, g1, s1, g2, s2):
    total, width = normed1.shape
    wide = wb.shape[0]
    rows = min(256, slots)
    bf, f32 = jnp.bfloat16, jnp.float32
    fixed = lambda r, n: pl.BlockSpec((r, n), lambda i, *_: (0, 0))
    body = lambda lens, *refs: turn_kernel(lens, slots, *refs)
    return pl.pallas_call(
        body,
        out_shape=[
            shape(total, width, bf), shape(total, width, bf), shape(total, wide, bf),
            shape(total, width, f32), shape(8, width, f32), shape(1, wide, f32),
        ],
        grid_spec=pltpu.PrefetchScalarGridSpec(
            num_scalar_prefetch=1,
            grid=(total // rows,),
            in_specs=[by_rows(rows, n) for n in (wide, width, wide, width)]
            + [whole(a) for a in (wb, bb, g1, s1, g2, s2)],
            out_specs=[by_rows(rows, n) for n in (width, width, wide, width)]
            + [fixed(8, width), fixed(1, wide)],
        ),
        compiler_params=kernel_params(),
        cost_estimate=cost(4 * total * width * wide, 3e7),
        name="turn",
    )(lengths, active, normed1, slope, cot, wb, bb, g1, s1, g2, s2)


def return_kernel(hidden_grad, h2_grad, normed1, inverse1, wi, wo, g1,
                  h1_grad_out, branch_grad_out, mixed_grad_out, sums_out):
    @pl.when(pl.program_id(0) == 0)
    def _():
        sums_out[...] = jnp.zeros_like(sums_out)

    after_grad = nt(hidden_grad[...], wi[...]) + h2_grad[...]
    normed = normed1[...]
    scaled = after_grad * g1[...]
    h1_grad = inverse1[:, 0:1] * (scaled - row_mean(scaled) - normed * row_mean(scaled * normed))
    h1_grad_out[...] = h1_grad
    low = h1_grad.astype(jnp.bfloat16)
    branch_grad_out[...] = low
    mixed_grad_out[...] = nt(low, wo[...]).astype(jnp.bfloat16)
    sums_out[0:1, :] += column_sum(after_grad * normed)
    sums_out[1:2, :] += column_sum(after_grad)
    sums_out[2:3, :] += column_sum(low.astype(jnp.float32))


def return_grad(hidden_grad, h2_grad, normed1, inverse1, wi, wo, g1):
    total, width = normed1.shape
    wide = wi.shape[1]
    rows = min(256, total)
    bf, f32 = jnp.bfloat16, jnp.float32
    return pl.pallas_call(
        return_kernel,
        out_shape=[
            shape(total, width, f32), shape(total, width, bf), shape(total, width, bf), shape(8, width, f32),
        ],
        grid=(total // rows,),
        in_specs=[by_rows(rows, n) for n in (wide, width, width, 128)] + [whole(a) for a in (wi, wo, g1)],
        out_specs=[by_rows(rows, width)] * 3 + [pl.BlockSpec((8, width), lambda i: (0, 0))],
        compiler_params=kernel_params(),
        cost_estimate=cost(2 * total * width * (width + wide), 3e7),
        name="return_grad",
    )(hidden_grad, h2_grad, normed1, inverse1, wi, wo, g1)


def input_kernel(h1_grad, grads, wq, wk, wv, out):
    total = h1_grad[...] + nt(grads[0], wq[...]) + nt(grads[1], wk[...]) + nt(grads[2], wv[...])
    out[...] = total.astype(jnp.bfloat16)


def input_grad_of(h1_grad, grads, wq, wk, wv):
    total, width = h1_grad.shape
    rows = min(256, total)
    return pl.pallas_call(
        input_kernel,
        out_shape=shape(total, width, jnp.bfloat16),
        grid=(total // rows,),
        in_specs=[by_rows(rows, width), pl.BlockSpec((3, rows, width), lambda i: (0, i, 0))]
        + [whole(a) for a in (wq, wk, wv)],
        out_specs=by_rows(rows, width),
        compiler_params=kernel_params(),
        cost_estimate=cost(6 * total * width * width, 2e7),
        name="input_grad",
    )(h1_grad, grads, wq, wk, wv)


def store_chunks(product, me, own, send):
    count = 2 * own.shape[0]
    rows = product.shape[0] // count
    for g in range(count):
        chunk = product[g * rows : (g + 1) * rows].astype(jnp.bfloat16)
        apart = g ^ me

        @pl.when(apart % 2 == 0)
        def _():
            own[apart // 2] = chunk

        @pl.when(apart % 2 == 1)
        def _():
            send[apart // 2] = chunk


def halves(count, rows, blocks, width):
    return [jax.ShapeDtypeStruct((count // 2, rows * blocks, width), jnp.bfloat16)] * 2


def back_weight_kernel(me, active, grad, own, send):
    step = pl.program_id(0)
    product = tn(active[...], grad[...]).astype(jnp.bfloat16)
    half = pl.num_programs(0) // 2

    @pl.when(step < half)
    def _():
        send[0] = product

    @pl.when(step >= half)
    def _():
        own[0] = product


def plain_weight_kernel(me, active, grad, own, send):
    store_chunks(tn(active[...], grad[...]), me[0], own, send)


def back_weight(me, active, grad, count):
    total, wide = active.shape
    width = grad.shape[1]
    rows = wide // count
    half = count // 2
    common = dict(
        out_shape=halves(count, rows, 1, width),
        compiler_params=kernel_params(),
        cost_estimate=cost(2 * total * wide * width, 1.3e7),
        name="back_weight",
    )
    if rows % 128 == 0:
        chunk = lambda t, me: ((2 * (t % half) + 1 - t // half) ^ me[0])
        return pl.pallas_call(
            back_weight_kernel,
            grid_spec=pltpu.PrefetchScalarGridSpec(
                num_scalar_prefetch=1,
                grid=(count,),
                in_specs=[pl.BlockSpec((total, rows), lambda t, me: (0, chunk(t, me))), whole(grad)],
                out_specs=[
                    pl.BlockSpec((1, rows, width), lambda t, me: (jnp.maximum(t - half, 0), 0, 0)),
                    pl.BlockSpec((1, rows, width), lambda t, me: (jnp.minimum(t, half - 1), 0, 0)),
                ],
            ),
            **common,
        )(me, active, grad)
    block = 256
    return pl.pallas_call(
        plain_weight_kernel,
        grid_spec=pltpu.PrefetchScalarGridSpec(
            num_scalar_prefetch=1,
            grid=(width // block,),
            in_specs=[whole(active), pl.BlockSpec((total, block), lambda j, me: (0, j))],
            out_specs=[pl.BlockSpec((half, rows, block), lambda j, me: (0, 0, j))] * 2,
        ),
        **common,
    )(me, active, grad)


def in_out_kernel(me, after, hidden_grad, mixed, branch_grad, own, send):
    last = pl.program_id(0) == pl.num_programs(0) - 1

    @pl.when(jnp.logical_not(last))
    def _():
        store_chunks(tn(after[...], hidden_grad[...]), me[0], own, send)

    @pl.when(last)
    def _():
        store_chunks(tn(mixed[...], branch_grad[...]), me[0], own, send)


def in_out_weight(me, after, hidden_grad, mixed, branch_grad, count):
    total, width = after.shape
    blocks = hidden_grad.shape[1] // width
    rows = width // count
    return pl.pallas_call(
        in_out_kernel,
        out_shape=halves(count, rows, blocks + 1, width),
        grid_spec=pltpu.PrefetchScalarGridSpec(
            num_scalar_prefetch=1,
            grid=(blocks + 1,),
            in_specs=[
                whole(after),
                pl.BlockSpec((total, width), lambda j, me: (0, jnp.minimum(j, blocks - 1))),
                whole(mixed),
                whole(branch_grad),
            ],
            out_specs=[pl.BlockSpec((count // 2, rows, width), lambda j, me: (0, j, 0))] * 2,
        ),
        compiler_params=kernel_params(),
        cost_estimate=cost(2 * total * width * width * (blocks + 1), 2e7),
        name="in_out_weight",
    )(me, after, hidden_grad, mixed, branch_grad)


def qkv_weight_kernel(me, rows, grads, own, send):
    store_chunks(tn(rows[...], grads[0]), me[0], own, send)


def qkv_weight(me, rows, grads, count):
    total, width = rows.shape
    chunk = width // count
    return pl.pallas_call(
        qkv_weight_kernel,
        out_shape=halves(count, chunk, 3, width),
        grid_spec=pltpu.PrefetchScalarGridSpec(
            num_scalar_prefetch=1,
            grid=(3,),
            in_specs=[whole(rows), pl.BlockSpec((1, total, width), lambda j, me: (j, 0, 0))],
            out_specs=[pl.BlockSpec((count // 2, chunk, width), lambda j, me: (0, j, 0))] * 2,
        ),
        compiler_params=kernel_params(),
        cost_estimate=cost(6 * total * width * width, 1e7),
        name="qkv_weight",
    )(me, rows, grads)


def pack_kernel(*refs):
    out = refs[-1]
    out[...] = jnp.zeros_like(out)
    at = 0
    for ref in refs[:-1]:
        size = ref.shape[1]
        for first in range(0, size, 128):
            n = min(128, size - first)
            out[at : at + 1, 0:n] = ref[:, first : first + n].astype(jnp.float32)
            at += 1


def spread_kernel(me, table, vectors_out, wide_out):
    count = table.shape[0]
    chunk = vectors_out.shape[1] // count
    wide_chunk = wide_out.shape[1] // count
    for g in range(count):
        tile = table[g ^ me[0]]
        vectors_out[:, g * chunk : (g + 1) * chunk] = tile[0:8, 0:chunk]
        for n, first in enumerate(range(0, wide_chunk, 128)):
            size = min(128, wide_chunk - first)
            wide_out[:, g * wide_chunk + first : g * wide_chunk + first + size] = tile[8 + n : 9 + n, 0:size]


def collect_kernel(me, vectors, wide, *outs):
    count = vectors.shape[1] // outs[0].shape[1]
    for g in range(count):

        @pl.when(g == me[0])
        def _():
            for i in range(8):
                n = outs[i].shape[1]
                outs[i][...] = vectors[i : i + 1, g * n : (g + 1) * n]
            n = outs[8].shape[1]
            outs[8][...] = wide[:, g * n : (g + 1) * n]


SMEM = lambda: pl.BlockSpec(memory_space=pltpu.SMEM)
VMEM = lambda: pl.BlockSpec(memory_space=pltpu.VMEM)


def pack(vectors):
    return pl.pallas_call(
        pack_kernel, out_shape=shape(16, 128, jnp.float32), in_specs=[VMEM()] * len(vectors), out_specs=VMEM(),
        compiler_params=kernel_params(), name="pack",
    )(*[v.reshape(1, -1) for v in vectors])


def spread(me, table, width, wide):
    return pl.pallas_call(
        spread_kernel, out_shape=[shape(8, width, jnp.float32), shape(1, wide, jnp.float32)],
        in_specs=[SMEM(), VMEM()], out_specs=[VMEM()] * 2, compiler_params=kernel_params(), name="spread",
    )(me, table)


def collect(me, vectors, wide, count):
    sizes = [vectors.shape[1] // count] * 8 + [wide.shape[1] // count]
    outs = pl.pallas_call(
        collect_kernel, out_shape=[shape(1, n, jnp.float32) for n in sizes],
        in_specs=[SMEM(), VMEM(), VMEM()], out_specs=[VMEM()] * 9, compiler_params=kernel_params(), name="collect",
    )(me, vectors, wide)
    return [o.reshape(-1) for o in outs]


def per_device(
    inputs, cotangent, lengths,
    query_weight, key_weight, value_weight, out_weight, in_weight, back_weight_shard,
    query_bias, value_bias, out_bias, in_bias, back_bias,
    first_gain, first_shift, second_gain, second_shift,
):
    index = lax.axis_index("group")
    me = index.reshape(1).astype(jnp.int32)
    count = lax.axis_size("group")
    bits = count.bit_length() - 1
    seqs, slots, width = inputs.shape
    total = seqs * slots
    chunk = query_weight.shape[0]
    wide = in_weight.shape[1]
    blocks = wide // width
    x = inputs.reshape(total, width)
    cot = cotangent.reshape(total, width)

    table = pack(
        [query_bias, value_bias, out_bias, back_bias, first_gain, first_shift, second_gain, second_shift, in_bias]
    )[None]
    in_blocks = [in_weight[:, n * width : (n + 1) * width] for n in range(blocks)]
    got_a = gather_group(jnp.concatenate([query_weight, key_weight, value_weight]), bits, ())
    for b in range(bits - 1, -1, -1):
        table = jnp.stack([table, swap_with(table, 1 << b)], axis=1).reshape((-1,) + table.shape[1:])
    got_b = gather_group(jnp.concatenate([out_weight] + in_blocks), bits, got_a[1])
    got_c = gather_group(back_weight_shard, bits, got_b[1])
    vectors, bi = spread(me, table, width, wide)
    bq, bv, bo, bb, g1, s1, g2, s2 = (vectors[i : i + 1] for i in range(8))
    full_a = place(got_a[0], index, count)
    full_b = place(got_b[0], index, count)
    full_c = place(got_c[0], index, count)
    wq, wk, wv = (full_a[:, n * chunk : (n + 1) * chunk].reshape(width, width) for n in range(3))
    wo = full_b[:, :chunk].reshape(width, width)
    wi = jnp.concatenate(
        [full_b[:, n * chunk : (n + 1) * chunk] for n in range(1, blocks + 1)], axis=2
    ).reshape(width, wide)
    wb = full_c.reshape(wide, width)

    q, k, v, mixed, probs = attend(lengths, x, wq, wk, wv, bq, bv)
    after_low, normed1, inverse1, active, slope = feed(mixed, x, wo, wi, bo, g1, s1, bi)
    layer_out, ffn_grad, hidden_grad, h2_grad, sums2, in_bias_sum = turn(
        lengths, slots, active, normed1, slope, cot, wb, bb, g1, s1, g2, s2
    )
    sum_c = reduce_all(*back_weight(me, active, ffn_grad, count), bits)
    h1_grad, branch_grad, mixed_grad, sums1 = return_grad(hidden_grad, h2_grad, normed1, inverse1, wi, wo, g1)
    sum_b = reduce_all(*in_out_weight(me, after_low, hidden_grad, mixed, branch_grad, count), bits)
    grads, attend_sums = attend_back(seqs, q, k, v, mixed_grad, probs)
    sum_a = reduce_all(*qkv_weight(me, x, grads, count), bits)
    input_grad = input_grad_of(h1_grad, grads, wq, wk, wv)

    small = jnp.concatenate(
        [
            jnp.sum(attend_sums, 0), sums1[2:3], sums2[2:3], sums1[0:2], sums2[0:2],
            in_bias_sum.reshape(blocks, width),
        ]
    )
    small = sum_everywhere(small, bits)
    vector_grads = collect(me, small[0:8], small[8:].reshape(1, wide), count)
    grad_q, grad_v, grad_o, grad_b, grad_g1, grad_s1, grad_g2, grad_s2, grad_i = vector_grads
    up = lambda a: a.astype(jnp.float32)
    in_sum = jnp.concatenate([sum_b[n * chunk : (n + 1) * chunk] for n in range(blocks)], axis=1)
    return (
        layer_out.reshape(inputs.shape), input_grad.reshape(inputs.shape),
        up(sum_a[:chunk]), up(sum_a[chunk : 2 * chunk]), up(sum_a[2 * chunk :]),
        up(sum_b[blocks * chunk :]), up(in_sum), up(sum_c),
        grad_q, grad_v, grad_o, grad_i, grad_b, grad_g1, grad_s1, grad_g2, grad_s2,
    )


def solution(mesh):
    return jax.shard_map(
        per_device,
        mesh=mesh,
        in_specs=(
            P(("group", "replica"), None, None),
            P(("group", "replica"), None, None),
            P(("group", "replica")),
            P("group", None),
            P("group", None),
            P("group", None),
            P("group", None),
            P("group", None),
            P("group", None),
            P("group"),
            P("group"),
            P("group"),
            P("group"),
            P("group"),
            P("group"),
            P("group"),
            P("group"),
            P("group"),
        ),
        out_specs=(
            P(("group", "replica"), None, None),
            P(("group", "replica"), None, None),
            P("group", None),
            P("group", None),
            P("group", None),
            P("group", None),
            P("group", None),
            P("group", None),
            P("group"),
            P("group"),
            P("group"),
            P("group"),
            P("group"),
            P("group"),
            P("group"),
            P("group"),
            P("group"),
        ),
        check_vma=False,
    )
```

time: 454 us -> 377 us (0.83); the launches traced: 446 us -> 375 us
  matrix products: 149 us -> 0 us
  Pallas kernels: 0 us -> 143 us
  local copies, waits for them, and re-layouts: 82.9 us -> 48 us
  other arithmetic: 44.9 us -> 18.3 us
  loops' own time: 9.11 us -> 0 us
  starting transfers between devices: 41 us -> 46.3 us
    dot_general x32 -> x0, matrix products: 149 us -> none  [the longest x6 49.2 us: project(): return jnp.dot(left, right, preferred_element_type=jnp.float32)]
    pallas_call x0 -> x12, Pallas kernels: none -> 143 us  [the longest x1 22.9 us: turn(): pl.pallas_call(body, out_shape=[shape(total, width, bf), shape(total, wid...]
    reduce_sum x10 -> x1, other arithmetic: 17.3 us -> 0.02 us  [per_device(): jnp.sum(attend_sums, 0)]
    convert_element_type x10 -> x3, other arithmetic: 19.8 us -> 3.17 us  [per_device(): up = lambda a: a.astype(jnp.float32)]
    unnamed x112 -> x32, local copies, waits for them, and re-layouts: 24.1 us -> 9.54 us
    while x33 -> x0, local copies, waits for them, and re-layouts: 13 us -> none  [the longest x4 7.73 us: per_device(): mixed_blocks, log_sums = lax.map(attend, (query_blocks, item_ids))]
    dynamic_update_slice x30, local copies, waits for them, and re-layouts: 7.35 us -> 18.6 us  [place(): full = lax.dynamic_update_slice(full, part[None], (me ^ d, at, 0))]
    convert_element_type x13 -> x0, local copies, waits for them, and re-layouts: 9.7 us -> none  [the longest x1 4.23 us: per_device(): query_grad_blocks.reshape(total_rows, model_width).astype(jnp.bfloat16)]
  transfers between devices with their start and end apart: 51 -> 59, of which waited for: 29 -> 25; matrix products, arithmetic and copies ran while one was open for 28% -> 15% of each run, Pallas kernels for 0% -> 20%
where the time goes in v2:
time: 377 us; the launch traced here: 375 us
  Pallas kernels  143 us (38%)
  waiting for transfers between devices  119 us (32%)
  local copies, waits for them, and re-layouts  48 us (13%)
  starting transfers between devices  46.3 us (12%)
  other arithmetic  18.3 us (5%)
    ppermute x59, waiting for transfers between devices, swap_with(): return lax.ppermute(array, AXES, pairs)  119 us
    ppermute x59, starting transfers between devices, swap_with(): return lax.ppermute(array, AXES, pairs)  46.3 us
    pallas_call x1, Pallas kernels, turn(): pl.pallas_call(body, out_shape=[shape(total, width, bf), shape(total, wid...  22.9 us
    pallas_call x1, Pallas kernels, attend_back(): pl.pallas_call(attend_back_kernel, out_shape=[jax.ShapeDtypeStruct((3, to...  21.5 us
    pallas_call x1, Pallas kernels, attend(): pl.pallas_call(attend_kernel, out_shape=[table] * 4 + [jax.ShapeDtypeStru...  20.3 us
    dynamic_update_slice x30, local copies, waits for them, and re-layouts, place(): full = lax.dynamic_update_slice(full, part[None], (me ^ d, at, 0))  18.6 us
    pallas_call x1, Pallas kernels, feed(): pl.pallas_call(feed_kernel, out_shape=[shape(total, width, bf), shape(tot...  17.7 us
    pallas_call x1, Pallas kernels, return_grad(): pl.pallas_call(return_kernel, out_shape=[shape(total, width, f32), shape(...  15.5 us
  transfers between devices with their start and end apart: 59, of which 25 were waited for; matrix products, arithmetic and copies ran while one was open for 15% of the time, Pallas kernels for 20%

profile of v2, /device:TPU:0, one launch (start us, length us, event | category | flops | bytes accessed | tf_op | source)
XLA Modules:
  0.0 375.1 jit_solution(17143069585904850184)
XLA Ops:
  5.4 3.0 collective-permute-start
  18.2 2.2 collective-permute-done.9
  21.4 2.7 collective-permute-done.10
  39.5 15.1 %collective-permute-done.2 = bf16[144,768]{1,0:T(8,128)(2,1)S(1)} collective-permute-done((bf16[144,768]{1,0:T(8,128)(2,1)S(1)}, bf16[144,768]{1,0:T(8,128)(2,1)S(1)}, u32[]{:S(2)}, u32[]{:S(2)}) %collective-permute-start.2) | collective-permute-done | bytes 221216 | tf_op jit(solution)/shard_map/ppermute | solution.py:27
  56.3 4.7 %collective-permute-done.3 = bf16[144,768]{1,0:T(8,128)(2,1)S(1)} collective-permute-done((bf16[144,768]{1,0:T(8,128)(2,1)S(1)}, bf16[144,768]{1,0:T(8,128)(2,1)S(1)}, u32[]{:S(2)}, u32[]{:S(2)}) %collective-permute-start.3) | collective-permute-done | bytes 221216 | tf_op jit(solution)/shard_map/ppermute | solution.py:27
  67.0 20.3 %attend.1 = (bf16[1024,768]{1,0:T(8,128)(2,1)}, bf16[1024,768]{1,0:T(8,128)(2,1)}, bf16[1024,768]{1,0:T(8,128)(2,1)}, bf16[1024,768]{1,0:T(8,128)(2,1)}, bf16[24,512,512]{2,1,0:T(8,128)(2,1)}) custom-call(s32[2]{0:T(128)} %lens.3, bf16[1024,768]{1,0:T(8,128)(2,1)} %bitcast.261, bf16[768,768]{1,0:T(8,128)(2,1)} %bitcast.244, bf16[768,768]{1,0:T(8,128)(2,1)} %bitcast.242, ...), custom_call_target="tpu_custom_call" | custom-call | flops 6845104128 | bytes 30000000 | tf_op jit(solution)/shard_map/attend/pallas_call | solution.py:194
  93.6 2.0 bitcast_dynamic-update-slice_fusion.4
  95.6 2.1 bitcast_dynamic-update-slice_fusion.3
  98.1 13.9 %collective-permute-done.14 = bf16[240,768]{1,0:T(8,128)(2,1)S(1)} collective-permute-done((bf16[240,768]{1,0:T(8,128)(2,1)S(1)}, bf16[240,768]{1,0:T(8,128)(2,1)S(1)}, u32[]{:S(2)}, u32[]{:S(2)}) %collective-permute-start.14) | collective-permute-done | bytes 368672 | tf_op jit(solution)/shard_map/ppermute | solution.py:27
  119.5 2.5 pad_maximum_fusion
  122.0 17.7 %feed.1 = (bf16[1024,768]{1,0:T(8,128)(2,1)}, f32[1024,768]{1,0:T(8,128)}, f32[1024,128]{1,0:T(8,128)}, bf16[1024,3072]{1,0:T(8,128)(2,1)}, bf16[1024,3072]{1,0:T(8,128)(2,1)}) custom-call(bf16[1024,768]{1,0:T(8,128)(2,1)} %get-tuple-element.59.mixed, bf16[1024,768]{1,0:T(8,128)(2,1)} %bitcast.262, bf16[768,768]{1,0:T(8,128)(2,1)} %bitcast.238, ...), custom_call_target="tpu_custom_call" | custom-call | flops 6039797760 | bytes 30000000 | tf_op jit(solution)/shard_map/feed/pallas_call | solution.py:312
  147.8 22.9 %turn.1 = (bf16[1024,768]{1,0:T(8,128)(2,1)}, bf16[1024,768]{1,0:T(8,128)(2,1)}, bf16[1024,3072]{1,0:T(8,128)(2,1)}, f32[1024,768]{1,0:T(8,128)}, f32[8,768]{1,0:T(8,128)}, /*index=5*/f32[1,3072]{1,0:T(1,128)}) custom-call(s32[2]{0:T(128)} %lens.3, bf16[1024,3072]{1,0:T(8,128)(2,1)} %get-tuple-element.62.refs_0_.active, ...), custom_call_target="tpu_custom_call" | custom-call | flops 9663676416 | bytes 30000000 | tf_op jit(solution)/shard_map/turn/pallas_call | solution.py:372
  170.7 15.5 %return_grad.1 = (f32[1024,768]{1,0:T(8,128)}, bf16[1024,768]{1,0:T(8,128)(2,1)}, bf16[1024,768]{1,0:T(8,128)(2,1)}, f32[8,768]{1,0:T(8,128)}) custom-call(bf16[1024,3072]{1,0:T(8,128)(2,1)} %get-tuple-element.67.hidden_grad, f32[1024,768]{1,0:T(8,128)} %get-tuple-element.68.h2_grad, f32[1024,768]{1,0:T(8,128)} %get-tuple-element.63.refs_1_.normed1, ...), custom_call_target="tpu_custom_call" | custom-call | flops 6039797760 | bytes 30000000 | tf_op jit(solution)/shard_map/return_grad/pallas_call | solution.py:416
  186.1 21.5 %attend_back.1 = (bf16[3,1024,768]{2,1,0:T(8,128)(2,1)}, f32[2,2,768]{2,1,0:T(2,128)}) custom-call(bf16[1024,768]{1,0:T(8,128)(2,1)} %get-tuple-element.71.q, bf16[1024,768]{1,0:T(8,128)(2,1)} %get-tuple-element.72.k, bf16[1024,768]{1,0:T(8,128)(2,1)} %get-tuple-element.73.v, bf16[1024,768]{1,0:T(8,128)(2,1)} %get-tuple-element.74.grad, ...), custom_call_target="tpu_custom_call" | custom-call | flops 5637144576 | bytes 30000000 | tf_op jit(solution)/shard_map/attend_back/pallas_call | solution.py:252
  207.6 8.1 %qkv_weight.1 = (bf16[4,288,768]{2,1,0:T(8,128)(2,1)}, bf16[4,288,768]{2,1,0:T(8,128)(2,1)}) custom-call(s32[1]{0:T(128)} %bitcast.14.me, bf16[1024,768]{1,0:T(8,128)(2,1)} %bitcast.263, bf16[3,1024,768]{2,1,0:T(8,128)(2,1)} %get-tuple-element.76.grads), custom_call_target="tpu_custom_call" | custom-call | flops 3623878656 | bytes 10000000 | tf_op jit(solution)/shard_map/qkv_weight/pallas_call | solution.py:571
  222.9 2.6 collective-permute-done.55
  226.6 11.3 %back_weight.1 = (bf16[4,384,768]{2,1,0:T(8,128)(2,1)}, bf16[4,384,768]{2,1,0:T(8,128)(2,1)}) custom-call(s32[1]{0:T(128)} %bitcast.14.me, bf16[1024,3072]{1,0:T(8,128)(2,1)} %get-tuple-element.62.refs_0_.active, bf16[1024,768]{1,0:T(8,128)(2,1)} %get-tuple-element.83.grad), custom_call_target="tpu_custom_call" | custom-call | flops 4831838208 | bytes 13000000 | tf_op jit(solution)/shard_map/back_weight/pallas_call | solution.py:502
  239.6 12.7 %in_out_weight.1 = (bf16[4,480,768]{2,1,0:T(8,128)(2,1)}, bf16[4,480,768]{2,1,0:T(8,128)(2,1)}) custom-call(s32[1]{0:T(128)} %bitcast.14.me, bf16[1024,768]{1,0:T(8,128)(2,1)} %get-tuple-element.79.after, bf16[1024,3072]{1,0:T(8,128)(2,1)} %get-tuple-element.67.hidden_grad, bf16[1024,768]{1,0:T(8,128)(2,1)} %get-tuple-element.59.mixed, ...), custom_call_target="tpu_custom_call" | custom-call | flops 6039797760 | bytes 20000000 | tf_op jit(solution)/shard_map/in_out_weight/pallas_call | solution.py:544
  252.5 2.7 collective-permute-start.58
  261.0 8.5 %input_grad.1 = bf16[1024,768]{1,0:T(8,128)(2,1)} custom-call(f32[1024,768]{1,0:T(8,128)} %get-tuple-element.70.h1_grad, bf16[3,1024,768]{2,1,0:T(8,128)(2,1)} %get-tuple-element.76.grads, bf16[768,768]{1,0:T(8,128)(2,1)} %bitcast.245, bf16[768,768]{1,0:T(8,128)(2,1)} %bitcast.243, bf16[768,768]{1,0:T(8,128)(2,1)} %bitcast.241), custom_call_target="tpu_custom_call" | custom-call | flops 3623878656 | bytes 20000000 | tf_op jit(solution)/shard_map/input_grad/pallas_call | solution.py:438
  275.4 2.2 add_convert_fusion.1
  280.7 2.2 collective-permute-done.34
  283.6 2.6 add_convert_fusion
  286.3 7.5 %collective-permute-done.47 = bf16[2,192,768]{2,1,0:T(8,128)(2,1)S(1)} collective-permute-done((bf16[2,192,768]{2,1,0:T(8,128)(2,1)S(1)}, bf16[2,192,768]{2,1,0:T(8,128)(2,1)S(1)}, u32[]{:S(2)}, u32[]{:S(2)}) %collective-permute-start.47) | collective-permute-done | bytes 589856 | tf_op jit(solution)/shard_map/ppermute | solution.py:27
  298.9 5.3 %collective-permute-done.48 = bf16[192,768]{1,0:T(8,128)(2,1)S(1)} collective-permute-done((bf16[192,768]{1,0:T(8,128)(2,1)S(1)}, bf16[192,768]{1,0:T(8,128)(2,1)S(1)}, u32[]{:S(2)}, u32[]{:S(2)}) %collective-permute-start.48) | collective-permute-done | bytes 294944 | tf_op jit(solution)/shard_map/ppermute | solution.py:27
  304.2 14.1 %collective-permute-done.50 = bf16[192,768]{1,0:T(8,128)(2,1)S(1)} collective-permute-done((bf16[192,768]{1,0:T(8,128)(2,1)S(1)}, bf16[192,768]{1,0:T(8,128)(2,1)S(1)}, u32[]{:S(2)}, u32[]{:S(2)}) %collective-permute-start.50) | collective-permute-done | bytes 294944 | tf_op jit(solution)/shard_map/ppermute | solution.py:27
  321.4 5.2 %collective-permute-done.40 = bf16[240,768]{1,0:T(8,128)(2,1)S(1)} collective-permute-done((bf16[240,768]{1,0:T(8,128)(2,1)S(1)}, bf16[240,768]{1,0:T(8,128)(2,1)S(1)}, u32[]{:S(2)}, u32[]{:S(2)}) %collective-permute-start.40) | collective-permute-done | bytes 368672 | tf_op jit(solution)/shard_map/ppermute | solution.py:27
  330.2 13.1 %collective-permute-done.43 = bf16[240,768]{1,0:T(8,128)(2,1)S(1)} collective-permute-done((bf16[240,768]{1,0:T(8,128)(2,1)S(1)}, bf16[240,768]{1,0:T(8,128)(2,1)S(1)}, u32[]{:S(2)}, u32[]{:S(2)}) %collective-permute-start.43) | collective-permute-done | bytes 368672 | tf_op jit(solution)/shard_map/ppermute | solution.py:27
  343.5 3.3 collective-permute-done.37
  348.1 2.2 collective-permute-start.53
  350.4 12.0 %collective-permute-done.44 = bf16[240,768]{1,0:T(8,128)(2,1)S(1)} collective-permute-done((bf16[240,768]{1,0:T(8,128)(2,1)S(1)}, bf16[240,768]{1,0:T(8,128)(2,1)S(1)}, u32[]{:S(2)}, u32[]{:S(2)}) %collective-permute-start.44) | collective-permute-done | bytes 368672 | tf_op jit(solution)/shard_map/ppermute | solution.py:27
  364.6 8.4 %collective-permute-done.45 = bf16[240,768]{1,0:T(8,128)(2,1)S(1)} collective-permute-done((bf16[240,768]{1,0:T(8,128)(2,1)S(1)}, bf16[240,768]{1,0:T(8,128)(2,1)S(1)}, u32[]{:S(2)}, u32[]{:S(2)}) %collective-permute-start.45) | collective-permute-done | bytes 368672 | tf_op jit(solution)/shard_map/ppermute | solution.py:27
  (239 shorter events, 104.0 us)
Async XLA Ops:
  5.4 25.5 %collective-permute-start = (bf16[288,768]{1,0:T(8,128)(2,1)}, bf16[288,768]{1,0:T(8,128)(2,1)}, u32[]{:S(2)}, u32[]{:S(2)}) collective-permute-start(bf16[288,768]{1,0:T(8,128)(2,1)} %constant_dynamic-update-slice_fusion), channel_id=1, source_target_pairs={{0,8},{1,9},{2,10},{3,11},{4,12},{5,13},{6,14},{7,15},{8,0},{9,1},... | collective-permute-start | bytes 1327112 | tf_op jit(solution)/shard_map/ppermute | solution.py:27
  8.4 22.6 %collective-permute-start.1 = (bf16[288,768]{1,0:T(8,128)(2,1)}, bf16[288,768]{1,0:T(8,128)(2,1)}, u32[]{:S(2)}, u32[]{:S(2)}) collective-permute-start(bf16[288,768]{1,0:T(8,128)(2,1)} %constant_dynamic-update-slice_fusion), channel_id=1, source_target_pairs={{0,16},{1,17},{2,18},{3,19},{4,20},{5,21},{6,22},{7,23},{8,24},{9,... | collective-permute-start | bytes 1327112 | tf_op jit(solution)/shard_map/ppermute | solution.py:27
  9.9 51.1 %collective-permute-start.4 = (bf16[288,768]{1,0:T(8,128)(2,1)}, bf16[288,768]{1,0:T(8,128)(2,1)}, u32[]{:S(2)}, u32[]{:S(2)}) collective-permute-start(bf16[288,768]{1,0:T(8,128)(2,1)} %constant_dynamic-update-slice_fusion), channel_id=1, source_target_pairs={{0,4},{1,5},{2,6},{3,7},{4,0},{5,1},{6,2},{7,3},{8,12},{9,13},{10,... | collective-permute-start | bytes 1327112 | tf_op jit(solution)/shard_map/ppermute | solution.py:27
  30.9 56.4 %collective-permute-start.12 = (bf16[480,768]{1,0:T(8,128)(2,1)}, bf16[480,768]{1,0:T(8,128)(2,1)}, u32[]{:S(2)}, u32[]{:S(2)}) collective-permute-start(bf16[480,768]{1,0:T(8,128)(2,1)} %slice_dynamic-update-slice_fusion), channel_id=1, source_target_pairs={{0,8},{1,9},{2,10},{3,11},{4,12},{5,13},{6,14},{7,15},{8,0},{9,1},... | collective-permute-start | bytes 2211848 | tf_op jit(solution)/shard_map/ppermute | solution.py:27
  31.3 56.0 %collective-permute-start.13 = (bf16[480,768]{1,0:T(8,128)(2,1)}, bf16[480,768]{1,0:T(8,128)(2,1)}, u32[]{:S(2)}, u32[]{:S(2)}) collective-permute-start(bf16[480,768]{1,0:T(8,128)(2,1)} %slice_dynamic-update-slice_fusion), channel_id=1, source_target_pairs={{0,16},{1,17},{2,18},{3,19},{4,20},{5,21},{6,22},{7,23},{8,24},{9,... | collective-permute-start | bytes 2211848 | tf_op jit(solution)/shard_map/ppermute | solution.py:27
  33.0 79.6 %collective-permute-start.16 = (bf16[480,768]{1,0:T(8,128)(2,1)}, bf16[480,768]{1,0:T(8,128)(2,1)}, u32[]{:S(2)}, u32[]{:S(2)}) collective-permute-start(bf16[480,768]{1,0:T(8,128)(2,1)} %slice_dynamic-update-slice_fusion), channel_id=1, source_target_pairs={{0,4},{1,5},{2,6},{3,7},{4,0},{5,1},{6,2},{7,3},{8,12},{9,13},{10,... | collective-permute-start | bytes 2211848 | tf_op jit(solution)/shard_map/ppermute | solution.py:27
  35.8 18.8 %collective-permute-start.2 = (bf16[144,768]{1,0:T(8,128)(2,1)S(1)}, bf16[144,768]{1,0:T(8,128)(2,1)S(1)}, u32[]{:S(2)}, u32[]{:S(2)}) collective-permute-start(bf16[144,768]{1,0:T(8,128)(2,1)S(1)} %slice.274), channel_id=1, source_target_pairs={{0,16},{1,17},{2,18},{3,19},{4,20},{5,21},{6,22},{7,23},{8,24},{9,... | collective-permute-start | bytes 663560 | tf_op jit(solution)/shard_map/ppermute | solution.py:27
  87.3 26.6 %collective-permute-start.21 = (bf16[384,768]{1,0:T(8,128)(2,1)S(1)}, bf16[384,768]{1,0:T(8,128)(2,1)S(1)}, u32[]{:S(2)}, u32[]{:S(2)}) collective-permute-start(bf16[384,768]{1,0:T(8,128)(2,1)S(1)} %copy-done.8), channel_id=1, source_target_pairs={{0,8},{1,9},{2,10},{3,11},{4,12},{5,13},{6,14},{7,15},{8,0},{9,1},... | collective-permute-start | bytes 1769480 | tf_op jit(solution)/shard_map/ppermute | solution.py:27
  89.0 25.5 %collective-permute-start.22 = (bf16[384,768]{1,0:T(8,128)(2,1)S(1)}, bf16[384,768]{1,0:T(8,128)(2,1)S(1)}, u32[]{:S(2)}, u32[]{:S(2)}) collective-permute-start(bf16[384,768]{1,0:T(8,128)(2,1)S(1)} %copy-done.8), channel_id=1, source_target_pairs={{0,16},{1,17},{2,18},{3,19},{4,20},{5,21},{6,22},{7,23},{8,24},{9,... | collective-permute-start | bytes 1769480 | tf_op jit(solution)/shard_map/ppermute | solution.py:27
  91.5 20.5 %collective-permute-start.14 = (bf16[240,768]{1,0:T(8,128)(2,1)S(1)}, bf16[240,768]{1,0:T(8,128)(2,1)S(1)}, u32[]{:S(2)}, u32[]{:S(2)}) collective-permute-start(bf16[240,768]{1,0:T(8,128)(2,1)S(1)} %slice.279), channel_id=1, source_target_pairs={{0,16},{1,17},{2,18},{3,19},{4,20},{5,21},{6,22},{7,23},{8,24},{9,... | collective-permute-start | bytes 1105928 | tf_op jit(solution)/shard_map/ppermute | solution.py:27
  93.1 18.9 %collective-permute-start.15 = (bf16[240,768]{1,0:T(8,128)(2,1)S(1)}, bf16[240,768]{1,0:T(8,128)(2,1)S(1)}, u32[]{:S(2)}, u32[]{:S(2)}) collective-permute-start(bf16[240,768]{1,0:T(8,128)(2,1)S(1)} %slice.280), channel_id=1, source_target_pairs={{0,8},{1,9},{2,10},{3,11},{4,12},{5,13},{6,14},{7,15},{8,0},{9,1},... | collective-permute-start | bytes 1105928 | tf_op jit(solution)/shard_map/ppermute | solution.py:27
  112.0 31.7 %collective-permute-start.25 = (bf16[384,768]{1,0:T(8,128)(2,1)S(1)}, bf16[384,768]{1,0:T(8,128)(2,1)S(1)}, u32[]{:S(2)}, u32[]{:S(2)}) collective-permute-start(bf16[384,768]{1,0:T(8,128)(2,1)S(1)} %copy-done.8), channel_id=1, source_target_pairs={{0,4},{1,5},{2,6},{3,7},{4,0},{5,1},{6,2},{7,3},{8,12},{9,13},{10,... | collective-permute-start | bytes 1769480 | tf_op jit(solution)/shard_map/ppermute | solution.py:27
  115.0 24.7 %collective-permute-start.23 = (bf16[192,768]{1,0:T(8,128)(2,1)S(1)}, bf16[192,768]{1,0:T(8,128)(2,1)}, u32[]{:S(2)}, u32[]{:S(2)}) collective-permute-start(bf16[192,768]{1,0:T(8,128)(2,1)S(1)} %slice.286), channel_id=1, source_target_pairs={{0,16},{1,17},{2,18},{3,19},{4,20},{5,21},{6,22},{7,23},{8,24},{9,... | collective-permute-start | bytes 884744 | tf_op jit(solution)/shard_map/ppermute | solution.py:27
  116.6 24.9 %collective-permute-start.24 = (bf16[192,768]{1,0:T(8,128)(2,1)S(1)}, bf16[192,768]{1,0:T(8,128)(2,1)}, u32[]{:S(2)}, u32[]{:S(2)}) collective-permute-start(bf16[192,768]{1,0:T(8,128)(2,1)S(1)} %slice.287), channel_id=1, source_target_pairs={{0,8},{1,9},{2,10},{3,11},{4,12},{5,13},{6,14},{7,15},{8,0},{9,1},... | collective-permute-start | bytes 884744 | tf_op jit(solution)/shard_map/ppermute | solution.py:27
  117.3 27.2 %collective-permute-start.26 = (bf16[384,768]{1,0:T(8,128)(2,1)S(1)}, bf16[384,768]{1,0:T(8,128)(2,1)S(1)}, u32[]{:S(2)}, u32[]{:S(2)}) collective-permute-start(bf16[384,768]{1,0:T(8,128)(2,1)S(1)} %collective-permute-done.21), channel_id=1, source_target_pairs={{0,4},{1,5},{2,6},{3,7},{4,0},{5,1},{6,2},{7,3},{8,12},{9,13},{10,... | collective-permute-start | bytes 1769480 | tf_op jit(solution)/shard_map/ppermute | solution.py:27
  117.4 28.0 %collective-permute-start.27 = (bf16[384,768]{1,0:T(8,128)(2,1)S(1)}, bf16[384,768]{1,0:T(8,128)(2,1)S(1)}, u32[]{:S(2)}, u32[]{:S(2)}) collective-permute-start(bf16[384,768]{1,0:T(8,128)(2,1)S(1)} %collective-permute-done.22), channel_id=1, source_target_pairs={{0,4},{1,5},{2,6},{3,7},{4,0},{5,1},{6,2},{7,3},{8,12},{9,13},{10,... | collective-permute-start | bytes 1769480 | tf_op jit(solution)/shard_map/ppermute | solution.py:27
  215.7 39.5 %collective-permute-start.30 = (bf16[4,288,768]{2,1,0:T(8,128)(2,1)}, bf16[4,288,768]{2,1,0:T(8,128)(2,1)S(1)}, u32[]{:S(2)}, u32[]{:S(2)}) collective-permute-start(bf16[4,288,768]{2,1,0:T(8,128)(2,1)} %get-tuple-element.78), channel_id=1, source_target_pairs={{0,4},{1,5},{2,6},{3,7},{4,0},{5,1},{6,2},{7,3},{8,12},{9,13},{10,... | collective-permute-start | bytes 5308424 | tf_op jit(solution)/shard_map/ppermute | solution.py:27
  238.0 37.4 %collective-permute-start.46 = (bf16[4,384,768]{2,1,0:T(8,128)(2,1)}, bf16[4,384,768]{2,1,0:T(8,128)(2,1)}, u32[]{:S(2)}, u32[]{:S(2)}) collective-permute-start(bf16[4,384,768]{2,1,0:T(8,128)(2,1)} %get-tuple-element.85), channel_id=1, source_target_pairs={{0,4},{1,5},{2,6},{3,7},{4,0},{5,1},{6,2},{7,3},{8,12},{9,13},{10,... | collective-permute-start | bytes 7077896 | tf_op jit(solution)/shard_map/ppermute | solution.py:27
  252.3 31.3 %collective-permute-start.38 = (bf16[4,480,768]{2,1,0:T(8,128)(2,1)}, bf16[4,480,768]{2,1,0:T(8,128)(2,1)}, u32[]{:S(2)}, u32[]{:S(2)}) collective-permute-start(bf16[4,480,768]{2,1,0:T(8,128)(2,1)} %get-tuple-element.82), channel_id=1, source_target_pairs={{0,4},{1,5},{2,6},{3,7},{4,0},{5,1},{6,2},{7,3},{8,12},{9,13},{10,... | collective-permute-start | bytes 8847368 | tf_op jit(solution)/shard_map/ppermute | solution.py:27
  252.5 16.9 %collective-permute-start.58 = (f32[12,768]{1,0:T(8,128)S(1)}, f32[12,768]{1,0:T(8,128)S(1)}, u32[]{:S(2)}, u32[]{:S(2)}) collective-permute-start(f32[12,768]{1,0:T(8,128)S(1)} %add.172), channel_id=1, source_target_pairs={{0,2},{1,3},{2,0},{3,1},{4,6},{5,7},{6,4},{7,5},{8,10},{9,11},{10,... | collective-permute-start | bytes 110600 | tf_op jit(solution)/shard_map/ppermute | solution.py:27
  258.3 15.0 %collective-permute-start.31 = (bf16[2,144,768]{2,1,0:T(8,128)(2,1)S(1)}, bf16[2,144,768]{2,1,0:T(8,128)(2,1)S(1)}, u32[]{:S(2)}, u32[]{:S(2)}) collective-permute-start(bf16[2,144,768]{2,1,0:T(8,128)(2,1)S(1)} %slice_bitcast_fusion.10), channel_id=1, source_target_pairs={{0,8},{1,9},{2,10},{3,11},{4,12},{5,13},{6,14},{7,15},{8,0},{9,1},... | collective-permute-start | bytes 1327112 | tf_op jit(solution)/shard_map/ppermute | solution.py:27
  277.7 16.2 %collective-permute-start.47 = (bf16[2,192,768]{2,1,0:T(8,128)(2,1)S(1)}, bf16[2,192,768]{2,1,0:T(8,128)(2,1)S(1)}, u32[]{:S(2)}, u32[]{:S(2)}) collective-permute-start(bf16[2,192,768]{2,1,0:T(8,128)(2,1)S(1)} %slice_bitcast_fusion.6), channel_id=1, source_target_pairs={{0,8},{1,9},{2,10},{3,11},{4,12},{5,13},{6,14},{7,15},{8,0},{9,1},... | collective-permute-start | bytes 1769480 | tf_op jit(solution)/shard_map/ppermute | solution.py:27
  283.0 15.4 %collective-permute-start.35 = (bf16[144,768]{1,0:T(8,128)(2,1)S(1)}, bf16[144,768]{1,0:T(8,128)(2,1)S(1)}, u32[]{:S(2)}, u32[]{:S(2)}) collective-permute-start(bf16[144,768]{1,0:T(8,128)(2,1)S(1)} %dynamic-slice_bitcast_fusion.2), channel_id=1, source_target_pairs={{0,1},{1,0},{2,3},{3,2},{4,5},{5,4},{6,7},{7,6},{8,9},{9,8},{10,11... | collective-permute-start | bytes 663560 | tf_op jit(solution)/shard_map/ppermute | solution.py:27
  295.4 23.0 %collective-permute-start.39 = (bf16[2,240,768]{2,1,0:T(8,128)(2,1)S(1)}, bf16[2,240,768]{2,1,0:T(8,128)(2,1)S(1)}, u32[]{:S(2)}, u32[]{:S(2)}) collective-permute-start(bf16[2,240,768]{2,1,0:T(8,128)(2,1)S(1)} %slice_bitcast_fusion.2), channel_id=1, source_target_pairs={{0,8},{1,9},{2,10},{3,11},{4,12},{5,13},{6,14},{7,15},{8,0},{9,1},... | collective-permute-start | bytes 2211848 | tf_op jit(solution)/shard_map/ppermute | solution.py:27
  295.9 22.5 %collective-permute-start.41 = (bf16[2,240,768]{2,1,0:T(8,128)(2,1)S(1)}, bf16[2,240,768]{2,1,0:T(8,128)(2,1)S(1)}, u32[]{:S(2)}, u32[]{:S(2)}) collective-permute-start(bf16[2,240,768]{2,1,0:T(8,128)(2,1)S(1)} %slice_bitcast_fusion), channel_id=1, source_target_pairs={{0,16},{1,17},{2,18},{3,19},{4,20},{5,21},{6,22},{7,23},{8,24},{9,... | collective-permute-start | bytes 2211848 | tf_op jit(solution)/shard_map/ppermute | solution.py:27
  297.0 21.3 %collective-permute-start.50 = (bf16[192,768]{1,0:T(8,128)(2,1)S(1)}, bf16[192,768]{1,0:T(8,128)(2,1)S(1)}, u32[]{:S(2)}, u32[]{:S(2)}) collective-permute-start(bf16[192,768]{1,0:T(8,128)(2,1)S(1)} %slice_bitcast_fusion.16), channel_id=1, source_target_pairs={{0,8},{1,9},{2,10},{3,11},{4,12},{5,13},{6,14},{7,15},{8,0},{9,1},... | collective-permute-start | bytes 884744 | tf_op jit(solution)/shard_map/ppermute | solution.py:27
  298.5 29.6 %collective-permute-start.36 = (bf16[144,768]{1,0:T(8,128)(2,1)S(1)}, bf16[144,768]{1,0:T(8,128)(2,1)S(1)}, u32[]{:S(2)}, u32[]{:S(2)}) collective-permute-start(bf16[144,768]{1,0:T(8,128)(2,1)S(1)} %fusion.13), channel_id=1, source_target_pairs={{0,2},{1,3},{2,0},{3,1},{4,6},{5,7},{6,4},{7,5},{8,10},{9,11},{10,... | collective-permute-start | bytes 663560 | tf_op jit(solution)/shard_map/ppermute | solution.py:27
  327.5 15.7 %collective-permute-start.43 = (bf16[240,768]{1,0:T(8,128)(2,1)S(1)}, bf16[240,768]{1,0:T(8,128)(2,1)S(1)}, u32[]{:S(2)}, u32[]{:S(2)}) collective-permute-start(bf16[240,768]{1,0:T(8,128)(2,1)S(1)} %dynamic-slice_bitcast_fusion), channel_id=1, source_target_pairs={{0,1},{1,0},{2,3},{3,2},{4,5},{5,4},{6,7},{7,6},{8,9},{9,8},{10,11... | collective-permute-start | bytes 1105928 | tf_op jit(solution)/shard_map/ppermute | solution.py:27
  328.1 18.6 %collective-permute-start.37 = (bf16[144,768]{1,0:T(8,128)(2,1)S(1)}, bf16[144,768]{1,0:T(8,128)(2,1)S(1)}, u32[]{:S(2)}, u32[]{:S(2)}) collective-permute-start(bf16[144,768]{1,0:T(8,128)(2,1)S(1)} %add_convert_fusion.5), channel_id=1, source_target_pairs={{0,1},{1,0},{2,3},{3,2},{4,5},{5,4},{6,7},{7,6},{8,9},{9,8},{10,11... | collective-permute-start | bytes 663560 | tf_op jit(solution)/shard_map/ppermute | solution.py:27
  329.8 18.2 %collective-permute-start.52 = (bf16[192,768]{1,0:T(8,128)(2,1)S(1)}, bf16[192,768]{1,0:T(8,128)(2,1)S(1)}, u32[]{:S(2)}, u32[]{:S(2)}) collective-permute-start(bf16[192,768]{1,0:T(8,128)(2,1)S(1)} %fusion.10), channel_id=1, source_target_pairs={{0,2},{1,3},{2,0},{3,1},{4,6},{5,7},{6,4},{7,5},{8,10},{9,11},{10,... | collective-permute-start | bytes 884744 | tf_op jit(solution)/shard_map/ppermute | solution.py:27
  343.4 18.9 %collective-permute-start.44 = (bf16[240,768]{1,0:T(8,128)(2,1)S(1)}, bf16[240,768]{1,0:T(8,128)(2,1)S(1)}, u32[]{:S(2)}, u32[]{:S(2)}) collective-permute-start(bf16[240,768]{1,0:T(8,128)(2,1)S(1)} %fusion.6), channel_id=1, source_target_pairs={{0,2},{1,3},{2,0},{3,1},{4,6},{5,7},{6,4},{7,5},{8,10},{9,11},{10,... | collective-permute-start | bytes 1105928 | tf_op jit(solution)/shard_map/ppermute | solution.py:27
  348.1 15.3 %collective-permute-start.53 = (bf16[192,768]{1,0:T(8,128)(2,1)S(1)}, bf16[192,768]{1,0:T(8,128)(2,1)S(1)}, u32[]{:S(2)}, u32[]{:S(2)}) collective-permute-start(bf16[192,768]{1,0:T(8,128)(2,1)S(1)} %add_convert_fusion.4), channel_id=1, source_target_pairs={{0,1},{1,0},{2,3},{3,2},{4,5},{5,4},{6,7},{7,6},{8,9},{9,8},{10,11... | collective-permute-start | bytes 884744 | tf_op jit(solution)/shard_map/ppermute | solution.py:27
  (39 other events, 301.0 us)

commit v3 on v2

--- a/solution.py
+++ b/solution.py
@@ -1,3 +1,5 @@
+import functools
+
 import jax
 import jax.numpy as jnp
 from jax import lax
@@ -53,9 +55,10 @@
                 got.append(swap_with(halves[d ^ last][which], last))
             pieces[d] = got
             halves[d] = got
+            last_got = got
     for d in list(pieces):
         pieces[d | 1] = [swap_with(p, 1) for p in pieces[d]]
-    return pieces, first
+    return pieces, first, last_got
 
 
 def place(pieces, me, group_size):
@@ -77,38 +80,50 @@
     return (left.astype(jnp.float32) + right.astype(jnp.float32)).astype(jnp.bfloat16)
 
 
-def reduce_all(own, send, bits):
+def reduction(own, send, bits):
+    received = swap_with(send, 1)
+    yield [received]
     rows, width = own.shape[1:]
-    chunks = add_low(own, swap_with(send, 1)).reshape((2,) * (bits - 1) + (rows, width))
+    chunks = add_low(own, received).reshape((2,) * (bits - 1) + (rows, width))
     half = rows // 32 * 16
-    done = []
-    for part, order in ((chunks[..., :half, :], 0), (chunks[..., half:, :], 1)):
-        left = list(range(1, bits))
-        for b in left[:] if order == 0 else left[::-1]:
+    parts = [chunks[..., :half, :], chunks[..., half:, :]]
+    lefts = [list(range(1, bits)), list(range(1, bits))]
+    for _ in range(1, bits):
+        kept, received = [], []
+        for part, left, end in zip(parts, lefts, (0, -1)):
+            b = left[end]
             axis = len(left) - 1 - left.index(b)
-            kept, away = (lax.index_in_dim(part, i, axis, keepdims=False) for i in (0, 1))
-            part = add_low(kept, swap_with(away, 1 << b))
+            keep, away = (lax.index_in_dim(part, i, axis, keepdims=False) for i in (0, 1))
+            kept.append(keep)
+            received.append(swap_with(away, 1 << b))
             left.remove(b)
-        done.append(part)
-    return sum_replicas(jnp.concatenate(done))
-
-
-def sum_replicas(total):
+        yield received
+        parts = [add_low(keep, got) for keep, got in zip(kept, received)]
+    total = jnp.concatenate(parts)
     replicas = lax.axis_size("replica")
-    if replicas == 1:
-        return total
-    rows, width = total.shape
-    at = lax.axis_index("replica")
-    pair = total.reshape(2, rows // 2, width)
-    kept = add_low(pick(pair, 0, at & 1), swap_with(pick(pair, 0, 1 - (at & 1)), 0, 1))
-    mask = 2
-    while mask < replicas:
-        kept = add_low(kept, swap_with(kept, 0, mask))
-        mask *= 2
-    other = swap_with(kept, 0, 1)
-    return jnp.where(
-        (at & 1) == 0, jnp.concatenate([kept, other]), jnp.concatenate([other, kept])
-    )
+    if replicas > 1:
+        at = lax.axis_index("replica")
+        pair = total.reshape(2, rows // 2, width)
+        received = swap_with(pick(pair, 0, 1 - (at & 1)), 0, 1)
+        yield [received]
+        kept = add_low(pick(pair, 0, at & 1), received)
+        mask = 2
+        while mask < replicas:
+            received = swap_with(kept, 0, mask)
+            yield [received]
+            kept = add_low(kept, received)
+            mask *= 2
+        other = swap_with(kept, 0, 1)
+        yield [other]
+        total = jnp.where(
+            (at & 1) == 0, jnp.concatenate([kept, other]), jnp.concatenate([other, kept])
+        )
+    yield total
+
+
+def finish(steps):
+    *_, last = steps
+    return last
 
 
 def sum_everywhere(array, bits):
@@ -121,6 +136,72 @@
     return array
 
 
+class Gathered:
+    def __init__(self, pieces, me, count, chunk, segments):
+        self.me, self.chunk = me, chunk
+        self.arrays, self.copies = [], []
+        if chunk % 16:
+            full = place(pieces, me[0], count)
+            self.plain(full, count, segments)
+            return
+        for d, parts in pieces.items():
+            at = 0
+            for part in parts:
+                for target, low, size, column in segments:
+                    start, stop = max(at, low), min(at + part.shape[0], low + size)
+                    if start < stop:
+                        self.copies.append(
+                            (len(self.arrays), start - at, stop - start, target, d, start - low, column)
+                        )
+                self.arrays.append(part)
+                at += part.shape[0]
+        self.fixed = False
+
+    def plain(self, full, count, segments):
+        width = full.shape[2]
+        for target, low, size, column in segments:
+            self.copies.append((len(self.arrays), 0, count * size, target, 0, 0, column))
+            self.arrays.append(full[:, low : low + size].reshape(count * size, width))
+        self.fixed = True
+
+    def specs(self):
+        return [pl.BlockSpec(memory_space=pl.ANY)] * len(self.arrays)
+
+    def transfers(self, me, refs, targets, sems, only=None):
+        out = []
+        for n, (which, row, rows, target, d, inner, column) in enumerate(self.copies):
+            if only is not None and target not in only:
+                continue
+            size = self.chunk
+            if self.fixed:
+                first = 0
+            else:
+                first = pl.multiple_of((me ^ d) * size + inner, 16)
+            width = self.arrays[which].shape[1]
+            out.append(
+                pltpu.make_async_copy(
+                    refs[which].at[pl.ds(row, rows)],
+                    targets[target].at[pl.ds(first, rows), pl.ds(column, width)],
+                    sems.at[n],
+                )
+            )
+        return out
+
+
+def fetch(plan, me, refs, targets, sems, first_step, only=None):
+    @pl.when(first_step)
+    def _():
+        for copy in plan.transfers(me, refs, targets, sems, only):
+            copy.start()
+
+
+def arrive(plan, me, refs, targets, sems, first_step, only=None):
+    @pl.when(first_step)
+    def _():
+        for copy in plan.transfers(me, refs, targets, sems, only):
+            copy.wait()
+
+
 VMEM_LIMIT = 60 * 1024 * 1024
 GROUP_HEADS = 4
 GROUP_COLS = GROUP_HEADS * HEAD_DIM
@@ -152,17 +233,23 @@
     return jnp.where(keep, pair, jnp.zeros_like(pair))
 
 
-def attend_kernel(lens, x, wq, wk, wv, bq, bv, q_out, k_out, v_out, mixed_out, probs_out):
+def attend_kernel(plan, seq, aliased, lens, me, x, bq, bv, *refs):
+    pieces = len(plan.arrays)
+    q_out, k_out, v_out, mixed_out, probs_out, wq, wk, wv, sems = refs[pieces + aliased :]
+    group = pl.program_id(0)
+    fetch(plan, me[0], refs, (wq, wk, wv), sems, group == 0)
+    arrive(plan, me[0], refs, (wq, wk, wv), sems, group == 0)
+    cols = pl.ds(pl.multiple_of(group * GROUP_COLS, GROUP_COLS), GROUP_COLS)
     slots = x.shape[0]
     rows = x[...]
-    q = ((nn(rows, wq[...]) + bq[...]).astype(jnp.bfloat16) * 0.125).astype(jnp.bfloat16)
-    k = nn(rows, wk[...]).astype(jnp.bfloat16)
-    v = (nn(rows, wv[...]) + bv[...]).astype(jnp.bfloat16)
+    q = ((nn(rows, wq[:, cols]) + bq[...]).astype(jnp.bfloat16) * 0.125).astype(jnp.bfloat16)
+    k = nn(rows, wk[:, cols]).astype(jnp.bfloat16)
+    v = (nn(rows, wv[:, cols]) + bv[...]).astype(jnp.bfloat16)
     q_out[...] = q
     k_out[...] = k
     v_out[...] = v
     turned = v.astype(jnp.float32).T.astype(jnp.bfloat16)
-    valid = lax.broadcasted_iota(jnp.int32, (slots, 1), 0) < lens[pl.program_id(0)]
+    valid = lax.broadcasted_iota(jnp.int32, (slots, 1), 0) < lens[seq]
     block = min(256, slots)
     for head in range(GROUP_HEADS):
         pair = slice(head // 2 * 128, head // 2 * 128 + 128)
@@ -182,39 +269,41 @@
     mixed_out[...] = joined.T.astype(jnp.bfloat16)
 
 
-def attend(lengths, rows, wq, wk, wv, bq, bv):
+def attend(lengths, seq, rows, plan, bq, bv, before=()):
     seqs = lengths.shape[0]
     total, width = rows.shape
     slots = total // seqs
     groups = width // GROUP_COLS
-    weight = pl.BlockSpec((width, GROUP_COLS), lambda s, j, lens: (0, j))
-    bias = pl.BlockSpec((1, GROUP_COLS), lambda s, j, lens: (0, j))
-    part = pl.BlockSpec((slots, GROUP_COLS), lambda s, j, lens: (s, j))
+    bias = pl.BlockSpec((1, GROUP_COLS), lambda j, *_: (0, j))
+    part = pl.BlockSpec((slots, GROUP_COLS), lambda j, *_: (seq, j))
     table = jax.ShapeDtypeStruct((total, width), jnp.bfloat16)
-    return pl.pallas_call(
-        attend_kernel,
+    anywhere = pl.BlockSpec(memory_space=pl.ANY)
+    first_alias = 5 + len(plan.arrays)
+    return pl.pallas_call(
+        functools.partial(attend_kernel, plan, seq, len(before)),
         out_shape=[table] * 4
         + [jax.ShapeDtypeStruct((seqs * groups * GROUP_HEADS, slots, slots), jnp.bfloat16)],
         grid_spec=pltpu.PrefetchScalarGridSpec(
-            num_scalar_prefetch=1,
-            grid=(seqs, groups),
-            in_specs=[pl.BlockSpec((slots, width), lambda s, j, lens: (s, 0))]
-            + [weight] * 3
-            + [bias] * 2,
+            num_scalar_prefetch=2,
+            grid=(groups,),
+            in_specs=[pl.BlockSpec((slots, width), lambda j, *_: (seq, 0))]
+            + [bias] * 2
+            + plan.specs()
+            + [anywhere] * len(before),
             out_specs=[part] * 4
-            + [
-                pl.BlockSpec(
-                    (GROUP_HEADS, slots, slots), lambda s, j, lens: (s * groups + j, 0, 0)
-                )
-            ],
+            + [pl.BlockSpec((GROUP_HEADS, slots, slots), lambda j, *_: (seq * groups + j, 0, 0))],
+            scratch_shapes=[pltpu.VMEM((width, width), jnp.bfloat16)] * 3
+            + [pltpu.SemaphoreType.DMA((len(plan.copies),))],
         ),
+        input_output_aliases={first_alias + n: n for n in range(len(before))},
         compiler_params=kernel_params(),
-        cost_estimate=cost(6 * total * width * width + 8 * total * slots * width, 3e7),
-        name="attend",
-    )(lengths, rows, wq, wk, wv, bq, bv)
-
-
-def attend_back_kernel(q, k, v, grad, probs, grads_out, sums_out, held):
+        cost_estimate=cost((6 * total * width * width + 8 * total * slots * width) / seqs, 1.5e7),
+        name=f"attend{seq}",
+    )(lengths, plan.me, rows, bq, bv, *plan.arrays, *before)
+
+
+def attend_back_kernel(q, k, v, grad, probs, *refs):
+    grads_out, sums_out, held = refs[-3:]
     slots = q.shape[0]
     block = min(256, slots)
     key_turned = k[...].astype(jnp.float32).T.astype(jnp.bfloat16)
@@ -244,36 +333,42 @@
     sums_out[0, 1:2, :] = jnp.sum(grads_out[2].astype(jnp.float32), axis=0, keepdims=True)
 
 
-def attend_back(seqs, q, k, v, grad, probs):
+def attend_back(seqs, seq, q, k, v, grad, probs, before=()):
     total, width = q.shape
     slots = total // seqs
     groups = width // GROUP_COLS
-    part = pl.BlockSpec((slots, GROUP_COLS), lambda s, j: (s, j))
+    part = pl.BlockSpec((slots, GROUP_COLS), lambda j: (seq, j))
     return pl.pallas_call(
         attend_back_kernel,
         out_shape=[
             jax.ShapeDtypeStruct((3, total, width), jnp.bfloat16),
-            jax.ShapeDtypeStruct((seqs, 2, width), jnp.float32),
+            jax.ShapeDtypeStruct((1, 2, width), jnp.float32),
         ],
-        grid=(seqs, groups),
+        grid=(groups,),
         in_specs=[part] * 4
-        + [pl.BlockSpec((GROUP_HEADS, slots, slots), lambda s, j: (s * groups + j, 0, 0))],
+        + [pl.BlockSpec((GROUP_HEADS, slots, slots), lambda j: (seq * groups + j, 0, 0))]
+        + [pl.BlockSpec(memory_space=pl.ANY)] * len(before),
         out_specs=[
-            pl.BlockSpec((3, slots, GROUP_COLS), lambda s, j: (0, s, j)),
-            pl.BlockSpec((1, 2, GROUP_COLS), lambda s, j: (s, 0, j)),
+            pl.BlockSpec((3, slots, GROUP_COLS), lambda j: (0, seq, j)),
+            pl.BlockSpec((1, 2, GROUP_COLS), lambda j: (0, 0, j)),
         ],
         scratch_shapes=[pltpu.VMEM((slots, slots), jnp.bfloat16)],
+        input_output_aliases={5: 0} if before else {},
         compiler_params=kernel_params(),
-        cost_estimate=cost(14 * total * slots * width, 3e7),
-        name="attend_back",
-    )(q, k, v, grad, probs)
+        cost_estimate=cost(14 * total * slots * width / seqs, 1.5e7),
+        name=f"attend_back{seq}",
+    )(q, k, v, grad, probs, *before)
 
 
 def row_mean(array):
     return jnp.mean(array, -1, keepdims=True)
 
 
-def feed_kernel(mixed, x, wo, wi, bo, g1, s1, bi, after_out, normed_out, inverse_out, active_out, slope_out):
+def feed_kernel(plan, aliased, me, mixed, x, bo, g1, s1, bi, *refs):
+    after_out, normed_out, inverse_out, active_out, slope_out, wo, wi, sems = refs[len(plan.arrays) + aliased :]
+    first = pl.program_id(0) == 0
+    fetch(plan, me[0], refs, (wo, wi), sems, first)
+    arrive(plan, me[0], refs, (wo, wi), sems, first, (0,))
     hidden_in = x[...].astype(jnp.float32) + (nn(mixed[...], wo[...]) + bo[...])
     centre = hidden_in - row_mean(hidden_in)
     inverse = lax.rsqrt(row_mean(centre * centre) + NORM_EPS)
@@ -282,6 +377,7 @@
     normed_out[...] = normed
     inverse_out[...] = jnp.broadcast_to(inverse, inverse_out.shape)
     after_out[...] = after
+    arrive(plan, me[0], refs, (wo, wi), sems, first, (1,))
     width = after.shape[1]
     for at in range(0, wi.shape[1], width):
         cols = slice(at, at + width)
@@ -304,33 +400,57 @@
     return jax.ShapeDtypeStruct((rows, width), dtype)
 
 
-def feed(mixed, x, wo, wi, bo, g1, s1, bi):
+def row_blocks(total, parts, part):
+    rows = min(256, total // parts)
+    steps = total // parts // rows
+    spec = lambda width: pl.BlockSpec((rows, width), lambda i, *_: (i + part * steps, 0))
+    return rows, steps, spec
+
+
+ANYWHERE = lambda: pl.BlockSpec(memory_space=pl.ANY)
+
+
+def feed(parts, part, mixed, x, plan, bo, g1, s1, bi, before=()):
     total, width = x.shape
-    wide = wi.shape[1]
-    rows = min(256, total)
+    wide = bi.shape[1]
+    rows, steps, spec = row_blocks(total, parts, part)
     bf, f32 = jnp.bfloat16, jnp.float32
-    return pl.pallas_call(
-        feed_kernel,
+    aliases = {7 + len(plan.arrays) + n: n for n in range(len(before))}
+    return pl.pallas_call(
+        functools.partial(feed_kernel, plan, len(before)),
         out_shape=[
             shape(total, width, bf), shape(total, width, f32), shape(total, 128, f32),
             shape(total, wide, bf), shape(total, wide, bf),
         ],
-        grid=(total // rows,),
-        in_specs=[by_rows(rows, width)] * 2 + [whole(a) for a in (wo, wi, bo, g1, s1, bi)],
-        out_specs=[by_rows(rows, n) for n in (width, width, 128, wide, wide)],
+        grid_spec=pltpu.PrefetchScalarGridSpec(
+            num_scalar_prefetch=1,
+            grid=(steps,),
+            in_specs=[spec(width)] * 2 + [whole(a) for a in (bo, g1, s1, bi)] + plan.specs()
+            + [ANYWHERE()] * len(before),
+            out_specs=[spec(n) for n in (width, width, 128, wide, wide)],
+            scratch_shapes=[
+                pltpu.VMEM((width, width), bf), pltpu.VMEM((width, wide), bf),
+                pltpu.SemaphoreType.DMA((len(plan.copies),)),
+            ],
+        ),
+        input_output_aliases=aliases,
         compiler_params=kernel_params(),
-        cost_estimate=cost(2 * total * width * (width + wide), 3e7),
-        name="feed",
-    )(mixed, x, wo, wi, bo, g1, s1, bi)
+        cost_estimate=cost(2 * total * width * (width + wide) / parts * 3, 1.5e7),
+        name=f"feed{part}",
+    )(plan.me, mixed, x, bo, g1, s1, bi, *plan.arrays, *before)
 
 
 def column_sum(array):
     return jnp.sum(array, axis=0, keepdims=True)
 
 
-def turn_kernel(lens, slots, active, normed1, slope, cot, wb, bb, g1, s1, g2, s2,
-                layer_out, ffn_grad_out, hidden_grad_out, h2_grad_out, sums_out, wide_sums_out):
+def turn_kernel(plan, slots, lens, me, active, normed1, slope, cot, bb, g1, s1, g2, s2, *refs):
+    (
+        layer_out, ffn_grad_out, hidden_grad_out, h2_grad_out, sums_out, wide_sums_out, wb, sems,
+    ) = refs[len(plan.arrays) :]
     step = pl.program_id(0)
+    fetch(plan, me[0], refs, (wb,), sems, step == 0)
+    arrive(plan, me[0], refs, (wb,), sems, step == 0)
 
     @pl.when(step == 0)
     def _():
@@ -362,36 +482,40 @@
         wide_sums_out[:, cols] += column_sum(piece.astype(jnp.float32))
 
 
-def turn(lengths, slots, active, normed1, slope, cot, wb, bb, g1, s1, g2, s2):
+def turn(lengths, slots, active, normed1, slope, cot, plan, bb, g1, s1, g2, s2):
     total, width = normed1.shape
-    wide = wb.shape[0]
+    wide = active.shape[1]
     rows = min(256, slots)
     bf, f32 = jnp.bfloat16, jnp.float32
     fixed = lambda r, n: pl.BlockSpec((r, n), lambda i, *_: (0, 0))
-    body = lambda lens, *refs: turn_kernel(lens, slots, *refs)
-    return pl.pallas_call(
-        body,
+    return pl.pallas_call(
+        functools.partial(turn_kernel, plan, slots),
         out_shape=[
             shape(total, width, bf), shape(total, width, bf), shape(total, wide, bf),
             shape(total, width, f32), shape(8, width, f32), shape(1, wide, f32),
         ],
         grid_spec=pltpu.PrefetchScalarGridSpec(
-            num_scalar_prefetch=1,
+            num_scalar_prefetch=2,
             grid=(total // rows,),
             in_specs=[by_rows(rows, n) for n in (wide, width, wide, width)]
-            + [whole(a) for a in (wb, bb, g1, s1, g2, s2)],
+            + [whole(a) for a in (bb, g1, s1, g2, s2)] + plan.specs(),
             out_specs=[by_rows(rows, n) for n in (width, width, wide, width)]
             + [fixed(8, width), fixed(1, wide)],
+            scratch_shapes=[pltpu.VMEM((wide, width), bf), pltpu.SemaphoreType.DMA((len(plan.copies),))],
         ),
         compiler_params=kernel_params(),
         cost_estimate=cost(4 * total * width * wide, 3e7),
         name="turn",
-    )(lengths, active, normed1, slope, cot, wb, bb, g1, s1, g2, s2)
-
-
-def return_kernel(hidden_grad, h2_grad, normed1, inverse1, wi, wo, g1,
-                  h1_grad_out, branch_grad_out, mixed_grad_out, sums_out):
-    @pl.when(pl.program_id(0) == 0)
+    )(lengths, plan.me, active, normed1, slope, cot, bb, g1, s1, g2, s2, *plan.arrays)
+
+
+def return_kernel(plan, aliased, me, hidden_grad, h2_grad, normed1, inverse1, g1, *refs):
+    h1_grad_out, branch_grad_out, mixed_grad_out, sums_out, wo, wi, sems = refs[len(plan.arrays) + aliased :]
+    start = pl.program_id(0) == 0
+    fetch(plan, me[0], refs, (wo, wi), sems, start)
+    arrive(plan, me[0], refs, (wo, wi), sems, start)
+
+    @pl.when(start)
     def _():
         sums_out[...] = jnp.zeros_like(sums_out)
 
@@ -408,44 +532,62 @@
     sums_out[2:3, :] += column_sum(low.astype(jnp.float32))
 
 
-def return_grad(hidden_grad, h2_grad, normed1, inverse1, wi, wo, g1):
+def return_grad(parts, part, hidden_grad, h2_grad, normed1, inverse1, plan, g1, before=()):
     total, width = normed1.shape
-    wide = wi.shape[1]
-    rows = min(256, total)
+    wide = hidden_grad.shape[1]
+    rows, steps, spec = row_blocks(total, parts, part)
     bf, f32 = jnp.bfloat16, jnp.float32
-    return pl.pallas_call(
-        return_kernel,
+    aliases = {6 + len(plan.arrays) + n: n for n in range(len(before))}
+    return pl.pallas_call(
+        functools.partial(return_kernel, plan, len(before)),
         out_shape=[
             shape(total, width, f32), shape(total, width, bf), shape(total, width, bf), shape(8, width, f32),
         ],
-        grid=(total // rows,),
-        in_specs=[by_rows(rows, n) for n in (wide, width, width, 128)] + [whole(a) for a in (wi, wo, g1)],
-        out_specs=[by_rows(rows, width)] * 3 + [pl.BlockSpec((8, width), lambda i: (0, 0))],
+        grid_spec=pltpu.PrefetchScalarGridSpec(
+            num_scalar_prefetch=1,
+            grid=(steps,),
+            in_specs=[spec(n) for n in (wide, width, width, 128)] + [whole(g1)] + plan.specs()
+            + [ANYWHERE()] * len(before),
+            out_specs=[spec(width)] * 3 + [pl.BlockSpec((8, width), lambda i, *_: (0, 0))],
+            scratch_shapes=[
+                pltpu.VMEM((width, width), bf), pltpu.VMEM((width, wide), bf),
+                pltpu.SemaphoreType.DMA((len(plan.copies),)),
+            ],
+        ),
+        input_output_aliases=aliases,
         compiler_params=kernel_params(),
-        cost_estimate=cost(2 * total * width * (width + wide), 3e7),
-        name="return_grad",
-    )(hidden_grad, h2_grad, normed1, inverse1, wi, wo, g1)
-
-
-def input_kernel(h1_grad, grads, wq, wk, wv, out):
+        cost_estimate=cost(2 * total * width * (width + wide) / parts, 1.5e7),
+        name=f"return_grad{part}",
+    )(plan.me, hidden_grad, h2_grad, normed1, inverse1, g1, *plan.arrays, *before)
+
+
+def input_kernel(plan, me, h1_grad, grads, *refs):
+    out, wq, wk, wv, sems = refs[len(plan.arrays) :]
+    start = pl.program_id(0) == 0
+    fetch(plan, me[0], refs, (wq, wk, wv), sems, start)
+    arrive(plan, me[0], refs, (wq, wk, wv), sems, start)
     total = h1_grad[...] + nt(grads[0], wq[...]) + nt(grads[1], wk[...]) + nt(grads[2], wv[...])
     out[...] = total.astype(jnp.bfloat16)
 
 
-def input_grad_of(h1_grad, grads, wq, wk, wv):
+def input_grad_of(h1_grad, grads, plan):
     total, width = h1_grad.shape
-    rows = min(256, total)
-    return pl.pallas_call(
-        input_kernel,
+    rows, steps, spec = row_blocks(total, 1, 0)
+    return pl.pallas_call(
+        functools.partial(input_kernel, plan),
         out_shape=shape(total, width, jnp.bfloat16),
-        grid=(total // rows,),
-        in_specs=[by_rows(rows, width), pl.BlockSpec((3, rows, width), lambda i: (0, i, 0))]
-        + [whole(a) for a in (wq, wk, wv)],
-        out_specs=by_rows(rows, width),
+        grid_spec=pltpu.PrefetchScalarGridSpec(
+            num_scalar_prefetch=1,
+            grid=(steps,),
+            in_specs=[spec(width), pl.BlockSpec((3, rows, width), lambda i, *_: (0, i, 0))] + plan.specs(),
+            out_specs=spec(width),
+            scratch_shapes=[pltpu.VMEM((width, width), jnp.bfloat16)] * 3
+            + [pltpu.SemaphoreType.DMA((len(plan.copies),))],
+        ),
         compiler_params=kernel_params(),
         cost_estimate=cost(6 * total * width * width, 2e7),
         name="input_grad",
-    )(h1_grad, grads, wq, wk, wv)
+    )(plan.me, h1_grad, grads, *plan.arrays)
 
 
 def store_chunks(product, me, own, send):
@@ -672,35 +814,64 @@
     got_a = gather_group(jnp.concatenate([query_weight, key_weight, value_weight]), bits, ())
     for b in range(bits - 1, -1, -1):
         table = jnp.stack([table, swap_with(table, 1 << b)], axis=1).reshape((-1,) + table.shape[1:])
-    got_b = gather_group(jnp.concatenate([out_weight] + in_blocks), bits, got_a[1])
-    got_c = gather_group(back_weight_shard, bits, got_b[1])
+    got_b = gather_group(jnp.concatenate([out_weight] + in_blocks), bits, got_a[2])
+    got_c = gather_group(back_weight_shard, bits, got_b[2])
     vectors, bi = spread(me, table, width, wide)
     bq, bv, bo, bb, g1, s1, g2, s2 = (vectors[i : i + 1] for i in range(8))
-    full_a = place(got_a[0], index, count)
-    full_b = place(got_b[0], index, count)
-    full_c = place(got_c[0], index, count)
-    wq, wk, wv = (full_a[:, n * chunk : (n + 1) * chunk].reshape(width, width) for n in range(3))
-    wo = full_b[:, :chunk].reshape(width, width)
-    wi = jnp.concatenate(
-        [full_b[:, n * chunk : (n + 1) * chunk] for n in range(1, blocks + 1)], axis=2
-    ).reshape(width, wide)
-    wb = full_c.reshape(wide, width)
-
-    q, k, v, mixed, probs = attend(lengths, x, wq, wk, wv, bq, bv)
-    after_low, normed1, inverse1, active, slope = feed(mixed, x, wo, wi, bo, g1, s1, bi)
+    third = [(n, n * chunk, chunk, 0) for n in range(3)]
+    plan_a = Gathered(got_a[0], me, count, chunk, third)
+    plan_b = Gathered(
+        got_b[0], me, count, chunk,
+        [(0, 0, chunk, 0)] + [(1, (n + 1) * chunk, chunk, n * width) for n in range(blocks)],
+    )
+    back_chunk = back_weight_shard.shape[0]
+    plan_c = Gathered(got_c[0], me, count, back_chunk, [(0, 0, back_chunk, 0)])
+
+    made = ()
+    for seq in range(seqs):
+        ready = got_b[1] if seq == seqs - 1 else ()
+        made = attend(lengths, seq, after(x, *ready) if seq else x, plan_a, bq, bv, made)
+    q, k, v, mixed, probs = made
+    fed = feed(2, 0, mixed, x, plan_b, bo, g1, s1, bi)
+    fed = feed(2, 1, mixed, after(x, *got_c[1]), plan_b, bo, g1, s1, bi, fed)
+    after_low, normed1, inverse1, active, slope = fed
     layer_out, ffn_grad, hidden_grad, h2_grad, sums2, in_bias_sum = turn(
-        lengths, slots, active, normed1, slope, cot, wb, bb, g1, s1, g2, s2
+        lengths, slots, active, normed1, slope, cot, plan_c, bb, g1, s1, g2, s2
     )
-    sum_c = reduce_all(*back_weight(me, active, ffn_grad, count), bits)
-    h1_grad, branch_grad, mixed_grad, sums1 = return_grad(hidden_grad, h2_grad, normed1, inverse1, wi, wo, g1)
-    sum_b = reduce_all(*in_out_weight(me, after_low, hidden_grad, mixed, branch_grad, count), bits)
-    grads, attend_sums = attend_back(seqs, q, k, v, mixed_grad, probs)
-    sum_a = reduce_all(*qkv_weight(me, x, grads, count), bits)
-    input_grad = input_grad_of(h1_grad, grads, wq, wk, wv)
+    own, send = back_weight(me, active, ffn_grad, count)
+    hidden_grad, send = lax.optimization_barrier((hidden_grad, send))
+    red_c = reduction(own, send, bits)
+    came = next(red_c)
+    back = return_grad(2, 0, hidden_grad, h2_grad, normed1, inverse1, plan_b, g1)
+    h2_grad = after(h2_grad, *came, back[3])
+    came = next(red_c)
+    h1_grad, branch_grad, mixed_grad, more = return_grad(
+        2, 1, hidden_grad, h2_grad, normed1, inverse1, plan_b, g1, back[:3]
+    )
+    sums1 = back[3] + more
+    own, send = in_out_weight(me, after_low, hidden_grad, mixed, branch_grad, count)
+    red_b = reduction(own, send, bits)
+    came_b = next(red_b)
+    mixed_grad = after(mixed_grad, send, *came)
+    came = next(red_c)
+    first = attend_back(seqs, 0, q, k, v, mixed_grad, probs)
+    grads, sums_at = first
+    attend_sums = sums_at[0]
+    for seq in range(1, seqs):
+        mixed_grad = after(mixed_grad, attend_sums, *came, *came_b)
+        came, came_b = next(red_c), next(red_b)
+        grads, sums_at = attend_back(seqs, seq, q, k, v, mixed_grad, probs, (grads,))
+        attend_sums = attend_sums + sums_at[0]
+    own, send = qkv_weight(me, after(x, *came, *came_b), grads, count)
+    came, came_b = next(red_c), next(red_b)
+    red_a = reduction(own, send, bits)
+    came_a = next(red_a)
+    input_grad = input_grad_of(after(h1_grad, own, *came, *came_a), grads, plan_a)
+    sum_c, sum_b, sum_a = finish(red_c), finish(red_b), finish(red_a)
 
     small = jnp.concatenate(
         [
-            jnp.sum(attend_sums, 0), sums1[2:3], sums2[2:3], sums1[0:2], sums2[0:2],
+            attend_sums, sums1[2:3], sums2[2:3], sums1[0:2], sums2[0:2],
             in_bias_sum.reshape(blocks, width),
         ]
     )

time: 377 us -> 382 us (1.013)
  Pallas kernels: 143 us -> 172 us
  waiting for transfers between devices: 119 us -> 96.3 us
  local copies, waits for them, and re-layouts: 48 us -> 27.7 us
  starting transfers between devices: 46.3 us -> 54.2 us
  other arithmetic: 18.3 us -> 26.1 us
    pallas_call x5 -> x8, Pallas kernels: 84.8 us -> 111 us  [the longest x2 28.2 us: attend(): pl.pallas_call(functools.partial(attend_kernel, plan, seq, len(before)),...]
    ppermute x59, waiting for transfers between devices: 119 us -> 96.3 us  [swap_with(): return lax.ppermute(array, AXES, pairs)]
    dynamic_update_slice x30 -> x0, local copies, waits for them, and re-layouts: 18.6 us -> none  [place(): full = lax.dynamic_update_slice(full, part[None], (me ^ d, at, 0))]
    ppermute x59, starting transfers between devices: 46.3 us -> 54.2 us  [swap_with(): return lax.ppermute(array, AXES, pairs)]
    convert_element_type x18, other arithmetic: 8.52 us -> 16.2 us  [add_low(): (left.astype(jnp.float32) + right.astype(jnp.float32)).astype(jnp.bfloat16)]
    pallas_call x1 -> x2, Pallas kernels: 21.5 us -> 24.3 us  [attend_back(): pl.pallas_call(attend_back_kernel, out_shape=[jax.ShapeDtypeStruct((3, to...]
    unnamed x32 -> x70, local copies, waits for them, and re-layouts: 9.54 us -> 8.18 us
  transfers between devices with their start and end apart: 59 -> 59, of which waited for: 25 -> 25; matrix products, arithmetic and copies ran while one was open for 15% -> 12% of each run, Pallas kernels for 20% -> 30%
where the time goes in v3:
time: 382 us; the launch traced here: 378 us
  Pallas kernels  172 us (45%)
  waiting for transfers between devices  96.3 us (25%)
  starting transfers between devices  54.2 us (14%)
  local copies, waits for them, and re-layouts  27.7 us (7%)
  other arithmetic  26.1 us (7%)
    ppermute x59, waiting for transfers between devices, swap_with(): return lax.ppermute(array, AXES, pairs)  96.3 us
    ppermute x59, starting transfers between devices, swap_with(): return lax.ppermute(array, AXES, pairs)  54.2 us
    pallas_call x2, Pallas kernels, attend(): pl.pallas_call(functools.partial(attend_kernel, plan, seq, len(before)),...  28.2 us
    pallas_call x2, Pallas kernels, feed(): pl.pallas_call(functools.partial(feed_kernel, plan, len(before)), out_sha...  25.3 us
    pallas_call x2, Pallas kernels, attend_back(): pl.pallas_call(attend_back_kernel, out_shape=[jax.ShapeDtypeStruct((3, to...  24.3 us
    pallas_call x1, Pallas kernels, turn(): pl.pallas_call(functools.partial(turn_kernel, plan, slots), out_shape=[sh...  24.1 us
    pallas_call x2, Pallas kernels, return_grad(): pl.pallas_call(functools.partial(return_kernel, plan, len(before)), out_s...  23.4 us
    convert_element_type x18, other arithmetic, add_low(): (left.astype(jnp.float32) + right.astype(jnp.float32)).astype(jnp.bfloat16)  16.2 us
  transfers between devices with their start and end apart: 59, of which 25 were waited for; matrix products, arithmetic and copies ran while one was open for 12% of the time, Pallas kernels for 30%

profile of v3, /device:TPU:0, one launch (start us, length us, event | category | flops | bytes accessed | tf_op | source)
XLA Modules:
  0.0 377.8 jit_solution(12690406800391001382)
XLA Ops:
  3.5 3.0 collective-permute-start
  10.0 6.8 %collective-permute-done.refs_1_ = bf16[288,768]{1,0:T(8,128)(2,1)} collective-permute-done((bf16[288,768]{1,0:T(8,128)(2,1)S(1)}, bf16[288,768]{1,0:T(8,128)(2,1)}, u32[]{:S(2)}, u32[]{:S(2)}) %collective-permute-start) | collective-permute-done | bytes 442400 | tf_op jit(solution)/shard_map/ppermute | solution.py:29
  22.1 2.3 collective-permute-done.1.refs_3_
  28.7 14.2 %collective-permute-done.4.refs_1_ = bf16[480,768]{1,0:T(8,128)(2,1)S(1)} collective-permute-done((bf16[480,768]{1,0:T(8,128)(2,1)S(1)}, bf16[480,768]{1,0:T(8,128)(2,1)S(1)}, u32[]{:S(2)}, u32[]{:S(2)}) %collective-permute-start.4) | collective-permute-done | bytes 737312 | tf_op jit(solution)/shard_map/ppermute | solution.py:29
  50.1 2.3 collective-permute-done.6
  54.1 2.8 collective-permute-done.7
  68.5 6.5 %collective-permute-done.16.refs_1_ = bf16[384,768]{1,0:T(8,128)(2,1)} collective-permute-done((bf16[384,768]{1,0:T(8,128)(2,1)}, bf16[384,768]{1,0:T(8,128)(2,1)}, u32[]{:S(2)}, u32[]{:S(2)}) %collective-permute-start.16) | collective-permute-done | bytes 589856 | tf_op jit(solution)/shard_map/ppermute | solution.py:29
  75.9 14.1 %attend0.1 = (bf16[1024,768]{1,0:T(8,128)(2,1)}, bf16[1024,768]{1,0:T(8,128)(2,1)}, bf16[1024,768]{1,0:T(8,128)(2,1)}, bf16[1024,768]{1,0:T(8,128)(2,1)}, bf16[24,512,512]{2,1,0:T(8,128)(2,1)}) custom-call(s32[2]{0:T(128)} %lens.5, s32[1]{0:T(128)} %bitcast.me, bf16[1024,768]{1,0:T(8,128)(2,1)} %bitcast.173, f32[1,768]{1,0:T(1,128)} %get-tuple-element.170.bq, ...), custom_call_target="tpu_custom_call" | custom-call | flops 3422552064 | bytes 15000000 | tf_op jit(solution)/shard_map/attend0/pallas_call | solution.py:282
  90.1 14.1 %attend1.1 = (bf16[1024,768]{1,0:T(8,128)(2,1)}, bf16[1024,768]{1,0:T(8,128)(2,1)}, bf16[1024,768]{1,0:T(8,128)(2,1)}, bf16[1024,768]{1,0:T(8,128)(2,1)}, bf16[24,512,512]{2,1,0:T(8,128)(2,1)}) custom-call(s32[2]{0:T(128)} %lens.5, s32[1]{0:T(128)} %bitcast.me, ...), custom_call_target="tpu_custom_call", output_to_operand_aliasing={{0}: (15, {}), {1}: (16, {}), {2}: (17, {}), {3}: (18, {}),... | custom-call | flops 3422552064 | bytes 15000000 | tf_op jit(solution)/shard_map/attend1/pallas_call | solution.py:282
  110.4 12.6 %feed0.1 = (bf16[1024,768]{1,0:T(8,128)(2,1)}, f32[1024,768]{1,0:T(8,128)}, f32[1024,128]{1,0:T(8,128)}, bf16[1024,3072]{1,0:T(8,128)(2,1)}, bf16[1024,3072]{1,0:T(8,128)(2,1)}) custom-call(s32[1]{0:T(128)} %bitcast.me, bf16[1024,768]{1,0:T(8,128)(2,1)} %get-tuple-element.91.mixed, bf16[1024,768]{1,0:T(8,128)(2,1)} %bitcast.175, ...), custom_call_target="tpu_custom_call" | custom-call | flops 9059696640 | bytes 15000000 | tf_op jit(solution)/shard_map/feed0/pallas_call | solution.py:419
  124.0 12.7 %feed1.1 = (bf16[1024,768]{1,0:T(8,128)(2,1)}, f32[1024,768]{1,0:T(8,128)}, f32[1024,128]{1,0:T(8,128)}, bf16[1024,3072]{1,0:T(8,128)(2,1)}, bf16[1024,3072]{1,0:T(8,128)(2,1)}) custom-call(s32[1]{0:T(128)} %bitcast.me, bf16[1024,768]{1,0:T(8,128)(2,1)} %get-tuple-element.91.mixed, ...), custom_call_target="tpu_custom_call", output_to_operand_aliasing={{0}: (17, {}), {1}: (18, {}), {2}: (19, {}), {3}: (20, {}),... | custom-call | flops 9059696640 | bytes 15000000 | tf_op jit(solution)/shard_map/feed1/pallas_call | solution.py:419
  138.2 24.1 %turn.1 = (bf16[1024,768]{1,0:T(8,128)(2,1)}, bf16[1024,768]{1,0:T(8,128)(2,1)}, bf16[1024,3072]{1,0:T(8,128)(2,1)}, f32[1024,768]{1,0:T(8,128)}, f32[8,768]{1,0:T(8,128)}, /*index=5*/f32[1,3072]{1,0:T(1,128)}) custom-call(s32[2]{0:T(128)} %lens.5, s32[1]{0:T(128)} %bitcast.me, bf16[1024,3072]{1,0:T(8,128)(2,1)} %get-tuple-element.100.active, ...), custom_call_target="tpu_custom_call" | custom-call | flops 9663676416 | bytes 30000000 | tf_op jit(solution)/shard_map/turn/pallas_call | solution.py:491
  162.3 11.4 %back_weight.1 = (bf16[4,384,768]{2,1,0:T(8,128)(2,1)}, bf16[4,384,768]{2,1,0:T(8,128)(2,1)}) custom-call(s32[1]{0:T(128)} %bitcast.me, bf16[1024,3072]{1,0:T(8,128)(2,1)} %get-tuple-element.100.active, bf16[1024,768]{1,0:T(8,128)(2,1)} %get-tuple-element.105.grad), custom_call_target="tpu_custom_call" | custom-call | flops 4831838208 | bytes 13000000 | tf_op jit(solution)/shard_map/back_weight/pallas_call | solution.py:644
  173.8 11.4 %return_grad0.1 = (f32[1024,768]{1,0:T(8,128)}, bf16[1024,768]{1,0:T(8,128)(2,1)}, bf16[1024,768]{1,0:T(8,128)(2,1)}, f32[8,768]{1,0:T(8,128)}) custom-call(s32[1]{0:T(128)} %bitcast.me, bf16[1024,3072]{1,0:T(8,128)(2,1)} %get-tuple-element.107.hidden_grad, f32[1024,768]{1,0:T(8,128)} %get-tuple-element.112.h2_grad, f32[1024,768]{1,0:T(8,128)} %get-tuple-element.101.normed1, ...), custom_call_target="tpu_custom_call" | custom-call | flops 3019898880 | bytes 15000000 | tf_op jit(solution)/shard_map/return_grad0/pallas_call | solution.py:541
  185.2 12.0 %return_grad1.1 = (f32[1024,768]{1,0:T(8,128)}, bf16[1024,768]{1,0:T(8,128)(2,1)}, bf16[1024,768]{1,0:T(8,128)(2,1)}, f32[8,768]{1,0:T(8,128)}) custom-call(s32[1]{0:T(128)} %bitcast.me, bf16[1024,3072]{1,0:T(8,128)(2,1)} %get-tuple-element.107.hidden_grad, ...), custom_call_target="tpu_custom_call", output_to_operand_aliasing={{0}: (16, {}), {1}: (17, {}), {2}: (18, {})} | custom-call | flops 3019898880 | bytes 15000000 | tf_op jit(solution)/shard_map/return_grad1/pallas_call | solution.py:541
  197.2 12.9 %in_out_weight.1 = (bf16[4,480,768]{2,1,0:T(8,128)(2,1)}, bf16[4,480,768]{2,1,0:T(8,128)(2,1)}) custom-call(s32[1]{0:T(128)} %bitcast.me, bf16[1024,768]{1,0:T(8,128)(2,1)} %get-tuple-element.118.after, bf16[1024,3072]{1,0:T(8,128)(2,1)} %get-tuple-element.107.hidden_grad, bf16[1024,768]{1,0:T(8,128)(2,1)} %get-tuple-element.91.mixed, ...), custom_call_target="tpu_custom_call" | custom-call | flops 6039797760 | bytes 20000000 | tf_op jit(solution)/shard_map/in_out_weight/pallas_call | solution.py:686
  210.6 2.9 add_convert_fusion.1
  215.5 13.7 %collective-permute-done.31 = bf16[2,192,768]{2,1,0:T(8,128)(2,1)} collective-permute-done((bf16[2,192,768]{2,1,0:T(8,128)(2,1)S(1)}, bf16[2,192,768]{2,1,0:T(8,128)(2,1)}, u32[]{:S(2)}, u32[]{:S(2)}) %collective-permute-start.31) | collective-permute-done | bytes 589856 | tf_op jit(solution)/shard_map/ppermute | solution.py:29
  233.8 12.1 %attend_back0.1 = (bf16[3,1024,768]{2,1,0:T(8,128)(2,1)}, f32[1,2,768]{2,1,0:T(2,128)}) custom-call(bf16[1024,768]{1,0:T(8,128)(2,1)} %get-tuple-element.123.q, bf16[1024,768]{1,0:T(8,128)(2,1)} %get-tuple-element.124.k, bf16[1024,768]{1,0:T(8,128)(2,1)} %get-tuple-element.125.v, bf16[1024,768]{1,0:T(8,128)(2,1)} %get-tuple-element.130.grad, ...), custom_call_target="tpu_custom_call" | custom-call | flops 2818572288 | bytes 15000000 | tf_op jit(solution)/shard_map/attend_back0/pallas_call | solution.py:341
  246.0 3.4 add_convert_fusion
  258.2 12.2 %attend_back1.1 = (bf16[3,1024,768]{2,1,0:T(8,128)(2,1)}, f32[1,2,768]{2,1,0:T(2,128)}) custom-call(bf16[1024,768]{1,0:T(8,128)(2,1)} %get-tuple-element.123.q, bf16[1024,768]{1,0:T(8,128)(2,1)} %get-tuple-element.124.k, bf16[1024,768]{1,0:T(8,128)(2,1)} %get-tuple-element.125.v, ...), custom_call_target="tpu_custom_call", output_to_operand_aliasing={{0}: (5, {})} | custom-call | flops 2818572288 | bytes 15000000 | tf_op jit(solution)/shard_map/attend_back1/pallas_call | solution.py:341
  274.4 8.3 %qkv_weight.1 = (bf16[4,288,768]{2,1,0:T(8,128)(2,1)}, bf16[4,288,768]{2,1,0:T(8,128)(2,1)}) custom-call(s32[1]{0:T(128)} %bitcast.me, bf16[1024,768]{1,0:T(8,128)(2,1)} %bitcast.177, bf16[3,1024,768]{2,1,0:T(8,128)(2,1)} %get-tuple-element.132.grads), custom_call_target="tpu_custom_call" | custom-call | flops 3623878656 | bytes 10000000 | tf_op jit(solution)/shard_map/qkv_weight/pallas_call | solution.py:713
  290.3 2.7 collective-permute-start.39
  292.9 3.0 collective-permute-done.50
  301.6 2.8 collective-permute-done.55
  310.7 4.9 %collective-permute-done.39 = bf16[192,768]{1,0:T(8,128)(2,1)} collective-permute-done((bf16[192,768]{1,0:T(8,128)(2,1)S(1)}, bf16[192,768]{1,0:T(8,128)(2,1)}, u32[]{:S(2)}, u32[]{:S(2)}) %collective-permute-start.39) | collective-permute-done | bytes 294944 | tf_op jit(solution)/shard_map/ppermute | solution.py:29
  316.7 6.8 %collective-permute-done.57 = f32[12,768]{1,0:T(8,128)S(1)} collective-permute-done((f32[12,768]{1,0:T(8,128)S(1)}, f32[12,768]{1,0:T(8,128)S(1)}, u32[]{:S(2)}, u32[]{:S(2)}) %collective-permute-start.57) | collective-permute-done | bytes 36896 | tf_op jit(solution)/shard_map/ppermute | solution.py:29
  325.1 2.5 collective-permute-start.52
  344.7 3.7 collective-permute-done.42
  351.2 4.9 %collective-permute-done.45 = bf16[144,768]{1,0:T(8,128)(2,1)S(1)} collective-permute-done((bf16[144,768]{1,0:T(8,128)(2,1)S(1)}, bf16[144,768]{1,0:T(8,128)(2,1)S(1)}, u32[]{:S(2)}, u32[]{:S(2)}) %collective-permute-start.45) | collective-permute-done | bytes 221216 | tf_op jit(solution)/shard_map/ppermute | solution.py:29
  358.4 7.5 %collective-permute-done.46 = bf16[144,768]{1,0:T(8,128)(2,1)S(1)} collective-permute-done((bf16[144,768]{1,0:T(8,128)(2,1)S(1)}, bf16[144,768]{1,0:T(8,128)(2,1)S(1)}, u32[]{:S(2)}, u32[]{:S(2)}) %collective-permute-start.46) | collective-permute-done | bytes 221216 | tf_op jit(solution)/shard_map/ppermute | solution.py:29
  366.8 9.7 %input_grad.1 = bf16[1024,768]{1,0:T(8,128)(2,1)} custom-call(s32[1]{0:T(128)} %bitcast.me, f32[1024,768]{1,0:T(8,128)} %get-tuple-element.135.h1_grad, bf16[3,1024,768]{2,1,0:T(8,128)(2,1)} %get-tuple-element.132.grads, bf16[288,768]{1,0:T(8,128)(2,1)} %copy-done.12, bf16[288,768]{1,0:T(8,128)(2,1)} %collective-permute-done.refs_1_, ...), custom_call_target="tpu_custom_call" | custom-call | flops 3623878656 | bytes 20000000 | tf_op jit(solution)/shard_map/input_grad/pallas_call | solution.py:576
  (246 shorter events, 111.8 us)
Async XLA Ops:
  3.5 13.3 %collective-permute-start = (bf16[288,768]{1,0:T(8,128)(2,1)S(1)}, bf16[288,768]{1,0:T(8,128)(2,1)}, u32[]{:S(2)}, u32[]{:S(2)}) collective-permute-start(bf16[288,768]{1,0:T(8,128)(2,1)S(1)} %constant_dynamic-update-slice_fusion.1.refs_0_), channel_id=1, source_target_pairs={{0,8},{1,9},{2,10},{3,11},{4,12},{5,13},{6,14},{7,15},{8,0},{9,1},... | collective-permute-start | bytes 1327112 | tf_op jit(solution)/shard_map/ppermute | solution.py:29
  26.7 16.2 %collective-permute-start.4 = (bf16[480,768]{1,0:T(8,128)(2,1)S(1)}, bf16[480,768]{1,0:T(8,128)(2,1)S(1)}, u32[]{:S(2)}, u32[]{:S(2)}) collective-permute-start(bf16[480,768]{1,0:T(8,128)(2,1)S(1)} %slice_dynamic-update-slice_fusion.refs_0_), channel_id=1, source_target_pairs={{0,8},{1,9},{2,10},{3,11},{4,12},{5,13},{6,14},{7,15},{8,0},{9,1},... | collective-permute-start | bytes 2211848 | tf_op jit(solution)/shard_map/ppermute | solution.py:29
  28.2 16.6 %collective-permute-start.5 = (bf16[480,768]{1,0:T(8,128)(2,1)S(1)}, bf16[480,768]{1,0:T(8,128)(2,1)S(1)}, u32[]{:S(2)}, u32[]{:S(2)}) collective-permute-start(bf16[480,768]{1,0:T(8,128)(2,1)S(1)} %slice_dynamic-update-slice_fusion.refs_0_), channel_id=1, source_target_pairs={{0,16},{1,17},{2,18},{3,19},{4,20},{5,21},{6,22},{7,23},{8,24},{9,... | collective-permute-start | bytes 2211848 | tf_op jit(solution)/shard_map/ppermute | solution.py:29
  43.7 13.2 %collective-permute-start.14 = (bf16[240,768]{1,0:T(8,128)(2,1)}, bf16[240,768]{1,0:T(8,128)(2,1)S(1)}, u32[]{:S(2)}, u32[]{:S(2)}) collective-permute-start(bf16[240,768]{1,0:T(8,128)(2,1)} %slice.244), channel_id=1, source_target_pairs={{0,16},{1,17},{2,18},{3,19},{4,20},{5,21},{6,22},{7,23},{8,24},{9,... | collective-permute-start | bytes 1105928 | tf_op jit(solution)/shard_map/ppermute | solution.py:29
  44.5 15.9 %collective-permute-start.9 = (bf16[288,768]{1,0:T(8,128)(2,1)S(1)}, bf16[288,768]{1,0:T(8,128)(2,1)S(1)}, u32[]{:S(2)}, u32[]{:S(2)}) collective-permute-start(bf16[288,768]{1,0:T(8,128)(2,1)S(1)} %constant_dynamic-update-slice_fusion.1.refs_0_), channel_id=1, source_target_pairs={{0,4},{1,5},{2,6},{3,7},{4,0},{5,1},{6,2},{7,3},{8,12},{9,13},{10,... | collective-permute-start | bytes 1327112 | tf_op jit(solution)/shard_map/ppermute | solution.py:29
  59.3 15.7 %collective-permute-start.16 = (bf16[384,768]{1,0:T(8,128)(2,1)}, bf16[384,768]{1,0:T(8,128)(2,1)}, u32[]{:S(2)}, u32[]{:S(2)}) collective-permute-start(bf16[384,768]{1,0:T(8,128)(2,1)} %refs_0_), channel_id=1, source_target_pairs={{0,8},{1,9},{2,10},{3,11},{4,12},{5,13},{6,14},{7,15},{8,0},{9,1},... | collective-permute-start | bytes 1769480 | tf_op jit(solution)/shard_map/ppermute | solution.py:29
  60.5 15.4 %collective-permute-start.17 = (bf16[384,768]{1,0:T(8,128)(2,1)}, bf16[384,768]{1,0:T(8,128)(2,1)}, u32[]{:S(2)}, u32[]{:S(2)}) collective-permute-start(bf16[384,768]{1,0:T(8,128)(2,1)} %refs_0_), channel_id=1, source_target_pairs={{0,16},{1,17},{2,18},{3,19},{4,20},{5,21},{6,22},{7,23},{8,24},{9,... | collective-permute-start | bytes 1769480 | tf_op jit(solution)/shard_map/ppermute | solution.py:29
  65.7 41.9 %collective-permute-start.18 = (bf16[480,768]{1,0:T(8,128)(2,1)S(1)}, bf16[480,768]{1,0:T(8,128)(2,1)S(1)}, u32[]{:S(2)}, u32[]{:S(2)}) collective-permute-start(bf16[480,768]{1,0:T(8,128)(2,1)S(1)} %slice_dynamic-update-slice_fusion.refs_0_), channel_id=1, source_target_pairs={{0,4},{1,5},{2,6},{3,7},{4,0},{5,1},{6,2},{7,3},{8,12},{9,13},{10,... | collective-permute-start | bytes 2211848 | tf_op jit(solution)/shard_map/ppermute | solution.py:29
  66.2 44.1 %collective-permute-start.19 = (bf16[480,768]{1,0:T(8,128)(2,1)S(1)}, bf16[480,768]{1,0:T(8,128)(2,1)}, u32[]{:S(2)}, u32[]{:S(2)}) collective-permute-start(bf16[480,768]{1,0:T(8,128)(2,1)S(1)} %collective-permute-done.4.refs_1_), channel_id=1, source_target_pairs={{0,4},{1,5},{2,6},{3,7},{4,0},{5,1},{6,2},{7,3},{8,12},{9,13},{10,... | collective-permute-start | bytes 2211848 | tf_op jit(solution)/shard_map/ppermute | solution.py:29
  66.3 44.0 %collective-permute-start.20 = (bf16[480,768]{1,0:T(8,128)(2,1)S(1)}, bf16[480,768]{1,0:T(8,128)(2,1)}, u32[]{:S(2)}, u32[]{:S(2)}) collective-permute-start(bf16[480,768]{1,0:T(8,128)(2,1)S(1)} %collective-permute-done.5.refs_2_), channel_id=1, source_target_pairs={{0,4},{1,5},{2,6},{3,7},{4,0},{5,1},{6,2},{7,3},{8,12},{9,13},{10,... | collective-permute-start | bytes 2211848 | tf_op jit(solution)/shard_map/ppermute | solution.py:29
  75.0 33.1 %collective-permute-start.21 = (bf16[240,768]{1,0:T(8,128)(2,1)S(1)}, bf16[240,768]{1,0:T(8,128)(2,1)S(1)}, u32[]{:S(2)}, u32[]{:S(2)}) collective-permute-start(bf16[240,768]{1,0:T(8,128)(2,1)S(1)} %collective-permute-done.14.refs_3_), channel_id=1, source_target_pairs={{0,4},{1,5},{2,6},{3,7},{4,0},{5,1},{6,2},{7,3},{8,12},{9,13},{10,... | collective-permute-start | bytes 1105928 | tf_op jit(solution)/shard_map/ppermute | solution.py:29
  75.9 33.7 %collective-permute-start.22 = (bf16[240,768]{1,0:T(8,128)(2,1)}, bf16[240,768]{1,0:T(8,128)(2,1)}, u32[]{:S(2)}, u32[]{:S(2)}) collective-permute-start(bf16[240,768]{1,0:T(8,128)(2,1)} %collective-permute-done.15.refs_4_), channel_id=1, source_target_pairs={{0,4},{1,5},{2,6},{3,7},{4,0},{5,1},{6,2},{7,3},{8,12},{9,13},{10,... | collective-permute-start | bytes 1105928 | tf_op jit(solution)/shard_map/ppermute | solution.py:29
  107.5 29.2 %collective-permute-start.25 = (bf16[384,768]{1,0:T(8,128)(2,1)}, bf16[384,768]{1,0:T(8,128)(2,1)S(1)}, u32[]{:S(2)}, u32[]{:S(2)}) collective-permute-start(bf16[384,768]{1,0:T(8,128)(2,1)} %refs_0_), channel_id=1, source_target_pairs={{0,4},{1,5},{2,6},{3,7},{4,0},{5,1},{6,2},{7,3},{8,12},{9,13},{10,... | collective-permute-start | bytes 1769480 | tf_op jit(solution)/shard_map/ppermute | solution.py:29
  108.1 15.4 %collective-permute-start.23 = (bf16[192,768]{1,0:T(8,128)(2,1)}, bf16[192,768]{1,0:T(8,128)(2,1)S(1)}, u32[]{:S(2)}, u32[]{:S(2)}) collective-permute-start(bf16[192,768]{1,0:T(8,128)(2,1)} %slice.246), channel_id=1, source_target_pairs={{0,16},{1,17},{2,18},{3,19},{4,20},{5,21},{6,22},{7,23},{8,24},{9,... | collective-permute-start | bytes 884744 | tf_op jit(solution)/shard_map/ppermute | solution.py:29
  109.6 14.0 %collective-permute-start.24 = (bf16[192,768]{1,0:T(8,128)(2,1)}, bf16[192,768]{1,0:T(8,128)(2,1)S(1)}, u32[]{:S(2)}, u32[]{:S(2)}) collective-permute-start(bf16[192,768]{1,0:T(8,128)(2,1)} %slice.247), channel_id=1, source_target_pairs={{0,8},{1,9},{2,10},{3,11},{4,12},{5,13},{6,14},{7,15},{8,0},{9,1},... | collective-permute-start | bytes 884744 | tf_op jit(solution)/shard_map/ppermute | solution.py:29
  122.9 13.9 %collective-permute-start.26 = (bf16[384,768]{1,0:T(8,128)(2,1)}, bf16[384,768]{1,0:T(8,128)(2,1)S(1)}, u32[]{:S(2)}, u32[]{:S(2)}) collective-permute-start(bf16[384,768]{1,0:T(8,128)(2,1)} %collective-permute-done.16.refs_1_), channel_id=1, source_target_pairs={{0,4},{1,5},{2,6},{3,7},{4,0},{5,1},{6,2},{7,3},{8,12},{9,13},{10,... | collective-permute-start | bytes 1769480 | tf_op jit(solution)/shard_map/ppermute | solution.py:29
  123.0 13.8 %collective-permute-start.27 = (bf16[384,768]{1,0:T(8,128)(2,1)}, bf16[384,768]{1,0:T(8,128)(2,1)S(1)}, u32[]{:S(2)}, u32[]{:S(2)}) collective-permute-start(bf16[384,768]{1,0:T(8,128)(2,1)} %collective-permute-done.17.refs_2_), channel_id=1, source_target_pairs={{0,4},{1,5},{2,6},{3,7},{4,0},{5,1},{6,2},{7,3},{8,12},{9,13},{10,... | collective-permute-start | bytes 1769480 | tf_op jit(solution)/shard_map/ppermute | solution.py:29
  123.5 13.3 %collective-permute-start.28 = (bf16[192,768]{1,0:T(8,128)(2,1)S(1)}, bf16[192,768]{1,0:T(8,128)(2,1)S(1)}, u32[]{:S(2)}, u32[]{:S(2)}) collective-permute-start(bf16[192,768]{1,0:T(8,128)(2,1)S(1)} %collective-permute-done.23.refs_3_), channel_id=1, source_target_pairs={{0,4},{1,5},{2,6},{3,7},{4,0},{5,1},{6,2},{7,3},{8,12},{9,13},{10,... | collective-permute-start | bytes 884744 | tf_op jit(solution)/shard_map/ppermute | solution.py:29
  210.1 35.9 %collective-permute-start.36 = (bf16[4,480,768]{2,1,0:T(8,128)(2,1)}, bf16[4,480,768]{2,1,0:T(8,128)(2,1)}, u32[]{:S(2)}, u32[]{:S(2)}) collective-permute-start(bf16[4,480,768]{2,1,0:T(8,128)(2,1)} %get-tuple-element.121), channel_id=1, source_target_pairs={{0,4},{1,5},{2,6},{3,7},{4,0},{5,1},{6,2},{7,3},{8,12},{9,13},{10,... | collective-permute-start | bytes 8847368 | tf_op jit(solution)/shard_map/ppermute | solution.py:29
  213.6 15.5 %collective-permute-start.31 = (bf16[2,192,768]{2,1,0:T(8,128)(2,1)S(1)}, bf16[2,192,768]{2,1,0:T(8,128)(2,1)}, u32[]{:S(2)}, u32[]{:S(2)}) collective-permute-start(bf16[2,192,768]{2,1,0:T(8,128)(2,1)S(1)} %slice_bitcast_fusion.6), channel_id=1, source_target_pairs={{0,8},{1,9},{2,10},{3,11},{4,12},{5,13},{6,14},{7,15},{8,0},{9,1},... | collective-permute-start | bytes 1769480 | tf_op jit(solution)/shard_map/ppermute | solution.py:29
  215.0 15.2 %collective-permute-start.33 = (bf16[2,192,768]{2,1,0:T(8,128)(2,1)S(1)}, bf16[2,192,768]{2,1,0:T(8,128)(2,1)}, u32[]{:S(2)}, u32[]{:S(2)}) collective-permute-start(bf16[2,192,768]{2,1,0:T(8,128)(2,1)S(1)} %slice_bitcast_fusion.4), channel_id=1, source_target_pairs={{0,16},{1,17},{2,18},{3,19},{4,20},{5,21},{6,22},{7,23},{8,24},{9,... | collective-permute-start | bytes 1769480 | tf_op jit(solution)/shard_map/ppermute | solution.py:29
  231.7 14.2 %collective-permute-start.32 = (bf16[192,768]{1,0:T(8,128)(2,1)S(1)}, bf16[192,768]{1,0:T(8,128)(2,1)S(1)}, u32[]{:S(2)}, u32[]{:S(2)}) collective-permute-start(bf16[192,768]{1,0:T(8,128)(2,1)S(1)} %slice_bitcast_fusion.18), channel_id=1, source_target_pairs={{0,16},{1,17},{2,18},{3,19},{4,20},{5,21},{6,22},{7,23},{8,24},{9,... | collective-permute-start | bytes 884744 | tf_op jit(solution)/shard_map/ppermute | solution.py:29
  233.0 21.0 %collective-permute-start.34 = (bf16[192,768]{1,0:T(8,128)(2,1)}, bf16[192,768]{1,0:T(8,128)(2,1)}, u32[]{:S(2)}, u32[]{:S(2)}) collective-permute-start(bf16[192,768]{1,0:T(8,128)(2,1)} %slice_bitcast_fusion.16), channel_id=1, source_target_pairs={{0,8},{1,9},{2,10},{3,11},{4,12},{5,13},{6,14},{7,15},{8,0},{9,1},... | collective-permute-start | bytes 884744 | tf_op jit(solution)/shard_map/ppermute | solution.py:29
  250.4 20.0 %collective-permute-start.37 = (bf16[2,240,768]{2,1,0:T(8,128)(2,1)}, bf16[2,240,768]{2,1,0:T(8,128)(2,1)}, u32[]{:S(2)}, u32[]{:S(2)}) collective-permute-start(bf16[2,240,768]{2,1,0:T(8,128)(2,1)} %slice_bitcast_fusion.3), channel_id=1, source_target_pairs={{0,8},{1,9},{2,10},{3,11},{4,12},{5,13},{6,14},{7,15},{8,0},{9,1},... | collective-permute-start | bytes 2211848 | tf_op jit(solution)/shard_map/ppermute | solution.py:29
  252.5 17.9 %collective-permute-start.38 = (bf16[2,240,768]{2,1,0:T(8,128)(2,1)}, bf16[2,240,768]{2,1,0:T(8,128)(2,1)}, u32[]{:S(2)}, u32[]{:S(2)}) collective-permute-start(bf16[2,240,768]{2,1,0:T(8,128)(2,1)} %slice_bitcast_fusion.2), channel_id=1, source_target_pairs={{0,16},{1,17},{2,18},{3,19},{4,20},{5,21},{6,22},{7,23},{8,24},{9,... | collective-permute-start | bytes 2211848 | tf_op jit(solution)/shard_map/ppermute | solution.py:29
  256.6 17.7 %collective-permute-start.35 = (bf16[192,768]{1,0:T(8,128)(2,1)}, bf16[192,768]{1,0:T(8,128)(2,1)}, u32[]{:S(2)}, u32[]{:S(2)}) collective-permute-start(bf16[192,768]{1,0:T(8,128)(2,1)} %dynamic-slice_bitcast_fusion.1), channel_id=1, source_target_pairs={{0,1},{1,0},{2,3},{3,2},{4,5},{5,4},{6,7},{7,6},{8,9},{9,8},{10,11... | collective-permute-start | bytes 884744 | tf_op jit(solution)/shard_map/ppermute | solution.py:29
  282.7 44.9 %collective-permute-start.40 = (bf16[4,288,768]{2,1,0:T(8,128)(2,1)}, bf16[4,288,768]{2,1,0:T(8,128)(2,1)}, u32[]{:S(2)}, u32[]{:S(2)}) collective-permute-start(bf16[4,288,768]{2,1,0:T(8,128)(2,1)} %get-tuple-element.134), channel_id=1, source_target_pairs={{0,4},{1,5},{2,6},{3,7},{4,0},{5,1},{6,2},{7,3},{8,12},{9,13},{10,... | collective-permute-start | bytes 5308424 | tf_op jit(solution)/shard_map/ppermute | solution.py:29
  290.3 25.3 %collective-permute-start.39 = (bf16[192,768]{1,0:T(8,128)(2,1)S(1)}, bf16[192,768]{1,0:T(8,128)(2,1)}, u32[]{:S(2)}, u32[]{:S(2)}) collective-permute-start(bf16[192,768]{1,0:T(8,128)(2,1)S(1)} %fusion.10), channel_id=1, source_target_pairs={{0,2},{1,3},{2,0},{3,1},{4,6},{5,7},{6,4},{7,5},{8,10},{9,11},{10,... | collective-permute-start | bytes 884744 | tf_op jit(solution)/shard_map/ppermute | solution.py:29
  296.1 28.2 %collective-permute-start.51 = (bf16[240,768]{1,0:T(8,128)(2,1)S(1)}, bf16[240,768]{1,0:T(8,128)(2,1)S(1)}, u32[]{:S(2)}, u32[]{:S(2)}) collective-permute-start(bf16[240,768]{1,0:T(8,128)(2,1)S(1)} %fusion.6), channel_id=1, source_target_pairs={{0,2},{1,3},{2,0},{3,1},{4,6},{5,7},{6,4},{7,5},{8,10},{9,11},{10,... | collective-permute-start | bytes 1105928 | tf_op jit(solution)/shard_map/ppermute | solution.py:29
  308.6 14.9 %collective-permute-start.57 = (f32[12,768]{1,0:T(8,128)S(1)}, f32[12,768]{1,0:T(8,128)S(1)}, u32[]{:S(2)}, u32[]{:S(2)}) collective-permute-start(f32[12,768]{1,0:T(8,128)S(1)} %add.125), channel_id=1, source_target_pairs={{0,1},{1,0},{2,3},{3,2},{4,5},{5,4},{6,7},{7,6},{8,9},{9,8},{10,11... | collective-permute-start | bytes 110600 | tf_op jit(solution)/shard_map/ppermute | solution.py:29
  316.6 15.8 %collective-permute-start.53 = (bf16[192,768]{1,0:T(8,128)(2,1)S(1)}, bf16[192,768]{1,0:T(8,128)(2,1)S(1)}, u32[]{:S(2)}, u32[]{:S(2)}) collective-permute-start(bf16[192,768]{1,0:T(8,128)(2,1)S(1)} %add_convert_fusion.4), channel_id=1, source_target_pairs={{0,1},{1,0},{2,3},{3,2},{4,5},{5,4},{6,7},{7,6},{8,9},{9,8},{10,11... | collective-permute-start | bytes 884744 | tf_op jit(solution)/shard_map/ppermute | solution.py:29
  325.1 13.4 %collective-permute-start.52 = (bf16[240,768]{1,0:T(8,128)(2,1)}, bf16[240,768]{1,0:T(8,128)(2,1)}, u32[]{:S(2)}, u32[]{:S(2)}) collective-permute-start(bf16[240,768]{1,0:T(8,128)(2,1)} %add_convert_fusion.3), channel_id=1, source_target_pairs={{0,1},{1,0},{2,3},{3,2},{4,5},{5,4},{6,7},{7,6},{8,9},{9,8},{10,11... | collective-permute-start | bytes 1105928 | tf_op jit(solution)/shard_map/ppermute | solution.py:29
  (58 other events, 712.0 us)

commit v4 on v3

--- a/solution.py
+++ b/solution.py
@@ -7,7 +7,6 @@
 from jax.experimental.pallas import tpu as pltpu
 from jax.sharding import PartitionSpec as P
 
-HEADS = 12
 HEAD_DIM = 64
 
 
@@ -34,31 +33,14 @@
 
 
 def gather_group(shard, bits, wait_for):
-    plane = [1 << b for b in range(1, bits)]
-    half = shard.shape[0] // 32 * 16
-    orders = (plane, plane[::-1])
-    cut = (slice(0, half), slice(half, None))
     shard = after(shard, *wait_for)
     pieces = {0: [shard]}
-    first = []
-    for mask in plane:
-        pieces[mask] = [swap_with(shard, mask)]
-        first.append(pieces[mask][0])
-    halves = {d: [p[0][c] for c in cut] for d, p in pieces.items()}
-    for count in range(2, len(plane) + 1):
-        for d in range(2, 1 << bits, 2):
-            if bin(d).count("1") != count:
-                continue
-            got = []
-            for which, order in enumerate(orders):
-                last = [m for m in order if m & d][-1]
-                got.append(swap_with(halves[d ^ last][which], last))
-            pieces[d] = got
-            halves[d] = got
-            last_got = got
+    for d in range(2, 1 << bits, 2):
+        pieces[d] = [swap_with(shard, d)]
+    far = [pieces[d][0] for d in range(2, 1 << bits, 2)]
     for d in list(pieces):
         pieces[d | 1] = [swap_with(p, 1) for p in pieces[d]]
-    return pieces, first, last_got
+    return pieces, far
 
 
 def place(pieces, me, group_size):
@@ -126,14 +108,17 @@
     return last
 
 
-def sum_everywhere(array, bits):
-    for b in range(bits):
-        array = array + swap_with(array, 1 << b)
+def everywhere(array, bits):
+    masks = [(1 << b, 0) for b in range(bits)]
     mask = 1
     while mask < lax.axis_size("replica"):
-        array = array + swap_with(array, 0, mask)
+        masks.append((0, mask))
         mask *= 2
-    return array
+    for group_mask, replica_mask in masks:
+        received = swap_with(array, group_mask, replica_mask)
+        yield [received]
+        array = array + received
+    yield array
 
 
 class Gathered:
@@ -233,12 +218,12 @@
     return jnp.where(keep, pair, jnp.zeros_like(pair))
 
 
-def attend_kernel(plan, seq, aliased, lens, me, x, bq, bv, *refs):
-    pieces = len(plan.arrays)
-    q_out, k_out, v_out, mixed_out, probs_out, wq, wk, wv, sems = refs[pieces + aliased :]
-    group = pl.program_id(0)
-    fetch(plan, me[0], refs, (wq, wk, wv), sems, group == 0)
-    arrive(plan, me[0], refs, (wq, wk, wv), sems, group == 0)
+def attend_kernel(plan, lens, me, x, bq, bv, *refs):
+    q_out, k_out, v_out, mixed_out, probs_out, wq, wk, wv, sems = refs[len(plan.arrays) :]
+    seq, group = pl.program_id(0), pl.program_id(1)
+    start = jnp.logical_and(seq == 0, group == 0)
+    fetch(plan, me[0], refs, (wq, wk, wv), sems, start)
+    arrive(plan, me[0], refs, (wq, wk, wv), sems, start)
     cols = pl.ds(pl.multiple_of(group * GROUP_COLS, GROUP_COLS), GROUP_COLS)
     slots = x.shape[0]
     rows = x[...]
@@ -269,37 +254,33 @@
     mixed_out[...] = joined.T.astype(jnp.bfloat16)
 
 
-def attend(lengths, seq, rows, plan, bq, bv, before=()):
+def attend(lengths, rows, plan, bq, bv):
     seqs = lengths.shape[0]
     total, width = rows.shape
     slots = total // seqs
     groups = width // GROUP_COLS
-    bias = pl.BlockSpec((1, GROUP_COLS), lambda j, *_: (0, j))
-    part = pl.BlockSpec((slots, GROUP_COLS), lambda j, *_: (seq, j))
+    bias = pl.BlockSpec((1, GROUP_COLS), lambda s, j, *_: (0, j))
+    part = pl.BlockSpec((slots, GROUP_COLS), lambda s, j, *_: (s, j))
     table = jax.ShapeDtypeStruct((total, width), jnp.bfloat16)
-    anywhere = pl.BlockSpec(memory_space=pl.ANY)
-    first_alias = 5 + len(plan.arrays)
-    return pl.pallas_call(
-        functools.partial(attend_kernel, plan, seq, len(before)),
+    return pl.pallas_call(
+        functools.partial(attend_kernel, plan),
         out_shape=[table] * 4
         + [jax.ShapeDtypeStruct((seqs * groups * GROUP_HEADS, slots, slots), jnp.bfloat16)],
         grid_spec=pltpu.PrefetchScalarGridSpec(
             num_scalar_prefetch=2,
-            grid=(groups,),
-            in_specs=[pl.BlockSpec((slots, width), lambda j, *_: (seq, 0))]
+            grid=(seqs, groups),
+            in_specs=[pl.BlockSpec((slots, width), lambda s, j, *_: (s, 0))]
             + [bias] * 2
-            + plan.specs()
-            + [anywhere] * len(before),
+            + plan.specs(),
             out_specs=[part] * 4
-            + [pl.BlockSpec((GROUP_HEADS, slots, slots), lambda j, *_: (seq * groups + j, 0, 0))],
+            + [pl.BlockSpec((GROUP_HEADS, slots, slots), lambda s, j, *_: (s * groups + j, 0, 0))],
             scratch_shapes=[pltpu.VMEM((width, width), jnp.bfloat16)] * 3
             + [pltpu.SemaphoreType.DMA((len(plan.copies),))],
         ),
-        input_output_aliases={first_alias + n: n for n in range(len(before))},
         compiler_params=kernel_params(),
-        cost_estimate=cost((6 * total * width * width + 8 * total * slots * width) / seqs, 1.5e7),
-        name=f"attend{seq}",
-    )(lengths, plan.me, rows, bq, bv, *plan.arrays, *before)
+        cost_estimate=cost((6 * total * width * width + 8 * total * slots * width), 3e7),
+        name="attend",
+    )(lengths, plan.me, rows, bq, bv, *plan.arrays)
 
 
 def attend_back_kernel(q, k, v, grad, probs, *refs):
@@ -356,7 +337,6 @@
         input_output_aliases={5: 0} if before else {},
         compiler_params=kernel_params(),
         cost_estimate=cost(14 * total * slots * width / seqs, 1.5e7),
-        name=f"attend_back{seq}",
     )(q, k, v, grad, probs, *before)
 
 
@@ -413,7 +393,7 @@
 def feed(parts, part, mixed, x, plan, bo, g1, s1, bi, before=()):
     total, width = x.shape
     wide = bi.shape[1]
-    rows, steps, spec = row_blocks(total, parts, part)
+    _, steps, spec = row_blocks(total, parts, part)
     bf, f32 = jnp.bfloat16, jnp.float32
     aliases = {7 + len(plan.arrays) + n: n for n in range(len(before))}
     return pl.pallas_call(
@@ -436,7 +416,6 @@
         input_output_aliases=aliases,
         compiler_params=kernel_params(),
         cost_estimate=cost(2 * total * width * (width + wide) / parts * 3, 1.5e7),
-        name=f"feed{part}",
     )(plan.me, mixed, x, bo, g1, s1, bi, *plan.arrays, *before)
 
 
@@ -535,7 +514,7 @@
 def return_grad(parts, part, hidden_grad, h2_grad, normed1, inverse1, plan, g1, before=()):
     total, width = normed1.shape
     wide = hidden_grad.shape[1]
-    rows, steps, spec = row_blocks(total, parts, part)
+    _, steps, spec = row_blocks(total, parts, part)
     bf, f32 = jnp.bfloat16, jnp.float32
     aliases = {6 + len(plan.arrays) + n: n for n in range(len(before))}
     return pl.pallas_call(
@@ -557,7 +536,6 @@
         input_output_aliases=aliases,
         compiler_params=kernel_params(),
         cost_estimate=cost(2 * total * width * (width + wide) / parts, 1.5e7),
-        name=f"return_grad{part}",
     )(plan.me, hidden_grad, h2_grad, normed1, inverse1, g1, *plan.arrays, *before)
 
 
@@ -807,34 +785,28 @@
     x = inputs.reshape(total, width)
     cot = cotangent.reshape(total, width)
 
+    in_blocks = [in_weight[:, n * width : (n + 1) * width] for n in range(blocks)]
+    got_a, far_a = gather_group(jnp.concatenate([query_weight, key_weight, value_weight]), bits, ())
     table = pack(
         [query_bias, value_bias, out_bias, back_bias, first_gain, first_shift, second_gain, second_shift, in_bias]
     )[None]
-    in_blocks = [in_weight[:, n * width : (n + 1) * width] for n in range(blocks)]
-    got_a = gather_group(jnp.concatenate([query_weight, key_weight, value_weight]), bits, ())
     for b in range(bits - 1, -1, -1):
-        table = jnp.stack([table, swap_with(table, 1 << b)], axis=1).reshape((-1,) + table.shape[1:])
-    got_b = gather_group(jnp.concatenate([out_weight] + in_blocks), bits, got_a[2])
-    got_c = gather_group(back_weight_shard, bits, got_b[2])
+        other = swap_with(table, 1 << b)
+        table = jnp.stack([table, other], axis=1).reshape((-1,) + table.shape[1:])
+    got_b, far_b = gather_group(jnp.concatenate([out_weight] + in_blocks), bits, far_a + [table])
     vectors, bi = spread(me, table, width, wide)
     bq, bv, bo, bb, g1, s1, g2, s2 = (vectors[i : i + 1] for i in range(8))
     third = [(n, n * chunk, chunk, 0) for n in range(3)]
-    plan_a = Gathered(got_a[0], me, count, chunk, third)
+    plan_a = Gathered(got_a, me, count, chunk, third)
     plan_b = Gathered(
-        got_b[0], me, count, chunk,
+        got_b, me, count, chunk,
         [(0, 0, chunk, 0)] + [(1, (n + 1) * chunk, chunk, n * width) for n in range(blocks)],
     )
+    q, k, v, mixed, probs = attend(lengths, x, plan_a, bq, bv)
     back_chunk = back_weight_shard.shape[0]
-    plan_c = Gathered(got_c[0], me, count, back_chunk, [(0, 0, back_chunk, 0)])
-
-    made = ()
-    for seq in range(seqs):
-        ready = got_b[1] if seq == seqs - 1 else ()
-        made = attend(lengths, seq, after(x, *ready) if seq else x, plan_a, bq, bv, made)
-    q, k, v, mixed, probs = made
-    fed = feed(2, 0, mixed, x, plan_b, bo, g1, s1, bi)
-    fed = feed(2, 1, mixed, after(x, *got_c[1]), plan_b, bo, g1, s1, bi, fed)
-    after_low, normed1, inverse1, active, slope = fed
+    got_c, _ = gather_group(back_weight_shard, bits, far_b + [mixed])
+    plan_c = Gathered(got_c, me, count, back_chunk, [(0, 0, back_chunk, 0)])
+    after_low, normed1, inverse1, active, slope = feed(1, 0, mixed, x, plan_b, bo, g1, s1, bi)
     layer_out, ffn_grad, hidden_grad, h2_grad, sums2, in_bias_sum = turn(
         lengths, slots, active, normed1, slope, cot, plan_c, bb, g1, s1, g2, s2
     )
@@ -842,40 +814,41 @@
     hidden_grad, send = lax.optimization_barrier((hidden_grad, send))
     red_c = reduction(own, send, bits)
     came = next(red_c)
-    back = return_grad(2, 0, hidden_grad, h2_grad, normed1, inverse1, plan_b, g1)
-    h2_grad = after(h2_grad, *came, back[3])
+    h1_grad, branch_grad, mixed_grad, sums1 = return_grad(
+        1, 0, hidden_grad, h2_grad, normed1, inverse1, plan_b, g1
+    )
+    branch_grad = after(branch_grad, *came)
     came = next(red_c)
-    h1_grad, branch_grad, mixed_grad, more = return_grad(
-        2, 1, hidden_grad, h2_grad, normed1, inverse1, plan_b, g1, back[:3]
-    )
-    sums1 = back[3] + more
     own, send = in_out_weight(me, after_low, hidden_grad, mixed, branch_grad, count)
     red_b = reduction(own, send, bits)
-    came_b = next(red_b)
     mixed_grad = after(mixed_grad, send, *came)
-    came = next(red_c)
-    first = attend_back(seqs, 0, q, k, v, mixed_grad, probs)
-    grads, sums_at = first
+    came, came_b = next(red_c), next(red_b)
+    grads, sums_at = attend_back(seqs, 0, q, k, v, mixed_grad, probs)
     attend_sums = sums_at[0]
     for seq in range(1, seqs):
         mixed_grad = after(mixed_grad, attend_sums, *came, *came_b)
         came, came_b = next(red_c), next(red_b)
         grads, sums_at = attend_back(seqs, seq, q, k, v, mixed_grad, probs, (grads,))
         attend_sums = attend_sums + sums_at[0]
-    own, send = qkv_weight(me, after(x, *came, *came_b), grads, count)
-    came, came_b = next(red_c), next(red_b)
-    red_a = reduction(own, send, bits)
-    came_a = next(red_a)
-    input_grad = input_grad_of(after(h1_grad, own, *came, *came_a), grads, plan_a)
-    sum_c, sum_b, sum_a = finish(red_c), finish(red_b), finish(red_a)
-
     small = jnp.concatenate(
         [
             attend_sums, sums1[2:3], sums2[2:3], sums1[0:2], sums2[0:2],
             in_bias_sum.reshape(blocks, width),
         ]
     )
-    small = sum_everywhere(small, bits)
+    small_steps = everywhere(small, bits)
+    rows_in = after(x, *came, *came_b)
+    came, came_b = next(red_c), next(red_b)
+    came_s = next(small_steps)
+    own, send = qkv_weight(me, rows_in, grads, count)
+    red_a = reduction(own, send, bits)
+    came_a = next(red_a)
+    h1_in = after(h1_grad, own, *came, *came_b, *came_s)
+    came, came_b = next(red_c), next(red_b)
+    came_s = next(small_steps)
+    input_grad = input_grad_of(h1_in, grads, plan_a)
+    sum_c, sum_b, sum_a = finish(red_c), finish(red_b), finish(red_a)
+    small = finish(small_steps)
     vector_grads = collect(me, small[0:8], small[8:].reshape(1, wide), count)
     grad_q, grad_v, grad_o, grad_b, grad_g1, grad_s1, grad_g2, grad_s2, grad_i = vector_grads
     up = lambda a: a.astype(jnp.float32)

time: 382 us -> 364 us (0.953)
  waiting for transfers between devices: 96.3 us -> 116 us
  Pallas kernels: 172 us -> 154 us
  starting transfers between devices: 54.2 us -> 41.7 us
    ppermute x59 -> x53, waiting for transfers between devices: 96.3 us -> 116 us  [swap_with(): return lax.ppermute(array, AXES, pairs)]
    ppermute x59 -> x53, starting transfers between devices: 54.2 us -> 41.7 us  [swap_with(): return lax.ppermute(array, AXES, pairs)]
    slice x6 -> x0, local copies, waits for them, and re-layouts: 6.93 us -> none  [gather_group(): halves = {d: [p[0][c] for c in cut] for d, p in pieces.items()}]
    pallas_call x2 -> x1, Pallas kernels: 23.4 us -> 16.8 us  [return_grad(): pl.pallas_call(functools.partial(return_kernel, plan, len(before)), out_s...]
    pallas_call x2 -> x1, Pallas kernels: 25.3 us -> 19.4 us  [feed(): pl.pallas_call(functools.partial(feed_kernel, plan, len(before)), out_sha...]
    pallas_call x2 -> x1, Pallas kernels: 28.2 us -> 22.6 us  [attend(): pl.pallas_call(functools.partial(attend_kernel, plan), out_shape=[table]...]
    unnamed x70 -> x54, local copies, waits for them, and re-layouts: 8.18 us -> 8.66 us
  transfers between devices with their start and end apart: 59 -> 53, of which waited for: 25 -> 20; matrix products, arithmetic and copies ran while one was open for 12% -> 11% of each run, Pallas kernels for 30% -> 29%
where the time goes in v4:
time: 364 us; the launch traced here: 362 us
  Pallas kernels  154 us (42%)
  waiting for transfers between devices  116 us (32%)
  starting transfers between devices  41.7 us (11%)
  other arithmetic  25.4 us (7%)
  local copies, waits for them, and re-layouts  24 us (7%)
    ppermute x53, waiting for transfers between devices, swap_with(): return lax.ppermute(array, AXES, pairs)  116 us
    ppermute x53, starting transfers between devices, swap_with(): return lax.ppermute(array, AXES, pairs)  41.7 us
    pallas_call x2, Pallas kernels, attend_back(): pl.pallas_call(attend_back_kernel, out_shape=[jax.ShapeDtypeStruct((3, to...  24.1 us
    pallas_call x1, Pallas kernels, turn(): pl.pallas_call(functools.partial(turn_kernel, plan, slots), out_shape=[sh...  24.1 us
    pallas_call x1, Pallas kernels, attend(): pl.pallas_call(functools.partial(attend_kernel, plan), out_shape=[table]...  22.6 us
    pallas_call x1, Pallas kernels, feed(): pl.pallas_call(functools.partial(feed_kernel, plan, len(before)), out_sha...  19.4 us
    convert_element_type x18, other arithmetic, add_low(): (left.astype(jnp.float32) + right.astype(jnp.float32)).astype(jnp.bfloat16)  17.6 us
    pallas_call x1, Pallas kernels, return_grad(): pl.pallas_call(functools.partial(return_kernel, plan, len(before)), out_s...  16.8 us
  transfers between devices with their start and end apart: 53, of which 20 were waited for; matrix products, arithmetic and copies ran while one was open for 11% of the time, Pallas kernels for 29%

profile of v4, /device:TPU:0, one launch (start us, length us, event | category | flops | bytes accessed | tf_op | source)
XLA Modules:
  0.0 362.4 jit_solution(15062464332514947529)
XLA Ops:
  3.5 3.0 collective-permute-start.3
  10.7 2.0 collective-permute-start
  14.6 13.2 %collective-permute-done = f32[1,16,128]{2,1,0:T(8,128)S(1)} collective-permute-done((f32[1,16,128]{2,1,0:T(8,128)}, f32[1,16,128]{2,1,0:T(8,128)S(1)}, u32[]{:S(2)}, u32[]{:S(2)}) %collective-permute-start) | collective-permute-done | bytes 8224 | tf_op jit(solution)/shard_map/ppermute | solution.py:28
  28.7 3.6 collective-permute-done.1
  35.7 2.0 collective-permute-start.11
  41.0 22.6 %attend.1 = (bf16[1024,768]{1,0:T(8,128)(2,1)}, bf16[1024,768]{1,0:T(8,128)(2,1)}, bf16[1024,768]{1,0:T(8,128)(2,1)}, bf16[1024,768]{1,0:T(8,128)(2,1)}, bf16[24,512,512]{2,1,0:T(8,128)(2,1)}) custom-call(s32[2]{0:T(128)} %lens.3, s32[1]{0:T(128)} %bitcast.me, bf16[1024,768]{1,0:T(8,128)(2,1)} %bitcast.191, f32[1,768]{1,0:T(1,128)} %get-tuple-element.138.bq, ...), custom_call_target="tpu_custom_call" | custom-call | flops 6845104128 | bytes 30000000 | tf_op jit(solution)/shard_map/attend/pallas_call | solution.py:265
  63.7 5.8 %collective-permute-done.11.refs_2_ = bf16[480,768]{1,0:T(8,128)(2,1)S(1)} collective-permute-done((bf16[480,768]{1,0:T(8,128)(2,1)S(1)}, bf16[480,768]{1,0:T(8,128)(2,1)S(1)}, u32[]{:S(2)}, u32[]{:S(2)}) %collective-permute-start.11) | collective-permute-done | bytes 737312 | tf_op jit(solution)/shard_map/ppermute | solution.py:28
  73.9 12.1 %collective-permute-done.17.refs_1_ = bf16[384,768]{1,0:T(8,128)(2,1)} collective-permute-done((bf16[384,768]{1,0:T(8,128)(2,1)}, bf16[384,768]{1,0:T(8,128)(2,1)}, u32[]{:S(2)}, u32[]{:S(2)}) %collective-permute-start.17) | collective-permute-done | bytes 589856 | tf_op jit(solution)/shard_map/ppermute | solution.py:28
  87.4 13.6 %collective-permute-done.18.refs_2_ = bf16[384,768]{1,0:T(8,128)(2,1)S(1)} collective-permute-done((bf16[384,768]{1,0:T(8,128)(2,1)}, bf16[384,768]{1,0:T(8,128)(2,1)S(1)}, u32[]{:S(2)}, u32[]{:S(2)}) %collective-permute-start.18) | collective-permute-done | bytes 589856 | tf_op jit(solution)/shard_map/ppermute | solution.py:28
  102.9 19.4 %shard_map.305 = (bf16[1024,768]{1,0:T(8,128)(2,1)}, f32[1024,768]{1,0:T(8,128)}, f32[1024,128]{1,0:T(8,128)}, bf16[1024,3072]{1,0:T(8,128)(2,1)}, bf16[1024,3072]{1,0:T(8,128)(2,1)}) custom-call(s32[1]{0:T(128)} %bitcast.me, bf16[1024,768]{1,0:T(8,128)(2,1)} %get-tuple-element.68.mixed, bf16[1024,768]{1,0:T(8,128)(2,1)} %bitcast.192, ...), custom_call_target="tpu_custom_call" | custom-call | flops 18119393280 | bytes 15000000 | tf_op jit(solution)/shard_map/pallas_call | solution.py:399
  122.3 24.1 %turn.1 = (bf16[1024,768]{1,0:T(8,128)(2,1)}, bf16[1024,768]{1,0:T(8,128)(2,1)}, bf16[1024,3072]{1,0:T(8,128)(2,1)}, f32[1024,768]{1,0:T(8,128)}, f32[8,768]{1,0:T(8,128)}, /*index=5*/f32[1,3072]{1,0:T(1,128)}) custom-call(s32[2]{0:T(128)} %lens.3, s32[1]{0:T(128)} %bitcast.me, bf16[1024,3072]{1,0:T(8,128)(2,1)} %get-tuple-element.71.active, ...), custom_call_target="tpu_custom_call" | custom-call | flops 9663676416 | bytes 30000000 | tf_op jit(solution)/shard_map/turn/pallas_call | solution.py:470
  146.4 11.3 %back_weight.1 = (bf16[4,384,768]{2,1,0:T(8,128)(2,1)}, bf16[4,384,768]{2,1,0:T(8,128)(2,1)}) custom-call(s32[1]{0:T(128)} %bitcast.me, bf16[1024,3072]{1,0:T(8,128)(2,1)} %get-tuple-element.71.active, bf16[1024,768]{1,0:T(8,128)(2,1)} %get-tuple-element.77.grad), custom_call_target="tpu_custom_call" | custom-call | flops 4831838208 | bytes 13000000 | tf_op jit(solution)/shard_map/back_weight/pallas_call | solution.py:622
  157.9 16.8 %shard_map.306 = (f32[1024,768]{1,0:T(8,128)}, bf16[1024,768]{1,0:T(8,128)(2,1)}, bf16[1024,768]{1,0:T(8,128)(2,1)}, f32[8,768]{1,0:T(8,128)}) custom-call(s32[1]{0:T(128)} %bitcast.me, bf16[1024,3072]{1,0:T(8,128)(2,1)} %get-tuple-element.79.hidden_grad, f32[1024,768]{1,0:T(8,128)} %get-tuple-element.80.h2_grad, f32[1024,768]{1,0:T(8,128)} %get-tuple-element.72.normed1, ...), custom_call_target="tpu_custom_call" | custom-call | flops 6039797760 | bytes 15000000 | tf_op jit(solution)/shard_map/pallas_call | solution.py:520
  174.8 13.4 %in_out_weight.1 = (bf16[4,480,768]{2,1,0:T(8,128)(2,1)}, bf16[4,480,768]{2,1,0:T(8,128)(2,1)}) custom-call(s32[1]{0:T(128)} %bitcast.me, bf16[1024,768]{1,0:T(8,128)(2,1)} %get-tuple-element.85.after, bf16[1024,3072]{1,0:T(8,128)(2,1)} %get-tuple-element.79.hidden_grad, bf16[1024,768]{1,0:T(8,128)(2,1)} %get-tuple-element.68.mixed, ...), custom_call_target="tpu_custom_call" | custom-call | flops 6039797760 | bytes 20000000 | tf_op jit(solution)/shard_map/in_out_weight/pallas_call | solution.py:664
  188.4 2.9 add_convert_fusion.1
  193.6 13.4 %collective-permute-done.25 = bf16[2,192,768]{2,1,0:T(8,128)(2,1)S(1)} collective-permute-done((bf16[2,192,768]{2,1,0:T(8,128)(2,1)S(1)}, bf16[2,192,768]{2,1,0:T(8,128)(2,1)S(1)}, u32[]{:S(2)}, u32[]{:S(2)}) %collective-permute-start.25) | collective-permute-done | bytes 589856 | tf_op jit(solution)/shard_map/ppermute | solution.py:28
  226.4 2.6 add_convert_fusion
  232.7 12.1 %shard_map.307 = (bf16[3,1024,768]{2,1,0:T(8,128)(2,1)}, f32[1,2,768]{2,1,0:T(2,128)}) custom-call(bf16[1024,768]{1,0:T(8,128)(2,1)} %get-tuple-element.91.q, bf16[1024,768]{1,0:T(8,128)(2,1)} %get-tuple-element.92.k, bf16[1024,768]{1,0:T(8,128)(2,1)} %get-tuple-element.93.v, bf16[1024,768]{1,0:T(8,128)(2,1)} %get-tuple-element.98.grad, ...), custom_call_target="tpu_custom_call" | custom-call | flops 2818572288 | bytes 15000000 | tf_op jit(solution)/shard_map/pallas_call | solution.py:322
  246.5 2.6 collective-permute-start.33
  249.1 12.1 %shard_map.308 = (bf16[3,1024,768]{2,1,0:T(8,128)(2,1)}, f32[1,2,768]{2,1,0:T(2,128)}) custom-call(bf16[1024,768]{1,0:T(8,128)(2,1)} %get-tuple-element.91.q, bf16[1024,768]{1,0:T(8,128)(2,1)} %get-tuple-element.92.k, bf16[1024,768]{1,0:T(8,128)(2,1)} %get-tuple-element.93.v, ...), custom_call_target="tpu_custom_call", output_to_operand_aliasing={{0}: (5, {})} | custom-call | flops 2818572288 | bytes 15000000 | tf_op jit(solution)/shard_map/pallas_call | solution.py:322
  264.6 8.1 %qkv_weight.1 = (bf16[4,288,768]{2,1,0:T(8,128)(2,1)}, bf16[4,288,768]{2,1,0:T(8,128)(2,1)}) custom-call(s32[1]{0:T(128)} %bitcast.me, bf16[1024,768]{1,0:T(8,128)(2,1)} %bitcast.193, bf16[3,1024,768]{2,1,0:T(8,128)(2,1)} %get-tuple-element.100.grads), custom_call_target="tpu_custom_call" | custom-call | flops 3623878656 | bytes 10000000 | tf_op jit(solution)/shard_map/qkv_weight/pallas_call | solution.py:691
  276.0 7.7 %collective-permute-done.35 = bf16[240,768]{1,0:T(8,128)(2,1)S(1)} collective-permute-done((bf16[240,768]{1,0:T(8,128)(2,1)S(1)}, bf16[240,768]{1,0:T(8,128)(2,1)S(1)}, u32[]{:S(2)}, u32[]{:S(2)}) %collective-permute-start.35) | collective-permute-done | bytes 368672 | tf_op jit(solution)/shard_map/ppermute | solution.py:28
  287.5 2.6 collective-permute-done.49
  291.4 2.8 collective-permute-done.50
  295.8 2.6 collective-permute-done.51
  299.9 3.6 collective-permute-done.52
  304.6 1.9 add_convert_fusion.2
  312.0 8.3 %collective-permute-done.46 = bf16[240,768]{1,0:T(8,128)(2,1)} collective-permute-done((bf16[240,768]{1,0:T(8,128)(2,1)S(1)}, bf16[240,768]{1,0:T(8,128)(2,1)}, u32[]{:S(2)}, u32[]{:S(2)}) %collective-permute-start.46) | collective-permute-done | bytes 368672 | tf_op jit(solution)/shard_map/ppermute | solution.py:28
  325.0 5.0 %collective-permute-done.39 = bf16[144,768]{1,0:T(8,128)(2,1)S(1)} collective-permute-done((bf16[144,768]{1,0:T(8,128)(2,1)S(1)}, bf16[144,768]{1,0:T(8,128)(2,1)S(1)}, u32[]{:S(2)}, u32[]{:S(2)}) %collective-permute-start.39) | collective-permute-done | bytes 221216 | tf_op jit(solution)/shard_map/ppermute | solution.py:28
  333.0 9.7 %input_grad.1 = bf16[1024,768]{1,0:T(8,128)(2,1)} custom-call(s32[1]{0:T(128)} %bitcast.me, f32[1024,768]{1,0:T(8,128)} %get-tuple-element.106.h1_grad, bf16[3,1024,768]{2,1,0:T(8,128)(2,1)} %get-tuple-element.100.grads, bf16[288,768]{1,0:T(8,128)(2,1)} %copy-done.8, bf16[288,768]{1,0:T(8,128)(2,1)} %copy-done.22, ...), custom_call_target="tpu_custom_call" | custom-call | flops 3623878656 | bytes 20000000 | tf_op jit(solution)/shard_map/input_grad/pallas_call | solution.py:554
  343.9 10.2 %collective-permute-done.43 = bf16[144,768]{1,0:T(8,128)(2,1)S(1)} collective-permute-done((bf16[144,768]{1,0:T(8,128)(2,1)S(1)}, bf16[144,768]{1,0:T(8,128)(2,1)S(1)}, u32[]{:S(2)}, u32[]{:S(2)}) %collective-permute-start.43) | collective-permute-done | bytes 221216 | tf_op jit(solution)/shard_map/ppermute | solution.py:28
  355.3 6.0 %collective-permute-done.44 = bf16[144,768]{1,0:T(8,128)(2,1)S(1)} collective-permute-done((bf16[144,768]{1,0:T(8,128)(2,1)S(1)}, bf16[144,768]{1,0:T(8,128)(2,1)S(1)}, u32[]{:S(2)}, u32[]{:S(2)}) %collective-permute-start.44) | collective-permute-done | bytes 221216 | tf_op jit(solution)/shard_map/ppermute | solution.py:28
  (208 shorter events, 83.9 us)
Async XLA Ops:
  3.5 25.1 %collective-permute-start.3 = (bf16[288,768]{1,0:T(8,128)(2,1)S(1)}, bf16[288,768]{1,0:T(8,128)(2,1)S(1)}, u32[]{:S(2)}, u32[]{:S(2)}) collective-permute-start(bf16[288,768]{1,0:T(8,128)(2,1)S(1)} %constant_dynamic-update-slice_fusion.refs_0_), channel_id=1, source_target_pairs={{0,8},{1,9},{2,10},{3,11},{4,12},{5,13},{6,14},{7,15},{8,0},{9,1},... | collective-permute-start | bytes 1327112 | tf_op jit(solution)/shard_map/ppermute | solution.py:28
  6.5 25.8 %collective-permute-start.4 = (bf16[288,768]{1,0:T(8,128)(2,1)S(1)}, bf16[288,768]{1,0:T(8,128)(2,1)}, u32[]{:S(2)}, u32[]{:S(2)}) collective-permute-start(bf16[288,768]{1,0:T(8,128)(2,1)S(1)} %constant_dynamic-update-slice_fusion.refs_0_), channel_id=1, source_target_pairs={{0,16},{1,17},{2,18},{3,19},{4,20},{5,21},{6,22},{7,23},{8,24},{9,... | collective-permute-start | bytes 1327112 | tf_op jit(solution)/shard_map/ppermute | solution.py:28
  8.1 24.8 %collective-permute-start.5 = (bf16[288,768]{1,0:T(8,128)(2,1)S(1)}, bf16[288,768]{1,0:T(8,128)(2,1)}, u32[]{:S(2)}, u32[]{:S(2)}) collective-permute-start(bf16[288,768]{1,0:T(8,128)(2,1)S(1)} %constant_dynamic-update-slice_fusion.refs_0_), channel_id=1, source_target_pairs={{0,24},{1,25},{2,26},{3,27},{4,28},{5,29},{6,30},{7,31},{8,16},{9,... | collective-permute-start | bytes 1327112 | tf_op jit(solution)/shard_map/ppermute | solution.py:28
  8.1 27.6 %collective-permute-start.6 = (bf16[288,768]{1,0:T(8,128)(2,1)S(1)}, bf16[288,768]{1,0:T(8,128)(2,1)}, u32[]{:S(2)}, u32[]{:S(2)}) collective-permute-start(bf16[288,768]{1,0:T(8,128)(2,1)S(1)} %constant_dynamic-update-slice_fusion.refs_0_), channel_id=1, source_target_pairs={{0,4},{1,5},{2,6},{3,7},{4,0},{5,1},{6,2},{7,3},{8,12},{9,13},{10,... | collective-permute-start | bytes 1327112 | tf_op jit(solution)/shard_map/ppermute | solution.py:28
  10.7 17.1 %collective-permute-start = (f32[1,16,128]{2,1,0:T(8,128)}, f32[1,16,128]{2,1,0:T(8,128)S(1)}, u32[]{:S(2)}, u32[]{:S(2)}) collective-permute-start(f32[1,16,128]{2,1,0:T(8,128)} %bitcast.177), channel_id=1, source_target_pairs={{0,16},{1,17},{2,18},{3,19},{4,20},{5,21},{6,22},{7,23},{8,24},{9,... | collective-permute-start | bytes 24584 | tf_op jit(solution)/shard_map/ppermute | solution.py:28
  35.7 27.9 %collective-permute-start.10 = (bf16[480,768]{1,0:T(8,128)(2,1)S(1)}, bf16[480,768]{1,0:T(8,128)(2,1)S(1)}, u32[]{:S(2)}, u32[]{:S(2)}) collective-permute-start(bf16[480,768]{1,0:T(8,128)(2,1)S(1)} %slice_dynamic-update-slice_fusion.refs_0_), channel_id=1, source_target_pairs={{0,8},{1,9},{2,10},{3,11},{4,12},{5,13},{6,14},{7,15},{8,0},{9,1},... | collective-permute-start | bytes 2211848 | tf_op jit(solution)/shard_map/ppermute | solution.py:28
  35.7 33.7 %collective-permute-start.11 = (bf16[480,768]{1,0:T(8,128)(2,1)S(1)}, bf16[480,768]{1,0:T(8,128)(2,1)S(1)}, u32[]{:S(2)}, u32[]{:S(2)}) collective-permute-start(bf16[480,768]{1,0:T(8,128)(2,1)S(1)} %slice_dynamic-update-slice_fusion.refs_0_), channel_id=1, source_target_pairs={{0,16},{1,17},{2,18},{3,19},{4,20},{5,21},{6,22},{7,23},{8,24},{9,... | collective-permute-start | bytes 2211848 | tf_op jit(solution)/shard_map/ppermute | solution.py:28
  37.8 33.4 %collective-permute-start.12 = (bf16[480,768]{1,0:T(8,128)(2,1)S(1)}, bf16[480,768]{1,0:T(8,128)(2,1)}, u32[]{:S(2)}, u32[]{:S(2)}) collective-permute-start(bf16[480,768]{1,0:T(8,128)(2,1)S(1)} %slice_dynamic-update-slice_fusion.refs_0_), channel_id=1, source_target_pairs={{0,24},{1,25},{2,26},{3,27},{4,28},{5,29},{6,30},{7,31},{8,16},{9,... | collective-permute-start | bytes 2211848 | tf_op jit(solution)/shard_map/ppermute | solution.py:28
  40.9 31.5 %collective-permute-start.13 = (bf16[480,768]{1,0:T(8,128)(2,1)S(1)}, bf16[480,768]{1,0:T(8,128)(2,1)}, u32[]{:S(2)}, u32[]{:S(2)}) collective-permute-start(bf16[480,768]{1,0:T(8,128)(2,1)S(1)} %slice_dynamic-update-slice_fusion.refs_0_), channel_id=1, source_target_pairs={{0,4},{1,5},{2,6},{3,7},{4,0},{5,1},{6,2},{7,3},{8,12},{9,13},{10,... | collective-permute-start | bytes 2211848 | tf_op jit(solution)/shard_map/ppermute | solution.py:28
  71.8 29.6 %collective-permute-start.14 = (bf16[480,768]{1,0:T(8,128)(2,1)S(1)}, bf16[480,768]{1,0:T(8,128)(2,1)S(1)}, u32[]{:S(2)}, u32[]{:S(2)}) collective-permute-start(bf16[480,768]{1,0:T(8,128)(2,1)S(1)} %collective-permute-done.10.refs_1_), channel_id=1, source_target_pairs={{0,4},{1,5},{2,6},{3,7},{4,0},{5,1},{6,2},{7,3},{8,12},{9,13},{10,... | collective-permute-start | bytes 2211848 | tf_op jit(solution)/shard_map/ppermute | solution.py:28
  71.8 29.7 %collective-permute-start.15 = (bf16[480,768]{1,0:T(8,128)(2,1)S(1)}, bf16[480,768]{1,0:T(8,128)(2,1)S(1)}, u32[]{:S(2)}, u32[]{:S(2)}) collective-permute-start(bf16[480,768]{1,0:T(8,128)(2,1)S(1)} %collective-permute-done.11.refs_2_), channel_id=1, source_target_pairs={{0,4},{1,5},{2,6},{3,7},{4,0},{5,1},{6,2},{7,3},{8,12},{9,13},{10,... | collective-permute-start | bytes 2211848 | tf_op jit(solution)/shard_map/ppermute | solution.py:28
  72.4 30.5 %collective-permute-start.16 = (bf16[480,768]{1,0:T(8,128)(2,1)}, bf16[480,768]{1,0:T(8,128)(2,1)}, u32[]{:S(2)}, u32[]{:S(2)}) collective-permute-start(bf16[480,768]{1,0:T(8,128)(2,1)} %collective-permute-done.12.refs_3_), channel_id=1, source_target_pairs={{0,4},{1,5},{2,6},{3,7},{4,0},{5,1},{6,2},{7,3},{8,12},{9,13},{10,... | collective-permute-start | bytes 2211848 | tf_op jit(solution)/shard_map/ppermute | solution.py:28
  72.4 28.6 %collective-permute-start.18 = (bf16[384,768]{1,0:T(8,128)(2,1)}, bf16[384,768]{1,0:T(8,128)(2,1)S(1)}, u32[]{:S(2)}, u32[]{:S(2)}) collective-permute-start(bf16[384,768]{1,0:T(8,128)(2,1)} %refs_0_), channel_id=1, source_target_pairs={{0,16},{1,17},{2,18},{3,19},{4,20},{5,21},{6,22},{7,23},{8,24},{9,... | collective-permute-start | bytes 1769480 | tf_op jit(solution)/shard_map/ppermute | solution.py:28
  86.0 15.0 %collective-permute-start.19 = (bf16[384,768]{1,0:T(8,128)(2,1)}, bf16[384,768]{1,0:T(8,128)(2,1)S(1)}, u32[]{:S(2)}, u32[]{:S(2)}) collective-permute-start(bf16[384,768]{1,0:T(8,128)(2,1)} %refs_0_), channel_id=1, source_target_pairs={{0,24},{1,25},{2,26},{3,27},{4,28},{5,29},{6,30},{7,31},{8,16},{9,... | collective-permute-start | bytes 1769480 | tf_op jit(solution)/shard_map/ppermute | solution.py:28
  101.0 21.3 %collective-permute-start.20 = (bf16[384,768]{1,0:T(8,128)(2,1)}, bf16[384,768]{1,0:T(8,128)(2,1)}, u32[]{:S(2)}, u32[]{:S(2)}) collective-permute-start(bf16[384,768]{1,0:T(8,128)(2,1)} %refs_0_), channel_id=1, source_target_pairs={{0,4},{1,5},{2,6},{3,7},{4,0},{5,1},{6,2},{7,3},{8,12},{9,13},{10,... | collective-permute-start | bytes 1769480 | tf_op jit(solution)/shard_map/ppermute | solution.py:28
  101.0 21.3 %collective-permute-start.21 = (bf16[384,768]{1,0:T(8,128)(2,1)}, bf16[384,768]{1,0:T(8,128)(2,1)}, u32[]{:S(2)}, u32[]{:S(2)}) collective-permute-start(bf16[384,768]{1,0:T(8,128)(2,1)} %collective-permute-done.17.refs_1_), channel_id=1, source_target_pairs={{0,4},{1,5},{2,6},{3,7},{4,0},{5,1},{6,2},{7,3},{8,12},{9,13},{10,... | collective-permute-start | bytes 1769480 | tf_op jit(solution)/shard_map/ppermute | solution.py:28
  101.5 20.8 %collective-permute-start.22 = (bf16[384,768]{1,0:T(8,128)(2,1)S(1)}, bf16[384,768]{1,0:T(8,128)(2,1)}, u32[]{:S(2)}, u32[]{:S(2)}) collective-permute-start(bf16[384,768]{1,0:T(8,128)(2,1)S(1)} %collective-permute-done.18.refs_2_), channel_id=1, source_target_pairs={{0,4},{1,5},{2,6},{3,7},{4,0},{5,1},{6,2},{7,3},{8,12},{9,13},{10,... | collective-permute-start | bytes 1769480 | tf_op jit(solution)/shard_map/ppermute | solution.py:28
  102.5 19.8 %collective-permute-start.23 = (bf16[384,768]{1,0:T(8,128)(2,1)S(1)}, bf16[384,768]{1,0:T(8,128)(2,1)}, u32[]{:S(2)}, u32[]{:S(2)}) collective-permute-start(bf16[384,768]{1,0:T(8,128)(2,1)S(1)} %collective-permute-done.19.refs_3_), channel_id=1, source_target_pairs={{0,4},{1,5},{2,6},{3,7},{4,0},{5,1},{6,2},{7,3},{8,12},{9,13},{10,... | collective-permute-start | bytes 1769480 | tf_op jit(solution)/shard_map/ppermute | solution.py:28
  157.8 17.0 %collective-permute-start.24 = (bf16[4,384,768]{2,1,0:T(8,128)(2,1)}, bf16[4,384,768]{2,1,0:T(8,128)(2,1)S(1)}, u32[]{:S(2)}, u32[]{:S(2)}) collective-permute-start(bf16[4,384,768]{2,1,0:T(8,128)(2,1)} %get-tuple-element.84), channel_id=1, source_target_pairs={{0,4},{1,5},{2,6},{3,7},{4,0},{5,1},{6,2},{7,3},{8,12},{9,13},{10,... | collective-permute-start | bytes 7077896 | tf_op jit(solution)/shard_map/ppermute | solution.py:28
  188.2 36.7 %collective-permute-start.30 = (bf16[4,480,768]{2,1,0:T(8,128)(2,1)}, bf16[4,480,768]{2,1,0:T(8,128)(2,1)S(1)}, u32[]{:S(2)}, u32[]{:S(2)}) collective-permute-start(bf16[4,480,768]{2,1,0:T(8,128)(2,1)} %get-tuple-element.89), channel_id=1, source_target_pairs={{0,4},{1,5},{2,6},{3,7},{4,0},{5,1},{6,2},{7,3},{8,12},{9,13},{10,... | collective-permute-start | bytes 8847368 | tf_op jit(solution)/shard_map/ppermute | solution.py:28
  191.5 15.5 %collective-permute-start.25 = (bf16[2,192,768]{2,1,0:T(8,128)(2,1)S(1)}, bf16[2,192,768]{2,1,0:T(8,128)(2,1)S(1)}, u32[]{:S(2)}, u32[]{:S(2)}) collective-permute-start(bf16[2,192,768]{2,1,0:T(8,128)(2,1)S(1)} %slice_bitcast_fusion.6), channel_id=1, source_target_pairs={{0,8},{1,9},{2,10},{3,11},{4,12},{5,13},{6,14},{7,15},{8,0},{9,1},... | collective-permute-start | bytes 1769480 | tf_op jit(solution)/shard_map/ppermute | solution.py:28
  192.9 15.2 %collective-permute-start.27 = (bf16[2,192,768]{2,1,0:T(8,128)(2,1)S(1)}, bf16[2,192,768]{2,1,0:T(8,128)(2,1)S(1)}, u32[]{:S(2)}, u32[]{:S(2)}) collective-permute-start(bf16[2,192,768]{2,1,0:T(8,128)(2,1)S(1)} %slice_bitcast_fusion.4), channel_id=1, source_target_pairs={{0,16},{1,17},{2,18},{3,19},{4,20},{5,21},{6,22},{7,23},{8,24},{9,... | collective-permute-start | bytes 1769480 | tf_op jit(solution)/shard_map/ppermute | solution.py:28
  223.2 21.5 %collective-permute-start.29 = (bf16[192,768]{1,0:T(8,128)(2,1)}, bf16[192,768]{1,0:T(8,128)(2,1)}, u32[]{:S(2)}, u32[]{:S(2)}) collective-permute-start(bf16[192,768]{1,0:T(8,128)(2,1)} %dynamic-slice_bitcast_fusion.1), channel_id=1, source_target_pairs={{0,1},{1,0},{2,3},{3,2},{4,5},{5,4},{6,7},{7,6},{8,9},{9,8},{10,11... | collective-permute-start | bytes 884744 | tf_op jit(solution)/shard_map/ppermute | solution.py:28
  230.8 30.3 %collective-permute-start.31 = (bf16[2,240,768]{2,1,0:T(8,128)(2,1)}, bf16[2,240,768]{2,1,0:T(8,128)(2,1)}, u32[]{:S(2)}, u32[]{:S(2)}) collective-permute-start(bf16[2,240,768]{2,1,0:T(8,128)(2,1)} %slice_bitcast_fusion.3), channel_id=1, source_target_pairs={{0,8},{1,9},{2,10},{3,11},{4,12},{5,13},{6,14},{7,15},{8,0},{9,1},... | collective-permute-start | bytes 2211848 | tf_op jit(solution)/shard_map/ppermute | solution.py:28
  231.4 29.8 %collective-permute-start.32 = (bf16[2,240,768]{2,1,0:T(8,128)(2,1)}, bf16[2,240,768]{2,1,0:T(8,128)(2,1)}, u32[]{:S(2)}, u32[]{:S(2)}) collective-permute-start(bf16[2,240,768]{2,1,0:T(8,128)(2,1)} %slice_bitcast_fusion.2), channel_id=1, source_target_pairs={{0,16},{1,17},{2,18},{3,19},{4,20},{5,21},{6,22},{7,23},{8,24},{9,... | collective-permute-start | bytes 2211848 | tf_op jit(solution)/shard_map/ppermute | solution.py:28
  246.5 27.8 %collective-permute-start.33 = (bf16[192,768]{1,0:T(8,128)(2,1)}, bf16[192,768]{1,0:T(8,128)(2,1)S(1)}, u32[]{:S(2)}, u32[]{:S(2)}) collective-permute-start(bf16[192,768]{1,0:T(8,128)(2,1)} %fusion.10), channel_id=1, source_target_pairs={{0,2},{1,3},{2,0},{3,1},{4,6},{5,7},{6,4},{7,5},{8,10},{9,11},{10,... | collective-permute-start | bytes 884744 | tf_op jit(solution)/shard_map/ppermute | solution.py:28
  272.7 31.9 %collective-permute-start.37 = (bf16[4,288,768]{2,1,0:T(8,128)(2,1)}, bf16[4,288,768]{2,1,0:T(8,128)(2,1)}, u32[]{:S(2)}, u32[]{:S(2)}) collective-permute-start(bf16[4,288,768]{2,1,0:T(8,128)(2,1)} %get-tuple-element.107), channel_id=1, source_target_pairs={{0,4},{1,5},{2,6},{3,7},{4,0},{5,1},{6,2},{7,3},{8,12},{9,13},{10,... | collective-permute-start | bytes 5308424 | tf_op jit(solution)/shard_map/ppermute | solution.py:28
  275.4 23.4 %collective-permute-start.48 = (bf16[192,768]{1,0:T(8,128)(2,1)S(1)}, bf16[192,768]{1,0:T(8,128)(2,1)S(1)}, u32[]{:S(2)}, u32[]{:S(2)}) collective-permute-start(bf16[192,768]{1,0:T(8,128)(2,1)S(1)} %add_convert_fusion.4), channel_id=1, source_target_pairs={{0,1},{1,0},{2,3},{3,2},{4,5},{5,4},{6,7},{7,6},{8,9},{9,8},{10,11... | collective-permute-start | bytes 884744 | tf_op jit(solution)/shard_map/ppermute | solution.py:28
  284.0 20.1 %collective-permute-start.45 = (bf16[240,768]{1,0:T(8,128)(2,1)S(1)}, bf16[240,768]{1,0:T(8,128)(2,1)S(1)}, u32[]{:S(2)}, u32[]{:S(2)}) collective-permute-start(bf16[240,768]{1,0:T(8,128)(2,1)S(1)} %dynamic-slice_bitcast_fusion), channel_id=1, source_target_pairs={{0,1},{1,0},{2,3},{3,2},{4,5},{5,4},{6,7},{7,6},{8,9},{9,8},{10,11... | collective-permute-start | bytes 1105928 | tf_op jit(solution)/shard_map/ppermute | solution.py:28
  304.2 16.1 %collective-permute-start.46 = (bf16[240,768]{1,0:T(8,128)(2,1)S(1)}, bf16[240,768]{1,0:T(8,128)(2,1)}, u32[]{:S(2)}, u32[]{:S(2)}) collective-permute-start(bf16[240,768]{1,0:T(8,128)(2,1)S(1)} %fusion.6), channel_id=1, source_target_pairs={{0,2},{1,3},{2,0},{3,1},{4,6},{5,7},{6,4},{7,5},{8,10},{9,11},{10,... | collective-permute-start | bytes 1105928 | tf_op jit(solution)/shard_map/ppermute | solution.py:28
  306.6 14.9 %collective-permute-start.38 = (bf16[2,144,768]{2,1,0:T(8,128)(2,1)S(1)}, bf16[2,144,768]{2,1,0:T(8,128)(2,1)}, u32[]{:S(2)}, u32[]{:S(2)}) collective-permute-start(bf16[2,144,768]{2,1,0:T(8,128)(2,1)S(1)} %slice_bitcast_fusion.10), channel_id=1, source_target_pairs={{0,8},{1,9},{2,10},{3,11},{4,12},{5,13},{6,14},{7,15},{8,0},{9,1},... | collective-permute-start | bytes 1327112 | tf_op jit(solution)/shard_map/ppermute | solution.py:28
  321.4 21.3 %collective-permute-start.47 = (bf16[240,768]{1,0:T(8,128)(2,1)S(1)}, bf16[240,768]{1,0:T(8,128)(2,1)S(1)}, u32[]{:S(2)}, u32[]{:S(2)}) collective-permute-start(bf16[240,768]{1,0:T(8,128)(2,1)S(1)} %add_convert_fusion.3), channel_id=1, source_target_pairs={{0,1},{1,0},{2,3},{3,2},{4,5},{5,4},{6,7},{7,6},{8,9},{9,8},{10,11... | collective-permute-start | bytes 1105928 | tf_op jit(solution)/shard_map/ppermute | solution.py:28
  (44 other events, 460.7 us)

commit v5 on v4

--- a/solution.py
+++ b/solution.py
@@ -66,59 +66,55 @@
     received = swap_with(send, 1)
     yield [received]
     rows, width = own.shape[1:]
-    chunks = add_low(own, received).reshape((2,) * (bits - 1) + (rows, width))
     half = rows // 32 * 16
-    parts = [chunks[..., :half, :], chunks[..., half:, :]]
     lefts = [list(range(1, bits)), list(range(1, bits))]
-    for _ in range(1, bits):
+    split = None
+    if bits == 3:
+        split = split_add(own, received, half)
+    else:
+        chunks = add_low(own, received).reshape((2,) * (bits - 1) + (rows, width))
+        parts = [chunks[..., :half, :], chunks[..., half:, :]]
+    for step in range(1, bits):
         kept, received = [], []
-        for part, left, end in zip(parts, lefts, (0, -1)):
+        for n, (left, end) in enumerate(zip(lefts, (0, -1))):
             b = left[end]
             axis = len(left) - 1 - left.index(b)
-            keep, away = (lax.index_in_dim(part, i, axis, keepdims=False) for i in (0, 1))
+            if split and step == 1:
+                keep, away = split[2 * n : 2 * n + 2]
+            else:
+                keep, away = (lax.index_in_dim(parts[n], i, axis, keepdims=False) for i in (0, 1))
             kept.append(keep)
             received.append(swap_with(away, 1 << b))
             left.remove(b)
         yield received
         parts = [add_low(keep, got) for keep, got in zip(kept, received)]
     total = jnp.concatenate(parts)
-    replicas = lax.axis_size("replica")
-    if replicas > 1:
-        at = lax.axis_index("replica")
-        pair = total.reshape(2, rows // 2, width)
-        received = swap_with(pick(pair, 0, 1 - (at & 1)), 0, 1)
+    at = lax.axis_index("replica")
+    pair = total.reshape(2, rows // 2, width)
+    if lax.axis_size("replica") == 1:
+        yield pair[0], pair[1]
+        return
+    received = swap_with(pick(pair, 0, 1 - (at & 1)), 0, 1)
+    yield [received]
+    kept = add_low(pick(pair, 0, at & 1), received)
+    mask = 2
+    while mask < lax.axis_size("replica"):
+        received = swap_with(kept, 0, mask)
         yield [received]
-        kept = add_low(pick(pair, 0, at & 1), received)
-        mask = 2
-        while mask < replicas:
-            received = swap_with(kept, 0, mask)
-            yield [received]
-            kept = add_low(kept, received)
-            mask *= 2
-        other = swap_with(kept, 0, 1)
-        yield [other]
-        total = jnp.where(
-            (at & 1) == 0, jnp.concatenate([kept, other]), jnp.concatenate([other, kept])
-        )
-    yield total
+        kept = add_low(kept, received)
+        mask *= 2
+    other = swap_with(kept, 0, 1)
+    yield [other]
+    yield kept, other
+
+
+def in_order(odd, kept, other):
+    return jnp.where(odd, jnp.concatenate([other, kept]), jnp.concatenate([kept, other]))
 
 
 def finish(steps):
     *_, last = steps
     return last
-
-
-def everywhere(array, bits):
-    masks = [(1 << b, 0) for b in range(bits)]
-    mask = 1
-    while mask < lax.axis_size("replica"):
-        masks.append((0, mask))
-        mask *= 2
-    for group_mask, replica_mask in masks:
-        received = swap_with(array, group_mask, replica_mask)
-        yield [received]
-        array = array + received
-    yield array
 
 
 class Gathered:
@@ -681,26 +677,145 @@
     )(me, after, hidden_grad, mixed, branch_grad)
 
 
-def qkv_weight_kernel(me, rows, grads, own, send):
-    store_chunks(tn(rows[...], grads[0]), me[0], own, send)
-
-
-def qkv_weight(me, rows, grads, count):
+SMALL_ROWS = 16
+
+
+def row_stride(chunk):
+    return -(-chunk // 16) * 16
+
+
+def small_tile(vectors, wide, g, count, width):
+    size, wide_size = width // count, wide.shape[1] // count
+    part = slice(g * size, (g + 1) * size)
+    tops = [ref[rows, part] for ref, rows in vectors]
+    fill = lambda rows, used: jnp.zeros((rows, width - used), jnp.float32)
+    top = jnp.concatenate(tops, axis=0)
+    eight = jnp.concatenate([top, fill(8, size)], axis=1)
+    last = jnp.concatenate([wide[:, g * wide_size : (g + 1) * wide_size], fill(1, wide_size)], axis=1)
+    return jnp.concatenate([eight, last, jnp.zeros((7, width), jnp.float32)], axis=0).astype(jnp.bfloat16)
+
+
+def qkv_weight_kernel(me, rows, grads, attend_sums, sums1, sums2, wide, own, send):
+    step = pl.program_id(0)
+    count, width = 2 * own.shape[0], own.shape[2]
+    chunk = width // count
+    stride = row_stride(chunk)
+    product = tn(rows[...], grads[0])
+
+    def keep(g, first, value):
+        apart = g ^ me[0]
+        size = value.shape[0]
+
+        @pl.when(apart % 2 == 0)
+        def _():
+            own[apart // 2, first : first + size] = value
+
+        @pl.when(apart % 2 == 1)
+        def _():
+            send[apart // 2, first : first + size] = value
+
+    for n in range(3):
+
+        @pl.when(step == n)
+        def _():
+            for g in range(count):
+                keep(g, n * stride, product[g * chunk : (g + 1) * chunk].astype(jnp.bfloat16))
+
+    @pl.when(step == 0)
+    def _():
+        vectors = (
+            (attend_sums, slice(0, 2)), (sums1, slice(2, 3)), (sums2, slice(2, 3)),
+            (sums1, slice(0, 2)), (sums2, slice(0, 2)),
+        )
+        for g in range(count):
+            keep(g, 3 * stride, small_tile(vectors, wide, g, count, width))
+
+
+def qkv_weight(me, rows, grads, attend_sums, sums1, sums2, wide, count):
     total, width = rows.shape
-    chunk = width // count
+    tall = 3 * row_stride(width // count) + SMALL_ROWS
+    block = pl.BlockSpec((count // 2, tall, width), lambda j, me: (0, 0, 0))
     return pl.pallas_call(
         qkv_weight_kernel,
-        out_shape=halves(count, chunk, 3, width),
+        out_shape=halves(count, tall, 1, width),
         grid_spec=pltpu.PrefetchScalarGridSpec(
             num_scalar_prefetch=1,
             grid=(3,),
-            in_specs=[whole(rows), pl.BlockSpec((1, total, width), lambda j, me: (j, 0, 0))],
-            out_specs=[pl.BlockSpec((count // 2, chunk, width), lambda j, me: (0, j, 0))] * 2,
+            in_specs=[whole(rows), pl.BlockSpec((1, total, width), lambda j, me: (j, 0, 0))]
+            + [whole(a) for a in (attend_sums, sums1, sums2, wide)],
+            out_specs=[block] * 2,
         ),
         compiler_params=kernel_params(),
         cost_estimate=cost(6 * total * width * width, 1e7),
         name="qkv_weight",
-    )(me, rows, grads)
+    )(me, rows, grads, attend_sums, sums1, sums2, wide)
+
+
+def deliver_kernel(odd, kept, other, *outs):
+    first, second = kept[...].astype(jnp.float32), other[...].astype(jnp.float32)
+    swap = odd[0] == 1
+    both = jnp.concatenate([jnp.where(swap, second, first), jnp.where(swap, first, second)], axis=0)
+    chunk = outs[0].shape[0]
+    stride = row_stride(chunk)
+    for n in range(3):
+        outs[n][...] = both[n * stride : n * stride + chunk]
+    for n, out in enumerate(outs[3:]):
+        out[...] = both[3 * stride + n, 0 : out.shape[0]]
+
+
+def deliver(odd, kept, other, chunk, wide_chunk):
+    width = kept.shape[1]
+    sizes = [chunk] * 8 + [wide_chunk]
+    return pl.pallas_call(
+        deliver_kernel,
+        out_shape=[shape(chunk, width, jnp.float32)] * 3
+        + [jax.ShapeDtypeStruct((n,), jnp.float32) for n in sizes],
+        in_specs=[SMEM(), VMEM(), VMEM()],
+        out_specs=[VMEM()] * 12,
+        compiler_params=kernel_params(),
+        name="deliver",
+    )(odd, kept, other)
+
+
+def split_add_kernel(own, received, keep_x, away_x, keep_y, away_y):
+    slot = pl.program_id(0)
+    total = (own[0].astype(jnp.float32) + received[0].astype(jnp.float32)).astype(jnp.bfloat16)
+    half = keep_x.shape[1]
+    top, bottom = total[:half], total[half:]
+
+    @pl.when(slot % 2 == 0)
+    def _():
+        keep_x[0] = top
+
+    @pl.when(slot % 2 == 1)
+    def _():
+        away_x[0] = top
+
+    @pl.when(slot < 2)
+    def _():
+        keep_y[0] = bottom
+
+    @pl.when(slot >= 2)
+    def _():
+        away_y[0] = bottom
+
+
+def split_add(own, received, half):
+    _, rows, width = own.shape
+    block = lambda n, where: pl.BlockSpec((1, n, width), lambda s: (where(s), 0, 0))
+    table = lambda n: jax.ShapeDtypeStruct((2, n, width), jnp.bfloat16)
+    return pl.pallas_call(
+        split_add_kernel,
+        out_shape=[table(half)] * 2 + [table(rows - half)] * 2,
+        grid=(4,),
+        in_specs=[block(rows, lambda s: s)] * 2,
+        out_specs=[
+            block(half, lambda s: s // 2), block(half, lambda s: s // 2),
+            block(rows - half, lambda s: jnp.minimum(s, 1)), block(rows - half, lambda s: jnp.maximum(s - 2, 0)),
+        ],
+        compiler_params=kernel_params(),
+        name="split_add",
+    )(own, received)
 
 
 def pack_kernel(*refs):
@@ -727,19 +842,6 @@
             wide_out[:, g * wide_chunk + first : g * wide_chunk + first + size] = tile[8 + n : 9 + n, 0:size]
 
 
-def collect_kernel(me, vectors, wide, *outs):
-    count = vectors.shape[1] // outs[0].shape[1]
-    for g in range(count):
-
-        @pl.when(g == me[0])
-        def _():
-            for i in range(8):
-                n = outs[i].shape[1]
-                outs[i][...] = vectors[i : i + 1, g * n : (g + 1) * n]
-            n = outs[8].shape[1]
-            outs[8][...] = wide[:, g * n : (g + 1) * n]
-
-
 SMEM = lambda: pl.BlockSpec(memory_space=pltpu.SMEM)
 VMEM = lambda: pl.BlockSpec(memory_space=pltpu.VMEM)
 
@@ -756,15 +858,6 @@
         spread_kernel, out_shape=[shape(8, width, jnp.float32), shape(1, wide, jnp.float32)],
         in_specs=[SMEM(), VMEM()], out_specs=[VMEM()] * 2, compiler_params=kernel_params(), name="spread",
     )(me, table)
-
-
-def collect(me, vectors, wide, count):
-    sizes = [vectors.shape[1] // count] * 8 + [wide.shape[1] // count]
-    outs = pl.pallas_call(
-        collect_kernel, out_shape=[shape(1, n, jnp.float32) for n in sizes],
-        in_specs=[SMEM(), VMEM(), VMEM()], out_specs=[VMEM()] * 9, compiler_params=kernel_params(), name="collect",
-    )(me, vectors, wide)
-    return [o.reshape(-1) for o in outs]
 
 
 def per_device(
@@ -830,32 +923,24 @@
         came, came_b = next(red_c), next(red_b)
         grads, sums_at = attend_back(seqs, seq, q, k, v, mixed_grad, probs, (grads,))
         attend_sums = attend_sums + sums_at[0]
-    small = jnp.concatenate(
-        [
-            attend_sums, sums1[2:3], sums2[2:3], sums1[0:2], sums2[0:2],
-            in_bias_sum.reshape(blocks, width),
-        ]
-    )
-    small_steps = everywhere(small, bits)
     rows_in = after(x, *came, *came_b)
     came, came_b = next(red_c), next(red_b)
-    came_s = next(small_steps)
-    own, send = qkv_weight(me, rows_in, grads, count)
+    own, send = qkv_weight(me, rows_in, grads, attend_sums, sums1, sums2, in_bias_sum, count)
     red_a = reduction(own, send, bits)
     came_a = next(red_a)
-    h1_in = after(h1_grad, own, *came, *came_b, *came_s)
-    came, came_b = next(red_c), next(red_b)
-    came_s = next(small_steps)
+    h1_in = after(h1_grad, *came, *came_b, *came_a)
+    came, came_b, came_a = next(red_c), next(red_b), next(red_a)
     input_grad = input_grad_of(h1_in, grads, plan_a)
-    sum_c, sum_b, sum_a = finish(red_c), finish(red_b), finish(red_a)
-    small = finish(small_steps)
-    vector_grads = collect(me, small[0:8], small[8:].reshape(1, wide), count)
-    grad_q, grad_v, grad_o, grad_b, grad_g1, grad_s1, grad_g2, grad_s2, grad_i = vector_grads
+    odd = lax.axis_index("replica") & 1
+    sum_c, sum_b = (in_order(odd, *finish(steps)) for steps in (red_c, red_b))
+    (
+        grad_wq, grad_wk, grad_wv, grad_q, grad_v, grad_o, grad_b, grad_g1, grad_s1, grad_g2, grad_s2, grad_i,
+    ) = deliver(odd.reshape(1), *finish(red_a), chunk, wide // count)
     up = lambda a: a.astype(jnp.float32)
     in_sum = jnp.concatenate([sum_b[n * chunk : (n + 1) * chunk] for n in range(blocks)], axis=1)
     return (
         layer_out.reshape(inputs.shape), input_grad.reshape(inputs.shape),
-        up(sum_a[:chunk]), up(sum_a[chunk : 2 * chunk]), up(sum_a[2 * chunk :]),
+        grad_wq, grad_wk, grad_wv,
         up(sum_b[blocks * chunk :]), up(in_sum), up(sum_c),
         grad_q, grad_v, grad_o, grad_i, grad_b, grad_g1, grad_s1, grad_g2, grad_s2,
     )

time: 364 us -> 366 us (level)
  Pallas kernels: 154 us -> 172 us
  other arithmetic: 25.4 us -> 14.5 us
  local copies, waits for them, and re-layouts: 24 us -> 14.5 us
  waiting for transfers between devices: 116 us -> 121 us
    pallas_call x2 -> x5, Pallas kernels: 9.44 us -> 26.7 us  [the longest x3 14.9 us: split_add(): pl.pallas_call(split_add_kernel, out_shape=[table(half)] * 2 + [table(row...]
    convert_element_type x18, other arithmetic: 17.6 us -> 9.13 us  [add_low(): (left.astype(jnp.float32) + right.astype(jnp.float32)).astype(jnp.bfloat16)]
    slice x5 -> x0, local copies, waits for them, and re-layouts: 5.36 us -> none  [the longest x1 1.34 us: per_device(): sums1[0:2]]
    ppermute x53 -> x48, waiting for transfers between devices: 116 us -> 121 us  [swap_with(): return lax.ppermute(array, AXES, pairs)]
    ppermute x53 -> x48, starting transfers between devices: 41.7 us -> 42.5 us  [swap_with(): return lax.ppermute(array, AXES, pairs)]
    unnamed x54 -> x58, local copies, waits for them, and re-layouts: 8.66 us -> 8.37 us
  transfers between devices with their start and end apart: 53 -> 48, of which waited for: 20 -> 17; matrix products, arithmetic and copies ran while one was open for 11% -> 6% of each run, Pallas kernels for 29% -> 33%
where the time goes in v5:
time: 366 us; the launch traced here: 365 us
  Pallas kernels  172 us (47%)
  waiting for transfers between devices  121 us (33%)
  starting transfers between devices  42.5 us (12%)
  local copies, waits for them, and re-layouts  14.5 us (4%)
  other arithmetic  14.5 us (4%)
    ppermute x48, waiting for transfers between devices, swap_with(): return lax.ppermute(array, AXES, pairs)  121 us
    ppermute x48, starting transfers between devices, swap_with(): return lax.ppermute(array, AXES, pairs)  42.5 us
    pallas_call x2, Pallas kernels, attend_back(): pl.pallas_call(attend_back_kernel, out_shape=[jax.ShapeDtypeStruct((3, to...  24.4 us
    pallas_call x1, Pallas kernels, turn(): pl.pallas_call(functools.partial(turn_kernel, plan, slots), out_shape=[sh...  24.1 us
    pallas_call x1, Pallas kernels, attend(): pl.pallas_call(functools.partial(attend_kernel, plan), out_shape=[table]...  22.7 us
    pallas_call x1, Pallas kernels, feed(): pl.pallas_call(functools.partial(feed_kernel, plan, len(before)), out_sha...  19.4 us
    pallas_call x1, Pallas kernels, return_grad(): pl.pallas_call(functools.partial(return_kernel, plan, len(before)), out_s...  16.8 us
    pallas_call x3, Pallas kernels, split_add(): pl.pallas_call(split_add_kernel, out_shape=[table(half)] * 2 + [table(row...  14.9 us
  transfers between devices with their start and end apart: 48, of which 17 were waited for; matrix products, arithmetic and copies ran while one was open for 6% of the time, Pallas kernels for 33%

profile of v5, /device:TPU:0, one launch (start us, length us, event | category | flops | bytes accessed | tf_op | source)
XLA Modules:
  0.0 365.0 jit_solution(10329580447582158251)
XLA Ops:
  3.5 3.0 collective-permute-start.3
  14.6 13.2 %collective-permute-done = f32[1,16,128]{2,1,0:T(8,128)S(1)} collective-permute-done((f32[1,16,128]{2,1,0:T(8,128)}, f32[1,16,128]{2,1,0:T(8,128)S(1)}, u32[]{:S(2)}, u32[]{:S(2)}) %collective-permute-start) | collective-permute-done | bytes 8224 | tf_op jit(solution)/shard_map/ppermute | solution.py:28
  28.7 3.6 collective-permute-done.1
  35.7 2.0 collective-permute-start.11
  41.0 22.7 %attend.1 = (bf16[1024,768]{1,0:T(8,128)(2,1)}, bf16[1024,768]{1,0:T(8,128)(2,1)}, bf16[1024,768]{1,0:T(8,128)(2,1)}, bf16[1024,768]{1,0:T(8,128)(2,1)}, bf16[24,512,512]{2,1,0:T(8,128)(2,1)}) custom-call(s32[2]{0:T(128)} %lens.3, s32[1]{0:T(128)} %bitcast.me, bf16[1024,768]{1,0:T(8,128)(2,1)} %bitcast.113, f32[1,768]{1,0:T(1,128)} %get-tuple-element.159.bq, ...), custom_call_target="tpu_custom_call" | custom-call | flops 6845104128 | bytes 30000000 | tf_op jit(solution)/shard_map/attend/pallas_call | solution.py:261
  63.7 5.7 %collective-permute-done.11.refs_2_ = bf16[480,768]{1,0:T(8,128)(2,1)S(1)} collective-permute-done((bf16[480,768]{1,0:T(8,128)(2,1)S(1)}, bf16[480,768]{1,0:T(8,128)(2,1)S(1)}, u32[]{:S(2)}, u32[]{:S(2)}) %collective-permute-start.11) | collective-permute-done | bytes 737312 | tf_op jit(solution)/shard_map/ppermute | solution.py:28
  73.9 12.1 %collective-permute-done.17.refs_1_ = bf16[384,768]{1,0:T(8,128)(2,1)} collective-permute-done((bf16[384,768]{1,0:T(8,128)(2,1)}, bf16[384,768]{1,0:T(8,128)(2,1)}, u32[]{:S(2)}, u32[]{:S(2)}) %collective-permute-start.17) | collective-permute-done | bytes 589856 | tf_op jit(solution)/shard_map/ppermute | solution.py:28
  87.4 13.6 %collective-permute-done.18.refs_2_ = bf16[384,768]{1,0:T(8,128)(2,1)S(1)} collective-permute-done((bf16[384,768]{1,0:T(8,128)(2,1)}, bf16[384,768]{1,0:T(8,128)(2,1)S(1)}, u32[]{:S(2)}, u32[]{:S(2)}) %collective-permute-start.18) | collective-permute-done | bytes 589856 | tf_op jit(solution)/shard_map/ppermute | solution.py:28
  102.9 19.4 %shard_map.305 = (bf16[1024,768]{1,0:T(8,128)(2,1)}, f32[1024,768]{1,0:T(8,128)}, f32[1024,128]{1,0:T(8,128)}, bf16[1024,3072]{1,0:T(8,128)(2,1)}, bf16[1024,3072]{1,0:T(8,128)(2,1)}) custom-call(s32[1]{0:T(128)} %bitcast.me, bf16[1024,768]{1,0:T(8,128)(2,1)} %get-tuple-element.83.mixed, bf16[1024,768]{1,0:T(8,128)(2,1)} %bitcast.114, ...), custom_call_target="tpu_custom_call" | custom-call | flops 18119393280 | bytes 15000000 | tf_op jit(solution)/shard_map/pallas_call | solution.py:395
  122.3 24.1 %turn.1 = (bf16[1024,768]{1,0:T(8,128)(2,1)}, bf16[1024,768]{1,0:T(8,128)(2,1)}, bf16[1024,3072]{1,0:T(8,128)(2,1)}, f32[1024,768]{1,0:T(8,128)}, f32[8,768]{1,0:T(8,128)}, /*index=5*/f32[1,3072]{1,0:T(1,128)}) custom-call(s32[2]{0:T(128)} %lens.3, s32[1]{0:T(128)} %bitcast.me, bf16[1024,3072]{1,0:T(8,128)(2,1)} %get-tuple-element.86.active, ...), custom_call_target="tpu_custom_call" | custom-call | flops 9663676416 | bytes 30000000 | tf_op jit(solution)/shard_map/turn/pallas_call | solution.py:466
  146.4 11.3 %back_weight.1 = (bf16[4,384,768]{2,1,0:T(8,128)(2,1)}, bf16[4,384,768]{2,1,0:T(8,128)(2,1)}) custom-call(s32[1]{0:T(128)} %bitcast.me, bf16[1024,3072]{1,0:T(8,128)(2,1)} %get-tuple-element.86.active, bf16[1024,768]{1,0:T(8,128)(2,1)} %get-tuple-element.92.grad), custom_call_target="tpu_custom_call" | custom-call | flops 4831838208 | bytes 13000000 | tf_op jit(solution)/shard_map/back_weight/pallas_call | solution.py:618
  158.0 16.8 %shard_map.306 = (f32[1024,768]{1,0:T(8,128)}, bf16[1024,768]{1,0:T(8,128)(2,1)}, bf16[1024,768]{1,0:T(8,128)(2,1)}, f32[8,768]{1,0:T(8,128)}) custom-call(s32[1]{0:T(128)} %bitcast.me, bf16[1024,3072]{1,0:T(8,128)(2,1)} %get-tuple-element.94.hidden_grad, f32[1024,768]{1,0:T(8,128)} %get-tuple-element.95.h2_grad, f32[1024,768]{1,0:T(8,128)} %get-tuple-element.87.normed1, ...), custom_call_target="tpu_custom_call" | custom-call | flops 6039797760 | bytes 15000000 | tf_op jit(solution)/shard_map/pallas_call | solution.py:516
  174.8 13.3 %in_out_weight.1 = (bf16[4,480,768]{2,1,0:T(8,128)(2,1)}, bf16[4,480,768]{2,1,0:T(8,128)(2,1)}) custom-call(s32[1]{0:T(128)} %bitcast.me, bf16[1024,768]{1,0:T(8,128)(2,1)} %get-tuple-element.104.after, bf16[1024,3072]{1,0:T(8,128)(2,1)} %get-tuple-element.94.hidden_grad, bf16[1024,768]{1,0:T(8,128)(2,1)} %get-tuple-element.83.mixed, ...), custom_call_target="tpu_custom_call" | custom-call | flops 6039797760 | bytes 20000000 | tf_op jit(solution)/shard_map/in_out_weight/pallas_call | solution.py:660
  188.5 4.9 %split_add.3 = (bf16[2,192,768]{2,1,0:T(8,128)(2,1)}, bf16[2,192,768]{2,1,0:T(8,128)(2,1)}, bf16[2,192,768]{2,1,0:T(8,128)(2,1)}, bf16[2,192,768]{2,1,0:T(8,128)(2,1)}) custom-call(bf16[4,384,768]{2,1,0:T(8,128)(2,1)} %get-tuple-element.98.own, bf16[4,384,768]{2,1,0:T(8,128)(2,1)} %copy-done.2), custom_call_target="tpu_custom_call" | custom-call | tf_op jit(solution)/shard_map/split_add/pallas_call | solution.py:807
  195.4 13.6 %collective-permute-done.25 = bf16[2,192,768]{2,1,0:T(8,128)(2,1)S(1)} collective-permute-done((bf16[2,192,768]{2,1,0:T(8,128)(2,1)}, bf16[2,192,768]{2,1,0:T(8,128)(2,1)S(1)}, u32[]{:S(2)}, u32[]{:S(2)}) %collective-permute-start.25) | collective-permute-done | bytes 589856 | tf_op jit(solution)/shard_map/ppermute | solution.py:28
  214.3 12.1 %shard_map.307 = (bf16[3,1024,768]{2,1,0:T(8,128)(2,1)}, f32[1,2,768]{2,1,0:T(2,128)}) custom-call(bf16[1024,768]{1,0:T(8,128)(2,1)} %get-tuple-element.114.q, bf16[1024,768]{1,0:T(8,128)(2,1)} %get-tuple-element.115.k, bf16[1024,768]{1,0:T(8,128)(2,1)} %get-tuple-element.116.v, bf16[1024,768]{1,0:T(8,128)(2,1)} %get-tuple-element.121.grad, ...), custom_call_target="tpu_custom_call" | custom-call | flops 2818572288 | bytes 15000000 | tf_op jit(solution)/shard_map/pallas_call | solution.py:318
  229.1 5.5 %split_add.4 = (bf16[2,240,768]{2,1,0:T(8,128)(2,1)}, bf16[2,240,768]{2,1,0:T(8,128)(2,1)}, bf16[2,240,768]{2,1,0:T(8,128)(2,1)}, bf16[2,240,768]{2,1,0:T(8,128)(2,1)}) custom-call(bf16[4,480,768]{2,1,0:T(8,128)(2,1)} %get-tuple-element.107.own, bf16[4,480,768]{2,1,0:T(8,128)(2,1)} %copy-done), custom_call_target="tpu_custom_call" | custom-call | tf_op jit(solution)/shard_map/split_add/pallas_call | solution.py:807
  239.4 12.3 %shard_map.308 = (bf16[3,1024,768]{2,1,0:T(8,128)(2,1)}, f32[1,2,768]{2,1,0:T(2,128)}) custom-call(bf16[1024,768]{1,0:T(8,128)(2,1)} %get-tuple-element.114.q, bf16[1024,768]{1,0:T(8,128)(2,1)} %get-tuple-element.115.k, bf16[1024,768]{1,0:T(8,128)(2,1)} %get-tuple-element.116.v, ...), custom_call_target="tpu_custom_call", output_to_operand_aliasing={{0}: (5, {})} | custom-call | flops 2818572288 | bytes 15000000 | tf_op jit(solution)/shard_map/pallas_call | solution.py:318
  256.6 9.8 %qkv_weight.1 = (bf16[4,304,768]{2,1,0:T(8,128)(2,1)}, bf16[4,304,768]{2,1,0:T(8,128)(2,1)}) custom-call(s32[1]{0:T(128)} %bitcast.me, bf16[1024,768]{1,0:T(8,128)(2,1)} %bitcast.115, bf16[3,1024,768]{2,1,0:T(8,128)(2,1)} %get-tuple-element.123.grads, f32[2,768]{1,0:T(2,128)} %bitcast_add_fusion.attend_sums, f32[8,768]{1,0:T(8,128)} %get-tuple-element.125.sums1, ...), custom_call_target="tpu_custom_call" | custom-call | flops 3623878656 | bytes 10000000 | tf_op jit(solution)/shard_map/qkv_weight/pallas_call | solution.py:738
  268.7 2.7 collective-permute-start.30
  272.4 6.6 %collective-permute-done.35 = bf16[240,768]{1,0:T(8,128)(2,1)S(1)} collective-permute-done((bf16[240,768]{1,0:T(8,128)(2,1)S(1)}, bf16[240,768]{1,0:T(8,128)(2,1)S(1)}, u32[]{:S(2)}, u32[]{:S(2)}) %collective-permute-start.35) | collective-permute-done | bytes 368672 | tf_op jit(solution)/shard_map/ppermute | solution.py:28
  279.8 5.3 %collective-permute-done.30 = bf16[192,768]{1,0:T(8,128)(2,1)S(1)} collective-permute-done((bf16[192,768]{1,0:T(8,128)(2,1)S(1)}, bf16[192,768]{1,0:T(8,128)(2,1)S(1)}, u32[]{:S(2)}, u32[]{:S(2)}) %collective-permute-start.30) | collective-permute-done | bytes 294944 | tf_op jit(solution)/shard_map/ppermute | solution.py:28
  285.3 7.7 %collective-permute-done.44 = bf16[240,768]{1,0:T(8,128)(2,1)S(1)} collective-permute-done((bf16[240,768]{1,0:T(8,128)(2,1)S(1)}, bf16[240,768]{1,0:T(8,128)(2,1)S(1)}, u32[]{:S(2)}, u32[]{:S(2)}) %collective-permute-start.44) | collective-permute-done | bytes 368672 | tf_op jit(solution)/shard_map/ppermute | solution.py:28
  295.3 4.5 %split_add.5 = (bf16[2,144,768]{2,1,0:T(8,128)(2,1)}, bf16[2,144,768]{2,1,0:T(8,128)(2,1)}, bf16[2,160,768]{2,1,0:T(8,128)(2,1)}, bf16[2,160,768]{2,1,0:T(8,128)(2,1)}) custom-call(bf16[4,304,768]{2,1,0:T(8,128)(2,1)} %get-tuple-element.130.own, bf16[4,304,768]{2,1,0:T(8,128)(2,1)} %copy-done.3), custom_call_target="tpu_custom_call" | custom-call | tf_op jit(solution)/shard_map/split_add/pallas_call | solution.py:807
  302.4 10.1 %collective-permute-done.45 = bf16[240,768]{1,0:T(8,128)(2,1)S(1)} collective-permute-done((bf16[240,768]{1,0:T(8,128)(2,1)S(1)}, bf16[240,768]{1,0:T(8,128)(2,1)S(1)}, u32[]{:S(2)}, u32[]{:S(2)}) %collective-permute-start.45) | collective-permute-done | bytes 368672 | tf_op jit(solution)/shard_map/ppermute | solution.py:28
  314.9 11.9 %collective-permute-done.39 = bf16[2,160,768]{2,1,0:T(8,128)(2,1)S(1)} collective-permute-done((bf16[2,160,768]{2,1,0:T(8,128)(2,1)S(1)}, bf16[2,160,768]{2,1,0:T(8,128)(2,1)S(1)}, u32[]{:S(2)}, u32[]{:S(2)}) %collective-permute-start.39) | collective-permute-done | bytes 491552 | tf_op jit(solution)/shard_map/ppermute | solution.py:28
  330.1 3.0 collective-permute-done.40
  336.1 5.0 %collective-permute-done.41 = bf16[152,768]{1,0:T(8,128)(2,1)S(1)} collective-permute-done((bf16[152,768]{1,0:T(8,128)(2,1)S(1)}, bf16[152,768]{1,0:T(8,128)(2,1)S(1)}, u32[]{:S(2)}, u32[]{:S(2)}) %collective-permute-start.41) | collective-permute-done | bytes 233504 | tf_op jit(solution)/shard_map/ppermute | solution.py:28
  341.2 2.3 collective-permute-start.42
  344.6 5.3 %collective-permute-done.42 = bf16[152,768]{1,0:T(8,128)(2,1)S(1)} collective-permute-done((bf16[152,768]{1,0:T(8,128)(2,1)S(1)}, bf16[152,768]{1,0:T(8,128)(2,1)S(1)}, u32[]{:S(2)}, u32[]{:S(2)}) %collective-permute-start.42) | collective-permute-done | bytes 233504 | tf_op jit(solution)/shard_map/ppermute | solution.py:28
  349.9 2.4 collective-permute-start.43
  352.4 9.7 %input_grad.1 = bf16[1024,768]{1,0:T(8,128)(2,1)} custom-call(s32[1]{0:T(128)} %bitcast.me, f32[1024,768]{1,0:T(8,128)} %get-tuple-element.129.h1_grad, bf16[3,1024,768]{2,1,0:T(8,128)(2,1)} %get-tuple-element.123.grads, bf16[288,768]{1,0:T(8,128)(2,1)} %copy-done.15, bf16[288,768]{1,0:T(8,128)(2,1)} %copy-done.25, ...), custom_call_target="tpu_custom_call" | custom-call | flops 3623878656 | bytes 20000000 | tf_op jit(solution)/shard_map/input_grad/pallas_call | solution.py:550
  (182 shorter events, 67.8 us)
Async XLA Ops:
  3.5 25.1 %collective-permute-start.3 = (bf16[288,768]{1,0:T(8,128)(2,1)S(1)}, bf16[288,768]{1,0:T(8,128)(2,1)S(1)}, u32[]{:S(2)}, u32[]{:S(2)}) collective-permute-start(bf16[288,768]{1,0:T(8,128)(2,1)S(1)} %constant_dynamic-update-slice_fusion.refs_0_), channel_id=1, source_target_pairs={{0,8},{1,9},{2,10},{3,11},{4,12},{5,13},{6,14},{7,15},{8,0},{9,1},... | collective-permute-start | bytes 1327112 | tf_op jit(solution)/shard_map/ppermute | solution.py:28
  6.5 25.8 %collective-permute-start.4 = (bf16[288,768]{1,0:T(8,128)(2,1)S(1)}, bf16[288,768]{1,0:T(8,128)(2,1)}, u32[]{:S(2)}, u32[]{:S(2)}) collective-permute-start(bf16[288,768]{1,0:T(8,128)(2,1)S(1)} %constant_dynamic-update-slice_fusion.refs_0_), channel_id=1, source_target_pairs={{0,16},{1,17},{2,18},{3,19},{4,20},{5,21},{6,22},{7,23},{8,24},{9,... | collective-permute-start | bytes 1327112 | tf_op jit(solution)/shard_map/ppermute | solution.py:28
  8.1 24.8 %collective-permute-start.5 = (bf16[288,768]{1,0:T(8,128)(2,1)S(1)}, bf16[288,768]{1,0:T(8,128)(2,1)}, u32[]{:S(2)}, u32[]{:S(2)}) collective-permute-start(bf16[288,768]{1,0:T(8,128)(2,1)S(1)} %constant_dynamic-update-slice_fusion.refs_0_), channel_id=1, source_target_pairs={{0,24},{1,25},{2,26},{3,27},{4,28},{5,29},{6,30},{7,31},{8,16},{9,... | collective-permute-start | bytes 1327112 | tf_op jit(solution)/shard_map/ppermute | solution.py:28
  8.1 27.6 %collective-permute-start.6 = (bf16[288,768]{1,0:T(8,128)(2,1)S(1)}, bf16[288,768]{1,0:T(8,128)(2,1)}, u32[]{:S(2)}, u32[]{:S(2)}) collective-permute-start(bf16[288,768]{1,0:T(8,128)(2,1)S(1)} %constant_dynamic-update-slice_fusion.refs_0_), channel_id=1, source_target_pairs={{0,4},{1,5},{2,6},{3,7},{4,0},{5,1},{6,2},{7,3},{8,12},{9,13},{10,... | collective-permute-start | bytes 1327112 | tf_op jit(solution)/shard_map/ppermute | solution.py:28
  10.7 17.1 %collective-permute-start = (f32[1,16,128]{2,1,0:T(8,128)}, f32[1,16,128]{2,1,0:T(8,128)S(1)}, u32[]{:S(2)}, u32[]{:S(2)}) collective-permute-start(f32[1,16,128]{2,1,0:T(8,128)} %bitcast.99), channel_id=1, source_target_pairs={{0,16},{1,17},{2,18},{3,19},{4,20},{5,21},{6,22},{7,23},{8,24},{9,... | collective-permute-start | bytes 24584 | tf_op jit(solution)/shard_map/ppermute | solution.py:28
  35.7 28.0 %collective-permute-start.10 = (bf16[480,768]{1,0:T(8,128)(2,1)S(1)}, bf16[480,768]{1,0:T(8,128)(2,1)S(1)}, u32[]{:S(2)}, u32[]{:S(2)}) collective-permute-start(bf16[480,768]{1,0:T(8,128)(2,1)S(1)} %slice_dynamic-update-slice_fusion.refs_0_), channel_id=1, source_target_pairs={{0,8},{1,9},{2,10},{3,11},{4,12},{5,13},{6,14},{7,15},{8,0},{9,1},... | collective-permute-start | bytes 2211848 | tf_op jit(solution)/shard_map/ppermute | solution.py:28
  35.7 33.7 %collective-permute-start.11 = (bf16[480,768]{1,0:T(8,128)(2,1)S(1)}, bf16[480,768]{1,0:T(8,128)(2,1)S(1)}, u32[]{:S(2)}, u32[]{:S(2)}) collective-permute-start(bf16[480,768]{1,0:T(8,128)(2,1)S(1)} %slice_dynamic-update-slice_fusion.refs_0_), channel_id=1, source_target_pairs={{0,16},{1,17},{2,18},{3,19},{4,20},{5,21},{6,22},{7,23},{8,24},{9,... | collective-permute-start | bytes 2211848 | tf_op jit(solution)/shard_map/ppermute | solution.py:28
  37.8 33.4 %collective-permute-start.12 = (bf16[480,768]{1,0:T(8,128)(2,1)S(1)}, bf16[480,768]{1,0:T(8,128)(2,1)}, u32[]{:S(2)}, u32[]{:S(2)}) collective-permute-start(bf16[480,768]{1,0:T(8,128)(2,1)S(1)} %slice_dynamic-update-slice_fusion.refs_0_), channel_id=1, source_target_pairs={{0,24},{1,25},{2,26},{3,27},{4,28},{5,29},{6,30},{7,31},{8,16},{9,... | collective-permute-start | bytes 2211848 | tf_op jit(solution)/shard_map/ppermute | solution.py:28
  40.9 31.5 %collective-permute-start.13 = (bf16[480,768]{1,0:T(8,128)(2,1)S(1)}, bf16[480,768]{1,0:T(8,128)(2,1)}, u32[]{:S(2)}, u32[]{:S(2)}) collective-permute-start(bf16[480,768]{1,0:T(8,128)(2,1)S(1)} %slice_dynamic-update-slice_fusion.refs_0_), channel_id=1, source_target_pairs={{0,4},{1,5},{2,6},{3,7},{4,0},{5,1},{6,2},{7,3},{8,12},{9,13},{10,... | collective-permute-start | bytes 2211848 | tf_op jit(solution)/shard_map/ppermute | solution.py:28
  71.8 29.6 %collective-permute-start.14 = (bf16[480,768]{1,0:T(8,128)(2,1)S(1)}, bf16[480,768]{1,0:T(8,128)(2,1)S(1)}, u32[]{:S(2)}, u32[]{:S(2)}) collective-permute-start(bf16[480,768]{1,0:T(8,128)(2,1)S(1)} %collective-permute-done.10.refs_1_), channel_id=1, source_target_pairs={{0,4},{1,5},{2,6},{3,7},{4,0},{5,1},{6,2},{7,3},{8,12},{9,13},{10,... | collective-permute-start | bytes 2211848 | tf_op jit(solution)/shard_map/ppermute | solution.py:28
  71.8 29.7 %collective-permute-start.15 = (bf16[480,768]{1,0:T(8,128)(2,1)S(1)}, bf16[480,768]{1,0:T(8,128)(2,1)S(1)}, u32[]{:S(2)}, u32[]{:S(2)}) collective-permute-start(bf16[480,768]{1,0:T(8,128)(2,1)S(1)} %collective-permute-done.11.refs_2_), channel_id=1, source_target_pairs={{0,4},{1,5},{2,6},{3,7},{4,0},{5,1},{6,2},{7,3},{8,12},{9,13},{10,... | collective-permute-start | bytes 2211848 | tf_op jit(solution)/shard_map/ppermute | solution.py:28
  72.4 30.5 %collective-permute-start.16 = (bf16[480,768]{1,0:T(8,128)(2,1)}, bf16[480,768]{1,0:T(8,128)(2,1)}, u32[]{:S(2)}, u32[]{:S(2)}) collective-permute-start(bf16[480,768]{1,0:T(8,128)(2,1)} %collective-permute-done.12.refs_3_), channel_id=1, source_target_pairs={{0,4},{1,5},{2,6},{3,7},{4,0},{5,1},{6,2},{7,3},{8,12},{9,13},{10,... | collective-permute-start | bytes 2211848 | tf_op jit(solution)/shard_map/ppermute | solution.py:28
  72.4 28.6 %collective-permute-start.18 = (bf16[384,768]{1,0:T(8,128)(2,1)}, bf16[384,768]{1,0:T(8,128)(2,1)S(1)}, u32[]{:S(2)}, u32[]{:S(2)}) collective-permute-start(bf16[384,768]{1,0:T(8,128)(2,1)} %refs_0_), channel_id=1, source_target_pairs={{0,16},{1,17},{2,18},{3,19},{4,20},{5,21},{6,22},{7,23},{8,24},{9,... | collective-permute-start | bytes 1769480 | tf_op jit(solution)/shard_map/ppermute | solution.py:28
  101.0 21.3 %collective-permute-start.20 = (bf16[384,768]{1,0:T(8,128)(2,1)}, bf16[384,768]{1,0:T(8,128)(2,1)}, u32[]{:S(2)}, u32[]{:S(2)}) collective-permute-start(bf16[384,768]{1,0:T(8,128)(2,1)} %refs_0_), channel_id=1, source_target_pairs={{0,4},{1,5},{2,6},{3,7},{4,0},{5,1},{6,2},{7,3},{8,12},{9,13},{10,... | collective-permute-start | bytes 1769480 | tf_op jit(solution)/shard_map/ppermute | solution.py:28
  101.0 21.3 %collective-permute-start.21 = (bf16[384,768]{1,0:T(8,128)(2,1)}, bf16[384,768]{1,0:T(8,128)(2,1)}, u32[]{:S(2)}, u32[]{:S(2)}) collective-permute-start(bf16[384,768]{1,0:T(8,128)(2,1)} %collective-permute-done.17.refs_1_), channel_id=1, source_target_pairs={{0,4},{1,5},{2,6},{3,7},{4,0},{5,1},{6,2},{7,3},{8,12},{9,13},{10,... | collective-permute-start | bytes 1769480 | tf_op jit(solution)/shard_map/ppermute | solution.py:28
  101.5 20.8 %collective-permute-start.22 = (bf16[384,768]{1,0:T(8,128)(2,1)S(1)}, bf16[384,768]{1,0:T(8,128)(2,1)}, u32[]{:S(2)}, u32[]{:S(2)}) collective-permute-start(bf16[384,768]{1,0:T(8,128)(2,1)S(1)} %collective-permute-done.18.refs_2_), channel_id=1, source_target_pairs={{0,4},{1,5},{2,6},{3,7},{4,0},{5,1},{6,2},{7,3},{8,12},{9,13},{10,... | collective-permute-start | bytes 1769480 | tf_op jit(solution)/shard_map/ppermute | solution.py:28
  102.5 19.8 %collective-permute-start.23 = (bf16[384,768]{1,0:T(8,128)(2,1)S(1)}, bf16[384,768]{1,0:T(8,128)(2,1)}, u32[]{:S(2)}, u32[]{:S(2)}) collective-permute-start(bf16[384,768]{1,0:T(8,128)(2,1)S(1)} %collective-permute-done.19.refs_3_), channel_id=1, source_target_pairs={{0,4},{1,5},{2,6},{3,7},{4,0},{5,1},{6,2},{7,3},{8,12},{9,13},{10,... | collective-permute-start | bytes 1769480 | tf_op jit(solution)/shard_map/ppermute | solution.py:28
  157.8 17.0 %collective-permute-start.24 = (bf16[4,384,768]{2,1,0:T(8,128)(2,1)}, bf16[4,384,768]{2,1,0:T(8,128)(2,1)S(1)}, u32[]{:S(2)}, u32[]{:S(2)}) collective-permute-start(bf16[4,384,768]{2,1,0:T(8,128)(2,1)} %get-tuple-element.99), channel_id=1, source_target_pairs={{0,4},{1,5},{2,6},{3,7},{4,0},{5,1},{6,2},{7,3},{8,12},{9,13},{10,... | collective-permute-start | bytes 7077896 | tf_op jit(solution)/shard_map/ppermute | solution.py:28
  188.2 39.4 %collective-permute-start.31 = (bf16[4,480,768]{2,1,0:T(8,128)(2,1)}, bf16[4,480,768]{2,1,0:T(8,128)(2,1)S(1)}, u32[]{:S(2)}, u32[]{:S(2)}) collective-permute-start(bf16[4,480,768]{2,1,0:T(8,128)(2,1)} %get-tuple-element.108), channel_id=1, source_target_pairs={{0,4},{1,5},{2,6},{3,7},{4,0},{5,1},{6,2},{7,3},{8,12},{9,13},{10,... | collective-permute-start | bytes 8847368 | tf_op jit(solution)/shard_map/ppermute | solution.py:28
  194.7 17.2 %collective-permute-start.27 = (bf16[2,192,768]{2,1,0:T(8,128)(2,1)}, bf16[2,192,768]{2,1,0:T(8,128)(2,1)}, u32[]{:S(2)}, u32[]{:S(2)}) collective-permute-start(bf16[2,192,768]{2,1,0:T(8,128)(2,1)} %get-tuple-element.103), channel_id=1, source_target_pairs={{0,16},{1,17},{2,18},{3,19},{4,20},{5,21},{6,22},{7,23},{8,24},{9,... | collective-permute-start | bytes 1769480 | tf_op jit(solution)/shard_map/ppermute | solution.py:28
  210.3 16.2 %collective-permute-start.26 = (bf16[192,768]{1,0:T(8,128)(2,1)S(1)}, bf16[192,768]{1,0:T(8,128)(2,1)}, u32[]{:S(2)}, u32[]{:S(2)}) collective-permute-start(bf16[192,768]{1,0:T(8,128)(2,1)S(1)} %slice_bitcast_fusion.6), channel_id=1, source_target_pairs={{0,16},{1,17},{2,18},{3,19},{4,20},{5,21},{6,22},{7,23},{8,24},{9,... | collective-permute-start | bytes 884744 | tf_op jit(solution)/shard_map/ppermute | solution.py:28
  213.8 22.3 %collective-permute-start.28 = (bf16[192,768]{1,0:T(8,128)(2,1)}, bf16[192,768]{1,0:T(8,128)(2,1)}, u32[]{:S(2)}, u32[]{:S(2)}) collective-permute-start(bf16[192,768]{1,0:T(8,128)(2,1)} %slice_bitcast_fusion.4), channel_id=1, source_target_pairs={{0,8},{1,9},{2,10},{3,11},{4,12},{5,13},{6,14},{7,15},{8,0},{9,1},... | collective-permute-start | bytes 884744 | tf_op jit(solution)/shard_map/ppermute | solution.py:28
  234.7 18.4 %collective-permute-start.32 = (bf16[2,240,768]{2,1,0:T(8,128)(2,1)}, bf16[2,240,768]{2,1,0:T(8,128)(2,1)}, u32[]{:S(2)}, u32[]{:S(2)}) collective-permute-start(bf16[2,240,768]{2,1,0:T(8,128)(2,1)} %get-tuple-element.110), channel_id=1, source_target_pairs={{0,8},{1,9},{2,10},{3,11},{4,12},{5,13},{6,14},{7,15},{8,0},{9,1},... | collective-permute-start | bytes 2211848 | tf_op jit(solution)/shard_map/ppermute | solution.py:28
  237.3 19.3 %collective-permute-start.29 = (bf16[192,768]{1,0:T(8,128)(2,1)S(1)}, bf16[192,768]{1,0:T(8,128)(2,1)S(1)}, u32[]{:S(2)}, u32[]{:S(2)}) collective-permute-start(bf16[192,768]{1,0:T(8,128)(2,1)S(1)} %dynamic-slice_bitcast_fusion.1), channel_id=1, source_target_pairs={{0,1},{1,0},{2,3},{3,2},{4,5},{5,4},{6,7},{7,6},{8,9},{9,8},{10,11... | collective-permute-start | bytes 884744 | tf_op jit(solution)/shard_map/ppermute | solution.py:28
  238.9 17.7 %collective-permute-start.34 = (bf16[2,240,768]{2,1,0:T(8,128)(2,1)}, bf16[2,240,768]{2,1,0:T(8,128)(2,1)S(1)}, u32[]{:S(2)}, u32[]{:S(2)}) collective-permute-start(bf16[2,240,768]{2,1,0:T(8,128)(2,1)} %get-tuple-element.112), channel_id=1, source_target_pairs={{0,16},{1,17},{2,18},{3,19},{4,20},{5,21},{6,22},{7,23},{8,24},{9,... | collective-permute-start | bytes 2211848 | tf_op jit(solution)/shard_map/ppermute | solution.py:28
  255.1 16.2 %collective-permute-start.33 = (bf16[240,768]{1,0:T(8,128)(2,1)}, bf16[240,768]{1,0:T(8,128)(2,1)}, u32[]{:S(2)}, u32[]{:S(2)}) collective-permute-start(bf16[240,768]{1,0:T(8,128)(2,1)} %slice_bitcast_fusion.3), channel_id=1, source_target_pairs={{0,16},{1,17},{2,18},{3,19},{4,20},{5,21},{6,22},{7,23},{8,24},{9,... | collective-permute-start | bytes 1105928 | tf_op jit(solution)/shard_map/ppermute | solution.py:28
  266.4 27.6 %collective-permute-start.36 = (bf16[4,304,768]{2,1,0:T(8,128)(2,1)}, bf16[4,304,768]{2,1,0:T(8,128)(2,1)S(1)}, u32[]{:S(2)}, u32[]{:S(2)}) collective-permute-start(bf16[4,304,768]{2,1,0:T(8,128)(2,1)} %get-tuple-element.128), channel_id=1, source_target_pairs={{0,4},{1,5},{2,6},{3,7},{4,0},{5,1},{6,2},{7,3},{8,12},{9,13},{10,... | collective-permute-start | bytes 5603336 | tf_op jit(solution)/shard_map/ppermute | solution.py:28
  268.7 16.5 %collective-permute-start.30 = (bf16[192,768]{1,0:T(8,128)(2,1)S(1)}, bf16[192,768]{1,0:T(8,128)(2,1)S(1)}, u32[]{:S(2)}, u32[]{:S(2)}) collective-permute-start(bf16[192,768]{1,0:T(8,128)(2,1)S(1)} %fusion.4), channel_id=1, source_target_pairs={{0,2},{1,3},{2,0},{3,1},{4,6},{5,7},{6,4},{7,5},{8,10},{9,11},{10,... | collective-permute-start | bytes 884744 | tf_op jit(solution)/shard_map/ppermute | solution.py:28
  285.2 16.0 %collective-permute-start.47 = (bf16[192,768]{1,0:T(8,128)(2,1)S(1)}, bf16[192,768]{1,0:T(8,128)(2,1)S(1)}, u32[]{:S(2)}, u32[]{:S(2)}) collective-permute-start(bf16[192,768]{1,0:T(8,128)(2,1)S(1)} %add_convert_fusion.7), channel_id=1, source_target_pairs={{0,1},{1,0},{2,3},{3,2},{4,5},{5,4},{6,7},{7,6},{8,9},{9,8},{10,11... | collective-permute-start | bytes 884744 | tf_op jit(solution)/shard_map/ppermute | solution.py:28
  293.1 19.3 %collective-permute-start.45 = (bf16[240,768]{1,0:T(8,128)(2,1)S(1)}, bf16[240,768]{1,0:T(8,128)(2,1)S(1)}, u32[]{:S(2)}, u32[]{:S(2)}) collective-permute-start(bf16[240,768]{1,0:T(8,128)(2,1)S(1)} %fusion), channel_id=1, source_target_pairs={{0,2},{1,3},{2,0},{3,1},{4,6},{5,7},{6,4},{7,5},{8,10},{9,11},{10,... | collective-permute-start | bytes 1105928 | tf_op jit(solution)/shard_map/ppermute | solution.py:28
  312.5 15.9 %collective-permute-start.46 = (bf16[240,768]{1,0:T(8,128)(2,1)S(1)}, bf16[240,768]{1,0:T(8,128)(2,1)S(1)}, u32[]{:S(2)}, u32[]{:S(2)}) collective-permute-start(bf16[240,768]{1,0:T(8,128)(2,1)S(1)} %add_convert_fusion.6), channel_id=1, source_target_pairs={{0,1},{1,0},{2,3},{3,2},{4,5},{5,4},{6,7},{7,6},{8,9},{9,8},{10,11... | collective-permute-start | bytes 1105928 | tf_op jit(solution)/shard_map/ppermute | solution.py:28
  314.1 16.0 %collective-permute-start.38 = (bf16[144,768]{1,0:T(8,128)(2,1)S(1)}, bf16[144,768]{1,0:T(8,128)(2,1)S(1)}, u32[]{:S(2)}, u32[]{:S(2)}) collective-permute-start(bf16[144,768]{1,0:T(8,128)(2,1)S(1)} %slice_bitcast_fusion.10), channel_id=1, source_target_pairs={{0,16},{1,17},{2,18},{3,19},{4,20},{5,21},{6,22},{7,23},{8,24},{9,... | collective-permute-start | bytes 663560 | tf_op jit(solution)/shard_map/ppermute | solution.py:28
  (42 other events, 534.6 us)

commit v6 on v5

--- a/solution.py
+++ b/solution.py
@@ -68,21 +68,14 @@
     rows, width = own.shape[1:]
     half = rows // 32 * 16
     lefts = [list(range(1, bits)), list(range(1, bits))]
-    split = None
-    if bits == 3:
-        split = split_add(own, received, half)
-    else:
-        chunks = add_low(own, received).reshape((2,) * (bits - 1) + (rows, width))
-        parts = [chunks[..., :half, :], chunks[..., half:, :]]
-    for step in range(1, bits):
+    chunks = add_low(own, received).reshape((2,) * (bits - 1) + (rows, width))
+    parts = [chunks[..., :half, :], chunks[..., half:, :]]
+    for _ in range(1, bits):
         kept, received = [], []
         for n, (left, end) in enumerate(zip(lefts, (0, -1))):
             b = left[end]
             axis = len(left) - 1 - left.index(b)
-            if split and step == 1:
-                keep, away = split[2 * n : 2 * n + 2]
-            else:
-                keep, away = (lax.index_in_dim(parts[n], i, axis, keepdims=False) for i in (0, 1))
+            keep, away = (lax.index_in_dim(parts[n], i, axis, keepdims=False) for i in (0, 1))
             kept.append(keep)
             received.append(swap_with(away, 1 << b))
             left.remove(b)
@@ -100,7 +93,8 @@
     mask = 2
     while mask < lax.axis_size("replica"):
         received = swap_with(kept, 0, mask)
-        yield [received]
+        wait_for = yield [received]
+        received = after(received, *(wait_for or ()))
         kept = add_low(kept, received)
         mask *= 2
     other = swap_with(kept, 0, 1)
@@ -775,47 +769,6 @@
         compiler_params=kernel_params(),
         name="deliver",
     )(odd, kept, other)
-
-
-def split_add_kernel(own, received, keep_x, away_x, keep_y, away_y):
-    slot = pl.program_id(0)
-    total = (own[0].astype(jnp.float32) + received[0].astype(jnp.float32)).astype(jnp.bfloat16)
-    half = keep_x.shape[1]
-    top, bottom = total[:half], total[half:]
-
-    @pl.when(slot % 2 == 0)
-    def _():
-        keep_x[0] = top
-
-    @pl.when(slot % 2 == 1)
-    def _():
-        away_x[0] = top
-
-    @pl.when(slot < 2)
-    def _():
-        keep_y[0] = bottom
-
-    @pl.when(slot >= 2)
-    def _():
-        away_y[0] = bottom
-
-
-def split_add(own, received, half):
-    _, rows, width = own.shape
-    block = lambda n, where: pl.BlockSpec((1, n, width), lambda s: (where(s), 0, 0))
-    table = lambda n: jax.ShapeDtypeStruct((2, n, width), jnp.bfloat16)
-    return pl.pallas_call(
-        split_add_kernel,
-        out_shape=[table(half)] * 2 + [table(rows - half)] * 2,
-        grid=(4,),
-        in_specs=[block(rows, lambda s: s)] * 2,
-        out_specs=[
-            block(half, lambda s: s // 2), block(half, lambda s: s // 2),
-            block(rows - half, lambda s: jnp.minimum(s, 1)), block(rows - half, lambda s: jnp.maximum(s - 2, 0)),
-        ],
-        compiler_params=kernel_params(),
-        name="split_add",
-    )(own, received)
 
 
 def pack_kernel(*refs):
@@ -928,9 +881,12 @@
     own, send = qkv_weight(me, rows_in, grads, attend_sums, sums1, sums2, in_bias_sum, count)
     red_a = reduction(own, send, bits)
     came_a = next(red_a)
+    came_b = came_b + next(red_b)
     h1_in = after(h1_grad, *came, *came_b, *came_a)
     came, came_b, came_a = next(red_c), next(red_b), next(red_a)
     input_grad = input_grad_of(h1_in, grads, plan_a)
+    next(red_a)
+    red_b.send(next(red_a))
     odd = lax.axis_index("replica") & 1
     sum_c, sum_b = (in_order(odd, *finish(steps)) for steps in (red_c, red_b))
     (

time: 366 us -> 340 us (0.929)
  waiting for transfers between devices: 121 us -> 99.7 us
  Pallas kernels: 172 us -> 156 us
  starting transfers between devices: 42.5 us -> 47.8 us
  other arithmetic: 14.5 us -> 19.1 us
    ppermute x48, waiting for transfers between devices: 121 us -> 99.7 us  [swap_with(): return lax.ppermute(array, AXES, pairs)]
    pallas_call x3 -> x0, Pallas kernels: 14.9 us -> none  [split_add(): pl.pallas_call(split_add_kernel, out_shape=[table(half)] * 2 + [table(row...]
    ppermute x48, starting transfers between devices: 42.5 us -> 47.8 us  [swap_with(): return lax.ppermute(array, AXES, pairs)]
    convert_element_type x18 -> x19, other arithmetic: 9.13 us -> 13.7 us  [add_low(): (left.astype(jnp.float32) + right.astype(jnp.float32)).astype(jnp.bfloat16)]
    unnamed x58 -> x40, local copies, waits for them, and re-layouts: 8.37 us -> 6.31 us
  transfers between devices with their start and end apart: 48 -> 48, of which waited for: 17 -> 16; matrix products, arithmetic and copies ran while one was open for 6% -> 9% of each run, Pallas kernels for 33% -> 28%
where the time goes in v6:
time: 340 us; the launch traced here: 339 us
  Pallas kernels  156 us (46%)
  waiting for transfers between devices  99.7 us (29%)
  starting transfers between devices  47.8 us (14%)
  other arithmetic  19.1 us (6%)
  local copies, waits for them, and re-layouts  15.2 us (4%)
    ppermute x48, waiting for transfers between devices, swap_with(): return lax.ppermute(array, AXES, pairs)  99.7 us
    ppermute x48, starting transfers between devices, swap_with(): return lax.ppermute(array, AXES, pairs)  47.8 us
    pallas_call x2, Pallas kernels, attend_back(): pl.pallas_call(attend_back_kernel, out_shape=[jax.ShapeDtypeStruct((3, to...  24.2 us
    pallas_call x1, Pallas kernels, turn(): pl.pallas_call(functools.partial(turn_kernel, plan, slots), out_shape=[sh...  24.1 us
    pallas_call x1, Pallas kernels, attend(): pl.pallas_call(functools.partial(attend_kernel, plan), out_shape=[table]...  22.6 us
    pallas_call x1, Pallas kernels, feed(): pl.pallas_call(functools.partial(feed_kernel, plan, len(before)), out_sha...  19.3 us
    pallas_call x1, Pallas kernels, return_grad(): pl.pallas_call(functools.partial(return_kernel, plan, len(before)), out_s...  16.9 us
    convert_element_type x19, other arithmetic, add_low(): (left.astype(jnp.float32) + right.astype(jnp.float32)).astype(jnp.bfloat16)  13.7 us
  transfers between devices with their start and end apart: 48, of which 16 were waited for; matrix products, arithmetic and copies ran while one was open for 9% of the time, Pallas kernels for 28%

profile of v6, /device:TPU:0, one launch (start us, length us, event | category | flops | bytes accessed | tf_op | source)
XLA Modules:
  0.0 339.1 jit_solution(13627044976041834289)
XLA Ops:
  3.5 3.0 collective-permute-start.3
  14.6 13.2 %collective-permute-done = f32[1,16,128]{2,1,0:T(8,128)S(1)} collective-permute-done((f32[1,16,128]{2,1,0:T(8,128)}, f32[1,16,128]{2,1,0:T(8,128)S(1)}, u32[]{:S(2)}, u32[]{:S(2)}) %collective-permute-start) | collective-permute-done | bytes 8224 | tf_op jit(solution)/shard_map/ppermute | solution.py:28
  28.7 3.6 %collective-permute-done.1 = f32[2,16,128]{2,1,0:T(8,128)S(1)} collective-permute-done((f32[2,16,128]{2,1,0:T(8,128)S(1)}, f32[2,16,128]{2,1,0:T(8,128)S(1)}, u32[]{:S(2)}, u32[]{:S(2)}) %collective-permute-start.1) | collective-permute-done | bytes 16416 | tf_op jit(solution)/shard_map/ppermute | solution.py:28
  35.7 2.0 collective-permute-start.11
  41.0 22.6 %attend.1 = (bf16[1024,768]{1,0:T(8,128)(2,1)}, bf16[1024,768]{1,0:T(8,128)(2,1)}, bf16[1024,768]{1,0:T(8,128)(2,1)}, bf16[1024,768]{1,0:T(8,128)(2,1)}, bf16[24,512,512]{2,1,0:T(8,128)(2,1)}) custom-call(s32[2]{0:T(128)} %lens.3, s32[1]{0:T(128)} %bitcast.me, bf16[1024,768]{1,0:T(8,128)(2,1)} %bitcast.178, f32[1,768]{1,0:T(1,128)} %get-tuple-element.141.bq, ...), custom_call_target="tpu_custom_call" | custom-call | flops 6845104128 | bytes 30000000 | tf_op jit(solution)/shard_map/attend/pallas_call | solution.py:255
  63.7 5.8 %collective-permute-done.11.refs_2_ = bf16[480,768]{1,0:T(8,128)(2,1)S(1)} collective-permute-done((bf16[480,768]{1,0:T(8,128)(2,1)S(1)}, bf16[480,768]{1,0:T(8,128)(2,1)S(1)}, u32[]{:S(2)}, u32[]{:S(2)}) %collective-permute-start.11) | collective-permute-done | bytes 737312 | tf_op jit(solution)/shard_map/ppermute | solution.py:28
  73.9 12.1 %collective-permute-done.17.refs_1_ = bf16[384,768]{1,0:T(8,128)(2,1)} collective-permute-done((bf16[384,768]{1,0:T(8,128)(2,1)}, bf16[384,768]{1,0:T(8,128)(2,1)}, u32[]{:S(2)}, u32[]{:S(2)}) %collective-permute-start.17) | collective-permute-done | bytes 589856 | tf_op jit(solution)/shard_map/ppermute | solution.py:28
  87.4 13.6 %collective-permute-done.18.refs_2_ = bf16[384,768]{1,0:T(8,128)(2,1)S(1)} collective-permute-done((bf16[384,768]{1,0:T(8,128)(2,1)}, bf16[384,768]{1,0:T(8,128)(2,1)S(1)}, u32[]{:S(2)}, u32[]{:S(2)}) %collective-permute-start.18) | collective-permute-done | bytes 589856 | tf_op jit(solution)/shard_map/ppermute | solution.py:28
  102.9 19.3 %shard_map.305 = (bf16[1024,768]{1,0:T(8,128)(2,1)}, f32[1024,768]{1,0:T(8,128)}, f32[1024,128]{1,0:T(8,128)}, bf16[1024,3072]{1,0:T(8,128)(2,1)}, bf16[1024,3072]{1,0:T(8,128)(2,1)}) custom-call(s32[1]{0:T(128)} %bitcast.me, bf16[1024,768]{1,0:T(8,128)(2,1)} %get-tuple-element.72.mixed, bf16[1024,768]{1,0:T(8,128)(2,1)} %bitcast.179, ...), custom_call_target="tpu_custom_call" | custom-call | flops 18119393280 | bytes 15000000 | tf_op jit(solution)/shard_map/pallas_call | solution.py:389
  122.3 24.1 %turn.1 = (bf16[1024,768]{1,0:T(8,128)(2,1)}, bf16[1024,768]{1,0:T(8,128)(2,1)}, bf16[1024,3072]{1,0:T(8,128)(2,1)}, f32[1024,768]{1,0:T(8,128)}, f32[8,768]{1,0:T(8,128)}, /*index=5*/f32[1,3072]{1,0:T(1,128)}) custom-call(s32[2]{0:T(128)} %lens.3, s32[1]{0:T(128)} %bitcast.me, bf16[1024,3072]{1,0:T(8,128)(2,1)} %get-tuple-element.75.active, ...), custom_call_target="tpu_custom_call" | custom-call | flops 9663676416 | bytes 30000000 | tf_op jit(solution)/shard_map/turn/pallas_call | solution.py:460
  146.4 11.4 %back_weight.1 = (bf16[4,384,768]{2,1,0:T(8,128)(2,1)}, bf16[4,384,768]{2,1,0:T(8,128)(2,1)}) custom-call(s32[1]{0:T(128)} %bitcast.me, bf16[1024,3072]{1,0:T(8,128)(2,1)} %get-tuple-element.75.active, bf16[1024,768]{1,0:T(8,128)(2,1)} %get-tuple-element.81.grad), custom_call_target="tpu_custom_call" | custom-call | flops 4831838208 | bytes 13000000 | tf_op jit(solution)/shard_map/back_weight/pallas_call | solution.py:612
  157.9 16.9 %shard_map.306 = (f32[1024,768]{1,0:T(8,128)}, bf16[1024,768]{1,0:T(8,128)(2,1)}, bf16[1024,768]{1,0:T(8,128)(2,1)}, f32[8,768]{1,0:T(8,128)}) custom-call(s32[1]{0:T(128)} %bitcast.me, bf16[1024,3072]{1,0:T(8,128)(2,1)} %get-tuple-element.83.hidden_grad, f32[1024,768]{1,0:T(8,128)} %get-tuple-element.84.h2_grad, f32[1024,768]{1,0:T(8,128)} %get-tuple-element.76.normed1, ...), custom_call_target="tpu_custom_call" | custom-call | flops 6039797760 | bytes 15000000 | tf_op jit(solution)/shard_map/pallas_call | solution.py:510
  174.9 13.3 %in_out_weight.1 = (bf16[4,480,768]{2,1,0:T(8,128)(2,1)}, bf16[4,480,768]{2,1,0:T(8,128)(2,1)}) custom-call(s32[1]{0:T(128)} %bitcast.me, bf16[1024,768]{1,0:T(8,128)(2,1)} %get-tuple-element.89.after, bf16[1024,3072]{1,0:T(8,128)(2,1)} %get-tuple-element.83.hidden_grad, bf16[1024,768]{1,0:T(8,128)(2,1)} %get-tuple-element.72.mixed, ...), custom_call_target="tpu_custom_call" | custom-call | flops 6039797760 | bytes 20000000 | tf_op jit(solution)/shard_map/in_out_weight/pallas_call | solution.py:654
  188.5 2.9 add_convert_fusion.1
  194.4 13.6 %collective-permute-done.25 = bf16[2,192,768]{2,1,0:T(8,128)(2,1)S(1)} collective-permute-done((bf16[2,192,768]{2,1,0:T(8,128)(2,1)}, bf16[2,192,768]{2,1,0:T(8,128)(2,1)S(1)}, u32[]{:S(2)}, u32[]{:S(2)}) %collective-permute-start.25) | collective-permute-done | bytes 589856 | tf_op jit(solution)/shard_map/ppermute | solution.py:28
  213.5 12.1 %shard_map.307 = (bf16[3,1024,768]{2,1,0:T(8,128)(2,1)}, f32[1,2,768]{2,1,0:T(2,128)}) custom-call(bf16[1024,768]{1,0:T(8,128)(2,1)} %get-tuple-element.95.q, bf16[1024,768]{1,0:T(8,128)(2,1)} %get-tuple-element.96.k, bf16[1024,768]{1,0:T(8,128)(2,1)} %get-tuple-element.97.v, bf16[1024,768]{1,0:T(8,128)(2,1)} %get-tuple-element.102.grad, ...), custom_call_target="tpu_custom_call" | custom-call | flops 2818572288 | bytes 15000000 | tf_op jit(solution)/shard_map/pallas_call | solution.py:312
  225.7 3.4 %add_convert_fusion = bf16[4,480,768]{2,1,0:T(8,128)(2,1)S(1)} fusion(bf16[4,480,768]{2,1,0:T(8,128)(2,1)} %collective-permute-done.31, bf16[4,480,768]{2,1,0:T(8,128)(2,1)} %get-tuple-element.92), kind=kLoop, calls=%fused_computation | loop fusion | flops 5898240 | bytes 8847360 | tf_op jit(solution)/shard_map/convert_element_type | solution.py:62
  235.2 12.1 %shard_map.308 = (bf16[3,1024,768]{2,1,0:T(8,128)(2,1)}, f32[1,2,768]{2,1,0:T(2,128)}) custom-call(bf16[1024,768]{1,0:T(8,128)(2,1)} %get-tuple-element.95.q, bf16[1024,768]{1,0:T(8,128)(2,1)} %get-tuple-element.96.k, bf16[1024,768]{1,0:T(8,128)(2,1)} %get-tuple-element.97.v, ...), custom_call_target="tpu_custom_call", output_to_operand_aliasing={{0}: (5, {})} | custom-call | flops 2818572288 | bytes 15000000 | tf_op jit(solution)/shard_map/pallas_call | solution.py:312
  249.5 9.4 %qkv_weight.1 = (bf16[4,304,768]{2,1,0:T(8,128)(2,1)}, bf16[4,304,768]{2,1,0:T(8,128)(2,1)}) custom-call(s32[1]{0:T(128)} %bitcast.me, bf16[1024,768]{1,0:T(8,128)(2,1)} %bitcast.180, bf16[3,1024,768]{2,1,0:T(8,128)(2,1)} %get-tuple-element.104.grads, f32[2,768]{1,0:T(2,128)} %bitcast_add_fusion.attend_sums, f32[8,768]{1,0:T(8,128)} %get-tuple-element.106.sums1, ...), custom_call_target="tpu_custom_call" | custom-call | flops 3623878656 | bytes 10000000 | tf_op jit(solution)/shard_map/qkv_weight/pallas_call | solution.py:732
  259.9 2.7 collective-permute-start.30
  266.3 10.3 %collective-permute-done.30 = bf16[192,768]{1,0:T(8,128)(2,1)S(1)} collective-permute-done((bf16[192,768]{1,0:T(8,128)(2,1)S(1)}, bf16[192,768]{1,0:T(8,128)(2,1)S(1)}, u32[]{:S(2)}, u32[]{:S(2)}) %collective-permute-start.30) | collective-permute-done | bytes 294944 | tf_op jit(solution)/shard_map/ppermute | solution.py:28
  277.7 2.1 add_convert_fusion.2
  283.3 8.4 %collective-permute-done.38 = bf16[2,144,768]{2,1,0:T(8,128)(2,1)S(1)} collective-permute-done((bf16[2,144,768]{2,1,0:T(8,128)(2,1)S(1)}, bf16[2,144,768]{2,1,0:T(8,128)(2,1)S(1)}, u32[]{:S(2)}, u32[]{:S(2)}) %collective-permute-start.38) | collective-permute-done | bytes 442400 | tf_op jit(solution)/shard_map/ppermute | solution.py:28
  292.4 2.0 collective-permute-done.40
  294.6 2.4 collective-permute-start.41
  297.1 2.2 collective-permute-start.45
  304.0 9.6 %collective-permute-done.45 = bf16[240,768]{1,0:T(8,128)(2,1)S(1)} collective-permute-done((bf16[240,768]{1,0:T(8,128)(2,1)S(1)}, bf16[240,768]{1,0:T(8,128)(2,1)S(1)}, u32[]{:S(2)}, u32[]{:S(2)}) %collective-permute-start.45) | collective-permute-done | bytes 368672 | tf_op jit(solution)/shard_map/ppermute | solution.py:28
  314.5 4.2 %collective-permute-start.43 = (bf16[152,768]{1,0:T(8,128)(2,1)S(1)}, bf16[152,768]{1,0:T(8,128)(2,1)S(1)}, u32[]{:S(2)}, u32[]{:S(2)}) collective-permute-start(bf16[152,768]{1,0:T(8,128)(2,1)S(1)} %fusion.14), channel_id=1, source_target_pairs={{0,2},{1,3},{2,0},{3,1},{4,6},{5,7},{6,4},{7,5},{8,10},{9,11},{10,... | collective-permute-start | bytes 700424 | tf_op jit(solution)/shard_map/ppermute | solution.py:28
  318.7 9.7 %input_grad.1 = bf16[1024,768]{1,0:T(8,128)(2,1)} custom-call(s32[1]{0:T(128)} %bitcast.me, f32[1024,768]{1,0:T(8,128)} %get-tuple-element.110.h1_grad, bf16[3,1024,768]{2,1,0:T(8,128)(2,1)} %get-tuple-element.104.grads, bf16[288,768]{1,0:T(8,128)(2,1)} %copy-done.7, bf16[288,768]{1,0:T(8,128)(2,1)} %copy-done.16, ...), custom_call_target="tpu_custom_call" | custom-call | flops 3623878656 | bytes 20000000 | tf_op jit(solution)/shard_map/input_grad/pallas_call | solution.py:544
  328.5 3.2 collective-permute-start.44
  333.9 2.3 collective-permute-done.44.other
  336.9 2.0 deliver.1
  (168 shorter events, 62.2 us)
Async XLA Ops:
  3.5 25.1 %collective-permute-start.3 = (bf16[288,768]{1,0:T(8,128)(2,1)S(1)}, bf16[288,768]{1,0:T(8,128)(2,1)S(1)}, u32[]{:S(2)}, u32[]{:S(2)}) collective-permute-start(bf16[288,768]{1,0:T(8,128)(2,1)S(1)} %constant_dynamic-update-slice_fusion.refs_0_), channel_id=1, source_target_pairs={{0,8},{1,9},{2,10},{3,11},{4,12},{5,13},{6,14},{7,15},{8,0},{9,1},... | collective-permute-start | bytes 1327112 | tf_op jit(solution)/shard_map/ppermute | solution.py:28
  6.5 25.8 %collective-permute-start.4 = (bf16[288,768]{1,0:T(8,128)(2,1)S(1)}, bf16[288,768]{1,0:T(8,128)(2,1)}, u32[]{:S(2)}, u32[]{:S(2)}) collective-permute-start(bf16[288,768]{1,0:T(8,128)(2,1)S(1)} %constant_dynamic-update-slice_fusion.refs_0_), channel_id=1, source_target_pairs={{0,16},{1,17},{2,18},{3,19},{4,20},{5,21},{6,22},{7,23},{8,24},{9,... | collective-permute-start | bytes 1327112 | tf_op jit(solution)/shard_map/ppermute | solution.py:28
  8.1 24.8 %collective-permute-start.5 = (bf16[288,768]{1,0:T(8,128)(2,1)S(1)}, bf16[288,768]{1,0:T(8,128)(2,1)}, u32[]{:S(2)}, u32[]{:S(2)}) collective-permute-start(bf16[288,768]{1,0:T(8,128)(2,1)S(1)} %constant_dynamic-update-slice_fusion.refs_0_), channel_id=1, source_target_pairs={{0,24},{1,25},{2,26},{3,27},{4,28},{5,29},{6,30},{7,31},{8,16},{9,... | collective-permute-start | bytes 1327112 | tf_op jit(solution)/shard_map/ppermute | solution.py:28
  8.1 27.6 %collective-permute-start.6 = (bf16[288,768]{1,0:T(8,128)(2,1)S(1)}, bf16[288,768]{1,0:T(8,128)(2,1)}, u32[]{:S(2)}, u32[]{:S(2)}) collective-permute-start(bf16[288,768]{1,0:T(8,128)(2,1)S(1)} %constant_dynamic-update-slice_fusion.refs_0_), channel_id=1, source_target_pairs={{0,4},{1,5},{2,6},{3,7},{4,0},{5,1},{6,2},{7,3},{8,12},{9,13},{10,... | collective-permute-start | bytes 1327112 | tf_op jit(solution)/shard_map/ppermute | solution.py:28
  10.7 17.1 %collective-permute-start = (f32[1,16,128]{2,1,0:T(8,128)}, f32[1,16,128]{2,1,0:T(8,128)S(1)}, u32[]{:S(2)}, u32[]{:S(2)}) collective-permute-start(f32[1,16,128]{2,1,0:T(8,128)} %bitcast.164), channel_id=1, source_target_pairs={{0,16},{1,17},{2,18},{3,19},{4,20},{5,21},{6,22},{7,23},{8,24},{9,... | collective-permute-start | bytes 24584 | tf_op jit(solution)/shard_map/ppermute | solution.py:28
  35.7 27.9 %collective-permute-start.10 = (bf16[480,768]{1,0:T(8,128)(2,1)S(1)}, bf16[480,768]{1,0:T(8,128)(2,1)S(1)}, u32[]{:S(2)}, u32[]{:S(2)}) collective-permute-start(bf16[480,768]{1,0:T(8,128)(2,1)S(1)} %slice_dynamic-update-slice_fusion.refs_0_), channel_id=1, source_target_pairs={{0,8},{1,9},{2,10},{3,11},{4,12},{5,13},{6,14},{7,15},{8,0},{9,1},... | collective-permute-start | bytes 2211848 | tf_op jit(solution)/shard_map/ppermute | solution.py:28
  35.7 33.7 %collective-permute-start.11 = (bf16[480,768]{1,0:T(8,128)(2,1)S(1)}, bf16[480,768]{1,0:T(8,128)(2,1)S(1)}, u32[]{:S(2)}, u32[]{:S(2)}) collective-permute-start(bf16[480,768]{1,0:T(8,128)(2,1)S(1)} %slice_dynamic-update-slice_fusion.refs_0_), channel_id=1, source_target_pairs={{0,16},{1,17},{2,18},{3,19},{4,20},{5,21},{6,22},{7,23},{8,24},{9,... | collective-permute-start | bytes 2211848 | tf_op jit(solution)/shard_map/ppermute | solution.py:28
  37.8 33.4 %collective-permute-start.12 = (bf16[480,768]{1,0:T(8,128)(2,1)S(1)}, bf16[480,768]{1,0:T(8,128)(2,1)}, u32[]{:S(2)}, u32[]{:S(2)}) collective-permute-start(bf16[480,768]{1,0:T(8,128)(2,1)S(1)} %slice_dynamic-update-slice_fusion.refs_0_), channel_id=1, source_target_pairs={{0,24},{1,25},{2,26},{3,27},{4,28},{5,29},{6,30},{7,31},{8,16},{9,... | collective-permute-start | bytes 2211848 | tf_op jit(solution)/shard_map/ppermute | solution.py:28
  40.9 31.5 %collective-permute-start.13 = (bf16[480,768]{1,0:T(8,128)(2,1)S(1)}, bf16[480,768]{1,0:T(8,128)(2,1)}, u32[]{:S(2)}, u32[]{:S(2)}) collective-permute-start(bf16[480,768]{1,0:T(8,128)(2,1)S(1)} %slice_dynamic-update-slice_fusion.refs_0_), channel_id=1, source_target_pairs={{0,4},{1,5},{2,6},{3,7},{4,0},{5,1},{6,2},{7,3},{8,12},{9,13},{10,... | collective-permute-start | bytes 2211848 | tf_op jit(solution)/shard_map/ppermute | solution.py:28
  71.8 29.6 %collective-permute-start.14 = (bf16[480,768]{1,0:T(8,128)(2,1)S(1)}, bf16[480,768]{1,0:T(8,128)(2,1)S(1)}, u32[]{:S(2)}, u32[]{:S(2)}) collective-permute-start(bf16[480,768]{1,0:T(8,128)(2,1)S(1)} %collective-permute-done.10.refs_1_), channel_id=1, source_target_pairs={{0,4},{1,5},{2,6},{3,7},{4,0},{5,1},{6,2},{7,3},{8,12},{9,13},{10,... | collective-permute-start | bytes 2211848 | tf_op jit(solution)/shard_map/ppermute | solution.py:28
  71.8 29.7 %collective-permute-start.15 = (bf16[480,768]{1,0:T(8,128)(2,1)S(1)}, bf16[480,768]{1,0:T(8,128)(2,1)S(1)}, u32[]{:S(2)}, u32[]{:S(2)}) collective-permute-start(bf16[480,768]{1,0:T(8,128)(2,1)S(1)} %collective-permute-done.11.refs_2_), channel_id=1, source_target_pairs={{0,4},{1,5},{2,6},{3,7},{4,0},{5,1},{6,2},{7,3},{8,12},{9,13},{10,... | collective-permute-start | bytes 2211848 | tf_op jit(solution)/shard_map/ppermute | solution.py:28
  72.4 30.5 %collective-permute-start.16 = (bf16[480,768]{1,0:T(8,128)(2,1)}, bf16[480,768]{1,0:T(8,128)(2,1)}, u32[]{:S(2)}, u32[]{:S(2)}) collective-permute-start(bf16[480,768]{1,0:T(8,128)(2,1)} %collective-permute-done.12.refs_3_), channel_id=1, source_target_pairs={{0,4},{1,5},{2,6},{3,7},{4,0},{5,1},{6,2},{7,3},{8,12},{9,13},{10,... | collective-permute-start | bytes 2211848 | tf_op jit(solution)/shard_map/ppermute | solution.py:28
  72.4 28.6 %collective-permute-start.18 = (bf16[384,768]{1,0:T(8,128)(2,1)}, bf16[384,768]{1,0:T(8,128)(2,1)S(1)}, u32[]{:S(2)}, u32[]{:S(2)}) collective-permute-start(bf16[384,768]{1,0:T(8,128)(2,1)} %refs_0_), channel_id=1, source_target_pairs={{0,16},{1,17},{2,18},{3,19},{4,20},{5,21},{6,22},{7,23},{8,24},{9,... | collective-permute-start | bytes 1769480 | tf_op jit(solution)/shard_map/ppermute | solution.py:28
  86.0 15.0 %collective-permute-start.19 = (bf16[384,768]{1,0:T(8,128)(2,1)}, bf16[384,768]{1,0:T(8,128)(2,1)S(1)}, u32[]{:S(2)}, u32[]{:S(2)}) collective-permute-start(bf16[384,768]{1,0:T(8,128)(2,1)} %refs_0_), channel_id=1, source_target_pairs={{0,24},{1,25},{2,26},{3,27},{4,28},{5,29},{6,30},{7,31},{8,16},{9,... | collective-permute-start | bytes 1769480 | tf_op jit(solution)/shard_map/ppermute | solution.py:28
  101.0 21.3 %collective-permute-start.20 = (bf16[384,768]{1,0:T(8,128)(2,1)}, bf16[384,768]{1,0:T(8,128)(2,1)}, u32[]{:S(2)}, u32[]{:S(2)}) collective-permute-start(bf16[384,768]{1,0:T(8,128)(2,1)} %refs_0_), channel_id=1, source_target_pairs={{0,4},{1,5},{2,6},{3,7},{4,0},{5,1},{6,2},{7,3},{8,12},{9,13},{10,... | collective-permute-start | bytes 1769480 | tf_op jit(solution)/shard_map/ppermute | solution.py:28
  101.0 21.3 %collective-permute-start.21 = (bf16[384,768]{1,0:T(8,128)(2,1)}, bf16[384,768]{1,0:T(8,128)(2,1)}, u32[]{:S(2)}, u32[]{:S(2)}) collective-permute-start(bf16[384,768]{1,0:T(8,128)(2,1)} %collective-permute-done.17.refs_1_), channel_id=1, source_target_pairs={{0,4},{1,5},{2,6},{3,7},{4,0},{5,1},{6,2},{7,3},{8,12},{9,13},{10,... | collective-permute-start | bytes 1769480 | tf_op jit(solution)/shard_map/ppermute | solution.py:28
  101.5 20.8 %collective-permute-start.22 = (bf16[384,768]{1,0:T(8,128)(2,1)S(1)}, bf16[384,768]{1,0:T(8,128)(2,1)}, u32[]{:S(2)}, u32[]{:S(2)}) collective-permute-start(bf16[384,768]{1,0:T(8,128)(2,1)S(1)} %collective-permute-done.18.refs_2_), channel_id=1, source_target_pairs={{0,4},{1,5},{2,6},{3,7},{4,0},{5,1},{6,2},{7,3},{8,12},{9,13},{10,... | collective-permute-start | bytes 1769480 | tf_op jit(solution)/shard_map/ppermute | solution.py:28
  102.5 19.7 %collective-permute-start.23 = (bf16[384,768]{1,0:T(8,128)(2,1)S(1)}, bf16[384,768]{1,0:T(8,128)(2,1)}, u32[]{:S(2)}, u32[]{:S(2)}) collective-permute-start(bf16[384,768]{1,0:T(8,128)(2,1)S(1)} %collective-permute-done.19.refs_3_), channel_id=1, source_target_pairs={{0,4},{1,5},{2,6},{3,7},{4,0},{5,1},{6,2},{7,3},{8,12},{9,13},{10,... | collective-permute-start | bytes 1769480 | tf_op jit(solution)/shard_map/ppermute | solution.py:28
  157.7 17.1 %collective-permute-start.24 = (bf16[4,384,768]{2,1,0:T(8,128)(2,1)}, bf16[4,384,768]{2,1,0:T(8,128)(2,1)S(1)}, u32[]{:S(2)}, u32[]{:S(2)}) collective-permute-start(bf16[4,384,768]{2,1,0:T(8,128)(2,1)} %get-tuple-element.88), channel_id=1, source_target_pairs={{0,4},{1,5},{2,6},{3,7},{4,0},{5,1},{6,2},{7,3},{8,12},{9,13},{10,... | collective-permute-start | bytes 7077896 | tf_op jit(solution)/shard_map/ppermute | solution.py:28
  188.2 37.5 %collective-permute-start.31 = (bf16[4,480,768]{2,1,0:T(8,128)(2,1)}, bf16[4,480,768]{2,1,0:T(8,128)(2,1)}, u32[]{:S(2)}, u32[]{:S(2)}) collective-permute-start(bf16[4,480,768]{2,1,0:T(8,128)(2,1)} %get-tuple-element.93), channel_id=1, source_target_pairs={{0,4},{1,5},{2,6},{3,7},{4,0},{5,1},{6,2},{7,3},{8,12},{9,13},{10,... | collective-permute-start | bytes 8847368 | tf_op jit(solution)/shard_map/ppermute | solution.py:28
  192.3 15.7 %collective-permute-start.25 = (bf16[2,192,768]{2,1,0:T(8,128)(2,1)}, bf16[2,192,768]{2,1,0:T(8,128)(2,1)S(1)}, u32[]{:S(2)}, u32[]{:S(2)}) collective-permute-start(bf16[2,192,768]{2,1,0:T(8,128)(2,1)} %slice_bitcast_fusion.6), channel_id=1, source_target_pairs={{0,8},{1,9},{2,10},{3,11},{4,12},{5,13},{6,14},{7,15},{8,0},{9,1},... | collective-permute-start | bytes 1769480 | tf_op jit(solution)/shard_map/ppermute | solution.py:28
  193.7 15.3 %collective-permute-start.27 = (bf16[2,192,768]{2,1,0:T(8,128)(2,1)S(1)}, bf16[2,192,768]{2,1,0:T(8,128)(2,1)}, u32[]{:S(2)}, u32[]{:S(2)}) collective-permute-start(bf16[2,192,768]{2,1,0:T(8,128)(2,1)S(1)} %slice_bitcast_fusion.4), channel_id=1, source_target_pairs={{0,16},{1,17},{2,18},{3,19},{4,20},{5,21},{6,22},{7,23},{8,24},{9,... | collective-permute-start | bytes 1769480 | tf_op jit(solution)/shard_map/ppermute | solution.py:28
  210.5 15.1 %collective-permute-start.26 = (bf16[192,768]{1,0:T(8,128)(2,1)S(1)}, bf16[192,768]{1,0:T(8,128)(2,1)S(1)}, u32[]{:S(2)}, u32[]{:S(2)}) collective-permute-start(bf16[192,768]{1,0:T(8,128)(2,1)S(1)} %slice_bitcast_fusion.18), channel_id=1, source_target_pairs={{0,16},{1,17},{2,18},{3,19},{4,20},{5,21},{6,22},{7,23},{8,24},{9,... | collective-permute-start | bytes 884744 | tf_op jit(solution)/shard_map/ppermute | solution.py:28
  212.7 20.1 %collective-permute-start.28 = (bf16[192,768]{1,0:T(8,128)(2,1)}, bf16[192,768]{1,0:T(8,128)(2,1)S(1)}, u32[]{:S(2)}, u32[]{:S(2)}) collective-permute-start(bf16[192,768]{1,0:T(8,128)(2,1)} %slice_bitcast_fusion.16), channel_id=1, source_target_pairs={{0,8},{1,9},{2,10},{3,11},{4,12},{5,13},{6,14},{7,15},{8,0},{9,1},... | collective-permute-start | bytes 884744 | tf_op jit(solution)/shard_map/ppermute | solution.py:28
  230.0 18.6 %collective-permute-start.32 = (bf16[2,240,768]{2,1,0:T(8,128)(2,1)}, bf16[2,240,768]{2,1,0:T(8,128)(2,1)}, u32[]{:S(2)}, u32[]{:S(2)}) collective-permute-start(bf16[2,240,768]{2,1,0:T(8,128)(2,1)} %slice_bitcast_fusion.2), channel_id=1, source_target_pairs={{0,8},{1,9},{2,10},{3,11},{4,12},{5,13},{6,14},{7,15},{8,0},{9,1},... | collective-permute-start | bytes 2211848 | tf_op jit(solution)/shard_map/ppermute | solution.py:28
  232.1 17.4 %collective-permute-start.34 = (bf16[2,240,768]{2,1,0:T(8,128)(2,1)}, bf16[2,240,768]{2,1,0:T(8,128)(2,1)}, u32[]{:S(2)}, u32[]{:S(2)}) collective-permute-start(bf16[2,240,768]{2,1,0:T(8,128)(2,1)} %slice_bitcast_fusion), channel_id=1, source_target_pairs={{0,16},{1,17},{2,18},{3,19},{4,20},{5,21},{6,22},{7,23},{8,24},{9,... | collective-permute-start | bytes 2211848 | tf_op jit(solution)/shard_map/ppermute | solution.py:28
  258.8 18.8 %collective-permute-start.37 = (bf16[4,304,768]{2,1,0:T(8,128)(2,1)}, bf16[4,304,768]{2,1,0:T(8,128)(2,1)}, u32[]{:S(2)}, u32[]{:S(2)}) collective-permute-start(bf16[4,304,768]{2,1,0:T(8,128)(2,1)} %get-tuple-element.109), channel_id=1, source_target_pairs={{0,4},{1,5},{2,6},{3,7},{4,0},{5,1},{6,2},{7,3},{8,12},{9,13},{10,... | collective-permute-start | bytes 5603336 | tf_op jit(solution)/shard_map/ppermute | solution.py:28
  259.9 16.7 %collective-permute-start.30 = (bf16[192,768]{1,0:T(8,128)(2,1)S(1)}, bf16[192,768]{1,0:T(8,128)(2,1)S(1)}, u32[]{:S(2)}, u32[]{:S(2)}) collective-permute-start(bf16[192,768]{1,0:T(8,128)(2,1)S(1)} %fusion.10), channel_id=1, source_target_pairs={{0,2},{1,3},{2,0},{3,1},{4,6},{5,7},{6,4},{7,5},{8,10},{9,11},{10,... | collective-permute-start | bytes 884744 | tf_op jit(solution)/shard_map/ppermute | solution.py:28
  276.7 26.2 %collective-permute-start.47 = (bf16[192,768]{1,0:T(8,128)(2,1)S(1)}, bf16[192,768]{1,0:T(8,128)(2,1)S(1)}, u32[]{:S(2)}, u32[]{:S(2)}) collective-permute-start(bf16[192,768]{1,0:T(8,128)(2,1)S(1)} %add_convert_fusion.4), channel_id=1, source_target_pairs={{0,1},{1,0},{2,3},{3,2},{4,5},{5,4},{6,7},{7,6},{8,9},{9,8},{10,11... | collective-permute-start | bytes 884744 | tf_op jit(solution)/shard_map/ppermute | solution.py:28
  280.5 16.5 %collective-permute-start.36 = (bf16[240,768]{1,0:T(8,128)(2,1)S(1)}, bf16[240,768]{1,0:T(8,128)(2,1)S(1)}, u32[]{:S(2)}, u32[]{:S(2)}) collective-permute-start(bf16[240,768]{1,0:T(8,128)(2,1)S(1)} %dynamic-slice_bitcast_fusion), channel_id=1, source_target_pairs={{0,1},{1,0},{2,3},{3,2},{4,5},{5,4},{6,7},{7,6},{8,9},{9,8},{10,11... | collective-permute-start | bytes 1105928 | tf_op jit(solution)/shard_map/ppermute | solution.py:28
  297.1 16.4 %collective-permute-start.45 = (bf16[240,768]{1,0:T(8,128)(2,1)S(1)}, bf16[240,768]{1,0:T(8,128)(2,1)S(1)}, u32[]{:S(2)}, u32[]{:S(2)}) collective-permute-start(bf16[240,768]{1,0:T(8,128)(2,1)S(1)} %fusion.6), channel_id=1, source_target_pairs={{0,2},{1,3},{2,0},{3,1},{4,6},{5,7},{6,4},{7,5},{8,10},{9,11},{10,... | collective-permute-start | bytes 1105928 | tf_op jit(solution)/shard_map/ppermute | solution.py:28
  313.6 18.1 %collective-permute-start.46 = (bf16[240,768]{1,0:T(8,128)(2,1)S(1)}, bf16[240,768]{1,0:T(8,128)(2,1)S(1)}, u32[]{:S(2)}, u32[]{:S(2)}) collective-permute-start(bf16[240,768]{1,0:T(8,128)(2,1)S(1)} %add_convert_fusion.3), channel_id=1, source_target_pairs={{0,1},{1,0},{2,3},{3,2},{4,5},{5,4},{6,7},{7,6},{8,9},{9,8},{10,11... | collective-permute-start | bytes 1105928 | tf_op jit(solution)/shard_map/ppermute | solution.py:28
  (33 other events, 425.6 us)

commit v7 on v6

--- a/solution.py
+++ b/solution.py
@@ -71,15 +71,16 @@
     chunks = add_low(own, received).reshape((2,) * (bits - 1) + (rows, width))
     parts = [chunks[..., :half, :], chunks[..., half:, :]]
     for _ in range(1, bits):
-        kept, received = [], []
+        kept, received, leaving = [], [], []
         for n, (left, end) in enumerate(zip(lefts, (0, -1))):
             b = left[end]
             axis = len(left) - 1 - left.index(b)
             keep, away = (lax.index_in_dim(parts[n], i, axis, keepdims=False) for i in (0, 1))
             kept.append(keep)
+            leaving.append(away)
             received.append(swap_with(away, 1 << b))
             left.remove(b)
-        yield received
+        yield received + leaving
         parts = [add_low(keep, got) for keep, got in zip(kept, received)]
     total = jnp.concatenate(parts)
     at = lax.axis_index("replica")
@@ -88,7 +89,8 @@
         yield pair[0], pair[1]
         return
     received = swap_with(pick(pair, 0, 1 - (at & 1)), 0, 1)
-    yield [received]
+    wait_for = yield [received]
+    received = after(received, *(wait_for or ()))
     kept = add_low(pick(pair, 0, at & 1), received)
     mask = 2
     while mask < lax.axis_size("replica"):
@@ -681,7 +683,7 @@
 def small_tile(vectors, wide, g, count, width):
     size, wide_size = width // count, wide.shape[1] // count
     part = slice(g * size, (g + 1) * size)
-    tops = [ref[rows, part] for ref, rows in vectors]
+    tops = [sum(ref[0, :, part] for ref in vectors[0])] + [ref[rows, part] for ref, rows in vectors[1:]]
     fill = lambda rows, used: jnp.zeros((rows, width - used), jnp.float32)
     top = jnp.concatenate(tops, axis=0)
     eight = jnp.concatenate([top, fill(8, size)], axis=1)
@@ -689,7 +691,8 @@
     return jnp.concatenate([eight, last, jnp.zeros((7, width), jnp.float32)], axis=0).astype(jnp.bfloat16)
 
 
-def qkv_weight_kernel(me, rows, grads, attend_sums, sums1, sums2, wide, own, send):
+def qkv_weight_kernel(me, rows, grads, sums1, sums2, wide, *refs):
+    attend_sums, (own, send) = refs[:-2], refs[-2:]
     step = pl.program_id(0)
     count, width = 2 * own.shape[0], own.shape[2]
     chunk = width // count
@@ -718,7 +721,7 @@
     @pl.when(step == 0)
     def _():
         vectors = (
-            (attend_sums, slice(0, 2)), (sums1, slice(2, 3)), (sums2, slice(2, 3)),
+            attend_sums, (sums1, slice(2, 3)), (sums2, slice(2, 3)),
             (sums1, slice(0, 2)), (sums2, slice(0, 2)),
         )
         for g in range(count):
@@ -736,13 +739,13 @@
             num_scalar_prefetch=1,
             grid=(3,),
             in_specs=[whole(rows), pl.BlockSpec((1, total, width), lambda j, me: (j, 0, 0))]
-            + [whole(a) for a in (attend_sums, sums1, sums2, wide)],
+            + [whole(a) for a in (sums1, sums2, wide, *attend_sums)],
             out_specs=[block] * 2,
         ),
         compiler_params=kernel_params(),
         cost_estimate=cost(6 * total * width * width, 1e7),
         name="qkv_weight",
-    )(me, rows, grads, attend_sums, sums1, sums2, wide)
+    )(me, rows, grads, sums1, sums2, wide, *attend_sums)
 
 
 def deliver_kernel(odd, kept, other, *outs):
@@ -870,20 +873,21 @@
     mixed_grad = after(mixed_grad, send, *came)
     came, came_b = next(red_c), next(red_b)
     grads, sums_at = attend_back(seqs, 0, q, k, v, mixed_grad, probs)
-    attend_sums = sums_at[0]
+    attend_sums = [sums_at]
     for seq in range(1, seqs):
-        mixed_grad = after(mixed_grad, attend_sums, *came, *came_b)
+        mixed_grad = after(mixed_grad, *attend_sums, *came, *came_b)
         came, came_b = next(red_c), next(red_b)
         grads, sums_at = attend_back(seqs, seq, q, k, v, mixed_grad, probs, (grads,))
-        attend_sums = attend_sums + sums_at[0]
+        attend_sums = attend_sums + [sums_at]
     rows_in = after(x, *came, *came_b)
     came, came_b = next(red_c), next(red_b)
     own, send = qkv_weight(me, rows_in, grads, attend_sums, sums1, sums2, in_bias_sum, count)
     red_a = reduction(own, send, bits)
     came_a = next(red_a)
-    came_b = came_b + next(red_b)
-    h1_in = after(h1_grad, *came, *came_b, *came_a)
-    came, came_b, came_a = next(red_c), next(red_b), next(red_a)
+    came_b = came_b[:2] + next(red_b)
+    leaving = next(red_a)[-2:]
+    h1_in = after(h1_grad, *came, *came_b, *leaving)
+    came, _ = next(red_c), red_b.send(leaving)
     input_grad = input_grad_of(h1_in, grads, plan_a)
     next(red_a)
     red_b.send(next(red_a))

time: 340 us -> 343 us (level)
  waiting for transfers between devices: 99.7 us -> 105 us
    ppermute x48, waiting for transfers between devices: 99.7 us -> 105 us  [swap_with(): return lax.ppermute(array, AXES, pairs)]
    unnamed x40 -> x42, local copies, waits for them, and re-layouts: 6.31 us -> 7.86 us
  transfers between devices with their start and end apart: 48 -> 48, of which waited for: 16 -> 21; matrix products, arithmetic and copies ran while one was open for 9% -> 6% of each run, Pallas kernels for 28% -> 28%
where the time goes in v7:
time: 343 us; the launch traced here: 342 us
  Pallas kernels  156 us (45%)
  waiting for transfers between devices  105 us (31%)
  starting transfers between devices  44.7 us (13%)
  other arithmetic  17.7 us (5%)
  local copies, waits for them, and re-layouts  16.7 us (5%)
    ppermute x48, waiting for transfers between devices, swap_with(): return lax.ppermute(array, AXES, pairs)  105 us
    ppermute x48, starting transfers between devices, swap_with(): return lax.ppermute(array, AXES, pairs)  44.7 us
    pallas_call x2, Pallas kernels, attend_back(): pl.pallas_call(attend_back_kernel, out_shape=[jax.ShapeDtypeStruct((3, to...  24.4 us
    pallas_call x1, Pallas kernels, turn(): pl.pallas_call(functools.partial(turn_kernel, plan, slots), out_shape=[sh...  24.1 us
    pallas_call x1, Pallas kernels, attend(): pl.pallas_call(functools.partial(attend_kernel, plan), out_shape=[table]...  22.7 us
    pallas_call x1, Pallas kernels, feed(): pl.pallas_call(functools.partial(feed_kernel, plan, len(before)), out_sha...  19.3 us
    pallas_call x1, Pallas kernels, return_grad(): pl.pallas_call(functools.partial(return_kernel, plan, len(before)), out_s...  16.8 us
    convert_element_type x19, other arithmetic, add_low(): (left.astype(jnp.float32) + right.astype(jnp.float32)).astype(jnp.bfloat16)  13.6 us
  transfers between devices with their start and end apart: 48, of which 21 were waited for; matrix products, arithmetic and copies ran while one was open for 6% of the time, Pallas kernels for 28%

profile of v7, /device:TPU:0, one launch (start us, length us, event | category | flops | bytes accessed | tf_op | source)
XLA Modules:
  0.0 342.0 jit_solution(7024282523537287556)
XLA Ops:
  3.5 3.0 collective-permute-start.3
  14.6 13.2 %collective-permute-done = f32[1,16,128]{2,1,0:T(8,128)S(1)} collective-permute-done((f32[1,16,128]{2,1,0:T(8,128)}, f32[1,16,128]{2,1,0:T(8,128)S(1)}, u32[]{:S(2)}, u32[]{:S(2)}) %collective-permute-start) | collective-permute-done | bytes 8224 | tf_op jit(solution)/shard_map/ppermute | solution.py:28
  28.7 3.6 %collective-permute-done.1 = f32[2,16,128]{2,1,0:T(8,128)S(1)} collective-permute-done((f32[2,16,128]{2,1,0:T(8,128)S(1)}, f32[2,16,128]{2,1,0:T(8,128)S(1)}, u32[]{:S(2)}, u32[]{:S(2)}) %collective-permute-start.1) | collective-permute-done | bytes 16416 | tf_op jit(solution)/shard_map/ppermute | solution.py:28
  35.7 2.0 collective-permute-start.11
  41.0 22.7 %attend.1 = (bf16[1024,768]{1,0:T(8,128)(2,1)}, bf16[1024,768]{1,0:T(8,128)(2,1)}, bf16[1024,768]{1,0:T(8,128)(2,1)}, bf16[1024,768]{1,0:T(8,128)(2,1)}, bf16[24,512,512]{2,1,0:T(8,128)(2,1)}) custom-call(s32[2]{0:T(128)} %lens.3, s32[1]{0:T(128)} %bitcast.me, bf16[1024,768]{1,0:T(8,128)(2,1)} %bitcast.174, f32[1,768]{1,0:T(1,128)} %get-tuple-element.143.bq, ...), custom_call_target="tpu_custom_call" | custom-call | flops 6845104128 | bytes 30000000 | tf_op jit(solution)/shard_map/attend/pallas_call | solution.py:257
  63.7 5.7 %collective-permute-done.11.refs_2_ = bf16[480,768]{1,0:T(8,128)(2,1)S(1)} collective-permute-done((bf16[480,768]{1,0:T(8,128)(2,1)S(1)}, bf16[480,768]{1,0:T(8,128)(2,1)S(1)}, u32[]{:S(2)}, u32[]{:S(2)}) %collective-permute-start.11) | collective-permute-done | bytes 737312 | tf_op jit(solution)/shard_map/ppermute | solution.py:28
  73.9 12.1 %collective-permute-done.17.refs_1_ = bf16[384,768]{1,0:T(8,128)(2,1)} collective-permute-done((bf16[384,768]{1,0:T(8,128)(2,1)}, bf16[384,768]{1,0:T(8,128)(2,1)}, u32[]{:S(2)}, u32[]{:S(2)}) %collective-permute-start.17) | collective-permute-done | bytes 589856 | tf_op jit(solution)/shard_map/ppermute | solution.py:28
  87.4 13.6 %collective-permute-done.18.refs_2_ = bf16[384,768]{1,0:T(8,128)(2,1)S(1)} collective-permute-done((bf16[384,768]{1,0:T(8,128)(2,1)}, bf16[384,768]{1,0:T(8,128)(2,1)S(1)}, u32[]{:S(2)}, u32[]{:S(2)}) %collective-permute-start.18) | collective-permute-done | bytes 589856 | tf_op jit(solution)/shard_map/ppermute | solution.py:28
  102.9 19.3 %shard_map.305 = (bf16[1024,768]{1,0:T(8,128)(2,1)}, f32[1024,768]{1,0:T(8,128)}, f32[1024,128]{1,0:T(8,128)}, bf16[1024,3072]{1,0:T(8,128)(2,1)}, bf16[1024,3072]{1,0:T(8,128)(2,1)}) custom-call(s32[1]{0:T(128)} %bitcast.me, bf16[1024,768]{1,0:T(8,128)(2,1)} %get-tuple-element.73.mixed, bf16[1024,768]{1,0:T(8,128)(2,1)} %bitcast.175, ...), custom_call_target="tpu_custom_call" | custom-call | flops 18119393280 | bytes 15000000 | tf_op jit(solution)/shard_map/pallas_call | solution.py:391
  122.3 24.1 %turn.1 = (bf16[1024,768]{1,0:T(8,128)(2,1)}, bf16[1024,768]{1,0:T(8,128)(2,1)}, bf16[1024,3072]{1,0:T(8,128)(2,1)}, f32[1024,768]{1,0:T(8,128)}, f32[8,768]{1,0:T(8,128)}, /*index=5*/f32[1,3072]{1,0:T(1,128)}) custom-call(s32[2]{0:T(128)} %lens.3, s32[1]{0:T(128)} %bitcast.me, bf16[1024,3072]{1,0:T(8,128)(2,1)} %get-tuple-element.76.active, ...), custom_call_target="tpu_custom_call" | custom-call | flops 9663676416 | bytes 30000000 | tf_op jit(solution)/shard_map/turn/pallas_call | solution.py:462
  146.4 11.3 %back_weight.1 = (bf16[4,384,768]{2,1,0:T(8,128)(2,1)}, bf16[4,384,768]{2,1,0:T(8,128)(2,1)}) custom-call(s32[1]{0:T(128)} %bitcast.me, bf16[1024,3072]{1,0:T(8,128)(2,1)} %get-tuple-element.76.active, bf16[1024,768]{1,0:T(8,128)(2,1)} %get-tuple-element.82.grad), custom_call_target="tpu_custom_call" | custom-call | flops 4831838208 | bytes 13000000 | tf_op jit(solution)/shard_map/back_weight/pallas_call | solution.py:614
  157.8 16.8 %shard_map.306 = (f32[1024,768]{1,0:T(8,128)}, bf16[1024,768]{1,0:T(8,128)(2,1)}, bf16[1024,768]{1,0:T(8,128)(2,1)}, f32[8,768]{1,0:T(8,128)}) custom-call(s32[1]{0:T(128)} %bitcast.me, bf16[1024,3072]{1,0:T(8,128)(2,1)} %get-tuple-element.84.hidden_grad, f32[1024,768]{1,0:T(8,128)} %get-tuple-element.85.h2_grad, f32[1024,768]{1,0:T(8,128)} %get-tuple-element.77.normed1, ...), custom_call_target="tpu_custom_call" | custom-call | flops 6039797760 | bytes 15000000 | tf_op jit(solution)/shard_map/pallas_call | solution.py:512
  174.6 13.3 %in_out_weight.1 = (bf16[4,480,768]{2,1,0:T(8,128)(2,1)}, bf16[4,480,768]{2,1,0:T(8,128)(2,1)}) custom-call(s32[1]{0:T(128)} %bitcast.me, bf16[1024,768]{1,0:T(8,128)(2,1)} %get-tuple-element.90.after, bf16[1024,3072]{1,0:T(8,128)(2,1)} %get-tuple-element.84.hidden_grad, bf16[1024,768]{1,0:T(8,128)(2,1)} %get-tuple-element.73.mixed, ...), custom_call_target="tpu_custom_call" | custom-call | flops 6039797760 | bytes 20000000 | tf_op jit(solution)/shard_map/in_out_weight/pallas_call | solution.py:656
  188.3 2.9 add_convert_fusion.1
  193.4 13.4 %collective-permute-done.25 = bf16[2,192,768]{2,1,0:T(8,128)(2,1)S(1)} collective-permute-done((bf16[2,192,768]{2,1,0:T(8,128)(2,1)S(1)}, bf16[2,192,768]{2,1,0:T(8,128)(2,1)S(1)}, u32[]{:S(2)}, u32[]{:S(2)}) %collective-permute-start.25) | collective-permute-done | bytes 589856 | tf_op jit(solution)/shard_map/ppermute | solution.py:28
  212.7 5.4 %collective-permute-done.26 = bf16[192,768]{1,0:T(8,128)(2,1)} collective-permute-done((bf16[192,768]{1,0:T(8,128)(2,1)}, bf16[192,768]{1,0:T(8,128)(2,1)}, u32[]{:S(2)}, u32[]{:S(2)}) %collective-permute-start.26) | collective-permute-done | bytes 294944 | tf_op jit(solution)/shard_map/ppermute | solution.py:28
  221.9 3.4 add_convert_fusion
  231.6 12.1 %shard_map.307 = (bf16[3,1024,768]{2,1,0:T(8,128)(2,1)}, f32[1,2,768]{2,1,0:T(2,128)}) custom-call(bf16[1024,768]{1,0:T(8,128)(2,1)} %get-tuple-element.96.q, bf16[1024,768]{1,0:T(8,128)(2,1)} %get-tuple-element.97.k, bf16[1024,768]{1,0:T(8,128)(2,1)} %get-tuple-element.98.v, bf16[1024,768]{1,0:T(8,128)(2,1)} %get-tuple-element.103.grad, ...), custom_call_target="tpu_custom_call" | custom-call | flops 2818572288 | bytes 15000000 | tf_op jit(solution)/shard_map/pallas_call | solution.py:314
  243.7 12.3 %shard_map.308 = (bf16[3,1024,768]{2,1,0:T(8,128)(2,1)}, f32[1,2,768]{2,1,0:T(2,128)}) custom-call(bf16[1024,768]{1,0:T(8,128)(2,1)} %get-tuple-element.96.q, bf16[1024,768]{1,0:T(8,128)(2,1)} %get-tuple-element.97.k, bf16[1024,768]{1,0:T(8,128)(2,1)} %get-tuple-element.98.v, ...), custom_call_target="tpu_custom_call", output_to_operand_aliasing={{0}: (5, {})} | custom-call | flops 2818572288 | bytes 15000000 | tf_op jit(solution)/shard_map/pallas_call | solution.py:314
  256.1 9.5 %qkv_weight.1 = (bf16[4,304,768]{2,1,0:T(8,128)(2,1)}, bf16[4,304,768]{2,1,0:T(8,128)(2,1)}) custom-call(s32[1]{0:T(128)} %bitcast.me, bf16[1024,768]{1,0:T(8,128)(2,1)} %bitcast.176, bf16[3,1024,768]{2,1,0:T(8,128)(2,1)} %get-tuple-element.105.grads, f32[8,768]{1,0:T(8,128)} %get-tuple-element.106.sums1, f32[8,768]{1,0:T(8,128)} %get-tuple-element.107.sums2, ...), custom_call_target="tpu_custom_call" | custom-call | flops 3623878656 | bytes 10000000 | tf_op jit(solution)/shard_map/qkv_weight/pallas_call | solution.py:735
  269.5 2.7 collective-permute-start.30
  272.1 6.2 %collective-permute-done.33 = bf16[240,768]{1,0:T(8,128)(2,1)S(1)} collective-permute-done((bf16[240,768]{1,0:T(8,128)(2,1)S(1)}, bf16[240,768]{1,0:T(8,128)(2,1)S(1)}, u32[]{:S(2)}, u32[]{:S(2)}) %collective-permute-start.33) | collective-permute-done | bytes 368672 | tf_op jit(solution)/shard_map/ppermute | solution.py:28
  280.2 2.1 add_convert_fusion.2
  283.3 2.3 collective-permute-done.30
  287.1 6.4 %collective-permute-done.36 = bf16[240,768]{1,0:T(8,128)(2,1)S(1)} collective-permute-done((bf16[240,768]{1,0:T(8,128)(2,1)S(1)}, bf16[240,768]{1,0:T(8,128)(2,1)S(1)}, u32[]{:S(2)}, u32[]{:S(2)}) %collective-permute-start.36) | collective-permute-done | bytes 368672 | tf_op jit(solution)/shard_map/ppermute | solution.py:28
  295.4 4.6 %collective-permute-done.40 = bf16[2,160,768]{2,1,0:T(8,128)(2,1)S(1)} collective-permute-done((bf16[2,160,768]{2,1,0:T(8,128)(2,1)S(1)}, bf16[2,160,768]{2,1,0:T(8,128)(2,1)S(1)}, u32[]{:S(2)}, u32[]{:S(2)}) %collective-permute-start.40) | collective-permute-done | bytes 491552 | tf_op jit(solution)/shard_map/ppermute | solution.py:28
  301.7 3.2 collective-permute-start.45
  306.5 2.1 collective-permute-start.42
  309.7 9.2 %collective-permute-done.45 = bf16[240,768]{1,0:T(8,128)(2,1)S(1)} collective-permute-done((bf16[240,768]{1,0:T(8,128)(2,1)S(1)}, bf16[240,768]{1,0:T(8,128)(2,1)S(1)}, u32[]{:S(2)}, u32[]{:S(2)}) %collective-permute-start.45) | collective-permute-done | bytes 368672 | tf_op jit(solution)/shard_map/ppermute | solution.py:28
  321.0 9.7 %input_grad.1 = bf16[1024,768]{1,0:T(8,128)(2,1)} custom-call(s32[1]{0:T(128)} %bitcast.me, f32[1024,768]{1,0:T(8,128)} %get-tuple-element.112.h1_grad, bf16[3,1024,768]{2,1,0:T(8,128)(2,1)} %get-tuple-element.105.grads, bf16[288,768]{1,0:T(8,128)(2,1)} %copy-done.9, bf16[288,768]{1,0:T(8,128)(2,1)} %copy-done.17, ...), custom_call_target="tpu_custom_call" | custom-call | flops 3623878656 | bytes 20000000 | tf_op jit(solution)/shard_map/input_grad/pallas_call | solution.py:546
  331.6 2.7 collective-permute-start.44
  336.5 2.7 collective-permute-done.44.other
  (169 shorter events, 66.9 us)
Async XLA Ops:
  3.5 25.1 %collective-permute-start.3 = (bf16[288,768]{1,0:T(8,128)(2,1)S(1)}, bf16[288,768]{1,0:T(8,128)(2,1)S(1)}, u32[]{:S(2)}, u32[]{:S(2)}) collective-permute-start(bf16[288,768]{1,0:T(8,128)(2,1)S(1)} %constant_dynamic-update-slice_fusion.refs_0_), channel_id=1, source_target_pairs={{0,8},{1,9},{2,10},{3,11},{4,12},{5,13},{6,14},{7,15},{8,0},{9,1},... | collective-permute-start | bytes 1327112 | tf_op jit(solution)/shard_map/ppermute | solution.py:28
  6.5 25.8 %collective-permute-start.4 = (bf16[288,768]{1,0:T(8,128)(2,1)S(1)}, bf16[288,768]{1,0:T(8,128)(2,1)}, u32[]{:S(2)}, u32[]{:S(2)}) collective-permute-start(bf16[288,768]{1,0:T(8,128)(2,1)S(1)} %constant_dynamic-update-slice_fusion.refs_0_), channel_id=1, source_target_pairs={{0,16},{1,17},{2,18},{3,19},{4,20},{5,21},{6,22},{7,23},{8,24},{9,... | collective-permute-start | bytes 1327112 | tf_op jit(solution)/shard_map/ppermute | solution.py:28
  8.1 24.8 %collective-permute-start.5 = (bf16[288,768]{1,0:T(8,128)(2,1)S(1)}, bf16[288,768]{1,0:T(8,128)(2,1)}, u32[]{:S(2)}, u32[]{:S(2)}) collective-permute-start(bf16[288,768]{1,0:T(8,128)(2,1)S(1)} %constant_dynamic-update-slice_fusion.refs_0_), channel_id=1, source_target_pairs={{0,24},{1,25},{2,26},{3,27},{4,28},{5,29},{6,30},{7,31},{8,16},{9,... | collective-permute-start | bytes 1327112 | tf_op jit(solution)/shard_map/ppermute | solution.py:28
  8.1 27.6 %collective-permute-start.6 = (bf16[288,768]{1,0:T(8,128)(2,1)S(1)}, bf16[288,768]{1,0:T(8,128)(2,1)}, u32[]{:S(2)}, u32[]{:S(2)}) collective-permute-start(bf16[288,768]{1,0:T(8,128)(2,1)S(1)} %constant_dynamic-update-slice_fusion.refs_0_), channel_id=1, source_target_pairs={{0,4},{1,5},{2,6},{3,7},{4,0},{5,1},{6,2},{7,3},{8,12},{9,13},{10,... | collective-permute-start | bytes 1327112 | tf_op jit(solution)/shard_map/ppermute | solution.py:28
  10.7 17.1 %collective-permute-start = (f32[1,16,128]{2,1,0:T(8,128)}, f32[1,16,128]{2,1,0:T(8,128)S(1)}, u32[]{:S(2)}, u32[]{:S(2)}) collective-permute-start(f32[1,16,128]{2,1,0:T(8,128)} %bitcast.160), channel_id=1, source_target_pairs={{0,16},{1,17},{2,18},{3,19},{4,20},{5,21},{6,22},{7,23},{8,24},{9,... | collective-permute-start | bytes 24584 | tf_op jit(solution)/shard_map/ppermute | solution.py:28
  35.7 28.0 %collective-permute-start.10 = (bf16[480,768]{1,0:T(8,128)(2,1)S(1)}, bf16[480,768]{1,0:T(8,128)(2,1)S(1)}, u32[]{:S(2)}, u32[]{:S(2)}) collective-permute-start(bf16[480,768]{1,0:T(8,128)(2,1)S(1)} %slice_dynamic-update-slice_fusion.refs_0_), channel_id=1, source_target_pairs={{0,8},{1,9},{2,10},{3,11},{4,12},{5,13},{6,14},{7,15},{8,0},{9,1},... | collective-permute-start | bytes 2211848 | tf_op jit(solution)/shard_map/ppermute | solution.py:28
  35.7 33.7 %collective-permute-start.11 = (bf16[480,768]{1,0:T(8,128)(2,1)S(1)}, bf16[480,768]{1,0:T(8,128)(2,1)S(1)}, u32[]{:S(2)}, u32[]{:S(2)}) collective-permute-start(bf16[480,768]{1,0:T(8,128)(2,1)S(1)} %slice_dynamic-update-slice_fusion.refs_0_), channel_id=1, source_target_pairs={{0,16},{1,17},{2,18},{3,19},{4,20},{5,21},{6,22},{7,23},{8,24},{9,... | collective-permute-start | bytes 2211848 | tf_op jit(solution)/shard_map/ppermute | solution.py:28
  37.8 33.4 %collective-permute-start.12 = (bf16[480,768]{1,0:T(8,128)(2,1)S(1)}, bf16[480,768]{1,0:T(8,128)(2,1)}, u32[]{:S(2)}, u32[]{:S(2)}) collective-permute-start(bf16[480,768]{1,0:T(8,128)(2,1)S(1)} %slice_dynamic-update-slice_fusion.refs_0_), channel_id=1, source_target_pairs={{0,24},{1,25},{2,26},{3,27},{4,28},{5,29},{6,30},{7,31},{8,16},{9,... | collective-permute-start | bytes 2211848 | tf_op jit(solution)/shard_map/ppermute | solution.py:28
  40.9 31.5 %collective-permute-start.13 = (bf16[480,768]{1,0:T(8,128)(2,1)S(1)}, bf16[480,768]{1,0:T(8,128)(2,1)}, u32[]{:S(2)}, u32[]{:S(2)}) collective-permute-start(bf16[480,768]{1,0:T(8,128)(2,1)S(1)} %slice_dynamic-update-slice_fusion.refs_0_), channel_id=1, source_target_pairs={{0,4},{1,5},{2,6},{3,7},{4,0},{5,1},{6,2},{7,3},{8,12},{9,13},{10,... | collective-permute-start | bytes 2211848 | tf_op jit(solution)/shard_map/ppermute | solution.py:28
  71.1 14.9 %collective-permute-start.17 = (bf16[384,768]{1,0:T(8,128)(2,1)}, bf16[384,768]{1,0:T(8,128)(2,1)}, u32[]{:S(2)}, u32[]{:S(2)}) collective-permute-start(bf16[384,768]{1,0:T(8,128)(2,1)} %refs_0_), channel_id=1, source_target_pairs={{0,8},{1,9},{2,10},{3,11},{4,12},{5,13},{6,14},{7,15},{8,0},{9,1},... | collective-permute-start | bytes 1769480 | tf_op jit(solution)/shard_map/ppermute | solution.py:28
  71.8 29.6 %collective-permute-start.14 = (bf16[480,768]{1,0:T(8,128)(2,1)S(1)}, bf16[480,768]{1,0:T(8,128)(2,1)S(1)}, u32[]{:S(2)}, u32[]{:S(2)}) collective-permute-start(bf16[480,768]{1,0:T(8,128)(2,1)S(1)} %collective-permute-done.10.refs_1_), channel_id=1, source_target_pairs={{0,4},{1,5},{2,6},{3,7},{4,0},{5,1},{6,2},{7,3},{8,12},{9,13},{10,... | collective-permute-start | bytes 2211848 | tf_op jit(solution)/shard_map/ppermute | solution.py:28
  71.8 29.7 %collective-permute-start.15 = (bf16[480,768]{1,0:T(8,128)(2,1)S(1)}, bf16[480,768]{1,0:T(8,128)(2,1)S(1)}, u32[]{:S(2)}, u32[]{:S(2)}) collective-permute-start(bf16[480,768]{1,0:T(8,128)(2,1)S(1)} %collective-permute-done.11.refs_2_), channel_id=1, source_target_pairs={{0,4},{1,5},{2,6},{3,7},{4,0},{5,1},{6,2},{7,3},{8,12},{9,13},{10,... | collective-permute-start | bytes 2211848 | tf_op jit(solution)/shard_map/ppermute | solution.py:28
  72.4 30.5 %collective-permute-start.16 = (bf16[480,768]{1,0:T(8,128)(2,1)}, bf16[480,768]{1,0:T(8,128)(2,1)}, u32[]{:S(2)}, u32[]{:S(2)}) collective-permute-start(bf16[480,768]{1,0:T(8,128)(2,1)} %collective-permute-done.12.refs_3_), channel_id=1, source_target_pairs={{0,4},{1,5},{2,6},{3,7},{4,0},{5,1},{6,2},{7,3},{8,12},{9,13},{10,... | collective-permute-start | bytes 2211848 | tf_op jit(solution)/shard_map/ppermute | solution.py:28
  72.4 28.6 %collective-permute-start.18 = (bf16[384,768]{1,0:T(8,128)(2,1)}, bf16[384,768]{1,0:T(8,128)(2,1)S(1)}, u32[]{:S(2)}, u32[]{:S(2)}) collective-permute-start(bf16[384,768]{1,0:T(8,128)(2,1)} %refs_0_), channel_id=1, source_target_pairs={{0,16},{1,17},{2,18},{3,19},{4,20},{5,21},{6,22},{7,23},{8,24},{9,... | collective-permute-start | bytes 1769480 | tf_op jit(solution)/shard_map/ppermute | solution.py:28
  86.0 15.0 %collective-permute-start.19 = (bf16[384,768]{1,0:T(8,128)(2,1)}, bf16[384,768]{1,0:T(8,128)(2,1)S(1)}, u32[]{:S(2)}, u32[]{:S(2)}) collective-permute-start(bf16[384,768]{1,0:T(8,128)(2,1)} %refs_0_), channel_id=1, source_target_pairs={{0,24},{1,25},{2,26},{3,27},{4,28},{5,29},{6,30},{7,31},{8,16},{9,... | collective-permute-start | bytes 1769480 | tf_op jit(solution)/shard_map/ppermute | solution.py:28
  101.0 21.3 %collective-permute-start.20 = (bf16[384,768]{1,0:T(8,128)(2,1)}, bf16[384,768]{1,0:T(8,128)(2,1)}, u32[]{:S(2)}, u32[]{:S(2)}) collective-permute-start(bf16[384,768]{1,0:T(8,128)(2,1)} %refs_0_), channel_id=1, source_target_pairs={{0,4},{1,5},{2,6},{3,7},{4,0},{5,1},{6,2},{7,3},{8,12},{9,13},{10,... | collective-permute-start | bytes 1769480 | tf_op jit(solution)/shard_map/ppermute | solution.py:28
  101.0 21.3 %collective-permute-start.21 = (bf16[384,768]{1,0:T(8,128)(2,1)}, bf16[384,768]{1,0:T(8,128)(2,1)}, u32[]{:S(2)}, u32[]{:S(2)}) collective-permute-start(bf16[384,768]{1,0:T(8,128)(2,1)} %collective-permute-done.17.refs_1_), channel_id=1, source_target_pairs={{0,4},{1,5},{2,6},{3,7},{4,0},{5,1},{6,2},{7,3},{8,12},{9,13},{10,... | collective-permute-start | bytes 1769480 | tf_op jit(solution)/shard_map/ppermute | solution.py:28
  101.5 20.8 %collective-permute-start.22 = (bf16[384,768]{1,0:T(8,128)(2,1)S(1)}, bf16[384,768]{1,0:T(8,128)(2,1)}, u32[]{:S(2)}, u32[]{:S(2)}) collective-permute-start(bf16[384,768]{1,0:T(8,128)(2,1)S(1)} %collective-permute-done.18.refs_2_), channel_id=1, source_target_pairs={{0,4},{1,5},{2,6},{3,7},{4,0},{5,1},{6,2},{7,3},{8,12},{9,13},{10,... | collective-permute-start | bytes 1769480 | tf_op jit(solution)/shard_map/ppermute | solution.py:28
  102.5 19.8 %collective-permute-start.23 = (bf16[384,768]{1,0:T(8,128)(2,1)S(1)}, bf16[384,768]{1,0:T(8,128)(2,1)}, u32[]{:S(2)}, u32[]{:S(2)}) collective-permute-start(bf16[384,768]{1,0:T(8,128)(2,1)S(1)} %collective-permute-done.19.refs_3_), channel_id=1, source_target_pairs={{0,4},{1,5},{2,6},{3,7},{4,0},{5,1},{6,2},{7,3},{8,12},{9,13},{10,... | collective-permute-start | bytes 1769480 | tf_op jit(solution)/shard_map/ppermute | solution.py:28
  157.7 16.9 %collective-permute-start.24 = (bf16[4,384,768]{2,1,0:T(8,128)(2,1)}, bf16[4,384,768]{2,1,0:T(8,128)(2,1)S(1)}, u32[]{:S(2)}, u32[]{:S(2)}) collective-permute-start(bf16[4,384,768]{2,1,0:T(8,128)(2,1)} %get-tuple-element.89), channel_id=1, source_target_pairs={{0,4},{1,5},{2,6},{3,7},{4,0},{5,1},{6,2},{7,3},{8,12},{9,13},{10,... | collective-permute-start | bytes 7077896 | tf_op jit(solution)/shard_map/ppermute | solution.py:28
  188.0 32.3 %collective-permute-start.31 = (bf16[4,480,768]{2,1,0:T(8,128)(2,1)}, bf16[4,480,768]{2,1,0:T(8,128)(2,1)S(1)}, u32[]{:S(2)}, u32[]{:S(2)}) collective-permute-start(bf16[4,480,768]{2,1,0:T(8,128)(2,1)} %get-tuple-element.94), channel_id=1, source_target_pairs={{0,4},{1,5},{2,6},{3,7},{4,0},{5,1},{6,2},{7,3},{8,12},{9,13},{10,... | collective-permute-start | bytes 8847368 | tf_op jit(solution)/shard_map/ppermute | solution.py:28
  191.3 15.5 %collective-permute-start.25 = (bf16[2,192,768]{2,1,0:T(8,128)(2,1)S(1)}, bf16[2,192,768]{2,1,0:T(8,128)(2,1)S(1)}, u32[]{:S(2)}, u32[]{:S(2)}) collective-permute-start(bf16[2,192,768]{2,1,0:T(8,128)(2,1)S(1)} %slice_bitcast_fusion.6), channel_id=1, source_target_pairs={{0,8},{1,9},{2,10},{3,11},{4,12},{5,13},{6,14},{7,15},{8,0},{9,1},... | collective-permute-start | bytes 1769480 | tf_op jit(solution)/shard_map/ppermute | solution.py:28
  192.7 15.2 %collective-permute-start.27 = (bf16[2,192,768]{2,1,0:T(8,128)(2,1)S(1)}, bf16[2,192,768]{2,1,0:T(8,128)(2,1)S(1)}, u32[]{:S(2)}, u32[]{:S(2)}) collective-permute-start(bf16[2,192,768]{2,1,0:T(8,128)(2,1)S(1)} %slice_bitcast_fusion.4), channel_id=1, source_target_pairs={{0,16},{1,17},{2,18},{3,19},{4,20},{5,21},{6,22},{7,23},{8,24},{9,... | collective-permute-start | bytes 1769480 | tf_op jit(solution)/shard_map/ppermute | solution.py:28
  227.1 28.9 %collective-permute-start.32 = (bf16[2,240,768]{2,1,0:T(8,128)(2,1)}, bf16[2,240,768]{2,1,0:T(8,128)(2,1)}, u32[]{:S(2)}, u32[]{:S(2)}) collective-permute-start(bf16[2,240,768]{2,1,0:T(8,128)(2,1)} %slice_bitcast_fusion.2), channel_id=1, source_target_pairs={{0,8},{1,9},{2,10},{3,11},{4,12},{5,13},{6,14},{7,15},{8,0},{9,1},... | collective-permute-start | bytes 2211848 | tf_op jit(solution)/shard_map/ppermute | solution.py:28
  228.6 27.5 %collective-permute-start.34 = (bf16[2,240,768]{2,1,0:T(8,128)(2,1)}, bf16[2,240,768]{2,1,0:T(8,128)(2,1)}, u32[]{:S(2)}, u32[]{:S(2)}) collective-permute-start(bf16[2,240,768]{2,1,0:T(8,128)(2,1)} %slice_bitcast_fusion), channel_id=1, source_target_pairs={{0,16},{1,17},{2,18},{3,19},{4,20},{5,21},{6,22},{7,23},{8,24},{9,... | collective-permute-start | bytes 2211848 | tf_op jit(solution)/shard_map/ppermute | solution.py:28
  230.0 26.0 %collective-permute-start.29 = (bf16[192,768]{1,0:T(8,128)(2,1)}, bf16[192,768]{1,0:T(8,128)(2,1)S(1)}, u32[]{:S(2)}, u32[]{:S(2)}) collective-permute-start(bf16[192,768]{1,0:T(8,128)(2,1)} %dynamic-slice_bitcast_fusion.1), channel_id=1, source_target_pairs={{0,1},{1,0},{2,3},{3,2},{4,5},{5,4},{6,7},{7,6},{8,9},{9,8},{10,11... | collective-permute-start | bytes 884744 | tf_op jit(solution)/shard_map/ppermute | solution.py:28
  265.6 14.7 %collective-permute-start.37 = (bf16[4,304,768]{2,1,0:T(8,128)(2,1)}, bf16[4,304,768]{2,1,0:T(8,128)(2,1)}, u32[]{:S(2)}, u32[]{:S(2)}) collective-permute-start(bf16[4,304,768]{2,1,0:T(8,128)(2,1)} %get-tuple-element.111), channel_id=1, source_target_pairs={{0,4},{1,5},{2,6},{3,7},{4,0},{5,1},{6,2},{7,3},{8,12},{9,13},{10,... | collective-permute-start | bytes 5603336 | tf_op jit(solution)/shard_map/ppermute | solution.py:28
  269.5 16.1 %collective-permute-start.30 = (bf16[192,768]{1,0:T(8,128)(2,1)S(1)}, bf16[192,768]{1,0:T(8,128)(2,1)S(1)}, u32[]{:S(2)}, u32[]{:S(2)}) collective-permute-start(bf16[192,768]{1,0:T(8,128)(2,1)S(1)} %fusion.10), channel_id=1, source_target_pairs={{0,2},{1,3},{2,0},{3,1},{4,6},{5,7},{6,4},{7,5},{8,10},{9,11},{10,... | collective-permute-start | bytes 884744 | tf_op jit(solution)/shard_map/ppermute | solution.py:28
  285.7 22.9 %collective-permute-start.47 = (bf16[192,768]{1,0:T(8,128)(2,1)S(1)}, bf16[192,768]{1,0:T(8,128)(2,1)S(1)}, u32[]{:S(2)}, u32[]{:S(2)}) collective-permute-start(bf16[192,768]{1,0:T(8,128)(2,1)S(1)} %add_convert_fusion.4), channel_id=1, source_target_pairs={{0,1},{1,0},{2,3},{3,2},{4,5},{5,4},{6,7},{7,6},{8,9},{9,8},{10,11... | collective-permute-start | bytes 884744 | tf_op jit(solution)/shard_map/ppermute | solution.py:28
  285.8 14.2 %collective-permute-start.40 = (bf16[2,160,768]{2,1,0:T(8,128)(2,1)S(1)}, bf16[2,160,768]{2,1,0:T(8,128)(2,1)S(1)}, u32[]{:S(2)}, u32[]{:S(2)}) collective-permute-start(bf16[2,160,768]{2,1,0:T(8,128)(2,1)S(1)} %slice_bitcast_fusion.9), channel_id=1, source_target_pairs={{0,16},{1,17},{2,18},{3,19},{4,20},{5,21},{6,22},{7,23},{8,24},{9,... | collective-permute-start | bytes 1474568 | tf_op jit(solution)/shard_map/ppermute | solution.py:28
  301.7 17.2 %collective-permute-start.45 = (bf16[240,768]{1,0:T(8,128)(2,1)S(1)}, bf16[240,768]{1,0:T(8,128)(2,1)S(1)}, u32[]{:S(2)}, u32[]{:S(2)}) collective-permute-start(bf16[240,768]{1,0:T(8,128)(2,1)S(1)} %fusion.6), channel_id=1, source_target_pairs={{0,2},{1,3},{2,0},{3,1},{4,6},{5,7},{6,4},{7,5},{8,10},{9,11},{10,... | collective-permute-start | bytes 1105928 | tf_op jit(solution)/shard_map/ppermute | solution.py:28
  319.0 15.3 %collective-permute-start.46 = (bf16[240,768]{1,0:T(8,128)(2,1)S(1)}, bf16[240,768]{1,0:T(8,128)(2,1)S(1)}, u32[]{:S(2)}, u32[]{:S(2)}) collective-permute-start(bf16[240,768]{1,0:T(8,128)(2,1)S(1)} %add_convert_fusion.3), channel_id=1, source_target_pairs={{0,1},{1,0},{2,3},{3,2},{4,5},{5,4},{6,7},{7,6},{8,9},{9,8},{10,11... | collective-permute-start | bytes 1105928 | tf_op jit(solution)/shard_map/ppermute | solution.py:28
  (34 other events, 390.6 us)
